TPU v7x, 32 devices: a whole 2x2x4 slice. The times are simulated.
32 devices in a mesh: groups: 2 (over x), rows: 2 (over core), cols: 8 (over z, y).
Axes of the slice: x: 2, y: 2, z: 4, core: 2. Of those that a mesh axis runs over, the one named last changes fastest.
Arguments:
- texture: float32 [8192, 8192], P(('groups', 'rows'), 'cols'), parts along dimension 0, as said below
- sketch: float32 [8192, 256], P('cols'), may hold values from -0.0625 to 0.0625
Outputs:
- projected: float32 [512, 8192], P(('groups', 'rows'), 'cols'), parts along dimension 0
There are 2 independent parts, one for each index of `groups`. A program takes and returns all parts, laid end to end along the dimension named above; an argument that names none is the same for every part. Nothing has to cross between parts.
Inputs may be any that keep to these rules, and one draw needn't show every extreme that they name: `texture`: finite reals of moderate size.
All inputs are finite; a program needn't handle non-finite values.
Results may differ from a plain program's by a relative error of at most 0.00014.
Values sent between devices are 32-bit elements; how exact they have to be, the bound alone decides.
No kernel may reach another device: no remote copies, remote signals or barrier semaphores. Data moves between devices by JAX's collectives and lax.ppermute only.
A program may use at most 64 MiB of HBM per device.

v0:
```python
import jax
import jax.numpy as jnp
from jax import lax
from jax.sharding import PartitionSpec as P


def inner_rows(left, right):
    return lax.dot_general(
        left,
        right,
        (((0,), (0,)), ((), ())),
        precision=lax.Precision.HIGHEST,
        preferred_element_type=jnp.float32,
    )


def orthonormal(image, gram):
    lower = jnp.linalg.cholesky(gram)
    return lax.linalg.triangular_solve(lower, image, left_side=False, lower=True, transpose_a=True)


def per_device(texture, sketch):
    partial_image = jnp.dot(
        texture, sketch, precision=lax.Precision.HIGHEST, preferred_element_type=jnp.float32
    )
    image = lax.psum(partial_image, "cols")
    gram = lax.psum(inner_rows(image, image), "rows")
    basis = orthonormal(image, gram)
    return lax.psum_scatter(inner_rows(basis, texture), "rows", scatter_dimension=0, tiled=True)


def solution(mesh):
    placed = (P(("groups", "rows"), "cols"), P("cols", None))
    return jax.shard_map(
        per_device,
        mesh=mesh,
        in_specs=placed,
        out_specs=P(("groups", "rows"), "cols"),
        check_vma=False,
    )
```

profile of v0, /device:TPU:0, one launch (start us, length us, event | category | flops | bytes accessed | tf_op | source)
XLA Modules:
  0.0 244.9 jit_solution(6285239765288148525)
XLA Ops:
  6.5 1.2 copy-done
  7.8 10.0 %fusion.14 = f32[2048,256]{1,0:T(8,128)} fusion(f32[2048,1024]{1,0:T(8,128)} %param.2, f32[1024,256]{1,0:T(8,128)S(1)} %copy-done), kind=kOutput, calls=%fused_computation.33 | convolution fusion | flops 6442450944 | bytes 11534336 | tf_op jit(solution)/shard_map/dot_general | solution.py:23
  17.8 104.6 %all-reduce.4.cloned.1.call-done = f32[2048,256]{1,0:T(8,128)} async-done(((f32[2048,256]{1,0:T(8,128)}), f32[2048,256]{1,0:T(8,128)}) %all-reduce.4.cloned.1.call-update) | async-done | bytes 2097168 | tf_op jit(solution)/shard_map/psum | solution.py:26
  122.5 6.4 %fusion.15 = f32[256,256]{0,1:T(8,128)} fusion(f32[2048,256]{1,0:T(8,128)} %all-reduce.4.cloned.1.call-done), kind=kOutput, calls=%fused_computation.34 | convolution fusion | flops 1610612736 | bytes 2359296 | tf_op jit(solution)/shard_map/dot_general | solution.py:8
  129.1 17.9 %all-reduce.6.cloned.1.call-done = f32[256,256]{0,1:T(8,128)} async-done(((f32[256,256]{0,1:T(8,128)}), f32[256,256]{0,1:T(8,128)}) %all-reduce.6.cloned.1.call-update) | async-done | bytes 262160 | tf_op jit(solution)/shard_map/psum | solution.py:27
  147.0 1.1 copy.4
  148.1 1.0 fusion.6
  149.1 0.7 copy-done.3
  149.8 11.7 %cholesky.50 = f32[128,128]{1,0:T(8,128)S(1)} custom-call(f32[128,128]{1,0:T(8,128)S(1)} %cholesky.118), custom_call_target="Cholesky" | custom-call | tf_op jit(solution)/shard_map/jit(cholesky)/cholesky | solution.py:18
  161.6 9.8 %custom-call.14 = f32[1,128,128]{1,2,0:T(8,128)S(1)} custom-call(f32[1,128,128]{2,1,0:T(8,128)S(1)} %get-tuple-element.26), custom_call_target="InvertDiagBlocksLowerTriangular" | custom-call | tf_op jit(solution)/shard_map/jit(cholesky)/cholesky | solution.py:18
  171.4 1.0 constant_dynamic-update-slice_fusion.1
  172.5 1.1 convolution_subtract_fusion.1
  173.6 11.7 %cholesky.105 = f32[128,128]{1,0:T(8,128)S(1)} custom-call(f32[128,128]{1,0:T(8,128)S(1)} %convolution_subtract_fusion.1), custom_call_target="Cholesky" | custom-call | tf_op jit(solution)/shard_map/jit(cholesky)/cholesky | solution.py:18
  185.3 0.7 compare_reduce_fusion
  187.2 1.0 select_select_fusion
  188.3 5.3 %while.1 = (s32[]{:T(128)}, f32[256,256]{1,0:T(8,128)S(1)}, s32[2,2]{1,0:T(2,128)S(1)}, f32[2,128,128]{2,1,0:T(8,128)}, s32[]{:T(128)}) while((s32[]{:T(128)}, f32[256,256]{1,0:T(8,128)S(1)}, s32[2,2]{1,0:T(2,128)S(1)}, f32[2,128,128]{2,1,0:T(8,128)}, s32[]{:T(128)}) %tuple.23), condition=%wide.while_cond, body=%wide.while_body.sunk | while | flops 2 | bytes 132205 | solution.py:19
  189.1 2.0 bitcast_dynamic-update-slice_fusion.2
  191.6 2.0 bitcast_dynamic-update-slice_fusion.2
  193.6 20.5 %custom-call.15 = f32[2,128,128]{1,2,0:T(8,128)S(1)} custom-call(f32[2,128,128]{2,1,0:T(8,128)} %get-tuple-element.12), custom_call_target="InvertDiagBlocksLowerTriangular" | custom-call | tf_op jit(solution)/shard_map/triangular_solve | solution.py:19
  214.1 1.1 fusion.4
  215.2 1.8 convolution_subtract_fusion
  217.0 1.1 fusion.7
  218.1 10.4 %fusion = f32[256,1024]{1,0:T(8,128)} fusion(f32[2048,1024]{1,0:T(8,128)} %param.2, f32[2048,128]{0,1:T(8,128)S(1)} %fusion.7, f32[2048,128]{0,1:T(8,128)S(1)} %fusion.4), kind=kOutput, calls=%fused_computation.3 | convolution fusion | flops 6442975232 | bytes 11534336 | tf_op jit(solution)/shard_map/dot_general | solution.py:8
  228.5 9.9 %reduce-scatter.2.cloned.1.call-done = f32[128,1024]{1,0:T(8,128)} async-done(((f32[256,1024]{1,0:T(8,128)}), f32[128,1024]{1,0:T(8,128)}) %reduce-scatter.2.cloned.1.call-update) | async-done | bytes 524304 | tf_op jit(solution)/shard_map/reduce_scatter | solution.py:29
  (23 shorter events, 1.7 us)
Async XLA Ops:
  6.5 1.2 copy-start
  6.5 115.9 %all-reduce.4.cloned.1.call-start = ((), (), s32[]{:S(2)}) async-start(), calls=%async_computation.1 | async-start | bytes 4194304 | tf_op jit(solution)/shard_map/psum | solution.py:26
  17.8 129.2 %all-reduce.6.cloned.1.call-start = ((), (), s32[]{:S(2)}) async-start(), calls=%async_computation.2 | async-start | bytes 524288 | tf_op jit(solution)/shard_map/psum | solution.py:27
  128.9 85.3 %copy-start.1 = (f32[2048,256]{1,0:T(8,128)S(1)}, f32[2048,256]{1,0:T(8,128)}, u32[]{:S(2)}) copy-start(f32[2048,256]{1,0:T(8,128)} %all-reduce.4.cloned.1.call-done) | copy-start | bytes 6291460
  128.9 109.5 %reduce-scatter.2.cloned.1.call-start = ((), (), s32[]{:S(2)}) async-start(), calls=%async_computation.3 | async-start | bytes 1572864 | tf_op jit(solution)/shard_map/reduce_scatter | solution.py:29
  149.1 0.7 copy-start.3
  185.3 1.9 copy-start.2
Sparse Core Ops, SparseCore 0:
  17.9 104.5 all-reduce.3
  129.0 17.9 all-reduce.5
  228.7 9.6 reduce-scatter.1
where the time goes:
time: 245 us
  waiting for transfers between devices  132 us (54%)
  other arithmetic  56.4 us (23%)
  matrix products  32.9 us (13%)
  between operations  14.5 us (6%)
  local copies, waits for them, and re-layouts  8.23 us (3%)
    psum x1, waiting for transfers between devices, per_device(): image = lax.psum(partial_image, 'cols')  105 us
    another operation x6, other arithmetic, orthonormal(): lower = jnp.linalg.cholesky(gram)  34 us
    another operation x3, other arithmetic, orthonormal(): lax.linalg.triangular_solve(lower, image, left_side=False, lower=True, tr...  21.5 us
    psum x1, waiting for transfers between devices, per_device(): gram = lax.psum(inner_rows(image, image), 'rows')  17.9 us
    dot_general x2, matrix products, inner_rows(): lax.dot_general(left, right, (((0,), (0,)), ((), ())), precision=lax.Prec...  16.8 us
    dot_general x1, matrix products, per_device(): jnp.dot(texture, sketch, precision=lax.Precision.HIGHEST, preferred_eleme...  10 us
    reduce_scatter x1, waiting for transfers between devices, per_device(): lax.psum_scatter(inner_rows(basis, texture), 'rows', scatter_dimension=0,...  9.86 us
    another operation x6, local copies, waits for them, and re-layouts  5.13 us
  transfers between devices with their start and end apart: 3, of which 3 were waited for; matrix products, arithmetic and copies ran while one was open for 0% of the time, Pallas kernels for 0%

commit v1 on v0

v1 whole, which is shorter than its diff:
```python
import jax
import jax.numpy as jnp
from jax import lax
from jax.sharding import PartitionSpec as P

HIGH = lax.Precision.HIGH
CHUNKS = 4


def inner_rows(left, right):
    return lax.dot_general(
        left,
        right,
        (((0,), (0,)), ((), ())),
        precision=HIGH,
        preferred_element_type=jnp.float32,
    )


def line_sum(part, place):
    inward = [(0 + y, 2 + y) for y in range(2)] + [(6 + y, 4 + y) for y in range(2)]
    across = [(2 + y, 4 + y) for y in range(2)] + [(4 + y, 2 + y) for y in range(2)]
    outward = [(2 + y, 0 + y) for y in range(2)] + [(4 + y, 6 + y) for y in range(2)]
    part = part + lax.ppermute(part, "cols", inward)
    part = part + lax.ppermute(part, "cols", across)
    far = lax.ppermute(part, "cols", outward)
    return jnp.where((place == 1) | (place == 2), part, far)


def per_device(texture, sketch):
    cols = lax.axis_size("cols")
    rows = texture.shape[0]
    gram = jnp.zeros((sketch.shape[1],) * 2, jnp.float32)
    product = jnp.zeros((sketch.shape[1], texture.shape[1]), jnp.float32)
    if cols == 8:
        col = lax.axis_index("cols")
        side, place = lax.rem(col, 2), lax.div(col, 2)
        swap = [(c, c ^ 1) for c in range(cols)]
        span = rows // (2 * CHUNKS)
        blocks, halves = [], []
        for chunk in range(CHUNKS):
            own = lax.dynamic_slice_in_dim(texture, (2 * chunk + side) * span, span)
            other = lax.dynamic_slice_in_dim(texture, (2 * chunk + 1 - side) * span, span)
            theirs = jnp.dot(other, sketch, precision=HIGH, preferred_element_type=jnp.float32)
            mine = jnp.dot(own, sketch, precision=HIGH, preferred_element_type=jnp.float32)
            mine = mine + lax.ppermute(theirs, "cols", swap)
            image = line_sum(mine, place)
            halves.append((own, image))
            halves.append((other, lax.ppermute(image, "cols", swap)))
        for block, image in halves:
            gram = gram + inner_rows(image, image)
            product = product + inner_rows(image, block)
    else:
        image = lax.psum(jnp.dot(texture, sketch, precision=HIGH, preferred_element_type=jnp.float32), "cols")
        gram = inner_rows(image, image)
        product = inner_rows(image, texture)
    pair = [(0, 1), (1, 0)]
    gram = gram + lax.ppermute(gram, "rows", pair)
    product = product + lax.ppermute(product, "rows", pair)
    lower = jnp.linalg.cholesky(gram)
    eye = jnp.eye(gram.shape[0], dtype=jnp.float32)
    inverse = lax.linalg.triangular_solve(lower, eye, left_side=True, lower=True)
    span = gram.shape[0] // lax.axis_size("rows")
    inverse = lax.dynamic_slice_in_dim(inverse, lax.axis_index("rows") * span, span)
    return jnp.dot(inverse, product, precision=HIGH, preferred_element_type=jnp.float32)


def solution(mesh):
    placed = (P(("groups", "rows"), "cols"), P("cols", None))
    return jax.shard_map(
        per_device,
        mesh=mesh,
        in_specs=placed,
        out_specs=P(("groups", "rows"), "cols"),
        check_vma=False,
    )
```

time: 245 us -> 167 us (0.68)
  waiting for transfers between devices: 132 us -> 29.6 us
  starting transfers between devices: 0.27 us -> 32.8 us
  between operations: 14.5 us -> 1.91 us
  other arithmetic: 56.4 us -> 59.2 us
    psum x2 -> x0, waiting for transfers between devices: 123 us -> none  [the longest x1 105 us: per_device(): image = lax.psum(partial_image, 'cols')]
    ppermute x0 -> x22, starting transfers between devices: none -> 32.8 us  [the longest x4 13.5 us: line_sum(): part = part + lax.ppermute(part, 'cols', inward)]
    ppermute x0 -> x22, waiting for transfers between devices: none -> 29.6 us  [the longest x4 17.4 us: line_sum(): far = lax.ppermute(part, 'cols', outward)]
    reduce_scatter x1 -> x0, waiting for transfers between devices: 9.86 us -> none  [per_device(): lax.psum_scatter(inner_rows(basis, texture), 'rows', scatter_dimension=0,...]
    dot_general x3 -> x25, matrix products: 26.8 us -> 28.4 us  [the longest x16 12.5 us: inner_rows(): lax.dot_general(left, right, (((0,), (0,)), ((), ())), precision=HIGH, pr...]
  transfers between devices with their start and end apart: 3 -> 22, of which waited for: 3 -> 6; matrix products, arithmetic and copies ran while one was open for 0% -> 58% of each run, Pallas kernels for 0% -> 0%
where the time goes in v1:
time: 167 us; the launch traced here: 165 us
  other arithmetic  59.2 us (35%)
  matrix products  33.7 us (20%)
  starting transfers between devices  32.8 us (20%)
  waiting for transfers between devices  29.6 us (18%)
  local copies, waits for them, and re-layouts  8.18 us (5%)
  between operations  1.91 us (1%)
    another operation x6, other arithmetic, per_device(): lower = jnp.linalg.cholesky(gram)  35.6 us
    another operation x3, other arithmetic, per_device(): lax.linalg.triangular_solve(lower, eye, left_side=True, lower=True)  22.1 us
    ppermute x4, waiting for transfers between devices, line_sum(): far = lax.ppermute(part, 'cols', outward)  17.4 us
    ppermute x4, starting transfers between devices, line_sum(): part = part + lax.ppermute(part, 'cols', inward)  13.5 us
    dot_general x16, matrix products, inner_rows(): lax.dot_general(left, right, (((0,), (0,)), ((), ())), precision=HIGH, pr...  12.5 us
    ppermute x4, waiting for transfers between devices, per_device(): halves.append((other, lax.ppermute(image, 'cols', swap)))  8.3 us
    dot_general x4, matrix products, per_device(): jnp.dot(own, sketch, precision=HIGH, preferred_element_type=jnp.float32)  7.34 us
    dot_general x4, matrix products, per_device(): jnp.dot(other, sketch, precision=HIGH, preferred_element_type=jnp.float32)  7.3 us
  transfers between devices with their start and end apart: 22, of which 6 were waited for; matrix products, arithmetic and copies ran while one was open for 58% of the time, Pallas kernels for 0%

profile of v1, /device:TPU:0, one launch (start us, length us, event | category | flops | bytes accessed | tf_op | source)
XLA Modules:
  0.0 165.5 jit_solution(17618915995378276879)
XLA Ops:
  3.1 3.0 %collective-permute-start.15 = (f32[256,256]{1,0:T(8,128)S(1)}, f32[256,256]{1,0:T(8,128)S(1)}, u32[]{:S(2)}, u32[]{:S(2)}) collective-permute-start(f32[256,256]{1,0:T(8,128)S(1)} %fusion.16), channel_id=1, source_target_pairs={{0,1},{1,0},{2,3},{3,2},{4,5},{5,4},{6,7},{7,6},{8,9},{9,8},{10,11... | collective-permute-start | bytes 786440 | tf_op jit(solution)/shard_map/ppermute | solution.py:46
  9.8 2.1 %collective-permute-start.5 = (f32[256,256]{1,0:T(8,128)S(1)}, f32[256,256]{1,0:T(8,128)S(1)}, u32[]{:S(2)}, u32[]{:S(2)}) collective-permute-start(f32[256,256]{1,0:T(8,128)S(1)} %fusion.30), channel_id=1, source_target_pairs={{0,1},{1,0},{2,3},{3,2},{4,5},{5,4},{6,7},{7,6},{8,9},{9,8},{10,11... | collective-permute-start | bytes 786440 | tf_op jit(solution)/shard_map/ppermute | solution.py:46
  15.7 4.0 %collective-permute-start.16 = (f32[256,256]{1,0:T(8,128)S(1)}, f32[256,256]{1,0:T(8,128)S(1)}, u32[]{:S(2)}, u32[]{:S(2)}) collective-permute-start(f32[256,256]{1,0:T(8,128)S(1)} %convolution_add_fusion.2), channel_id=1, source_target_pairs={{0,2},{1,3},{6,4},{7,5},{8,10},{9,11},{14,12},{15,13},{16,18},{17,... | collective-permute-start | bytes 786440 | tf_op jit(solution)/shard_map/ppermute | solution.py:24
  19.7 1.8 %convolution_add_fusion.5 = f32[256,256]{1,0:T(8,128)S(1)} fusion(f32[256,256]{1,0:T(8,128)S(1)} %collective-permute-done, f32[1024,256]{1,0:T(8,128)S(1)} %copy-done, f32[2048,1024]{1,0:T(8,128)} %param.2, s32[]{:T(128)S(6)} %select_n.52), kind=kOutput, calls=%fused_computation.19 | convolution fusion | flops 402718720 | bytes 2621444 | tf_op jit(solution)/shard_map/dot_general | solution.py:45
  21.5 3.2 %collective-permute-start.1 = (f32[256,256]{1,0:T(8,128)S(1)}, f32[256,256]{1,0:T(8,128)S(1)}, u32[]{:S(2)}, u32[]{:S(2)}) collective-permute-start(f32[256,256]{1,0:T(8,128)S(1)} %convolution_add_fusion.5), channel_id=1, source_target_pairs={{0,2},{1,3},{6,4},{7,5},{8,10},{9,11},{14,12},{15,13},{16,18},{17,... | collective-permute-start | bytes 786440 | tf_op jit(solution)/shard_map/ppermute | solution.py:24
  24.7 1.8 %convolution_add_fusion.4 = f32[256,256]{1,0:T(8,128)S(1)} fusion(f32[256,256]{1,0:T(8,128)S(1)} %collective-permute-done.5, f32[1024,256]{1,0:T(8,128)S(1)} %copy-done, f32[2048,1024]{1,0:T(8,128)} %param.2, s32[]{:T(128)S(6)} %select_n.55), kind=kOutput, calls=%fused_computation.18 | convolution fusion | flops 402718720 | bytes 2621444 | tf_op jit(solution)/shard_map/dot_general | solution.py:45
  26.6 3.8 %collective-permute-start.6 = (f32[256,256]{1,0:T(8,128)S(1)}, f32[256,256]{1,0:T(8,128)S(1)}, u32[]{:S(2)}, u32[]{:S(2)}) collective-permute-start(f32[256,256]{1,0:T(8,128)S(1)} %convolution_add_fusion.4), channel_id=1, source_target_pairs={{0,2},{1,3},{6,4},{7,5},{8,10},{9,11},{14,12},{15,13},{16,18},{17,... | collective-permute-start | bytes 786440 | tf_op jit(solution)/shard_map/ppermute | solution.py:24
  30.4 1.8 %convolution_add_fusion.3 = f32[256,256]{1,0:T(8,128)S(1)} fusion(f32[256,256]{1,0:T(8,128)S(1)} %collective-permute-done.10, f32[1024,256]{1,0:T(8,128)S(1)} %copy-done, f32[2048,1024]{1,0:T(8,128)} %param.2, s32[]{:T(128)S(6)} %select_n.58), kind=kOutput, calls=%fused_computation.17 | convolution fusion | flops 402718720 | bytes 2621444 | tf_op jit(solution)/shard_map/dot_general | solution.py:45
  32.2 2.6 %collective-permute-start.11 = (f32[256,256]{1,0:T(8,128)S(1)}, f32[256,256]{1,0:T(8,128)S(1)}, u32[]{:S(2)}, u32[]{:S(2)}) collective-permute-start(f32[256,256]{1,0:T(8,128)S(1)} %convolution_add_fusion.3), channel_id=1, source_target_pairs={{0,2},{1,3},{6,4},{7,5},{8,10},{9,11},{14,12},{15,13},{16,18},{17,... | collective-permute-start | bytes 786440 | tf_op jit(solution)/shard_map/ppermute | solution.py:24
  37.4 3.5 %collective-permute-done.11 = f32[256,256]{1,0:T(8,128)S(1)} collective-permute-done((f32[256,256]{1,0:T(8,128)S(1)}, f32[256,256]{1,0:T(8,128)S(1)}, u32[]{:S(2)}, u32[]{:S(2)}) %collective-permute-start.11) | collective-permute-done | bytes 262176 | tf_op jit(solution)/shard_map/ppermute | solution.py:24
  47.3 8.2 %collective-permute-done.18 = f32[256,256]{1,0:T(8,128)S(1)} collective-permute-done((f32[256,256]{1,0:T(8,128)S(1)}, f32[256,256]{1,0:T(8,128)S(1)}, u32[]{:S(2)}, u32[]{:S(2)}) %collective-permute-start.18) | collective-permute-done | bytes 262176 | tf_op jit(solution)/shard_map/ppermute | solution.py:26
  57.5 9.2 %collective-permute-done.8 = f32[256,256]{1,0:T(8,128)S(1)} collective-permute-done((f32[256,256]{1,0:T(8,128)S(1)}, f32[256,256]{1,0:T(8,128)S(1)}, u32[]{:S(2)}, u32[]{:S(2)}) %collective-permute-start.8) | collective-permute-done | bytes 262176 | tf_op jit(solution)/shard_map/ppermute | solution.py:26
  66.8 1.9 %fusion.32 = f32[256,1024]{1,0:T(8,128)S(1)} fusion(f32[256,256]{1,0:T(8,128)S(1)} %broadcast_select_fusion.2, f32[2048,1024]{1,0:T(8,128)} %param.2, s32[]{:T(128)S(6)} %select_n.55), kind=kOutput, calls=%fused_computation.41 | convolution fusion | flops 402653184 | bytes 2359300 | tf_op jit(solution)/shard_map/dot_general | solution.py:11
  70.6 1.9 %fusion.18 = f32[256,1024]{1,0:T(8,128)S(1)} fusion(f32[256,256]{1,0:T(8,128)S(1)} %broadcast_select_fusion, f32[2048,1024]{1,0:T(8,128)} %param.2, s32[]{:T(128)S(6)} %select_n.61), kind=kOutput, calls=%fused_computation.27 | convolution fusion | flops 402653184 | bytes 2359300 | tf_op jit(solution)/shard_map/dot_general | solution.py:11
  72.5 2.0 %fusion.25 = f32[256,1024]{1,0:T(8,128)S(1)} fusion(f32[256,256]{1,0:T(8,128)S(1)} %broadcast_select_fusion.1, f32[2048,1024]{1,0:T(8,128)} %param.2, s32[]{:T(128)S(6)} %select_n.58), kind=kOutput, calls=%fused_computation.34 | convolution fusion | flops 402653184 | bytes 2359300 | tf_op jit(solution)/shard_map/dot_general | solution.py:11
  77.6 6.3 %collective-permute-done.4 = f32[256,256]{1,0:T(8,128)S(1)} collective-permute-done((f32[256,256]{1,0:T(8,128)S(1)}, f32[256,256]{1,0:T(8,128)S(1)}, u32[]{:S(2)}, u32[]{:S(2)}) %collective-permute-start.4) | collective-permute-done | bytes 262176 | tf_op jit(solution)/shard_map/ppermute | solution.py:49
  84.6 2.0 %collective-permute-done.14 = f32[256,256]{1,0:T(8,128)S(1)} collective-permute-done((f32[256,256]{1,0:T(8,128)S(1)}, f32[256,256]{1,0:T(8,128)S(1)}, u32[]{:S(2)}, u32[]{:S(2)}) %collective-permute-start.14) | collective-permute-done | bytes 262176 | tf_op jit(solution)/shard_map/ppermute | solution.py:49
  94.4 11.9 %cholesky.50 = f32[128,128]{1,0:T(8,128)S(1)} custom-call(f32[128,128]{1,0:T(8,128)S(1)} %cholesky.118), custom_call_target="Cholesky" | custom-call | tf_op jit(solution)/shard_map/jit(cholesky)/cholesky | solution.py:60
  106.3 10.4 %custom-call.14 = f32[1,128,128]{1,2,0:T(8,128)} custom-call(f32[1,128,128]{2,1,0:T(8,128)S(1)} %get-tuple-element.26), custom_call_target="InvertDiagBlocksLowerTriangular" | custom-call | tf_op jit(solution)/shard_map/jit(cholesky)/cholesky | solution.py:60
  119.6 12.5 %cholesky.105 = f32[128,128]{1,0:T(8,128)S(1)} custom-call(f32[128,128]{1,0:T(8,128)} %slice_subtract_fusion), custom_call_target="Cholesky" | custom-call | tf_op jit(solution)/shard_map/jit(cholesky)/cholesky | solution.py:60
  135.3 5.3 %while.1 = (s32[]{:T(128)}, f32[256,256]{1,0:T(8,128)S(1)}, s32[2,2]{1,0:T(2,128)S(1)}, f32[2,128,128]{2,1,0:T(8,128)}, s32[]{:T(128)}) while((s32[]{:T(128)}, f32[256,256]{1,0:T(8,128)S(1)}, s32[2,2]{1,0:T(2,128)S(1)}, f32[2,128,128]{2,1,0:T(8,128)}, s32[]{:T(128)}) %tuple.23), condition=%wide.while_cond, body=%wide.while_body.sunk | while | flops 2 | bytes 132205 | solution.py:62
  135.9 2.0 %bitcast_dynamic-update-slice_fusion.2 = f32[2,128,128]{2,1,0:T(8,128)} fusion(f32[2,128,128]{2,1,0:T(8,128)} %get-tuple-element.68, s32[]{:T(128)S(6)} %copy.25, f32[256,256]{1,0:T(8,128)S(1)} %get-tuple-element.71, s32[]{:T(128)} %bitcast.61, s32[]{:T(128)} %bitcast.62), kind=kLoop, calls=%fused_computation.clone.1 | loop fusion | bytes 132100 | tf_op jit(solution)/shard_map/triangular_solve
  138.5 2.0 %bitcast_dynamic-update-slice_fusion.2 = f32[2,128,128]{2,1,0:T(8,128)} fusion(f32[2,128,128]{2,1,0:T(8,128)} %get-tuple-element.68, s32[]{:T(128)S(6)} %copy.25, f32[256,256]{1,0:T(8,128)S(1)} %get-tuple-element.71, s32[]{:T(128)} %bitcast.61, s32[]{:T(128)} %bitcast.62), kind=kLoop, calls=%fused_computation.clone.1 | loop fusion | bytes 132100 | tf_op jit(solution)/shard_map/triangular_solve
  140.6 21.1 %custom-call.15 = f32[2,128,128]{1,2,0:T(8,128)} custom-call(f32[2,128,128]{2,1,0:T(8,128)} %get-tuple-element.12), custom_call_target="InvertDiagBlocksLowerTriangular" | custom-call | tf_op jit(solution)/shard_map/triangular_solve | solution.py:62
  (97 shorter events, 44.5 us)
Async XLA Ops:
  3.1 10.8 %collective-permute-start.15 = (f32[256,256]{1,0:T(8,128)S(1)}, f32[256,256]{1,0:T(8,128)S(1)}, u32[]{:S(2)}, u32[]{:S(2)}) collective-permute-start(f32[256,256]{1,0:T(8,128)S(1)} %fusion.16), channel_id=1, source_target_pairs={{0,1},{1,0},{2,3},{3,2},{4,5},{5,4},{6,7},{7,6},{8,9},{9,8},{10,11... | collective-permute-start | bytes 786440 | tf_op jit(solution)/shard_map/ppermute | solution.py:46
  7.9 11.7 %collective-permute-start = (f32[256,256]{1,0:T(8,128)S(1)}, f32[256,256]{1,0:T(8,128)S(1)}, u32[]{:S(2)}, u32[]{:S(2)}) collective-permute-start(f32[256,256]{1,0:T(8,128)S(1)} %fusion.37), channel_id=1, source_target_pairs={{0,1},{1,0},{2,3},{3,2},{4,5},{5,4},{6,7},{7,6},{8,9},{9,8},{10,11... | collective-permute-start | bytes 786440 | tf_op jit(solution)/shard_map/ppermute | solution.py:46
  9.8 14.9 %collective-permute-start.5 = (f32[256,256]{1,0:T(8,128)S(1)}, f32[256,256]{1,0:T(8,128)S(1)}, u32[]{:S(2)}, u32[]{:S(2)}) collective-permute-start(f32[256,256]{1,0:T(8,128)S(1)} %fusion.30), channel_id=1, source_target_pairs={{0,1},{1,0},{2,3},{3,2},{4,5},{5,4},{6,7},{7,6},{8,9},{9,8},{10,11... | collective-permute-start | bytes 786440 | tf_op jit(solution)/shard_map/ppermute | solution.py:46
  13.7 16.6 %collective-permute-start.10 = (f32[256,256]{1,0:T(8,128)S(1)}, f32[256,256]{1,0:T(8,128)S(1)}, u32[]{:S(2)}, u32[]{:S(2)}) collective-permute-start(f32[256,256]{1,0:T(8,128)S(1)} %fusion.23), channel_id=1, source_target_pairs={{0,1},{1,0},{2,3},{3,2},{4,5},{5,4},{6,7},{7,6},{8,9},{9,8},{10,11... | collective-permute-start | bytes 786440 | tf_op jit(solution)/shard_map/ppermute | solution.py:46
  15.7 19.1 %collective-permute-start.16 = (f32[256,256]{1,0:T(8,128)S(1)}, f32[256,256]{1,0:T(8,128)S(1)}, u32[]{:S(2)}, u32[]{:S(2)}) collective-permute-start(f32[256,256]{1,0:T(8,128)S(1)} %convolution_add_fusion.2), channel_id=1, source_target_pairs={{0,2},{1,3},{6,4},{7,5},{8,10},{9,11},{14,12},{15,13},{16,18},{17,... | collective-permute-start | bytes 786440 | tf_op jit(solution)/shard_map/ppermute | solution.py:24
  21.5 14.0 %collective-permute-start.1 = (f32[256,256]{1,0:T(8,128)S(1)}, f32[256,256]{1,0:T(8,128)S(1)}, u32[]{:S(2)}, u32[]{:S(2)}) collective-permute-start(f32[256,256]{1,0:T(8,128)S(1)} %convolution_add_fusion.5), channel_id=1, source_target_pairs={{0,2},{1,3},{6,4},{7,5},{8,10},{9,11},{14,12},{15,13},{16,18},{17,... | collective-permute-start | bytes 786440 | tf_op jit(solution)/shard_map/ppermute | solution.py:24
  26.6 10.1 %collective-permute-start.6 = (f32[256,256]{1,0:T(8,128)S(1)}, f32[256,256]{1,0:T(8,128)S(1)}, u32[]{:S(2)}, u32[]{:S(2)}) collective-permute-start(f32[256,256]{1,0:T(8,128)S(1)} %convolution_add_fusion.4), channel_id=1, source_target_pairs={{0,2},{1,3},{6,4},{7,5},{8,10},{9,11},{14,12},{15,13},{16,18},{17,... | collective-permute-start | bytes 786440 | tf_op jit(solution)/shard_map/ppermute | solution.py:24
  32.2 8.7 %collective-permute-start.11 = (f32[256,256]{1,0:T(8,128)S(1)}, f32[256,256]{1,0:T(8,128)S(1)}, u32[]{:S(2)}, u32[]{:S(2)}) collective-permute-start(f32[256,256]{1,0:T(8,128)S(1)} %convolution_add_fusion.3), channel_id=1, source_target_pairs={{0,2},{1,3},{6,4},{7,5},{8,10},{9,11},{14,12},{15,13},{16,18},{17,... | collective-permute-start | bytes 786440 | tf_op jit(solution)/shard_map/ppermute | solution.py:24
  34.9 6.8 %collective-permute-start.17 = (f32[256,256]{1,0:T(8,128)S(1)}, f32[256,256]{1,0:T(8,128)S(1)}, u32[]{:S(2)}, u32[]{:S(2)}) collective-permute-start(f32[256,256]{1,0:T(8,128)S(1)} %add.160), channel_id=1, source_target_pairs={{2,4},{3,5},{4,2},{5,3},{10,12},{11,13},{12,10},{13,11},{18,20},{1... | collective-permute-start | bytes 786440 | tf_op jit(solution)/shard_map/ppermute | solution.py:25
  35.6 7.5 %collective-permute-start.2 = (f32[256,256]{1,0:T(8,128)S(1)}, f32[256,256]{1,0:T(8,128)S(1)}, u32[]{:S(2)}, u32[]{:S(2)}) collective-permute-start(f32[256,256]{1,0:T(8,128)S(1)} %add.139), channel_id=1, source_target_pairs={{2,4},{3,5},{4,2},{5,3},{10,12},{11,13},{12,10},{13,11},{18,20},{1... | collective-permute-start | bytes 786440 | tf_op jit(solution)/shard_map/ppermute | solution.py:25
  36.7 7.7 %collective-permute-start.7 = (f32[256,256]{1,0:T(8,128)S(1)}, f32[256,256]{1,0:T(8,128)S(1)}, u32[]{:S(2)}, u32[]{:S(2)}) collective-permute-start(f32[256,256]{1,0:T(8,128)S(1)} %add.146), channel_id=1, source_target_pairs={{2,4},{3,5},{4,2},{5,3},{10,12},{11,13},{12,10},{13,11},{18,20},{1... | collective-permute-start | bytes 786440 | tf_op jit(solution)/shard_map/ppermute | solution.py:25
  41.0 4.8 %collective-permute-start.12 = (f32[256,256]{1,0:T(8,128)S(1)}, f32[256,256]{1,0:T(8,128)S(1)}, u32[]{:S(2)}, u32[]{:S(2)}) collective-permute-start(f32[256,256]{1,0:T(8,128)S(1)} %add.153), channel_id=1, source_target_pairs={{2,4},{3,5},{4,2},{5,3},{10,12},{11,13},{12,10},{13,11},{18,20},{1... | collective-permute-start | bytes 786440 | tf_op jit(solution)/shard_map/ppermute | solution.py:25
  41.7 13.8 %collective-permute-start.18 = (f32[256,256]{1,0:T(8,128)S(1)}, f32[256,256]{1,0:T(8,128)S(1)}, u32[]{:S(2)}, u32[]{:S(2)}) collective-permute-start(f32[256,256]{1,0:T(8,128)S(1)} %add.161), channel_id=1, source_target_pairs={{2,0},{3,1},{4,6},{5,7},{10,8},{11,9},{12,14},{13,15},{18,16},{19,... | collective-permute-start | bytes 786440 | tf_op jit(solution)/shard_map/ppermute | solution.py:26
  43.1 31.4 %collective-permute-start.3 = (f32[256,256]{1,0:T(8,128)S(1)}, f32[256,256]{1,0:T(8,128)S(1)}, u32[]{:S(2)}, u32[]{:S(2)}) collective-permute-start(f32[256,256]{1,0:T(8,128)S(1)} %add.140), channel_id=1, source_target_pairs={{2,0},{3,1},{4,6},{5,7},{10,8},{11,9},{12,14},{13,15},{18,16},{19,... | collective-permute-start | bytes 786440 | tf_op jit(solution)/shard_map/ppermute | solution.py:26
  44.5 22.2 %collective-permute-start.8 = (f32[256,256]{1,0:T(8,128)S(1)}, f32[256,256]{1,0:T(8,128)S(1)}, u32[]{:S(2)}, u32[]{:S(2)}) collective-permute-start(f32[256,256]{1,0:T(8,128)S(1)} %add.147), channel_id=1, source_target_pairs={{2,0},{3,1},{4,6},{5,7},{10,8},{11,9},{12,14},{13,15},{18,16},{19,... | collective-permute-start | bytes 786440 | tf_op jit(solution)/shard_map/ppermute | solution.py:26
  45.8 26.6 %collective-permute-start.13 = (f32[256,256]{1,0:T(8,128)S(1)}, f32[256,256]{1,0:T(8,128)S(1)}, u32[]{:S(2)}, u32[]{:S(2)}) collective-permute-start(f32[256,256]{1,0:T(8,128)S(1)} %add.154), channel_id=1, source_target_pairs={{2,0},{3,1},{4,6},{5,7},{10,8},{11,9},{12,14},{13,15},{18,16},{19,... | collective-permute-start | bytes 786440 | tf_op jit(solution)/shard_map/ppermute | solution.py:26
  55.5 21.6 %collective-permute-start.19 = (f32[256,256]{1,0:T(8,128)S(1)}, f32[256,256]{1,0:T(8,128)S(1)}, u32[]{:S(2)}, u32[]{:S(2)}) collective-permute-start(f32[256,256]{1,0:T(8,128)S(1)} %broadcast_select_fusion), channel_id=1, source_target_pairs={{0,1},{1,0},{2,3},{3,2},{4,5},{5,4},{6,7},{7,6},{8,9},{9,8},{10,11... | collective-permute-start | bytes 786440 | tf_op jit(solution)/shard_map/ppermute | solution.py:49
  57.5 30.0 %slice-start = ((s8[8388608]{0:T(1024)(128)(4,1)}), s8[4194304]{0:T(1024)(128)(4,1)S(1)}, s32[]{:S(2)}) async-start(s8[8388608]{0:T(1024)(128)(4,1)} %bitcast.63), calls=%async_computation | async-start | bytes 8388608
  69.0 15.2 %collective-permute-start.9 = (f32[256,256]{1,0:T(8,128)S(1)}, f32[256,256]{1,0:T(8,128)S(1)}, u32[]{:S(2)}, u32[]{:S(2)}) collective-permute-start(f32[256,256]{1,0:T(8,128)S(1)} %broadcast_select_fusion.2), channel_id=1, source_target_pairs={{0,1},{1,0},{2,3},{3,2},{4,5},{5,4},{6,7},{7,6},{8,9},{9,8},{10,11... | collective-permute-start | bytes 786440 | tf_op jit(solution)/shard_map/ppermute | solution.py:49
  72.5 15.0 %slice-start.1 = ((s8[8388608]{0:T(1024)(128)(4,1)}), s8[4194304]{0:T(1024)(128)(4,1)S(1)}, s32[]{:S(2)}) async-start(s8[8388608]{0:T(1024)(128)(4,1)} %bitcast.63), calls=%async_computation.1 | async-start | bytes 8388608
  74.6 9.2 %collective-permute-start.4 = (f32[256,256]{1,0:T(8,128)S(1)}, f32[256,256]{1,0:T(8,128)S(1)}, u32[]{:S(2)}, u32[]{:S(2)}) collective-permute-start(f32[256,256]{1,0:T(8,128)S(1)} %broadcast_select_fusion.3), channel_id=1, source_target_pairs={{0,1},{1,0},{2,3},{3,2},{4,5},{5,4},{6,7},{7,6},{8,9},{9,8},{10,11... | collective-permute-start | bytes 786440 | tf_op jit(solution)/shard_map/ppermute | solution.py:49
  75.6 11.1 %collective-permute-start.14 = (f32[256,256]{1,0:T(8,128)S(1)}, f32[256,256]{1,0:T(8,128)S(1)}, u32[]{:S(2)}, u32[]{:S(2)}) collective-permute-start(f32[256,256]{1,0:T(8,128)S(1)} %broadcast_select_fusion.1), channel_id=1, source_target_pairs={{0,1},{1,0},{2,3},{3,2},{4,5},{5,4},{6,7},{7,6},{8,9},{9,8},{10,11... | collective-permute-start | bytes 786440 | tf_op jit(solution)/shard_map/ppermute | solution.py:49
  87.5 4.4 %collective-permute-start.20 = (f32[256,256]{0,1:T(8,128)S(1)}, f32[256,256]{0,1:T(8,128)S(1)}, u32[]{:S(2)}, u32[]{:S(2)}) collective-permute-start(f32[256,256]{0,1:T(8,128)S(1)} %fusion.11), channel_id=1, source_target_pairs={{0,8},{8,0},{1,9},{9,1},{2,10},{10,2},{3,11},{11,3},{4,12},{12,4},... | collective-permute-start | bytes 786440 | tf_op jit(solution)/shard_map/ppermute | solution.py:58
  91.3 72.9 %collective-permute-start.21 = (f32[256,1024]{1,0:T(8,128)S(1)}, f32[256,1024]{1,0:T(8,128)S(1)}, u32[]{:S(2)}, u32[]{:S(2)}) collective-permute-start(f32[256,1024]{1,0:T(8,128)S(1)} %fusion.5), channel_id=1, source_target_pairs={{0,8},{8,0},{1,9},{9,1},{2,10},{10,2},{3,11},{11,3},{4,12},{12,4},... | collective-permute-start | bytes 3145736 | tf_op jit(solution)/shard_map/ppermute | solution.py:59
  (3 other events, 3.9 us)

commit v2 on v0

v2 whole, which is shorter than its diff:
```python
import functools

import jax
import jax.numpy as jnp
from jax import lax
from jax.experimental import pallas as pl
from jax.experimental.pallas import tpu as pltpu
from jax.sharding import PartitionSpec as P

HIGH = lax.Precision.HIGH
SPANS = (160, 176, 176)
BLOCK = 64


def inner_rows(left, right):
    return lax.dot_general(
        left,
        right,
        (((0,), (0,)), ((), ())),
        precision=HIGH,
        preferred_element_type=jnp.float32,
    )


def small_dot(left, right, dims):
    return lax.dot_general(
        left,
        right,
        (dims, ((), ())),
        precision=lax.Precision.HIGHEST,
        preferred_element_type=jnp.float32,
    )


def inverse_factor(block):
    size = block.shape[0]
    row = lax.broadcasted_iota(jnp.int32, block.shape, 0)
    col = lax.broadcasted_iota(jnp.int32, block.shape, 1)
    rows = lax.broadcasted_iota(jnp.int32, (size, 1), 0)
    pivots = jnp.ones((size, 1), jnp.float32)
    for j in range(size):
        pivot = block[j : j + 1, j : j + 1]
        factor = jnp.where(rows > j, block[:, j : j + 1] * (1.0 / pivot), 0.0)
        pivots = jnp.where(rows == j, pivot, pivots)
        line = jnp.where(col[0:1] == j, 1.0, block[j : j + 1, :])
        block = jnp.where((col == j) & (row != j), 0.0, block) - factor * line
    unit = jnp.where(col == row, 1.0, jnp.where(col < row, block, 0.0))
    return unit * lax.rsqrt(pivots)


def factor_kernel(gram_ref, far_ref, out_ref, work):
    size = gram_ref.shape[0]
    work[...] = gram_ref[...] + far_ref[...]
    for start in range(0, size, BLOCK):
        stop = start + BLOCK
        corner = inverse_factor(work[start:stop, start:stop])
        lane = lax.broadcasted_iota(jnp.int32, (BLOCK, size), 1)
        wide = jnp.concatenate(
            [jnp.zeros((BLOCK, start), jnp.float32)] * (start > 0)
            + [corner]
            + [jnp.zeros((BLOCK, size - stop), jnp.float32)] * (stop < size),
            axis=1,
        )
        lines = small_dot(corner, work[start:stop, :], ((1,), (0,)))
        lines = jnp.where((lane >= start) & (lane < stop), wide, lines)
        out_ref[start:stop, :] = jnp.where(lane < stop, lines, 0.0)
        if stop < size:
            factor = small_dot(work[stop:, start:stop], corner, ((1,), (1,)))
            lane = lax.broadcasted_iota(jnp.int32, (size - stop, size), 1)
            old = jnp.where((lane >= start) & (lane < stop), 0.0, work[stop:, :])
            work[stop:, :] = old - small_dot(factor, lines, ((1,), (0,)))


def inverse_cholesky(gram, far):
    whole = pl.BlockSpec(memory_space=pltpu.VMEM)
    return pl.pallas_call(
        factor_kernel,
        out_shape=jax.ShapeDtypeStruct(gram.shape, jnp.float32),
        in_specs=[whole, whole],
        out_specs=whole,
        scratch_shapes=[pltpu.VMEM(gram.shape, jnp.float32)],
        cost_estimate=pl.CostEstimate(flops=40_000_000, bytes_accessed=12 * gram.size, transcendentals=0),
    )(gram, far)


def after(values, *earlier):
    out = lax.optimization_barrier(tuple(values) + earlier)
    return out[: len(values)]


def summed_halves(texture, sketch):
    col = lax.axis_index("cols")
    side, place = lax.rem(col, 2), lax.div(col, 2)
    odd = lax.rem(place, 2)
    swap = {step: [(c, c ^ step) for c in range(8)] for step in (1, 2, 4)}
    send = lambda x, step: lax.ppermute(x, "cols", swap[step])
    starts = [4 * sum(SPANS[:k]) for k in range(len(SPANS))]
    half_rows = lambda k, s: lax.dynamic_slice_in_dim(texture, starts[k] + s * (2 * SPANS[k]), 2 * SPANS[k])
    own = [half_rows(k, side) for k in range(3)]
    other = [half_rows(k, 1 - side) for k in range(3)]
    sketched = lambda rows: jnp.dot(rows, sketch, precision=HIGH, preferred_element_type=jnp.float32)
    part = lambda x, k, which: lax.dynamic_slice_in_dim(x, which * SPANS[k], SPANS[k])

    def joined(mine, theirs):
        return jnp.where(odd == 0, jnp.concatenate([mine, theirs]), jnp.concatenate([theirs, mine]))

    y = [None] * 3
    quarter, other_quarter, half, far = [None] * 3, [None] * 3, [None] * 3, [None] * 3

    theirs = [sketched(x) for x in other]
    y[0] = send(theirs[0], 1)
    y[1] = send(theirs[1], 1)

    def settle(k):
        total = sketched(own[k]) + y[k]
        return part(total, k, odd), part(total, k, 1 - odd)

    quarter[0], out0 = settle(0)
    got0 = send(out0, 2)
    (theirs2,) = after([theirs[2]], y[0])
    y[2] = send(theirs2, 1)
    quarter[0] = quarter[0] + got0
    q0 = send(quarter[0], 4)
    quarter[1], out1 = settle(1)
    (out1,) = after([out1], got0)
    got1 = send(out1, 2)
    quarter[0] = quarter[0] + q0
    other_quarter[0] = send(quarter[0], 2)
    quarter[1] = quarter[1] + got1
    (s1,) = after([quarter[1]], q0)
    q1 = send(s1, 4)
    half[0] = joined(quarter[0], other_quarter[0])
    far[0] = send(half[0], 1)
    quarter[2], out2 = settle(2)
    (out2,) = after([out2], other_quarter[0])
    got2 = send(out2, 2)
    quarter[1] = quarter[1] + q1
    other_quarter[1] = send(quarter[1], 2)
    quarter[2] = quarter[2] + got2
    (s2,) = after([quarter[2]], q1)
    q2 = send(s2, 4)
    half[1] = joined(quarter[1], other_quarter[1])
    far[1] = send(half[1], 1)
    quarter[2] = quarter[2] + q2
    other_quarter[2] = send(quarter[2], 2)
    half[2] = joined(quarter[2], other_quarter[2])
    far[2] = send(half[2], 1)
    pairs = []
    for k in range(3):
        pairs += [(own[k], half[k]), (other[k], far[k])]
    return pairs


def per_device(texture, sketch):
    if lax.axis_size("cols") == 8 and texture.shape[0] == 4 * sum(SPANS):
        pairs = summed_halves(texture, sketch)
    else:
        partial = jnp.dot(texture, sketch, precision=HIGH, preferred_element_type=jnp.float32)
        pairs = [(texture, lax.psum(partial, "cols"))]
    gram, product = 0.0, 0.0
    for rows, image in pairs:
        gram = gram + inner_rows(image, image)
        product = product + inner_rows(image, rows)
    pair = [(0, 1), (1, 0)]
    inverse = inverse_cholesky(gram, lax.ppermute(gram, "rows", pair))
    product = product + lax.ppermute(product, "rows", pair)
    span = gram.shape[0] // lax.axis_size("rows")
    inverse = lax.dynamic_slice_in_dim(inverse, lax.axis_index("rows") * span, span)
    return jnp.dot(inverse, product, precision=HIGH, preferred_element_type=jnp.float32)


def solution(mesh):
    placed = (P(("groups", "rows"), "cols"), P("cols", None))
    return jax.shard_map(
        per_device,
        mesh=mesh,
        in_specs=placed,
        out_specs=P(("groups", "rows"), "cols"),
        check_vma=False,
    )
```

time: 245 us -> 110 us (0.45)
  waiting for transfers between devices: 132 us -> 22.8 us
  other arithmetic: 56.4 us -> 0.27 us
  Pallas kernels: 0 us -> 26.6 us
  starting transfers between devices: 0.27 us -> 25.6 us
  between operations: 14.5 us -> 0.3 us
  local copies, waits for them, and re-layouts: 8.23 us -> 1.29 us
    psum x2 -> x0, waiting for transfers between devices: 123 us -> none  [the longest x1 105 us: per_device(): image = lax.psum(partial_image, 'cols')]
    another operation x9 -> x0, other arithmetic: 55.4 us -> none  [the longest x6 34 us: orthonormal(): lower = jnp.linalg.cholesky(gram)]
    pallas_call x0 -> x1, Pallas kernels: none -> 26.6 us  [inverse_cholesky(): pl.pallas_call(factor_kernel, out_shape=jax.ShapeDtypeStruct(gram.shape,...]
    ppermute x0 -> x17, starting transfers between devices: none -> 25.6 us  [the longest x15 25 us: summed_halves(): send = lambda x, step: lax.ppermute(x, 'cols', swap[step])]
    ppermute x0 -> x17, waiting for transfers between devices: none -> 22.8 us  [the longest x15 21.5 us: summed_halves(): send = lambda x, step: lax.ppermute(x, 'cols', swap[step])]
    reduce_scatter x1 -> x0, waiting for transfers between devices: 9.86 us -> none  [per_device(): lax.psum_scatter(inner_rows(basis, texture), 'rows', scatter_dimension=0,...]
    another operation x5 -> x0, matrix products: 6.12 us -> none  [the longest x3 3.97 us: orthonormal(): lax.linalg.triangular_solve(lower, image, left_side=False, lower=True, tr...]
    dot_general x3 -> x19, matrix products: 26.8 us -> 32.5 us  [the longest x12 17.9 us: inner_rows(): lax.dot_general(left, right, (((0,), (0,)), ((), ())), precision=HIGH, pr...]
  transfers between devices with their start and end apart: 3 -> 17, of which waited for: 3 -> 10; matrix products, arithmetic and copies ran while one was open for 0% -> 21% of each run, Pallas kernels for 0% -> 24%
where the time goes in v2:
time: 110 us; the launch traced here: 109 us
  matrix products  32.5 us (30%)
  Pallas kernels  26.6 us (24%)
  starting transfers between devices  25.6 us (23%)
  waiting for transfers between devices  22.8 us (21%)
  local copies, waits for them, and re-layouts  1.29 us (1%)
    pallas_call x1, Pallas kernels, inverse_cholesky(): pl.pallas_call(factor_kernel, out_shape=jax.ShapeDtypeStruct(gram.shape,...  26.6 us
    ppermute x15, starting transfers between devices, summed_halves(): send = lambda x, step: lax.ppermute(x, 'cols', swap[step])  25 us
    ppermute x15, waiting for transfers between devices, summed_halves(): send = lambda x, step: lax.ppermute(x, 'cols', swap[step])  21.5 us
    dot_general x12, matrix products, inner_rows(): lax.dot_general(left, right, (((0,), (0,)), ((), ())), precision=HIGH, pr...  17.9 us
    dot_general x6, matrix products, summed_halves(): jnp.dot(rows, sketch, precision=HIGH, preferred_element_type=jnp.float32)  12.5 us
  transfers between devices with their start and end apart: 17, of which 10 were waited for; matrix products, arithmetic and copies ran while one was open for 21% of the time, Pallas kernels for 24%

profile of v2, /device:TPU:0, one launch (start us, length us, event | category | flops | bytes accessed | tf_op | source)
XLA Modules:
  0.0 109.4 jit_solution(486150423797825527)
XLA Ops:
  3.2 3.0 %collective-permute-start = (f32[320,256]{1,0:T(8,128)S(1)}, f32[320,256]{1,0:T(8,128)S(1)}, u32[]{:S(2)}, u32[]{:S(2)}) collective-permute-start(f32[320,256]{1,0:T(8,128)S(1)} %fusion.22), channel_id=1, source_target_pairs={{0,1},{1,0},{2,3},{3,2},{4,5},{5,4},{6,7},{7,6},{8,9},{9,8},{10,11... | collective-permute-start | bytes 983048 | tf_op jit(solution)/shard_map/ppermute | solution.py:96
  6.3 2.1 %fusion.14 = f32[352,256]{1,0:T(8,128)S(1)} fusion(f32[1024,256]{1,0:T(8,128)S(1)} %copy-done, f32[2048,1024]{1,0:T(8,128)} %param.2, s32[]{:T(128)S(6)} %select_n.63), kind=kOutput, calls=%fused_computation.15 | convolution fusion | flops 553648128 | bytes 2850820 | tf_op jit(solution)/shard_map/dot_general | solution.py:101
  8.5 2.1 %fusion.6 = f32[352,256]{1,0:T(8,128)S(1)} fusion(f32[1024,256]{1,0:T(8,128)S(1)} %copy-done, f32[2048,1024]{1,0:T(8,128)} %param.2, s32[]{:T(128)S(6)} %select_n.68), kind=kOutput, calls=%fused_computation.7 | convolution fusion | flops 553648128 | bytes 2850820 | tf_op jit(solution)/shard_map/dot_general | solution.py:101
  10.7 4.2 %collective-permute-done = f32[320,256]{1,0:T(8,128)S(1)} collective-permute-done((f32[320,256]{1,0:T(8,128)S(1)}, f32[320,256]{1,0:T(8,128)S(1)}, u32[]{:S(2)}, u32[]{:S(2)}) %collective-permute-start) | collective-permute-done | bytes 327712 | tf_op jit(solution)/shard_map/ppermute | solution.py:96
  14.8 2.0 %fusion.30 = f32[320,256]{1,0:T(8,128)S(1)} fusion(f32[320,256]{1,0:T(8,128)S(1)} %collective-permute-done, f32[1024,256]{1,0:T(8,128)S(1)} %copy-done, f32[2048,1024]{1,0:T(8,128)} %param.2, s32[]{:T(128)S(6)} %select_n.56), kind=kOutput, calls=%fused_computation.29 | convolution fusion | flops 503398400 | bytes 3014660 | tf_op jit(solution)/shard_map/dot_general | solution.py:101
  16.9 2.2 %collective-permute-start.1 = (f32[160,256]{1,0:T(8,128)S(1)}, f32[160,256]{1,0:T(8,128)S(1)}, u32[]{:S(2)}, u32[]{:S(2)}) collective-permute-start(f32[160,256]{1,0:T(8,128)S(1)} %constant_dynamic-slice_fusion.2), channel_id=1, source_target_pairs={{0,2},{1,3},{2,0},{3,1},{4,6},{5,7},{6,4},{7,5},{8,10},{9,11},{10,... | collective-permute-start | bytes 491528 | tf_op jit(solution)/shard_map/ppermute | solution.py:96
  22.5 2.1 %fusion.27 = f32[352,256]{1,0:T(8,128)S(1)} fusion(f32[352,256]{1,0:T(8,128)S(1)} %collective-permute-done.5, f32[1024,256]{1,0:T(8,128)S(1)} %copy-done, f32[2048,1024]{1,0:T(8,128)} %param.2, s32[]{:T(128)S(6)} %select_n.62), kind=kOutput, calls=%fused_computation.28 | convolution fusion | flops 553738240 | bytes 3211268 | tf_op jit(solution)/shard_map/dot_general | solution.py:101
  24.7 3.2 %collective-permute-start.2 = (f32[160,256]{1,0:T(8,128)S(1)}, f32[160,256]{1,0:T(8,128)S(1)}, u32[]{:S(2)}, u32[]{:S(2)}) collective-permute-start(f32[160,256]{1,0:T(8,128)S(1)} %dynamic-slice_add_fusion.2), channel_id=1, source_target_pairs={{0,4},{1,5},{2,6},{3,7},{4,0},{5,1},{6,2},{7,3},{8,12},{9,13},{10,... | collective-permute-start | bytes 491528 | tf_op jit(solution)/shard_map/ppermute | solution.py:96
  29.5 2.1 %fusion.10 = f32[352,256]{1,0:T(8,128)S(1)} fusion(f32[1024,256]{1,0:T(8,128)S(1)} %copy-done, f32[2048,1024]{1,0:T(8,128)} %param.2, s32[]{:T(128)S(6)} %select_n.67), kind=kOutput, calls=%fused_computation.11 | convolution fusion | flops 553648128 | bytes 2850820 | tf_op jit(solution)/shard_map/dot_general | solution.py:101
  31.6 2.3 %collective-permute-done.2 = f32[160,256]{1,0:T(8,128)S(1)} collective-permute-done((f32[160,256]{1,0:T(8,128)S(1)}, f32[160,256]{1,0:T(8,128)S(1)}, u32[]{:S(2)}, u32[]{:S(2)}) %collective-permute-start.2) | collective-permute-done | bytes 163872 | tf_op jit(solution)/shard_map/ppermute | solution.py:96
  34.9 3.1 %collective-permute-start.7 = (f32[176,256]{1,0:T(8,128)S(1)}, f32[176,256]{1,0:T(8,128)S(1)}, u32[]{:S(2)}, u32[]{:S(2)}) collective-permute-start(f32[176,256]{1,0:T(8,128)S(1)} %dynamic-slice_add_fusion.1), channel_id=1, source_target_pairs={{0,4},{1,5},{2,6},{3,7},{4,0},{5,1},{6,2},{7,3},{8,12},{9,13},{10,... | collective-permute-start | bytes 540680 | tf_op jit(solution)/shard_map/ppermute | solution.py:96
  38.1 3.6 %collective-permute-done.3 = f32[160,256]{1,0:T(8,128)S(1)} collective-permute-done((f32[160,256]{1,0:T(8,128)S(1)}, f32[160,256]{1,0:T(8,128)S(1)}, u32[]{:S(2)}, u32[]{:S(2)}) %collective-permute-start.3) | collective-permute-done | bytes 163872 | tf_op jit(solution)/shard_map/ppermute | solution.py:96
  43.2 2.6 %collective-permute-start.8 = (f32[176,256]{1,0:T(8,128)S(1)}, f32[176,256]{1,0:T(8,128)S(1)}, u32[]{:S(2)}, u32[]{:S(2)}) collective-permute-start(f32[176,256]{1,0:T(8,128)S(1)} %add.131), channel_id=1, source_target_pairs={{0,2},{1,3},{2,0},{3,1},{4,6},{5,7},{6,4},{7,5},{8,10},{9,11},{10,... | collective-permute-start | bytes 540680 | tf_op jit(solution)/shard_map/ppermute | solution.py:96
  45.8 2.9 %collective-permute-done.11 = f32[176,256]{1,0:T(8,128)S(1)} collective-permute-done((f32[176,256]{1,0:T(8,128)S(1)}, f32[176,256]{1,0:T(8,128)S(1)}, u32[]{:S(2)}, u32[]{:S(2)}) %collective-permute-start.11) | collective-permute-done | bytes 180256 | tf_op jit(solution)/shard_map/ppermute | solution.py:96
  48.7 2.1 %collective-permute-start.12 = (f32[176,256]{1,0:T(8,128)S(1)}, f32[176,256]{1,0:T(8,128)S(1)}, u32[]{:S(2)}, u32[]{:S(2)}) collective-permute-start(f32[176,256]{1,0:T(8,128)S(1)} %dynamic-slice_add_fusion), channel_id=1, source_target_pairs={{0,4},{1,5},{2,6},{3,7},{4,0},{5,1},{6,2},{7,3},{8,12},{9,13},{10,... | collective-permute-start | bytes 540680 | tf_op jit(solution)/shard_map/ppermute | solution.py:96
  53.5 2.4 %fusion.16 = f32[256,1024]{1,0:T(8,128)S(1)} fusion(f32[352,256]{1,0:T(8,128)S(1)} %maximum_select_fusion, f32[2048,1024]{1,0:T(8,128)} %param.2, s32[]{:T(128)S(6)} %select_n.62), kind=kOutput, calls=%fused_computation.17 | convolution fusion | flops 553648128 | bytes 2850820 | tf_op jit(solution)/shard_map/dot_general | solution.py:16
  55.9 2.4 %fusion.20 = f32[256,1024]{1,0:T(8,128)S(1)} fusion(f32[320,256]{1,0:T(8,128)S(1)} %collective-permute-done.4, f32[2048,1024]{1,0:T(8,128)} %param.2, s32[]{:T(128)S(6)} %select_n.57), kind=kOutput, calls=%fused_computation.21 | convolution fusion | flops 503316480 | bytes 2686980 | tf_op jit(solution)/shard_map/dot_general | solution.py:16
  60.3 3.5 %collective-permute-done.13 = f32[176,256]{1,0:T(8,128)S(1)} collective-permute-done((f32[176,256]{1,0:T(8,128)S(1)}, f32[176,256]{1,0:T(8,128)S(1)}, u32[]{:S(2)}, u32[]{:S(2)}) %collective-permute-start.13) | collective-permute-done | bytes 180256 | tf_op jit(solution)/shard_map/ppermute | solution.py:96
  64.6 2.4 %fusion.8 = f32[256,1024]{1,0:T(8,128)S(1)} fusion(f32[352,256]{1,0:T(8,128)S(1)} %maximum_select_fusion.1, f32[2048,1024]{1,0:T(8,128)} %param.2, s32[]{:T(128)S(6)} %select_n.67), kind=kOutput, calls=%fused_computation.9 | convolution fusion | flops 553648128 | bytes 2850820 | tf_op jit(solution)/shard_map/dot_general | solution.py:16
  67.0 2.4 %fusion.12 = f32[256,1024]{1,0:T(8,128)S(1)} fusion(f32[352,256]{1,0:T(8,128)S(1)} %collective-permute-done.9, f32[2048,1024]{1,0:T(8,128)} %param.2, s32[]{:T(128)S(6)} %select_n.63), kind=kOutput, calls=%fused_computation.13 | convolution fusion | flops 553648128 | bytes 2850820 | tf_op jit(solution)/shard_map/dot_general | solution.py:16
  71.4 2.4 %fusion.4 = f32[256,1024]{1,0:T(8,128)S(1)} fusion(f32[352,256]{1,0:T(8,128)S(1)} %collective-permute-done.14, f32[2048,1024]{1,0:T(8,128)} %param.2, s32[]{:T(128)S(6)} %select_n.68), kind=kOutput, calls=%fused_computation.5 | convolution fusion | flops 553648128 | bytes 2850820 | tf_op jit(solution)/shard_map/dot_general | solution.py:16
  73.8 2.8 %fusion.3 = f32[256,1024]{1,0:T(8,128)S(1)} fusion(f32[256,1024]{1,0:T(8,128)S(1)} %fusion.4, f32[256,1024]{1,0:T(8,128)S(1)} %fusion.8, f32[256,1024]{1,0:T(8,128)S(1)} %fusion.12, f32[256,1024]{1,0:T(8,128)S(1)} %fusion.16, f32[256,1024]{1,0:T(8,128)S(1)} %fusion.20, f32[320,256]{1,0:T(8,128)S(1)} %maximum_select_fusion.2, f32[2048,1024]{1,0:T(8,128)} %param.2, ...), kind=kOutput, calls=%fused_computation.4 | convolution fusion | flops 504627200 | bytes 7929860 | tf_op jit(solution)/shard_map/dot_general | solution.py:16
  80.7 26.6 %shard_map.28 = f32[256,256]{1,0:T(8,128)} custom-call(f32[256,256]{1,0:T(8,128)} %copy-done.1, f32[256,256]{1,0:T(8,128)} %collective-permute-done.15.far_ref), custom_call_target="tpu_custom_call" | custom-call | flops 40000000 | bytes 786432 | tf_op jit(solution)/shard_map/pallas_call | solution.py:76
  107.3 2.1 %fusion.37 = f32[128,1024]{1,0:T(8,128)} fusion(f32[256,1024]{1,0:T(8,128)S(1)} %fusion.3, f32[256,1024]{1,0:T(8,128)S(1)} %collective-permute-done.16, f32[256,256]{1,0:T(8,128)} %shard_map.28, s32[]{:T(128)S(6)} %select_n.70), kind=kOutput, calls=%fused_computation.35 | convolution fusion | flops 201588736 | bytes 2752516 | tf_op jit(solution)/shard_map/dot_general | solution.py:169
  (47 shorter events, 22.4 us)
Async XLA Ops:
  0.0 1.2 %copy-start = (f32[1024,256]{1,0:T(8,128)S(1)}, f32[1024,256]{1,0:T(8,128)}, u32[]{:S(2)}) copy-start(f32[1024,256]{1,0:T(8,128)} %param.3) | copy-start | bytes 3145732
  3.2 11.6 %collective-permute-start = (f32[320,256]{1,0:T(8,128)S(1)}, f32[320,256]{1,0:T(8,128)S(1)}, u32[]{:S(2)}, u32[]{:S(2)}) collective-permute-start(f32[320,256]{1,0:T(8,128)S(1)} %fusion.22), channel_id=1, source_target_pairs={{0,1},{1,0},{2,3},{3,2},{4,5},{5,4},{6,7},{7,6},{8,9},{9,8},{10,11... | collective-permute-start | bytes 983048 | tf_op jit(solution)/shard_map/ppermute | solution.py:96
  8.4 14.1 %collective-permute-start.5 = (f32[352,256]{1,0:T(8,128)S(1)}, f32[352,256]{1,0:T(8,128)S(1)}, u32[]{:S(2)}, u32[]{:S(2)}) collective-permute-start(f32[352,256]{1,0:T(8,128)S(1)} %fusion.14), channel_id=1, source_target_pairs={{0,1},{1,0},{2,3},{3,2},{4,5},{5,4},{6,7},{7,6},{8,9},{9,8},{10,11... | collective-permute-start | bytes 1081352 | tf_op jit(solution)/shard_map/ppermute | solution.py:96
  16.9 7.8 %collective-permute-start.1 = (f32[160,256]{1,0:T(8,128)S(1)}, f32[160,256]{1,0:T(8,128)S(1)}, u32[]{:S(2)}, u32[]{:S(2)}) collective-permute-start(f32[160,256]{1,0:T(8,128)S(1)} %constant_dynamic-slice_fusion.2), channel_id=1, source_target_pairs={{0,2},{1,3},{2,0},{3,1},{4,6},{5,7},{6,4},{7,5},{8,10},{9,11},{10,... | collective-permute-start | bytes 491528 | tf_op jit(solution)/shard_map/ppermute | solution.py:96
  19.1 19.0 %collective-permute-start.10 = (f32[352,256]{1,0:T(8,128)S(1)}, f32[352,256]{1,0:T(8,128)S(1)}, u32[]{:S(2)}, u32[]{:S(2)}) collective-permute-start(f32[352,256]{1,0:T(8,128)S(1)} %fusion.6), channel_id=1, source_target_pairs={{0,1},{1,0},{2,3},{3,2},{4,5},{5,4},{6,7},{7,6},{8,9},{9,8},{10,11... | collective-permute-start | bytes 1081352 | tf_op jit(solution)/shard_map/ppermute | solution.py:96
  24.7 9.2 %collective-permute-start.2 = (f32[160,256]{1,0:T(8,128)S(1)}, f32[160,256]{1,0:T(8,128)S(1)}, u32[]{:S(2)}, u32[]{:S(2)}) collective-permute-start(f32[160,256]{1,0:T(8,128)S(1)} %dynamic-slice_add_fusion.2), channel_id=1, source_target_pairs={{0,4},{1,5},{2,6},{3,7},{4,0},{5,1},{6,2},{7,3},{8,12},{9,13},{10,... | collective-permute-start | bytes 491528 | tf_op jit(solution)/shard_map/ppermute | solution.py:96
  27.9 6.9 %collective-permute-start.6 = (f32[176,256]{1,0:T(8,128)S(1)}, f32[176,256]{1,0:T(8,128)S(1)}, u32[]{:S(2)}, u32[]{:S(2)}) collective-permute-start(f32[176,256]{1,0:T(8,128)S(1)} %constant_dynamic-slice_fusion.1), channel_id=1, source_target_pairs={{0,2},{1,3},{2,0},{3,1},{4,6},{5,7},{6,4},{7,5},{8,10},{9,11},{10,... | collective-permute-start | bytes 540680 | tf_op jit(solution)/shard_map/ppermute | solution.py:96
  33.9 7.8 %collective-permute-start.3 = (f32[160,256]{1,0:T(8,128)S(1)}, f32[160,256]{1,0:T(8,128)S(1)}, u32[]{:S(2)}, u32[]{:S(2)}) collective-permute-start(f32[160,256]{1,0:T(8,128)S(1)} %add.121), channel_id=1, source_target_pairs={{0,2},{1,3},{2,0},{3,1},{4,6},{5,7},{6,4},{7,5},{8,10},{9,11},{10,... | collective-permute-start | bytes 491528 | tf_op jit(solution)/shard_map/ppermute | solution.py:96
  34.9 8.3 %collective-permute-start.7 = (f32[176,256]{1,0:T(8,128)S(1)}, f32[176,256]{1,0:T(8,128)S(1)}, u32[]{:S(2)}, u32[]{:S(2)}) collective-permute-start(f32[176,256]{1,0:T(8,128)S(1)} %dynamic-slice_add_fusion.1), channel_id=1, source_target_pairs={{0,4},{1,5},{2,6},{3,7},{4,0},{5,1},{6,2},{7,3},{8,12},{9,13},{10,... | collective-permute-start | bytes 540680 | tf_op jit(solution)/shard_map/ppermute | solution.py:96
  41.7 7.0 %collective-permute-start.11 = (f32[176,256]{1,0:T(8,128)S(1)}, f32[176,256]{1,0:T(8,128)S(1)}, u32[]{:S(2)}, u32[]{:S(2)}) collective-permute-start(f32[176,256]{1,0:T(8,128)S(1)} %constant_dynamic-slice_fusion), channel_id=1, source_target_pairs={{0,2},{1,3},{2,0},{3,1},{4,6},{5,7},{6,4},{7,5},{8,10},{9,11},{10,... | collective-permute-start | bytes 540680 | tf_op jit(solution)/shard_map/ppermute | solution.py:96
  41.7 14.1 %collective-permute-start.4 = (f32[320,256]{1,0:T(8,128)S(1)}, f32[320,256]{1,0:T(8,128)S(1)}, u32[]{:S(2)}, u32[]{:S(2)}) collective-permute-start(f32[320,256]{1,0:T(8,128)S(1)} %maximum_select_fusion.2), channel_id=1, source_target_pairs={{0,1},{1,0},{2,3},{3,2},{4,5},{5,4},{6,7},{7,6},{8,9},{9,8},{10,11... | collective-permute-start | bytes 983048 | tf_op jit(solution)/shard_map/ppermute | solution.py:96
  43.2 8.2 %collective-permute-start.8 = (f32[176,256]{1,0:T(8,128)S(1)}, f32[176,256]{1,0:T(8,128)S(1)}, u32[]{:S(2)}, u32[]{:S(2)}) collective-permute-start(f32[176,256]{1,0:T(8,128)S(1)} %add.131), channel_id=1, source_target_pairs={{0,2},{1,3},{2,0},{3,1},{4,6},{5,7},{6,4},{7,5},{8,10},{9,11},{10,... | collective-permute-start | bytes 540680 | tf_op jit(solution)/shard_map/ppermute | solution.py:96
  48.7 9.5 %collective-permute-start.12 = (f32[176,256]{1,0:T(8,128)S(1)}, f32[176,256]{1,0:T(8,128)S(1)}, u32[]{:S(2)}, u32[]{:S(2)}) collective-permute-start(f32[176,256]{1,0:T(8,128)S(1)} %dynamic-slice_add_fusion), channel_id=1, source_target_pairs={{0,4},{1,5},{2,6},{3,7},{4,0},{5,1},{6,2},{7,3},{8,12},{9,13},{10,... | collective-permute-start | bytes 540680 | tf_op jit(solution)/shard_map/ppermute | solution.py:96
  52.0 15.0 %collective-permute-start.9 = (f32[352,256]{1,0:T(8,128)S(1)}, f32[352,256]{1,0:T(8,128)S(1)}, u32[]{:S(2)}, u32[]{:S(2)}) collective-permute-start(f32[352,256]{1,0:T(8,128)S(1)} %maximum_select_fusion), channel_id=1, source_target_pairs={{0,1},{1,0},{2,3},{3,2},{4,5},{5,4},{6,7},{7,6},{8,9},{9,8},{10,11... | collective-permute-start | bytes 1081352 | tf_op jit(solution)/shard_map/ppermute | solution.py:96
  58.3 5.6 %collective-permute-start.13 = (f32[176,256]{1,0:T(8,128)S(1)}, f32[176,256]{1,0:T(8,128)S(1)}, u32[]{:S(2)}, u32[]{:S(2)}) collective-permute-start(f32[176,256]{1,0:T(8,128)S(1)} %add.140), channel_id=1, source_target_pairs={{0,2},{1,3},{2,0},{3,1},{4,6},{5,7},{6,4},{7,5},{8,10},{9,11},{10,... | collective-permute-start | bytes 540680 | tf_op jit(solution)/shard_map/ppermute | solution.py:96
  63.9 7.5 %collective-permute-start.14 = (f32[352,256]{1,0:T(8,128)S(1)}, f32[352,256]{1,0:T(8,128)S(1)}, u32[]{:S(2)}, u32[]{:S(2)}) collective-permute-start(f32[352,256]{1,0:T(8,128)S(1)} %maximum_select_fusion.1), channel_id=1, source_target_pairs={{0,1},{1,0},{2,3},{3,2},{4,5},{5,4},{6,7},{7,6},{8,9},{9,8},{10,11... | collective-permute-start | bytes 1081352 | tf_op jit(solution)/shard_map/ppermute | solution.py:96
  76.6 30.7 %collective-permute-start.16 = (f32[256,1024]{1,0:T(8,128)S(1)}, f32[256,1024]{1,0:T(8,128)S(1)}, u32[]{:S(2)}, u32[]{:S(2)}) collective-permute-start(f32[256,1024]{1,0:T(8,128)S(1)} %fusion.3), channel_id=1, source_target_pairs={{0,8},{8,0},{1,9},{9,1},{2,10},{10,2},{3,11},{11,3},{4,12},{12,4},... | collective-permute-start | bytes 3145736 | tf_op jit(solution)/shard_map/ppermute | solution.py:166
  78.8 1.9 %copy-start.1 = (f32[256,256]{1,0:T(8,128)}, f32[256,256]{1,0:T(8,128)S(1)}, u32[]{:S(2)}) copy-start(f32[256,256]{1,0:T(8,128)S(1)} %fusion.36.gram_ref) | copy-start | bytes 786436
  78.8 1.9 %collective-permute-start.15 = (f32[256,256]{1,0:T(8,128)S(1)}, f32[256,256]{1,0:T(8,128)}, u32[]{:S(2)}, u32[]{:S(2)}) collective-permute-start(f32[256,256]{1,0:T(8,128)S(1)} %fusion.36.gram_ref), channel_id=1, source_target_pairs={{0,8},{8,0},{1,9},{9,1},{2,10},{10,2},{3,11},{11,3},{4,12},{12,4},... | collective-permute-start | bytes 786440 | tf_op jit(solution)/shard_map/ppermute | solution.py:165

commit v3 on v2

v3 whole, which is shorter than its diff:
```python
import functools

import jax
import jax.numpy as jnp
from jax import lax
from jax.experimental import pallas as pl
from jax.experimental.pallas import tpu as pltpu
from jax.sharding import PartitionSpec as P

HIGH = lax.Precision.HIGH
ROWS = 128
WIDTH = 256
BLOCK = 64
LIGHT = pl.CostEstimate(flops=1000, bytes_accessed=1000, transcendentals=0)


def split(x):
    high = x.astype(jnp.bfloat16)
    return high, (x - high.astype(jnp.float32)).astype(jnp.bfloat16)


def three_passes(left, right, dims):
    (left_high, left_low), (right_high, right_low) = left, right
    dot = lambda x, y: lax.dot_general(x, y, (dims, ((), ())), preferred_element_type=jnp.float32)
    return dot(left_high, right_high) + (dot(left_low, right_high) + dot(left_high, right_low))


def sketch_kernel(blocks_ref, texture_ref, sketch_ref, *rest):
    outs, (high, low) = rest[:-2], rest[-2:]
    step = pl.program_id(0)

    @pl.when(step == 0)
    def _():
        high[...], low[...] = split(sketch_ref[...])

    result = three_passes(split(texture_ref[...]), (high[...], low[...]), ((1,), (0,)))
    for k, out in enumerate(outs):
        for part in range(2):

            @pl.when(step == 2 * k + part)
            def _():
                out[part * ROWS : (part + 1) * ROWS, :] = result


def sketched(texture, sketch, halves, earlier=()):
    blocks = jnp.stack([2 * h + part for h in halves for part in range(2)]).astype(jnp.int32)
    if earlier:
        (blocks,) = after([blocks], *earlier)
    scans, rank = sketch.shape
    whole = pl.BlockSpec(memory_space=pltpu.VMEM)
    work = 2 * len(halves) * ROWS
    return pl.pallas_call(
        sketch_kernel,
        out_shape=[jax.ShapeDtypeStruct((2 * ROWS, rank), jnp.float32)] * len(halves),
        grid_spec=pltpu.PrefetchScalarGridSpec(
            num_scalar_prefetch=1,
            grid=(2 * len(halves),),
            in_specs=[pl.BlockSpec((ROWS, scans), lambda i, b: (b[i], 0)), whole],
            out_specs=[whole] * len(halves),
            scratch_shapes=[pltpu.VMEM((scans, rank), jnp.bfloat16)] * 2,
        ),
        compiler_params=pltpu.CompilerParams(vmem_limit_bytes=16 << 20),
        cost_estimate=LIGHT,
    )(blocks, texture, sketch)


def gather_kernel(block_ref, image_ref, texture_ref, *rest):
    if len(rest) == 2:
        gram_ref, product_ref = rest
        old_gram = old_product = None
    else:
        old_gram, old_product, gram_ref, product_ref = rest
    image = split(image_ref[...].T)

    @pl.when(pl.program_id(0) == 0)
    def _():
        rows = split(image_ref[...])
        term = three_passes(image, rows, ((1,), (0,)))
        gram_ref[...] = term if old_gram is None else old_gram[...] + term

    term = three_passes(image, split(texture_ref[...]), ((1,), (0,)))
    product_ref[...] = term if old_product is None else old_product[...] + term


def gathered(half, image, texture, sums):
    rank, scans = image.shape[1], texture.shape[1]
    whole = pl.BlockSpec((rank, rank), lambda i, b: (0, 0))
    line = pl.BlockSpec((rank, WIDTH), lambda i, b: (0, i))
    return pl.pallas_call(
        gather_kernel,
        out_shape=[jax.ShapeDtypeStruct((rank, rank), jnp.float32), jax.ShapeDtypeStruct((rank, scans), jnp.float32)],
        grid_spec=pltpu.PrefetchScalarGridSpec(
            num_scalar_prefetch=1,
            grid=(scans // WIDTH,),
            in_specs=[
                pl.BlockSpec((2 * ROWS, rank), lambda i, b: (0, 0)),
                pl.BlockSpec((2 * ROWS, WIDTH), lambda i, b: (b[0], i)),
            ]
            + [whole, line][: len(sums)],
            out_specs=[whole, line],
        ),
        input_output_aliases={3: 0, 4: 1} if sums else {},
        compiler_params=pltpu.CompilerParams(vmem_limit_bytes=16 << 20),
        cost_estimate=LIGHT,
    )(half.reshape(1), image, texture, *sums)


def inner_rows(left, right):
    return lax.dot_general(
        left,
        right,
        (((0,), (0,)), ((), ())),
        precision=HIGH,
        preferred_element_type=jnp.float32,
    )


def small_dot(left, right, dims):
    return lax.dot_general(
        left,
        right,
        (dims, ((), ())),
        precision=lax.Precision.HIGHEST,
        preferred_element_type=jnp.float32,
    )


def inverse_factor(block):
    size = block.shape[0]
    row = lax.broadcasted_iota(jnp.int32, block.shape, 0)
    col = lax.broadcasted_iota(jnp.int32, block.shape, 1)
    rows = lax.broadcasted_iota(jnp.int32, (size, 1), 0)
    pivots = jnp.ones((size, 1), jnp.float32)
    for j in range(size):
        pivot = block[j : j + 1, j : j + 1]
        factor = jnp.where(rows > j, block[:, j : j + 1] * (1.0 / pivot), 0.0)
        pivots = jnp.where(rows == j, pivot, pivots)
        line = jnp.where(col[0:1] == j, 1.0, block[j : j + 1, :])
        block = jnp.where((col == j) & (row != j), 0.0, block) - factor * line
    unit = jnp.where(col == row, 1.0, jnp.where(col < row, block, 0.0))
    return unit * lax.rsqrt(pivots)


def factor_kernel(gram_ref, far_ref, out_ref, work):
    size = gram_ref.shape[0]
    work[...] = gram_ref[...] + far_ref[...]
    for start in range(0, size, BLOCK):
        stop = start + BLOCK
        corner = inverse_factor(work[start:stop, start:stop])
        lane = lax.broadcasted_iota(jnp.int32, (BLOCK, size), 1)
        wide = jnp.concatenate(
            [jnp.zeros((BLOCK, start), jnp.float32)] * (start > 0)
            + [corner]
            + [jnp.zeros((BLOCK, size - stop), jnp.float32)] * (stop < size),
            axis=1,
        )
        lines = small_dot(corner, work[start:stop, :], ((1,), (0,)))
        lines = jnp.where((lane >= start) & (lane < stop), wide, lines)
        out_ref[start:stop, :] = jnp.where(lane < stop, lines, 0.0)
        if stop < size:
            factor = small_dot(work[stop:, start:stop], corner, ((1,), (1,)))
            lane = lax.broadcasted_iota(jnp.int32, (size - stop, size), 1)
            old = jnp.where((lane >= start) & (lane < stop), 0.0, work[stop:, :])
            work[stop:, :] = old - small_dot(factor, lines, ((1,), (0,)))


def inverse_cholesky(gram, far):
    whole = pl.BlockSpec(memory_space=pltpu.VMEM)
    return pl.pallas_call(
        factor_kernel,
        out_shape=jax.ShapeDtypeStruct(gram.shape, jnp.float32),
        in_specs=[whole, whole],
        out_specs=whole,
        scratch_shapes=[pltpu.VMEM(gram.shape, jnp.float32)],
        compiler_params=pltpu.CompilerParams(vmem_limit_bytes=16 << 20),
        cost_estimate=LIGHT,
    )(gram, far)


def after(values, *earlier):
    out = lax.optimization_barrier(tuple(values) + earlier)
    return out[: len(values)]


def exchanged(texture, sketch):
    col = lax.axis_index("cols")
    side, place = lax.rem(col, 2), lax.div(col, 2)
    odd = lax.rem(place, 2)
    pairs = {step: [(c, c ^ step) for c in range(8)] for step in (1, 2, 4)}
    chunks = range(texture.shape[0] // (4 * ROWS))
    mine = [2 * k + side for k in chunks]
    theirs = [2 * k + 1 - side for k in chunks]
    last = [None]
    texture = pltpu.with_memory_space_constraint(texture, pltpu.HBM)

    def send(x, step):
        last[0] = x
        return lax.ppermute(x, "cols", pairs[step])

    def part(x, which):
        return lax.dynamic_slice_in_dim(x, which * ROWS, ROWS)

    def joined(own, other):
        return jnp.where(odd == 0, jnp.concatenate([own, other]), jnp.concatenate([other, own]))

    outward = []
    for h in theirs:
        outward += sketched(texture, sketch, [h], outward[-1:])
    y = [send(x, 1) for x in outward]
    own = sketched(texture, sketch, mine, outward[-1:])
    kept, half, far, sums = {}, {}, {}, [()]
    arriving = dict(enumerate(y))

    def arrived(k):
        (x,) = after([arriving[k]], last[0])
        return x

    def to_pair(k):
        total = own[k] + arrived(k)
        kept[k] = part(total, odd)
        arriving[k] = send(part(total, 1 - odd), 2)

    def to_line(k):
        kept[k] = kept[k] + arrived(k)
        arriving[k] = send(kept[k], 4)

    def back_to_pair(k):
        kept[k] = kept[k] + arrived(k)
        arriving[k] = send(kept[k], 2)

    def back_to_side(k):
        half[k] = joined(kept[k], arrived(k))
        arriving[k] = send(half[k], 1)

    def gather_own(k):
        (image,) = after([half[k]], last[0])
        sums[0] = gathered(mine[k], image, texture, sums[0])
        last[0] = sums[0][0]

    def gather_far(k):
        sums[0] = gathered(theirs[k], arrived(k), texture, sums[0])
        last[0] = sums[0][0]

    to_p, to_l, to_b, to_s, own_g, far_g = to_pair, to_line, back_to_pair, back_to_side, gather_own, gather_far
    order = [(to_p, 0), (to_p, 1), (to_l, 0), (to_p, 2), (to_l, 1), (to_b, 0), (to_p, 3), (to_l, 2), (to_s, 0)]
    order += [(to_b, 1), (to_l, 3), (own_g, 0), (to_s, 1), (to_b, 2), (own_g, 1), (far_g, 0), (to_b, 3), (to_s, 2)]
    order += [(own_g, 2), (far_g, 1), (to_s, 3), (own_g, 3), (far_g, 2), (far_g, 3)]
    for step, k in order:
        step(k)
    sums = sums[0]
    return sums


def per_device(texture, sketch):
    if lax.axis_size("cols") == 8 and texture.shape[0] == 16 * ROWS:
        gram, product = exchanged(texture, sketch)
    else:
        partial = jnp.dot(texture, sketch, precision=HIGH, preferred_element_type=jnp.float32)
        image = lax.psum(partial, "cols")
        gram, product = inner_rows(image, image), inner_rows(image, texture)
    pair = [(0, 1), (1, 0)]
    far = lax.ppermute(gram, "rows", pair)
    inverse = inverse_cholesky(gram, far)
    (product,) = after([product], far)
    product = product + lax.ppermute(product, "rows", pair)
    span = gram.shape[0] // lax.axis_size("rows")
    inverse = lax.dynamic_slice_in_dim(inverse, lax.axis_index("rows") * span, span)
    return jnp.dot(inverse, product, precision=HIGH, preferred_element_type=jnp.float32)


def solution(mesh):
    placed = (P(("groups", "rows"), "cols"), P("cols", None))
    return jax.shard_map(
        per_device,
        mesh=mesh,
        in_specs=placed,
        out_specs=P(("groups", "rows"), "cols"),
        check_vma=False,
    )
```

time: 110 us -> 118 us (1.073)
  Pallas kernels: 26.6 us -> 70.6 us
  matrix products: 32.5 us -> 1.24 us
  waiting for transfers between devices: 22.8 us -> 10.4 us
  starting transfers between devices: 25.6 us -> 32 us
  other arithmetic: 0.27 us -> 1.46 us
    pallas_call x0 -> x13, Pallas kernels: none -> 45.7 us  [the longest x8 28.4 us: gathered(): pl.pallas_call(gather_kernel, out_shape=[jax.ShapeDtypeStruct((rank, rank...]
    dot_general x18 -> x0, matrix products: 30.4 us -> none  [the longest x12 17.9 us: inner_rows(): lax.dot_general(left, right, (((0,), (0,)), ((), ())), precision=HIGH, pr...]
    ppermute x16 -> x21, waiting for transfers between devices: 22.8 us -> 10.4 us  [the longest x20 8.85 us: send(): return lax.ppermute(x, 'cols', pairs[step])]
    ppermute x16 -> x21, starting transfers between devices: 25.6 us -> 31.9 us  [the longest x20 31.8 us: send(): return lax.ppermute(x, 'cols', pairs[step])]
    pallas_call x1, Pallas kernels: 26.6 us -> 24.9 us  [inverse_cholesky(): pl.pallas_call(factor_kernel, out_shape=jax.ShapeDtypeStruct(gram.shape,...]
  transfers between devices with their start and end apart: 17 -> 22, of which waited for: 10 -> 6; matrix products, arithmetic and copies ran while one was open for 21% -> 1% of each run, Pallas kernels for 24% -> 55%
where the time goes in v3:
time: 118 us; the launch traced here: 117 us
  Pallas kernels  70.6 us (60%)
  starting transfers between devices  32 us (27%)
  waiting for transfers between devices  10.4 us (9%)
  other arithmetic  1.46 us (1%)
  local copies, waits for them, and re-layouts  1.39 us (1%)
  matrix products  1.24 us (1%)
    ppermute x20, starting transfers between devices, send(): return lax.ppermute(x, 'cols', pairs[step])  31.8 us
    pallas_call x8, Pallas kernels, gathered(): pl.pallas_call(gather_kernel, out_shape=[jax.ShapeDtypeStruct((rank, rank...  28.4 us
    pallas_call x1, Pallas kernels, inverse_cholesky(): pl.pallas_call(factor_kernel, out_shape=jax.ShapeDtypeStruct(gram.shape,...  24.9 us
    pallas_call x5, Pallas kernels, sketched(): pl.pallas_call(sketch_kernel, out_shape=[jax.ShapeDtypeStruct((2 * ROWS,...  17.3 us
    ppermute x20, waiting for transfers between devices, send(): return lax.ppermute(x, 'cols', pairs[step])  8.85 us
  transfers between devices with their start and end apart: 22, of which 6 were waited for; matrix products, arithmetic and copies ran while one was open for 1% of the time, Pallas kernels for 55%

profile of v3, /device:TPU:0, one launch (start us, length us, event | category | flops | bytes accessed | tf_op | source)
XLA Modules:
  0.0 117.4 jit_solution(16632745698619240044)
XLA Ops:
  1.3 2.5 %shard_map.28 = f32[256,256]{1,0:T(8,128)S(1)} custom-call(s32[2]{0:T(128)S(1)} %get-tuple-element.106.blocks_ref, f32[2048,1024]{1,0:T(8,128)} %texture_ref.25, f32[1024,256]{1,0:T(8,128)S(1)} %copy-done), custom_call_target="tpu_custom_call" | custom-call | flops 1000 | bytes 1000 | tf_op jit(solution)/shard_map/pallas_call | solution.py:52
  3.9 3.0 %collective-permute-start.1 = (f32[256,256]{1,0:T(8,128)S(1)}, f32[256,256]{1,0:T(8,128)}, u32[]{:S(2)}, u32[]{:S(2)}) collective-permute-start(f32[256,256]{1,0:T(8,128)S(1)} %shard_map.28), channel_id=1, source_target_pairs={{0,1},{1,0},{2,3},{3,2},{4,5},{5,4},{6,7},{7,6},{8,9},{9,8},{10,11... | collective-permute-start | bytes 786440 | tf_op jit(solution)/shard_map/ppermute | solution.py:198
  6.9 2.5 %shard_map.29 = f32[256,256]{1,0:T(8,128)S(1)} custom-call(s32[2]{0:T(128)S(1)} %get-tuple-element.54.blocks_ref, f32[2048,1024]{1,0:T(8,128)} %texture_ref.25, f32[1024,256]{1,0:T(8,128)S(1)} %copy-done), custom_call_target="tpu_custom_call" | custom-call | flops 1000 | bytes 1000 | tf_op jit(solution)/shard_map/pallas_call | solution.py:52
  9.6 2.5 %shard_map.30 = f32[256,256]{1,0:T(8,128)S(1)} custom-call(s32[2]{0:T(128)S(1)} %get-tuple-element.55.blocks_ref, f32[2048,1024]{1,0:T(8,128)} %texture_ref.25, f32[1024,256]{1,0:T(8,128)S(1)} %copy-done.1), custom_call_target="tpu_custom_call" | custom-call | flops 1000 | bytes 1000 | tf_op jit(solution)/shard_map/pallas_call | solution.py:52
  12.1 2.5 %shard_map.31 = f32[256,256]{1,0:T(8,128)S(1)} custom-call(s32[2]{0:T(128)S(1)} %get-tuple-element.56.blocks_ref, f32[2048,1024]{1,0:T(8,128)} %texture_ref.25, f32[1024,256]{1,0:T(8,128)S(1)} %copy-done.1), custom_call_target="tpu_custom_call" | custom-call | flops 1000 | bytes 1000 | tf_op jit(solution)/shard_map/pallas_call | solution.py:52
  14.8 7.1 %shard_map.32 = (f32[256,256]{1,0:T(8,128)S(1)}, f32[256,256]{1,0:T(8,128)S(1)}, f32[256,256]{1,0:T(8,128)S(1)}, f32[256,256]{1,0:T(8,128)S(1)}) custom-call(s32[8]{0:T(128)S(1)} %stack.71.blocks_ref, f32[2048,1024]{1,0:T(8,128)} %texture_ref.25, f32[1024,256]{1,0:T(8,128)S(1)} %copy-done.1), custom_call_target="tpu_custom_call" | custom-call | flops 1000 | bytes 1000 | tf_op jit(solution)/shard_map/pallas_call | solution.py:52
  29.0 2.6 %collective-permute-start.4 = (f32[128,256]{1,0:T(8,128)S(1)}, f32[128,256]{1,0:T(8,128)S(1)}, u32[]{:S(2)}, u32[]{:S(2)}) collective-permute-start(f32[128,256]{1,0:T(8,128)S(1)} %dynamic-slice_add_fusion.3), channel_id=1, source_target_pairs={{0,4},{1,5},{2,6},{3,7},{4,0},{5,1},{6,2},{7,3},{8,12},{9,13},{10,... | collective-permute-start | bytes 393224 | tf_op jit(solution)/shard_map/ppermute | solution.py:198
  31.5 2.8 %collective-permute-done.6 = f32[256,256]{1,0:T(8,128)S(1)} collective-permute-done((f32[256,256]{1,0:T(8,128)S(1)}, f32[256,256]{1,0:T(8,128)S(1)}, u32[]{:S(2)}, u32[]{:S(2)}) %collective-permute-start.6) | collective-permute-done | bytes 262176 | tf_op jit(solution)/shard_map/ppermute | solution.py:198
  34.5 3.0 %collective-permute-start.8 = (f32[128,256]{1,0:T(8,128)S(1)}, f32[128,256]{1,0:T(8,128)S(1)}, u32[]{:S(2)}, u32[]{:S(2)}) collective-permute-start(f32[128,256]{1,0:T(8,128)S(1)} %dynamic-slice_add_fusion.2), channel_id=1, source_target_pairs={{0,4},{1,5},{2,6},{3,7},{4,0},{5,1},{6,2},{7,3},{8,12},{9,13},{10,... | collective-permute-start | bytes 393224 | tf_op jit(solution)/shard_map/ppermute | solution.py:198
  37.6 2.9 %collective-permute-start.9 = (f32[128,256]{1,0:T(8,128)S(1)}, f32[128,256]{1,0:T(8,128)S(1)}, u32[]{:S(2)}, u32[]{:S(2)}) collective-permute-start(f32[128,256]{1,0:T(8,128)S(1)} %add.97), channel_id=1, source_target_pairs={{0,2},{1,3},{2,0},{3,1},{4,6},{5,7},{6,4},{7,5},{8,10},{9,11},{10,... | collective-permute-start | bytes 393224 | tf_op jit(solution)/shard_map/ppermute | solution.py:198
  40.6 3.0 %collective-permute-done.10 = f32[128,256]{1,0:T(8,128)S(1)} collective-permute-done((f32[128,256]{1,0:T(8,128)S(1)}, f32[128,256]{1,0:T(8,128)S(1)}, u32[]{:S(2)}, u32[]{:S(2)}) %collective-permute-start.10) | collective-permute-done | bytes 131104 | tf_op jit(solution)/shard_map/ppermute | solution.py:198
  43.7 2.5 %collective-permute-start.14 = (f32[128,256]{1,0:T(8,128)S(1)}, f32[128,256]{1,0:T(8,128)S(1)}, u32[]{:S(2)}, u32[]{:S(2)}) collective-permute-start(f32[128,256]{1,0:T(8,128)S(1)} %dynamic-slice_add_fusion), channel_id=1, source_target_pairs={{0,4},{1,5},{2,6},{3,7},{4,0},{5,1},{6,2},{7,3},{8,12},{9,13},{10,... | collective-permute-start | bytes 393224 | tf_op jit(solution)/shard_map/ppermute | solution.py:198
  48.2 2.9 %collective-permute-start.13 = (f32[128,256]{1,0:T(8,128)S(1)}, f32[128,256]{1,0:T(8,128)S(1)}, u32[]{:S(2)}, u32[]{:S(2)}) collective-permute-start(f32[128,256]{1,0:T(8,128)S(1)} %add.100), channel_id=1, source_target_pairs={{0,2},{1,3},{2,0},{3,1},{4,6},{5,7},{6,4},{7,5},{8,10},{9,11},{10,... | collective-permute-start | bytes 393224 | tf_op jit(solution)/shard_map/ppermute | solution.py:198
  51.2 3.5 %shard_map.33 = (f32[256,256]{1,0:T(8,128)S(1)}, f32[256,1024]{1,0:T(8,128)S(1)}) custom-call(s32[1]{0:T(128)} %bitcast.19.block_ref, f32[256,256]{1,0:T(8,128)S(1)} %maximum_select_fusion.image_ref, f32[2048,1024]{1,0:T(8,128)} %texture_ref.25), custom_call_target="tpu_custom_call" | custom-call | flops 1000 | bytes 1000 | tf_op jit(solution)/shard_map/pallas_call | solution.py:89
  55.9 3.7 %collective-permute-start.11 = (f32[128,256]{1,0:T(8,128)S(1)}, f32[128,256]{1,0:T(8,128)S(1)}, u32[]{:S(2)}, u32[]{:S(2)}) collective-permute-start(f32[128,256]{1,0:T(8,128)S(1)} %dynamic-slice_add_fusion.1), channel_id=1, source_target_pairs={{0,4},{1,5},{2,6},{3,7},{4,0},{5,1},{6,2},{7,3},{8,12},{9,13},{10,... | collective-permute-start | bytes 393224 | tf_op jit(solution)/shard_map/ppermute | solution.py:198
  59.6 2.5 %collective-permute-start.17 = (f32[128,256]{1,0:T(8,128)S(1)}, f32[128,256]{1,0:T(8,128)S(1)}, u32[]{:S(2)}, u32[]{:S(2)}) collective-permute-start(f32[128,256]{1,0:T(8,128)S(1)} %add.102), channel_id=1, source_target_pairs={{0,2},{1,3},{2,0},{3,1},{4,6},{5,7},{6,4},{7,5},{8,10},{9,11},{10,... | collective-permute-start | bytes 393224 | tf_op jit(solution)/shard_map/ppermute | solution.py:198
  62.1 3.5 %shard_map.34 = (f32[256,256]{1,0:T(8,128)S(1)}, f32[256,1024]{1,0:T(8,128)S(1)}) custom-call(s32[1]{0:T(128)} %bitcast.18.block_ref, f32[256,256]{1,0:T(8,128)S(1)} %maximum_select_fusion.1.image_ref, f32[2048,1024]{1,0:T(8,128)} %texture_ref.25, f32[256,256]{1,0:T(8,128)S(1)} %get-tuple-element.74.rest_0_, ...), custom_call_target="tpu_custom_call", output_to_operand_aliasing={{0}: (3, {}), {1}: (4, {})} | custom-call | flops 1000 | bytes 1000 | tf_op jit(solution)/shard_map/pallas_call | solution.py:89
  65.7 3.5 %shard_map.35 = (f32[256,256]{1,0:T(8,128)S(1)}, f32[256,1024]{1,0:T(8,128)S(1)}) custom-call(s32[1]{0:T(128)} %bitcast.17.block_ref, f32[256,256]{1,0:T(8,128)S(1)} %collective-permute-done.12.image_ref, f32[2048,1024]{1,0:T(8,128)} %texture_ref.25, f32[256,256]{1,0:T(8,128)S(1)} %get-tuple-element.79.rest_0_, ...), custom_call_target="tpu_custom_call", output_to_operand_aliasing={{0}: (3, {}), {1}: (4, {})} | custom-call | flops 1000 | bytes 1000 | tf_op jit(solution)/shard_map/pallas_call | solution.py:89
  70.7 3.5 %shard_map.36 = (f32[256,256]{1,0:T(8,128)S(1)}, f32[256,1024]{1,0:T(8,128)S(1)}) custom-call(s32[1]{0:T(128)} %bitcast.21.block_ref, f32[256,256]{1,0:T(8,128)S(1)} %maximum_select_fusion.2.image_ref, f32[2048,1024]{1,0:T(8,128)} %texture_ref.25, f32[256,256]{1,0:T(8,128)S(1)} %get-tuple-element.82.rest_0_, ...), custom_call_target="tpu_custom_call", output_to_operand_aliasing={{0}: (3, {}), {1}: (4, {})} | custom-call | flops 1000 | bytes 1000 | tf_op jit(solution)/shard_map/pallas_call | solution.py:89
  74.3 3.5 %shard_map.37 = (f32[256,256]{1,0:T(8,128)S(1)}, f32[256,1024]{1,0:T(8,128)S(1)}) custom-call(s32[1]{0:T(128)} %bitcast.20.block_ref, f32[256,256]{1,0:T(8,128)S(1)} %collective-permute-done.16.image_ref, f32[2048,1024]{1,0:T(8,128)} %texture_ref.25, f32[256,256]{1,0:T(8,128)S(1)} %get-tuple-element.87.rest_0_, ...), custom_call_target="tpu_custom_call", output_to_operand_aliasing={{0}: (3, {}), {1}: (4, {})} | custom-call | flops 1000 | bytes 1000 | tf_op jit(solution)/shard_map/pallas_call | solution.py:89
  78.7 3.5 %shard_map.38 = (f32[256,256]{1,0:T(8,128)S(1)}, f32[256,1024]{1,0:T(8,128)S(1)}) custom-call(s32[1]{0:T(128)} %bitcast.23.block_ref, f32[256,256]{1,0:T(8,128)S(1)} %maximum_select_fusion.3.image_ref, f32[2048,1024]{1,0:T(8,128)} %texture_ref.25, f32[256,256]{1,0:T(8,128)S(1)} %get-tuple-element.90.rest_0_, ...), custom_call_target="tpu_custom_call", output_to_operand_aliasing={{0}: (3, {}), {1}: (4, {})} | custom-call | flops 1000 | bytes 1000 | tf_op jit(solution)/shard_map/pallas_call | solution.py:89
  82.2 3.5 %shard_map.39 = (f32[256,256]{1,0:T(8,128)S(1)}, f32[256,1024]{1,0:T(8,128)S(1)}) custom-call(s32[1]{0:T(128)} %bitcast.22.block_ref, f32[256,256]{1,0:T(8,128)S(1)} %collective-permute-done.19.image_ref, f32[2048,1024]{1,0:T(8,128)} %texture_ref.25, f32[256,256]{1,0:T(8,128)S(1)} %get-tuple-element.94.rest_0_, ...), custom_call_target="tpu_custom_call", output_to_operand_aliasing={{0}: (3, {}), {1}: (4, {})} | custom-call | flops 1000 | bytes 1000 | tf_op jit(solution)/shard_map/pallas_call | solution.py:89
  85.8 3.7 %shard_map.40 = (f32[256,256]{1,0:T(8,128)S(1)}, f32[256,1024]{1,0:T(8,128)S(1)}) custom-call(s32[1]{0:T(128)} %bitcast.block_ref, f32[256,256]{1,0:T(8,128)S(1)} %collective-permute-done.18.image_ref, f32[2048,1024]{1,0:T(8,128)} %texture_ref.25, f32[256,256]{1,0:T(8,128)S(1)} %get-tuple-element.97.rest_0_, ...), custom_call_target="tpu_custom_call", output_to_operand_aliasing={{0}: (3, {}), {1}: (4, {})} | custom-call | flops 1000 | bytes 1000 | tf_op jit(solution)/shard_map/pallas_call | solution.py:89
  91.2 24.9 %shard_map.41 = f32[256,256]{1,0:T(8,128)S(1)} custom-call(f32[256,256]{1,0:T(8,128)S(1)} %get-tuple-element.100.gram_ref, f32[256,256]{1,0:T(8,128)S(1)} %collective-permute-done.20.far_ref), custom_call_target="tpu_custom_call" | custom-call | flops 1000 | bytes 1000 | tf_op jit(solution)/shard_map/pallas_call | solution.py:169
  (62 shorter events, 17.5 us)
Async XLA Ops:
  0.1 1.2 %copy-start = (f32[1024,256]{1,0:T(8,128)S(1)}, f32[1024,256]{1,0:T(8,128)}, u32[]{:S(2)}) copy-start(f32[1024,256]{1,0:T(8,128)} %sketch_ref.9) | copy-start | bytes 3145732
  1.3 8.3 %copy-start.1 = (f32[1024,256]{1,0:T(8,128)S(1)}, f32[1024,256]{1,0:T(8,128)}, u32[]{:S(2)}) copy-start(f32[1024,256]{1,0:T(8,128)} %sketch_ref.9) | copy-start | bytes 3145732
  3.9 18.1 %collective-permute-start.1 = (f32[256,256]{1,0:T(8,128)S(1)}, f32[256,256]{1,0:T(8,128)}, u32[]{:S(2)}, u32[]{:S(2)}) collective-permute-start(f32[256,256]{1,0:T(8,128)S(1)} %shard_map.28), channel_id=1, source_target_pairs={{0,1},{1,0},{2,3},{3,2},{4,5},{5,4},{6,7},{7,6},{8,9},{9,8},{10,11... | collective-permute-start | bytes 786440 | tf_op jit(solution)/shard_map/ppermute | solution.py:198
  9.4 17.7 %collective-permute-start.3 = (f32[256,256]{1,0:T(8,128)S(1)}, f32[256,256]{1,0:T(8,128)S(1)}, u32[]{:S(2)}, u32[]{:S(2)}) collective-permute-start(f32[256,256]{1,0:T(8,128)S(1)} %shard_map.29), channel_id=1, source_target_pairs={{0,1},{1,0},{2,3},{3,2},{4,5},{5,4},{6,7},{7,6},{8,9},{9,8},{10,11... | collective-permute-start | bytes 786440 | tf_op jit(solution)/shard_map/ppermute | solution.py:198
  22.9 6.0 %collective-permute-start.2 = (f32[128,256]{1,0:T(8,128)S(1)}, f32[128,256]{1,0:T(8,128)S(1)}, u32[]{:S(2)}, u32[]{:S(2)}) collective-permute-start(f32[128,256]{1,0:T(8,128)S(1)} %constant_dynamic-slice_fusion.3), channel_id=1, source_target_pairs={{0,2},{1,3},{2,0},{3,1},{4,6},{5,7},{6,4},{7,5},{8,10},{9,11},{10,... | collective-permute-start | bytes 393224 | tf_op jit(solution)/shard_map/ppermute | solution.py:198
  25.1 9.2 %collective-permute-start.6 = (f32[256,256]{1,0:T(8,128)S(1)}, f32[256,256]{1,0:T(8,128)S(1)}, u32[]{:S(2)}, u32[]{:S(2)}) collective-permute-start(f32[256,256]{1,0:T(8,128)S(1)} %shard_map.30), channel_id=1, source_target_pairs={{0,1},{1,0},{2,3},{3,2},{4,5},{5,4},{6,7},{7,6},{8,9},{9,8},{10,11... | collective-permute-start | bytes 786440 | tf_op jit(solution)/shard_map/ppermute | solution.py:198
  26.6 13.9 %collective-permute-start = (f32[256,256]{1,0:T(8,128)S(1)}, f32[256,256]{1,0:T(8,128)S(1)}, u32[]{:S(2)}, u32[]{:S(2)}) collective-permute-start(f32[256,256]{1,0:T(8,128)S(1)} %shard_map.31), channel_id=1, source_target_pairs={{0,1},{1,0},{2,3},{3,2},{4,5},{5,4},{6,7},{7,6},{8,9},{9,8},{10,11... | collective-permute-start | bytes 786440 | tf_op jit(solution)/shard_map/ppermute | solution.py:198
  27.2 7.4 %collective-permute-start.5 = (f32[128,256]{1,0:T(8,128)S(1)}, f32[128,256]{1,0:T(8,128)S(1)}, u32[]{:S(2)}, u32[]{:S(2)}) collective-permute-start(f32[128,256]{1,0:T(8,128)S(1)} %constant_dynamic-slice_fusion.2), channel_id=1, source_target_pairs={{0,2},{1,3},{2,0},{3,1},{4,6},{5,7},{6,4},{7,5},{8,10},{9,11},{10,... | collective-permute-start | bytes 393224 | tf_op jit(solution)/shard_map/ppermute | solution.py:198
  29.0 8.6 %collective-permute-start.4 = (f32[128,256]{1,0:T(8,128)S(1)}, f32[128,256]{1,0:T(8,128)S(1)}, u32[]{:S(2)}, u32[]{:S(2)}) collective-permute-start(f32[128,256]{1,0:T(8,128)S(1)} %dynamic-slice_add_fusion.3), channel_id=1, source_target_pairs={{0,4},{1,5},{2,6},{3,7},{4,0},{5,1},{6,2},{7,3},{8,12},{9,13},{10,... | collective-permute-start | bytes 393224 | tf_op jit(solution)/shard_map/ppermute | solution.py:198
  34.4 9.3 %collective-permute-start.10 = (f32[128,256]{1,0:T(8,128)S(1)}, f32[128,256]{1,0:T(8,128)S(1)}, u32[]{:S(2)}, u32[]{:S(2)}) collective-permute-start(f32[128,256]{1,0:T(8,128)S(1)} %constant_dynamic-slice_fusion.1), channel_id=1, source_target_pairs={{0,2},{1,3},{2,0},{3,1},{4,6},{5,7},{6,4},{7,5},{8,10},{9,11},{10,... | collective-permute-start | bytes 393224 | tf_op jit(solution)/shard_map/ppermute | solution.py:198
  34.5 13.7 %collective-permute-start.8 = (f32[128,256]{1,0:T(8,128)S(1)}, f32[128,256]{1,0:T(8,128)S(1)}, u32[]{:S(2)}, u32[]{:S(2)}) collective-permute-start(f32[128,256]{1,0:T(8,128)S(1)} %dynamic-slice_add_fusion.2), channel_id=1, source_target_pairs={{0,4},{1,5},{2,6},{3,7},{4,0},{5,1},{6,2},{7,3},{8,12},{9,13},{10,... | collective-permute-start | bytes 393224 | tf_op jit(solution)/shard_map/ppermute | solution.py:198
  37.6 8.9 %collective-permute-start.9 = (f32[128,256]{1,0:T(8,128)S(1)}, f32[128,256]{1,0:T(8,128)S(1)}, u32[]{:S(2)}, u32[]{:S(2)}) collective-permute-start(f32[128,256]{1,0:T(8,128)S(1)} %add.97), channel_id=1, source_target_pairs={{0,2},{1,3},{2,0},{3,1},{4,6},{5,7},{6,4},{7,5},{8,10},{9,11},{10,... | collective-permute-start | bytes 393224 | tf_op jit(solution)/shard_map/ppermute | solution.py:198
  40.5 10.6 %collective-permute-start.7 = (f32[128,256]{1,0:T(8,128)S(1)}, f32[128,256]{1,0:T(8,128)S(1)}, u32[]{:S(2)}, u32[]{:S(2)}) collective-permute-start(f32[128,256]{1,0:T(8,128)S(1)} %constant_dynamic-slice_fusion), channel_id=1, source_target_pairs={{0,2},{1,3},{2,0},{3,1},{4,6},{5,7},{6,4},{7,5},{8,10},{9,11},{10,... | collective-permute-start | bytes 393224 | tf_op jit(solution)/shard_map/ppermute | solution.py:198
  43.7 15.9 %collective-permute-start.14 = (f32[128,256]{1,0:T(8,128)S(1)}, f32[128,256]{1,0:T(8,128)S(1)}, u32[]{:S(2)}, u32[]{:S(2)}) collective-permute-start(f32[128,256]{1,0:T(8,128)S(1)} %dynamic-slice_add_fusion), channel_id=1, source_target_pairs={{0,4},{1,5},{2,6},{3,7},{4,0},{5,1},{6,2},{7,3},{8,12},{9,13},{10,... | collective-permute-start | bytes 393224 | tf_op jit(solution)/shard_map/ppermute | solution.py:198
  46.5 19.1 %collective-permute-start.12 = (f32[256,256]{1,0:T(8,128)S(1)}, f32[256,256]{1,0:T(8,128)S(1)}, u32[]{:S(2)}, u32[]{:S(2)}) collective-permute-start(f32[256,256]{1,0:T(8,128)S(1)} %maximum_select_fusion.image_ref), channel_id=1, source_target_pairs={{0,1},{1,0},{2,3},{3,2},{4,5},{5,4},{6,7},{7,6},{8,9},{9,8},{10,11... | collective-permute-start | bytes 786440 | tf_op jit(solution)/shard_map/ppermute | solution.py:198
  48.2 7.5 %collective-permute-start.13 = (f32[128,256]{1,0:T(8,128)S(1)}, f32[128,256]{1,0:T(8,128)S(1)}, u32[]{:S(2)}, u32[]{:S(2)}) collective-permute-start(f32[128,256]{1,0:T(8,128)S(1)} %add.100), channel_id=1, source_target_pairs={{0,2},{1,3},{2,0},{3,1},{4,6},{5,7},{6,4},{7,5},{8,10},{9,11},{10,... | collective-permute-start | bytes 393224 | tf_op jit(solution)/shard_map/ppermute | solution.py:198
  55.8 18.5 %collective-permute-start.16 = (f32[256,256]{1,0:T(8,128)S(1)}, f32[256,256]{1,0:T(8,128)S(1)}, u32[]{:S(2)}, u32[]{:S(2)}) collective-permute-start(f32[256,256]{1,0:T(8,128)S(1)} %maximum_select_fusion.1.image_ref), channel_id=1, source_target_pairs={{0,1},{1,0},{2,3},{3,2},{4,5},{5,4},{6,7},{7,6},{8,9},{9,8},{10,11... | collective-permute-start | bytes 786440 | tf_op jit(solution)/shard_map/ppermute | solution.py:198
  55.9 13.3 %collective-permute-start.11 = (f32[128,256]{1,0:T(8,128)S(1)}, f32[128,256]{1,0:T(8,128)S(1)}, u32[]{:S(2)}, u32[]{:S(2)}) collective-permute-start(f32[128,256]{1,0:T(8,128)S(1)} %dynamic-slice_add_fusion.1), channel_id=1, source_target_pairs={{0,4},{1,5},{2,6},{3,7},{4,0},{5,1},{6,2},{7,3},{8,12},{9,13},{10,... | collective-permute-start | bytes 393224 | tf_op jit(solution)/shard_map/ppermute | solution.py:198
  59.6 9.7 %collective-permute-start.17 = (f32[128,256]{1,0:T(8,128)S(1)}, f32[128,256]{1,0:T(8,128)S(1)}, u32[]{:S(2)}, u32[]{:S(2)}) collective-permute-start(f32[128,256]{1,0:T(8,128)S(1)} %add.102), channel_id=1, source_target_pairs={{0,2},{1,3},{2,0},{3,1},{4,6},{5,7},{6,4},{7,5},{8,10},{9,11},{10,... | collective-permute-start | bytes 393224 | tf_op jit(solution)/shard_map/ppermute | solution.py:198
  69.2 8.6 %collective-permute-start.15 = (f32[128,256]{1,0:T(8,128)S(1)}, f32[128,256]{1,0:T(8,128)S(1)}, u32[]{:S(2)}, u32[]{:S(2)}) collective-permute-start(f32[128,256]{1,0:T(8,128)S(1)} %add.103), channel_id=1, source_target_pairs={{0,2},{1,3},{2,0},{3,1},{4,6},{5,7},{6,4},{7,5},{8,10},{9,11},{10,... | collective-permute-start | bytes 393224 | tf_op jit(solution)/shard_map/ppermute | solution.py:198
  69.4 12.8 %collective-permute-start.19 = (f32[256,256]{1,0:T(8,128)S(1)}, f32[256,256]{1,0:T(8,128)S(1)}, u32[]{:S(2)}, u32[]{:S(2)}) collective-permute-start(f32[256,256]{1,0:T(8,128)S(1)} %maximum_select_fusion.2.image_ref), channel_id=1, source_target_pairs={{0,1},{1,0},{2,3},{3,2},{4,5},{5,4},{6,7},{7,6},{8,9},{9,8},{10,11... | collective-permute-start | bytes 786440 | tf_op jit(solution)/shard_map/ppermute | solution.py:198
  77.9 7.9 %collective-permute-start.18 = (f32[256,256]{1,0:T(8,128)S(1)}, f32[256,256]{1,0:T(8,128)S(1)}, u32[]{:S(2)}, u32[]{:S(2)}) collective-permute-start(f32[256,256]{1,0:T(8,128)S(1)} %maximum_select_fusion.3.image_ref), channel_id=1, source_target_pairs={{0,1},{1,0},{2,3},{3,2},{4,5},{5,4},{6,7},{7,6},{8,9},{9,8},{10,11... | collective-permute-start | bytes 786440 | tf_op jit(solution)/shard_map/ppermute | solution.py:198
  89.5 1.6 %collective-permute-start.20 = (f32[256,256]{1,0:T(8,128)S(1)}, f32[256,256]{1,0:T(8,128)S(1)}, u32[]{:S(2)}, u32[]{:S(2)}) collective-permute-start(f32[256,256]{1,0:T(8,128)S(1)} %get-tuple-element.100.gram_ref), channel_id=1, source_target_pairs={{0,8},{8,0},{1,9},{9,1},{2,10},{10,2},{3,11},{11,3},{4,12},{12,4},... | collective-permute-start | bytes 786440 | tf_op jit(solution)/shard_map/ppermute | solution.py:262
  91.1 25.0 %collective-permute-start.21 = (f32[256,1024]{1,0:T(8,128)S(1)}, f32[256,1024]{1,0:T(8,128)S(1)}, u32[]{:S(2)}, u32[]{:S(2)}) collective-permute-start(f32[256,1024]{1,0:T(8,128)S(1)} %get-tuple-element.102), channel_id=1, source_target_pairs={{0,8},{8,0},{1,9},{9,1},{2,10},{10,2},{3,11},{11,3},{4,12},{12,4},... | collective-permute-start | bytes 3145736 | tf_op jit(solution)/shard_map/ppermute | solution.py:265

commit v4 on v3

--- a/solution.py
+++ b/solution.py
@@ -9,100 +9,8 @@
 
 HIGH = lax.Precision.HIGH
 ROWS = 128
-WIDTH = 256
 BLOCK = 64
 LIGHT = pl.CostEstimate(flops=1000, bytes_accessed=1000, transcendentals=0)
-
-
-def split(x):
-    high = x.astype(jnp.bfloat16)
-    return high, (x - high.astype(jnp.float32)).astype(jnp.bfloat16)
-
-
-def three_passes(left, right, dims):
-    (left_high, left_low), (right_high, right_low) = left, right
-    dot = lambda x, y: lax.dot_general(x, y, (dims, ((), ())), preferred_element_type=jnp.float32)
-    return dot(left_high, right_high) + (dot(left_low, right_high) + dot(left_high, right_low))
-
-
-def sketch_kernel(blocks_ref, texture_ref, sketch_ref, *rest):
-    outs, (high, low) = rest[:-2], rest[-2:]
-    step = pl.program_id(0)
-
-    @pl.when(step == 0)
-    def _():
-        high[...], low[...] = split(sketch_ref[...])
-
-    result = three_passes(split(texture_ref[...]), (high[...], low[...]), ((1,), (0,)))
-    for k, out in enumerate(outs):
-        for part in range(2):
-
-            @pl.when(step == 2 * k + part)
-            def _():
-                out[part * ROWS : (part + 1) * ROWS, :] = result
-
-
-def sketched(texture, sketch, halves, earlier=()):
-    blocks = jnp.stack([2 * h + part for h in halves for part in range(2)]).astype(jnp.int32)
-    if earlier:
-        (blocks,) = after([blocks], *earlier)
-    scans, rank = sketch.shape
-    whole = pl.BlockSpec(memory_space=pltpu.VMEM)
-    work = 2 * len(halves) * ROWS
-    return pl.pallas_call(
-        sketch_kernel,
-        out_shape=[jax.ShapeDtypeStruct((2 * ROWS, rank), jnp.float32)] * len(halves),
-        grid_spec=pltpu.PrefetchScalarGridSpec(
-            num_scalar_prefetch=1,
-            grid=(2 * len(halves),),
-            in_specs=[pl.BlockSpec((ROWS, scans), lambda i, b: (b[i], 0)), whole],
-            out_specs=[whole] * len(halves),
-            scratch_shapes=[pltpu.VMEM((scans, rank), jnp.bfloat16)] * 2,
-        ),
-        compiler_params=pltpu.CompilerParams(vmem_limit_bytes=16 << 20),
-        cost_estimate=LIGHT,
-    )(blocks, texture, sketch)
-
-
-def gather_kernel(block_ref, image_ref, texture_ref, *rest):
-    if len(rest) == 2:
-        gram_ref, product_ref = rest
-        old_gram = old_product = None
-    else:
-        old_gram, old_product, gram_ref, product_ref = rest
-    image = split(image_ref[...].T)
-
-    @pl.when(pl.program_id(0) == 0)
-    def _():
-        rows = split(image_ref[...])
-        term = three_passes(image, rows, ((1,), (0,)))
-        gram_ref[...] = term if old_gram is None else old_gram[...] + term
-
-    term = three_passes(image, split(texture_ref[...]), ((1,), (0,)))
-    product_ref[...] = term if old_product is None else old_product[...] + term
-
-
-def gathered(half, image, texture, sums):
-    rank, scans = image.shape[1], texture.shape[1]
-    whole = pl.BlockSpec((rank, rank), lambda i, b: (0, 0))
-    line = pl.BlockSpec((rank, WIDTH), lambda i, b: (0, i))
-    return pl.pallas_call(
-        gather_kernel,
-        out_shape=[jax.ShapeDtypeStruct((rank, rank), jnp.float32), jax.ShapeDtypeStruct((rank, scans), jnp.float32)],
-        grid_spec=pltpu.PrefetchScalarGridSpec(
-            num_scalar_prefetch=1,
-            grid=(scans // WIDTH,),
-            in_specs=[
-                pl.BlockSpec((2 * ROWS, rank), lambda i, b: (0, 0)),
-                pl.BlockSpec((2 * ROWS, WIDTH), lambda i, b: (b[0], i)),
-            ]
-            + [whole, line][: len(sums)],
-            out_specs=[whole, line],
-        ),
-        input_output_aliases={3: 0, 4: 1} if sums else {},
-        compiler_params=pltpu.CompilerParams(vmem_limit_bytes=16 << 20),
-        cost_estimate=LIGHT,
-    )(half.reshape(1), image, texture, *sums)
 
 
 def inner_rows(left, right):
@@ -191,11 +99,17 @@
     mine = [2 * k + side for k in chunks]
     theirs = [2 * k + 1 - side for k in chunks]
     last = [None]
-    texture = pltpu.with_memory_space_constraint(texture, pltpu.HBM)
 
     def send(x, step):
         last[0] = x
         return lax.ppermute(x, "cols", pairs[step])
+
+    def rows_of(h):
+        return lax.dynamic_slice_in_dim(texture, 2 * ROWS * h, 2 * ROWS)
+
+    def sketched(h, *earlier):
+        (weights,) = after([sketch], *earlier)
+        return jnp.dot(rows_of(h), weights, precision=HIGH, preferred_element_type=jnp.float32)
 
     def part(x, which):
         return lax.dynamic_slice_in_dim(x, which * ROWS, ROWS)
@@ -203,11 +117,12 @@
     def joined(own, other):
         return jnp.where(odd == 0, jnp.concatenate([own, other]), jnp.concatenate([other, own]))
 
-    outward = []
+    outward, own = [], []
     for h in theirs:
-        outward += sketched(texture, sketch, [h], outward[-1:])
+        outward.append(sketched(h, *outward[-1:]))
     y = [send(x, 1) for x in outward]
-    own = sketched(texture, sketch, mine, outward[-1:])
+    for h in mine:
+        own.append(sketched(h, (own or outward)[-1]))
     kept, half, far, sums = {}, {}, {}, [()]
     arriving = dict(enumerate(y))
 
@@ -232,18 +147,20 @@
         half[k] = joined(kept[k], arrived(k))
         arriving[k] = send(half[k], 1)
 
-    def gather_own(k):
-        (image,) = after([half[k]], last[0])
-        sums[0] = gathered(mine[k], image, texture, sums[0])
+    def gather(rows, image):
+        terms = inner_rows(image, image), inner_rows(image, rows)
+        sums[0] = lax.optimization_barrier(tuple(map(jnp.add, sums[0], terms)) if sums[0] else terms)
         last[0] = sums[0][0]
 
+    def gather_own(k):
+        gather(rows_of(mine[k]), *after([half[k]], last[0]))
+
     def gather_far(k):
-        sums[0] = gathered(theirs[k], arrived(k), texture, sums[0])
-        last[0] = sums[0][0]
+        gather(rows_of(theirs[k]), arrived(k))
 
     to_p, to_l, to_b, to_s, own_g, far_g = to_pair, to_line, back_to_pair, back_to_side, gather_own, gather_far
     order = [(to_p, 0), (to_p, 1), (to_l, 0), (to_p, 2), (to_l, 1), (to_b, 0), (to_p, 3), (to_l, 2), (to_s, 0)]
-    order += [(to_b, 1), (to_l, 3), (own_g, 0), (to_s, 1), (to_b, 2), (own_g, 1), (far_g, 0), (to_b, 3), (to_s, 2)]
+    order += [(to_b, 1), (to_l, 3), (own_g, 0), (to_s, 1), (to_b, 2), (own_g, 1), (to_b, 3), (far_g, 0), (to_s, 2)]
     order += [(own_g, 2), (far_g, 1), (to_s, 3), (own_g, 3), (far_g, 2), (far_g, 3)]
     for step, k in order:
         step(k)

time: 118 us -> 105 us (0.89)
  Pallas kernels: 70.6 us -> 24.9 us
  matrix products: 1.24 us -> 29.8 us
  waiting for transfers between devices: 10.4 us -> 19.8 us
  starting transfers between devices: 32 us -> 25.9 us
    pallas_call x13 -> x0, Pallas kernels: 45.7 us -> none  [the longest x8 28.4 us: gathered(): pl.pallas_call(gather_kernel, out_shape=[jax.ShapeDtypeStruct((rank, rank...]
    dot_general x0 -> x24, matrix products: none -> 27.4 us  [the longest x8 15.3 us: sketched(): jnp.dot(rows_of(h), weights, precision=HIGH, preferred_element_type=jnp.f...]
    ppermute x20, waiting for transfers between devices: 8.85 us -> 18.2 us  [send(): return lax.ppermute(x, 'cols', pairs[step])]
    ppermute x20, starting transfers between devices: 31.8 us -> 25.7 us  [send(): return lax.ppermute(x, 'cols', pairs[step])]
    dot_general x1, matrix products: 1.24 us -> 2.46 us  [per_device(): jnp.dot(inverse, product, precision=HIGH, preferred_element_type=jnp.floa...]
  transfers between devices with their start and end apart: 22 -> 22, of which waited for: 6 -> 10; matrix products, arithmetic and copies ran while one was open for 1% -> 25% of each run, Pallas kernels for 55% -> 24%
where the time goes in v4:
time: 105 us; the launch traced here: 104 us
  matrix products  29.8 us (28%)
  starting transfers between devices  25.9 us (25%)
  Pallas kernels  24.9 us (24%)
  waiting for transfers between devices  19.8 us (19%)
  local copies, waits for them, and re-layouts  1.97 us (2%)
  other arithmetic  1.31 us (1%)
    ppermute x20, starting transfers between devices, send(): return lax.ppermute(x, 'cols', pairs[step])  25.7 us
    pallas_call x1, Pallas kernels, inverse_cholesky(): pl.pallas_call(factor_kernel, out_shape=jax.ShapeDtypeStruct(gram.shape,...  24.9 us
    ppermute x20, waiting for transfers between devices, send(): return lax.ppermute(x, 'cols', pairs[step])  18.2 us
    dot_general x8, matrix products, sketched(): jnp.dot(rows_of(h), weights, precision=HIGH, preferred_element_type=jnp.f...  15.3 us
    dot_general x16, matrix products, inner_rows(): lax.dot_general(left, right, (((0,), (0,)), ((), ())), precision=HIGH, pr...  12 us
    dot_general x1, matrix products, per_device(): jnp.dot(inverse, product, precision=HIGH, preferred_element_type=jnp.floa...  2.46 us
  transfers between devices with their start and end apart: 22, of which 10 were waited for; matrix products, arithmetic and copies ran while one was open for 25% of the time, Pallas kernels for 24%

profile of v4, /device:TPU:0, one launch (start us, length us, event | category | flops | bytes accessed | tf_op | source)
XLA Modules:
  0.0 104.1 jit_solution(14104578600742561680)
XLA Ops:
  3.1 3.0 %collective-permute-start = (f32[256,256]{1,0:T(8,128)S(1)}, f32[256,256]{1,0:T(8,128)}, u32[]{:S(2)}, u32[]{:S(2)}) collective-permute-start(f32[256,256]{1,0:T(8,128)S(1)} %fusion.12), channel_id=1, source_target_pairs={{0,1},{1,0},{2,3},{3,2},{4,5},{5,4},{6,7},{7,6},{8,9},{9,8},{10,11... | collective-permute-start | bytes 786440 | tf_op jit(solution)/shard_map/ppermute | solution.py:105
  6.1 2.5 %fusion.15 = f32[256,256]{1,0:T(8,128)} fusion(f32[1024,256]{1,0:T(8,128)S(1)} %copy-done, f32[2048,1024]{1,0:T(8,128)} %param.2, s32[]{:T(128)S(6)} %select_n.71), kind=kOutput, calls=%fused_computation.29 | convolution fusion | flops 402653184 | bytes 2359300 | tf_op jit(solution)/shard_map/dot_general | solution.py:112
  10.5 2.1 %collective-permute-start.5 = (f32[256,256]{1,0:T(8,128)S(1)}, f32[256,256]{1,0:T(8,128)S(1)}, u32[]{:S(2)}, u32[]{:S(2)}) collective-permute-start(f32[256,256]{1,0:T(8,128)S(1)} %fusion.18), channel_id=1, source_target_pairs={{0,1},{1,0},{2,3},{3,2},{4,5},{5,4},{6,7},{7,6},{8,9},{9,8},{10,11... | collective-permute-start | bytes 786440 | tf_op jit(solution)/shard_map/ppermute | solution.py:105
  12.5 1.8 %fusion.21 = f32[256,256]{1,0:T(8,128)S(1)} fusion(f32[1024,256]{1,0:T(8,128)S(1)} %copy-done, f32[2048,1024]{1,0:T(8,128)} %param.2, s32[]{:T(128)S(6)} %select_n.69), kind=kOutput, calls=%fused_computation.35 | convolution fusion | flops 402653184 | bytes 2359300 | tf_op jit(solution)/shard_map/dot_general | solution.py:112
  14.5 1.8 %fusion.25 = f32[256,256]{1,0:T(8,128)S(1)} fusion(f32[1024,256]{1,0:T(8,128)S(1)} %copy-done, f32[2048,1024]{1,0:T(8,128)} %param.2, s32[]{:T(128)S(6)} %select_n.68), kind=kOutput, calls=%fused_computation.39 | convolution fusion | flops 402653184 | bytes 2359300 | tf_op jit(solution)/shard_map/dot_general | solution.py:112
  16.3 1.8 %fusion.9 = f32[256,256]{1,0:T(8,128)S(1)} fusion(f32[1024,256]{1,0:T(8,128)S(1)} %copy-done, f32[2048,1024]{1,0:T(8,128)} %param.2, s32[]{:T(128)S(6)} %select_n.75), kind=kOutput, calls=%fused_computation.23 | convolution fusion | flops 402653184 | bytes 2359300 | tf_op jit(solution)/shard_map/dot_general | solution.py:112
  18.2 1.8 %fusion.6 = f32[256,256]{1,0:T(8,128)S(1)} fusion(f32[1024,256]{1,0:T(8,128)S(1)} %copy-done, f32[2048,1024]{1,0:T(8,128)} %param.2, s32[]{:T(128)S(6)} %select_n.76), kind=kOutput, calls=%fused_computation.20 | convolution fusion | flops 402653184 | bytes 2359300 | tf_op jit(solution)/shard_map/dot_general | solution.py:112
  21.7 2.1 %collective-permute-start.1 = (f32[128,256]{1,0:T(8,128)}, f32[128,256]{1,0:T(8,128)S(1)}, u32[]{:S(2)}, u32[]{:S(2)}) collective-permute-start(f32[128,256]{1,0:T(8,128)} %constant_dynamic-slice_fusion.3), channel_id=1, source_target_pairs={{0,2},{1,3},{2,0},{3,1},{4,6},{5,7},{6,4},{7,5},{8,10},{9,11},{10,... | collective-permute-start | bytes 393224 | tf_op jit(solution)/shard_map/ppermute | solution.py:105
  27.5 3.1 %collective-permute-start.3 = (f32[128,256]{1,0:T(8,128)S(1)}, f32[128,256]{1,0:T(8,128)S(1)}, u32[]{:S(2)}, u32[]{:S(2)}) collective-permute-start(f32[128,256]{1,0:T(8,128)S(1)} %dynamic-slice_add_fusion.3), channel_id=1, source_target_pairs={{0,4},{1,5},{2,6},{3,7},{4,0},{5,1},{6,2},{7,3},{8,12},{9,13},{10,... | collective-permute-start | bytes 393224 | tf_op jit(solution)/shard_map/ppermute | solution.py:105
  30.7 2.4 %collective-permute-start.7 = (f32[128,256]{1,0:T(8,128)S(1)}, f32[128,256]{1,0:T(8,128)S(1)}, u32[]{:S(2)}, u32[]{:S(2)}) collective-permute-start(f32[128,256]{1,0:T(8,128)S(1)} %constant_dynamic-slice_fusion.1), channel_id=1, source_target_pairs={{0,2},{1,3},{2,0},{3,1},{4,6},{5,7},{6,4},{7,5},{8,10},{9,11},{10,... | collective-permute-start | bytes 393224 | tf_op jit(solution)/shard_map/ppermute | solution.py:105
  35.0 2.4 %collective-permute-done.3 = f32[128,256]{1,0:T(8,128)S(1)} collective-permute-done((f32[128,256]{1,0:T(8,128)S(1)}, f32[128,256]{1,0:T(8,128)S(1)}, u32[]{:S(2)}, u32[]{:S(2)}) %collective-permute-start.3) | collective-permute-done | bytes 131104 | tf_op jit(solution)/shard_map/ppermute | solution.py:105
  39.7 3.1 %collective-permute-start.12 = (f32[128,256]{1,0:T(8,128)S(1)}, f32[128,256]{1,0:T(8,128)S(1)}, u32[]{:S(2)}, u32[]{:S(2)}) collective-permute-start(f32[128,256]{1,0:T(8,128)S(1)} %dynamic-slice_add_fusion.1), channel_id=1, source_target_pairs={{0,4},{1,5},{2,6},{3,7},{4,0},{5,1},{6,2},{7,3},{8,12},{9,13},{10,... | collective-permute-start | bytes 393224 | tf_op jit(solution)/shard_map/ppermute | solution.py:105
  42.8 2.8 %collective-permute-done.6 = f32[128,256]{1,0:T(8,128)S(1)} collective-permute-done((f32[128,256]{1,0:T(8,128)S(1)}, f32[128,256]{1,0:T(8,128)S(1)}, u32[]{:S(2)}, u32[]{:S(2)}) %collective-permute-start.6) | collective-permute-done | bytes 131104 | tf_op jit(solution)/shard_map/ppermute | solution.py:105
  45.7 2.7 %collective-permute-done.9 = f32[128,256]{1,0:T(8,128)S(1)} collective-permute-done((f32[128,256]{1,0:T(8,128)S(1)}, f32[128,256]{1,0:T(8,128)S(1)}, u32[]{:S(2)}, u32[]{:S(2)}) %collective-permute-start.9) | collective-permute-done | bytes 131104 | tf_op jit(solution)/shard_map/ppermute | solution.py:105
  48.4 1.9 %fusion.23 = f32[256,1024]{1,0:T(8,128)S(1)} fusion(f32[256,256]{1,0:T(8,128)S(1)} %maximum_select_fusion, f32[2048,1024]{1,0:T(8,128)} %param.2, s32[]{:T(128)S(6)} %select_n.68), kind=kOutput, calls=%fused_computation.37 | convolution fusion | flops 402653184 | bytes 2359300 | tf_op jit(solution)/shard_map/dot_general | solution.py:17
  50.7 2.6 %collective-permute-start.14 = (f32[128,256]{1,0:T(8,128)S(1)}, f32[128,256]{1,0:T(8,128)S(1)}, u32[]{:S(2)}, u32[]{:S(2)}) collective-permute-start(f32[128,256]{1,0:T(8,128)S(1)} %dynamic-slice_add_fusion), channel_id=1, source_target_pairs={{0,4},{1,5},{2,6},{3,7},{4,0},{5,1},{6,2},{7,3},{8,12},{9,13},{10,... | collective-permute-start | bytes 393224 | tf_op jit(solution)/shard_map/ppermute | solution.py:105
  53.7 2.5 %collective-permute-start.15 = (f32[128,256]{1,0:T(8,128)S(1)}, f32[128,256]{1,0:T(8,128)S(1)}, u32[]{:S(2)}, u32[]{:S(2)}) collective-permute-start(f32[128,256]{1,0:T(8,128)S(1)} %add.152), channel_id=1, source_target_pairs={{0,2},{1,3},{2,0},{3,1},{4,6},{5,7},{6,4},{7,5},{8,10},{9,11},{10,... | collective-permute-start | bytes 393224 | tf_op jit(solution)/shard_map/ppermute | solution.py:105
  56.8 1.9 %convolution_add_fusion.6 = f32[256,1024]{1,0:T(8,128)S(1)} fusion(f32[256,1024]{1,0:T(8,128)S(1)} %fusion.23, f32[256,256]{1,0:T(8,128)S(1)} %maximum_select_fusion.1, f32[2048,1024]{1,0:T(8,128)} %param.2, s32[]{:T(128)S(6)} %select_n.75), kind=kOutput, calls=%fused_computation.6 | convolution fusion | flops 402915328 | bytes 3407876 | tf_op jit(solution)/shard_map/dot_general | solution.py:17
  60.8 1.9 %convolution_add_fusion.5 = f32[256,1024]{1,0:T(8,128)S(1)} fusion(f32[256,1024]{1,0:T(8,128)S(1)} %convolution_add_fusion.6, f32[256,256]{1,0:T(8,128)S(1)} %collective-permute-done.13, f32[2048,1024]{1,0:T(8,128)} %param.2, s32[]{:T(128)S(6)} %select_n.72), kind=kOutput, calls=%fused_computation.5 | convolution fusion | flops 402915328 | bytes 3407876 | tf_op jit(solution)/shard_map/dot_general | solution.py:17
  64.3 2.2 %collective-permute-done.16 = f32[256,256]{1,0:T(8,128)S(1)} collective-permute-done((f32[256,256]{1,0:T(8,128)S(1)}, f32[256,256]{1,0:T(8,128)S(1)}, u32[]{:S(2)}, u32[]{:S(2)}) %collective-permute-start.16) | collective-permute-done | bytes 262176 | tf_op jit(solution)/shard_map/ppermute | solution.py:105
  68.8 2.0 %collective-permute-done.18 = f32[256,256]{1,0:T(8,128)S(1)} collective-permute-done((f32[256,256]{1,0:T(8,128)S(1)}, f32[256,256]{1,0:T(8,128)S(1)}, u32[]{:S(2)}, u32[]{:S(2)}) %collective-permute-start.18) | collective-permute-done | bytes 262176 | tf_op jit(solution)/shard_map/ppermute | solution.py:105
  71.9 2.1 %collective-permute-done.19 = f32[256,256]{1,0:T(8,128)S(1)} collective-permute-done((f32[256,256]{1,0:T(8,128)S(1)}, f32[256,256]{1,0:T(8,128)S(1)}, u32[]{:S(2)}, u32[]{:S(2)}) %collective-permute-start.19) | collective-permute-done | bytes 262176 | tf_op jit(solution)/shard_map/ppermute | solution.py:105
  76.7 24.9 %shard_map.28 = f32[256,256]{1,0:T(8,128)S(1)} custom-call(f32[256,256]{1,0:T(8,128)S(1)} %convolution_add_fusion.7.gram_ref, f32[256,256]{1,0:T(8,128)S(1)} %collective-permute-done.20.far_ref), custom_call_target="tpu_custom_call" | custom-call | flops 1000 | bytes 1000 | tf_op jit(solution)/shard_map/pallas_call | solution.py:77
  101.7 2.5 %fusion = f32[128,1024]{1,0:T(8,128)} fusion(f32[256,1024]{1,0:T(8,128)S(1)} %convolution_add_fusion, f32[256,1024]{1,0:T(8,128)} %collective-permute-done.21, f32[256,256]{1,0:T(8,128)S(1)} %shard_map.28, s32[]{:T(128)S(6)} %select_n.82), kind=kOutput, calls=%fused_computation.14 | convolution fusion | flops 201588736 | bytes 2752516 | tf_op jit(solution)/shard_map/dot_general | solution.py:185
  (73 shorter events, 25.8 us)
Async XLA Ops:
  3.1 17.0 %collective-permute-start = (f32[256,256]{1,0:T(8,128)S(1)}, f32[256,256]{1,0:T(8,128)}, u32[]{:S(2)}, u32[]{:S(2)}) collective-permute-start(f32[256,256]{1,0:T(8,128)S(1)} %fusion.12), channel_id=1, source_target_pairs={{0,1},{1,0},{2,3},{3,2},{4,5},{5,4},{6,7},{7,6},{8,9},{9,8},{10,11... | collective-permute-start | bytes 786440 | tf_op jit(solution)/shard_map/ppermute | solution.py:105
  8.6 17.0 %collective-permute-start.2 = (f32[256,256]{1,0:T(8,128)}, f32[256,256]{1,0:T(8,128)S(1)}, u32[]{:S(2)}, u32[]{:S(2)}) collective-permute-start(f32[256,256]{1,0:T(8,128)} %fusion.15), channel_id=1, source_target_pairs={{0,1},{1,0},{2,3},{3,2},{4,5},{5,4},{6,7},{7,6},{8,9},{9,8},{10,11... | collective-permute-start | bytes 786440 | tf_op jit(solution)/shard_map/ppermute | solution.py:105
  10.5 20.1 %collective-permute-start.5 = (f32[256,256]{1,0:T(8,128)S(1)}, f32[256,256]{1,0:T(8,128)S(1)}, u32[]{:S(2)}, u32[]{:S(2)}) collective-permute-start(f32[256,256]{1,0:T(8,128)S(1)} %fusion.18), channel_id=1, source_target_pairs={{0,1},{1,0},{2,3},{3,2},{4,5},{5,4},{6,7},{7,6},{8,9},{9,8},{10,11... | collective-permute-start | bytes 786440 | tf_op jit(solution)/shard_map/ppermute | solution.py:105
  14.4 24.8 %collective-permute-start.8 = (f32[256,256]{1,0:T(8,128)S(1)}, f32[256,256]{1,0:T(8,128)S(1)}, u32[]{:S(2)}, u32[]{:S(2)}) collective-permute-start(f32[256,256]{1,0:T(8,128)S(1)} %fusion.21), channel_id=1, source_target_pairs={{0,1},{1,0},{2,3},{3,2},{4,5},{5,4},{6,7},{7,6},{8,9},{9,8},{10,11... | collective-permute-start | bytes 786440 | tf_op jit(solution)/shard_map/ppermute | solution.py:105
  21.7 5.8 %collective-permute-start.1 = (f32[128,256]{1,0:T(8,128)}, f32[128,256]{1,0:T(8,128)S(1)}, u32[]{:S(2)}, u32[]{:S(2)}) collective-permute-start(f32[128,256]{1,0:T(8,128)} %constant_dynamic-slice_fusion.3), channel_id=1, source_target_pairs={{0,2},{1,3},{2,0},{3,1},{4,6},{5,7},{6,4},{7,5},{8,10},{9,11},{10,... | collective-permute-start | bytes 393224 | tf_op jit(solution)/shard_map/ppermute | solution.py:105
  25.7 8.8 %collective-permute-start.4 = (f32[128,256]{1,0:T(8,128)S(1)}, f32[128,256]{1,0:T(8,128)S(1)}, u32[]{:S(2)}, u32[]{:S(2)}) collective-permute-start(f32[128,256]{1,0:T(8,128)S(1)} %constant_dynamic-slice_fusion.2), channel_id=1, source_target_pairs={{0,2},{1,3},{2,0},{3,1},{4,6},{5,7},{6,4},{7,5},{8,10},{9,11},{10,... | collective-permute-start | bytes 393224 | tf_op jit(solution)/shard_map/ppermute | solution.py:105
  27.5 9.9 %collective-permute-start.3 = (f32[128,256]{1,0:T(8,128)S(1)}, f32[128,256]{1,0:T(8,128)S(1)}, u32[]{:S(2)}, u32[]{:S(2)}) collective-permute-start(f32[128,256]{1,0:T(8,128)S(1)} %dynamic-slice_add_fusion.3), channel_id=1, source_target_pairs={{0,4},{1,5},{2,6},{3,7},{4,0},{5,1},{6,2},{7,3},{8,12},{9,13},{10,... | collective-permute-start | bytes 393224 | tf_op jit(solution)/shard_map/ppermute | solution.py:105
  30.7 8.9 %collective-permute-start.7 = (f32[128,256]{1,0:T(8,128)S(1)}, f32[128,256]{1,0:T(8,128)S(1)}, u32[]{:S(2)}, u32[]{:S(2)}) collective-permute-start(f32[128,256]{1,0:T(8,128)S(1)} %constant_dynamic-slice_fusion.1), channel_id=1, source_target_pairs={{0,2},{1,3},{2,0},{3,1},{4,6},{5,7},{6,4},{7,5},{8,10},{9,11},{10,... | collective-permute-start | bytes 393224 | tf_op jit(solution)/shard_map/ppermute | solution.py:105
  34.5 11.1 %collective-permute-start.10 = (f32[128,256]{1,0:T(8,128)S(1)}, f32[128,256]{1,0:T(8,128)S(1)}, u32[]{:S(2)}, u32[]{:S(2)}) collective-permute-start(f32[128,256]{1,0:T(8,128)S(1)} %dynamic-slice_add_fusion.2), channel_id=1, source_target_pairs={{0,4},{1,5},{2,6},{3,7},{4,0},{5,1},{6,2},{7,3},{8,12},{9,13},{10,... | collective-permute-start | bytes 393224 | tf_op jit(solution)/shard_map/ppermute | solution.py:105
  37.4 25.8 %slice-start = ((s8[8388608]{0:T(1024)(128)(4,1)}), s8[4194304]{0:T(1024)(128)(4,1)S(1)}, s32[]{:S(2)}) async-start(s8[8388608]{0:T(1024)(128)(4,1)} %bitcast.32), calls=%async_computation | async-start | bytes 8388608
  37.4 8.2 %collective-permute-start.6 = (f32[128,256]{1,0:T(8,128)S(1)}, f32[128,256]{1,0:T(8,128)S(1)}, u32[]{:S(2)}, u32[]{:S(2)}) collective-permute-start(f32[128,256]{1,0:T(8,128)S(1)} %add.146), channel_id=1, source_target_pairs={{0,2},{1,3},{2,0},{3,1},{4,6},{5,7},{6,4},{7,5},{8,10},{9,11},{10,... | collective-permute-start | bytes 393224 | tf_op jit(solution)/shard_map/ppermute | solution.py:105
  39.2 9.2 %collective-permute-start.9 = (f32[128,256]{1,0:T(8,128)S(1)}, f32[128,256]{1,0:T(8,128)S(1)}, u32[]{:S(2)}, u32[]{:S(2)}) collective-permute-start(f32[128,256]{1,0:T(8,128)S(1)} %constant_dynamic-slice_fusion), channel_id=1, source_target_pairs={{0,2},{1,3},{2,0},{3,1},{4,6},{5,7},{6,4},{7,5},{8,10},{9,11},{10,... | collective-permute-start | bytes 393224 | tf_op jit(solution)/shard_map/ppermute | solution.py:105
  39.7 14.0 %collective-permute-start.12 = (f32[128,256]{1,0:T(8,128)S(1)}, f32[128,256]{1,0:T(8,128)S(1)}, u32[]{:S(2)}, u32[]{:S(2)}) collective-permute-start(f32[128,256]{1,0:T(8,128)S(1)} %dynamic-slice_add_fusion.1), channel_id=1, source_target_pairs={{0,4},{1,5},{2,6},{3,7},{4,0},{5,1},{6,2},{7,3},{8,12},{9,13},{10,... | collective-permute-start | bytes 393224 | tf_op jit(solution)/shard_map/ppermute | solution.py:105
  45.6 8.0 %collective-permute-start.11 = (f32[128,256]{1,0:T(8,128)S(1)}, f32[128,256]{1,0:T(8,128)S(1)}, u32[]{:S(2)}, u32[]{:S(2)}) collective-permute-start(f32[128,256]{1,0:T(8,128)S(1)} %add.150), channel_id=1, source_target_pairs={{0,2},{1,3},{2,0},{3,1},{4,6},{5,7},{6,4},{7,5},{8,10},{9,11},{10,... | collective-permute-start | bytes 393224 | tf_op jit(solution)/shard_map/ppermute | solution.py:105
  50.7 8.4 %collective-permute-start.14 = (f32[128,256]{1,0:T(8,128)S(1)}, f32[128,256]{1,0:T(8,128)S(1)}, u32[]{:S(2)}, u32[]{:S(2)}) collective-permute-start(f32[128,256]{1,0:T(8,128)S(1)} %dynamic-slice_add_fusion), channel_id=1, source_target_pairs={{0,4},{1,5},{2,6},{3,7},{4,0},{5,1},{6,2},{7,3},{8,12},{9,13},{10,... | collective-permute-start | bytes 393224 | tf_op jit(solution)/shard_map/ppermute | solution.py:105
  53.2 7.6 %collective-permute-start.13 = (f32[256,256]{1,0:T(8,128)S(1)}, f32[256,256]{1,0:T(8,128)S(1)}, u32[]{:S(2)}, u32[]{:S(2)}) collective-permute-start(f32[256,256]{1,0:T(8,128)S(1)} %maximum_select_fusion), channel_id=1, source_target_pairs={{0,1},{1,0},{2,3},{3,2},{4,5},{5,4},{6,7},{7,6},{8,9},{9,8},{10,11... | collective-permute-start | bytes 786440 | tf_op jit(solution)/shard_map/ppermute | solution.py:105
  53.7 9.5 %slice-start.1 = ((s8[8388608]{0:T(1024)(128)(4,1)}), s8[4194304]{0:T(1024)(128)(4,1)S(1)}, s32[]{:S(2)}) async-start(s8[8388608]{0:T(1024)(128)(4,1)} %bitcast.32), calls=%async_computation.1 | async-start | bytes 8388608
  53.7 9.4 %collective-permute-start.15 = (f32[128,256]{1,0:T(8,128)S(1)}, f32[128,256]{1,0:T(8,128)S(1)}, u32[]{:S(2)}, u32[]{:S(2)}) collective-permute-start(f32[128,256]{1,0:T(8,128)S(1)} %add.152), channel_id=1, source_target_pairs={{0,2},{1,3},{2,0},{3,1},{4,6},{5,7},{6,4},{7,5},{8,10},{9,11},{10,... | collective-permute-start | bytes 393224 | tf_op jit(solution)/shard_map/ppermute | solution.py:105
  56.3 10.2 %collective-permute-start.16 = (f32[256,256]{1,0:T(8,128)S(1)}, f32[256,256]{1,0:T(8,128)S(1)}, u32[]{:S(2)}, u32[]{:S(2)}) collective-permute-start(f32[256,256]{1,0:T(8,128)S(1)} %maximum_select_fusion.1), channel_id=1, source_target_pairs={{0,1},{1,0},{2,3},{3,2},{4,5},{5,4},{6,7},{7,6},{8,9},{9,8},{10,11... | collective-permute-start | bytes 786440 | tf_op jit(solution)/shard_map/ppermute | solution.py:105
  59.1 8.4 %collective-permute-start.17 = (f32[128,256]{1,0:T(8,128)S(1)}, f32[128,256]{1,0:T(8,128)S(1)}, u32[]{:S(2)}, u32[]{:S(2)}) collective-permute-start(f32[128,256]{1,0:T(8,128)S(1)} %add.155), channel_id=1, source_target_pairs={{0,2},{1,3},{2,0},{3,1},{4,6},{5,7},{6,4},{7,5},{8,10},{9,11},{10,... | collective-permute-start | bytes 393224 | tf_op jit(solution)/shard_map/ppermute | solution.py:105
  63.1 7.7 %collective-permute-start.18 = (f32[256,256]{1,0:T(8,128)S(1)}, f32[256,256]{1,0:T(8,128)S(1)}, u32[]{:S(2)}, u32[]{:S(2)}) collective-permute-start(f32[256,256]{1,0:T(8,128)S(1)} %maximum_select_fusion.2), channel_id=1, source_target_pairs={{0,1},{1,0},{2,3},{3,2},{4,5},{5,4},{6,7},{7,6},{8,9},{9,8},{10,11... | collective-permute-start | bytes 786440 | tf_op jit(solution)/shard_map/ppermute | solution.py:105
  67.5 6.4 %collective-permute-start.19 = (f32[256,256]{1,0:T(8,128)S(1)}, f32[256,256]{1,0:T(8,128)S(1)}, u32[]{:S(2)}, u32[]{:S(2)}) collective-permute-start(f32[256,256]{1,0:T(8,128)S(1)} %maximum_select_fusion.3), channel_id=1, source_target_pairs={{0,1},{1,0},{2,3},{3,2},{4,5},{5,4},{6,7},{7,6},{8,9},{9,8},{10,11... | collective-permute-start | bytes 786440 | tf_op jit(solution)/shard_map/ppermute | solution.py:105
  75.0 1.6 %collective-permute-start.20 = (f32[256,256]{1,0:T(8,128)S(1)}, f32[256,256]{1,0:T(8,128)S(1)}, u32[]{:S(2)}, u32[]{:S(2)}) collective-permute-start(f32[256,256]{1,0:T(8,128)S(1)} %convolution_add_fusion.7.gram_ref), channel_id=1, source_target_pairs={{0,8},{8,0},{1,9},{9,1},{2,10},{10,2},{3,11},{11,3},{4,12},{12,4},... | collective-permute-start | bytes 786440 | tf_op jit(solution)/shard_map/ppermute | solution.py:179
  76.6 25.0 %collective-permute-start.21 = (f32[256,1024]{1,0:T(8,128)S(1)}, f32[256,1024]{1,0:T(8,128)}, u32[]{:S(2)}, u32[]{:S(2)}) collective-permute-start(f32[256,1024]{1,0:T(8,128)S(1)} %convolution_add_fusion), channel_id=1, source_target_pairs={{0,8},{8,0},{1,9},{9,1},{2,10},{10,2},{3,11},{11,3},{4,12},{12,4},... | collective-permute-start | bytes 3145736 | tf_op jit(solution)/shard_map/ppermute | solution.py:182
  (1 other events, 1.2 us)

commit v5 on v4

--- a/solution.py
+++ b/solution.py
@@ -8,7 +8,10 @@
 from jax.sharding import PartitionSpec as P
 
 HIGH = lax.Precision.HIGH
-ROWS = 128
+SIZES = (128, 256, 128)
+MATMULS = [(0, True), (1, True), (0, False), (2, True), (1, False), (2, False)]
+STEPS = [("i", 0), ("l", 0), ("i", 1), ("i", 2), ("b", 0), ("l", 1), ("l", 2), ("o", 0), ("b", 1), ("g", 0), ("f", 0)]
+STEPS += [("o", 1), ("b", 2), ("g", 1), ("o", 2), ("f", 1), ("g", 2), ("f", 2)]
 BLOCK = 64
 LIGHT = pl.CostEstimate(flops=1000, bytes_accessed=1000, transcendentals=0)
 
@@ -91,61 +94,64 @@
 
 
 def exchanged(texture, sketch):
-    col = lax.axis_index("cols")
-    side, place = lax.rem(col, 2), lax.div(col, 2)
-    odd = lax.rem(place, 2)
-    pairs = {step: [(c, c ^ step) for c in range(8)] for step in (1, 2, 4)}
-    chunks = range(texture.shape[0] // (4 * ROWS))
-    mine = [2 * k + side for k in chunks]
-    theirs = [2 * k + 1 - side for k in chunks]
+    col, row = lax.axis_index("cols"), lax.axis_index("rows")
+    bits = lax.rem(col, 2), lax.rem(lax.div(col, 2), 2)
+    side = jnp.where(row == 0, bits[0], bits[1])
+    odd = jnp.where(row == 0, bits[1], bits[0])
+
+    def pairs(first_core, second_core):
+        return [(8 * r + c, 8 * r + (c ^ step)) for r, step in ((0, first_core), (1, second_core)) for c in range(8)]
+
+    outer, inner, line = pairs(1, 2), pairs(2, 1), pairs(4, 4)
+    chunks = range(len(SIZES))
+    starts = [4 * sum(SIZES[:k]) for k in chunks]
     last = [None]
 
-    def send(x, step):
+    def send(x, targets):
         last[0] = x
-        return lax.ppermute(x, "cols", pairs[step])
+        return lax.ppermute(x, ("rows", "cols"), targets)
 
-    def rows_of(h):
-        return lax.dynamic_slice_in_dim(texture, 2 * ROWS * h, 2 * ROWS)
+    def rows_of(k, which):
+        return lax.dynamic_slice_in_dim(texture, starts[k] + which * (2 * SIZES[k]), 2 * SIZES[k])
 
-    def sketched(h, *earlier):
+    def sketched(k, which, *earlier):
         (weights,) = after([sketch], *earlier)
-        return jnp.dot(rows_of(h), weights, precision=HIGH, preferred_element_type=jnp.float32)
+        return jnp.dot(rows_of(k, which), weights, precision=HIGH, preferred_element_type=jnp.float32)
 
     def part(x, which):
-        return lax.dynamic_slice_in_dim(x, which * ROWS, ROWS)
+        return lax.dynamic_slice_in_dim(x, which * (x.shape[0] // 2), x.shape[0] // 2)
 
     def joined(own, other):
         return jnp.where(odd == 0, jnp.concatenate([own, other]), jnp.concatenate([other, own]))
 
-    outward, own = [], []
-    for h in theirs:
-        outward.append(sketched(h, *outward[-1:]))
-    y = [send(x, 1) for x in outward]
-    for h in mine:
-        own.append(sketched(h, (own or outward)[-1]))
-    kept, half, far, sums = {}, {}, {}, [()]
-    arriving = dict(enumerate(y))
+    arriving, own, made = {}, {}, ()
+    for k, theirs in MATMULS:
+        made = (sketched(k, 1 - side if theirs else side, *made),)
+        if theirs:
+            arriving[k] = send(made[0], outer)
+        else:
+            own[k] = made[0]
+    kept, half, sums = {}, {}, [()]
 
     def arrived(k):
-        (x,) = after([arriving[k]], last[0])
-        return x
+        return after([arriving[k]], last[0])[0]
 
-    def to_pair(k):
+    def to_inner(k):
         total = own[k] + arrived(k)
         kept[k] = part(total, odd)
-        arriving[k] = send(part(total, 1 - odd), 2)
+        arriving[k] = send(part(total, 1 - odd), inner)
 
     def to_line(k):
         kept[k] = kept[k] + arrived(k)
-        arriving[k] = send(kept[k], 4)
+        arriving[k] = send(kept[k], line)
 
-    def back_to_pair(k):
+    def back_to_inner(k):
         kept[k] = kept[k] + arrived(k)
-        arriving[k] = send(kept[k], 2)
+        arriving[k] = send(kept[k], inner)
 
-    def back_to_side(k):
+    def back_to_outer(k):
         half[k] = joined(kept[k], arrived(k))
-        arriving[k] = send(half[k], 1)
+        arriving[k] = send(half[k], outer)
 
     def gather(rows, image):
         terms = inner_rows(image, image), inner_rows(image, rows)
@@ -153,23 +159,19 @@
         last[0] = sums[0][0]
 
     def gather_own(k):
-        gather(rows_of(mine[k]), *after([half[k]], last[0]))
+        gather(rows_of(k, side), *after([half[k]], last[0]))
 
     def gather_far(k):
-        gather(rows_of(theirs[k]), arrived(k))
+        gather(rows_of(k, 1 - side), arrived(k))
 
-    to_p, to_l, to_b, to_s, own_g, far_g = to_pair, to_line, back_to_pair, back_to_side, gather_own, gather_far
-    order = [(to_p, 0), (to_p, 1), (to_l, 0), (to_p, 2), (to_l, 1), (to_b, 0), (to_p, 3), (to_l, 2), (to_s, 0)]
-    order += [(to_b, 1), (to_l, 3), (own_g, 0), (to_s, 1), (to_b, 2), (own_g, 1), (to_b, 3), (far_g, 0), (to_s, 2)]
-    order += [(own_g, 2), (far_g, 1), (to_s, 3), (own_g, 3), (far_g, 2), (far_g, 3)]
-    for step, k in order:
-        step(k)
-    sums = sums[0]
-    return sums
+    steps = dict(i=to_inner, l=to_line, b=back_to_inner, o=back_to_outer, g=gather_own, f=gather_far)
+    for name, k in STEPS:
+        steps[name](k)
+    return sums[0]
 
 
 def per_device(texture, sketch):
-    if lax.axis_size("cols") == 8 and texture.shape[0] == 16 * ROWS:
+    if lax.axis_size("cols") == 8 and texture.shape[0] == 4 * sum(SIZES):
         gram, product = exchanged(texture, sketch)
     else:
         partial = jnp.dot(texture, sketch, precision=HIGH, preferred_element_type=jnp.float32)

time: 105 us -> 99.5 us (0.948)
  starting transfers between devices: 25.9 us -> 16.7 us
  waiting for transfers between devices: 19.8 us -> 26.5 us
  matrix products: 29.8 us -> 28 us
    ppermute x20 -> x15, starting transfers between devices: 25.7 us -> 16.5 us  [send(): return lax.ppermute(x, ('rows', 'cols'), targets)]
    ppermute x20 -> x15, waiting for transfers between devices: 18.2 us -> 25 us  [send(): return lax.ppermute(x, ('rows', 'cols'), targets)]
    dot_general x8 -> x6, matrix products: 15.3 us -> 13.2 us  [sketched(): jnp.dot(rows_of(k, which), weights, precision=HIGH, preferred_element_typ...]
    dot_general x16 -> x12, matrix products: 12 us -> 12.4 us  [inner_rows(): lax.dot_general(left, right, (((0,), (0,)), ((), ())), precision=HIGH, pr...]
  transfers between devices with their start and end apart: 22 -> 17, of which waited for: 10 -> 10; matrix products, arithmetic and copies ran while one was open for 25% -> 24% of each run, Pallas kernels for 24% -> 25%
where the time goes in v5:
time: 99.5 us; the launch traced here: 99 us
  matrix products  28 us (28%)
  waiting for transfers between devices  26.5 us (27%)
  Pallas kernels  24.9 us (25%)
  starting transfers between devices  16.7 us (17%)
  local copies, waits for them, and re-layouts  1.3 us (1%)
  other arithmetic  1.27 us (1%)
    ppermute x15, waiting for transfers between devices, send(): return lax.ppermute(x, ('rows', 'cols'), targets)  25 us
    pallas_call x1, Pallas kernels, inverse_cholesky(): pl.pallas_call(factor_kernel, out_shape=jax.ShapeDtypeStruct(gram.shape,...  24.9 us
    ppermute x15, starting transfers between devices, send(): return lax.ppermute(x, ('rows', 'cols'), targets)  16.5 us
    dot_general x6, matrix products, sketched(): jnp.dot(rows_of(k, which), weights, precision=HIGH, preferred_element_typ...  13.2 us
    dot_general x12, matrix products, inner_rows(): lax.dot_general(left, right, (((0,), (0,)), ((), ())), precision=HIGH, pr...  12.4 us
    dot_general x1, matrix products, per_device(): jnp.dot(inverse, product, precision=HIGH, preferred_element_type=jnp.floa...  2.45 us
  transfers between devices with their start and end apart: 17, of which 10 were waited for; matrix products, arithmetic and copies ran while one was open for 24% of the time, Pallas kernels for 25%

profile of v5, /device:TPU:0, one launch (start us, length us, event | category | flops | bytes accessed | tf_op | source)
XLA Modules:
  0.0 99.0 jit_solution(2016357465370639508)
XLA Ops:
  1.2 1.8 %fusion.23 = f32[256,256]{1,0:T(8,128)S(1)} fusion(f32[1024,256]{1,0:T(8,128)S(1)} %copy-done, f32[2048,1024]{1,0:T(8,128)} %param.2, s32[]{:T(128)S(6)} %select_n.73), kind=kOutput, calls=%fused_computation.27 | convolution fusion | flops 402653184 | bytes 2359300 | tf_op jit(solution)/shard_map/dot_general | solution.py:119
  3.1 3.0 %collective-permute-start = (f32[256,256]{1,0:T(8,128)S(1)}, f32[256,256]{1,0:T(8,128)S(1)}, u32[]{:S(2)}, u32[]{:S(2)}) collective-permute-start(f32[256,256]{1,0:T(8,128)S(1)} %fusion.23), channel_id=1, source_target_pairs={{0,1},{1,0},{2,3},{3,2},{4,5},{5,4},{6,7},{7,6},{8,10},{9,11},{10,... | collective-permute-start | bytes 786440 | tf_op jit(solution)/shard_map/ppermute | solution.py:112
  6.1 2.6 %fusion.6 = f32[512,256]{1,0:T(8,128)S(1)} fusion(f32[1024,256]{1,0:T(8,128)S(1)} %copy-done, f32[2048,1024]{1,0:T(8,128)} %param.2, s32[]{:T(128)S(6)} %select_n.72), kind=kOutput, calls=%fused_computation.6 | convolution fusion | flops 805306368 | bytes 3670020 | tf_op jit(solution)/shard_map/dot_general | solution.py:119
  8.8 1.8 %fusion.27 = f32[256,256]{1,0:T(8,128)S(1)} fusion(f32[1024,256]{1,0:T(8,128)S(1)} %copy-done, f32[2048,1024]{1,0:T(8,128)} %param.2, s32[]{:T(128)S(6)} %select_n.71), kind=kOutput, calls=%fused_computation.31 | convolution fusion | flops 402653184 | bytes 2359300 | tf_op jit(solution)/shard_map/dot_general | solution.py:119
  10.6 2.5 %fusion.20 = f32[256,256]{1,0:T(8,128)} fusion(f32[1024,256]{1,0:T(8,128)S(1)} %copy-done, f32[2048,1024]{1,0:T(8,128)} %param.2, s32[]{:T(128)S(6)} %select_n.74), kind=kOutput, calls=%fused_computation.24 | convolution fusion | flops 402653184 | bytes 2359300 | tf_op jit(solution)/shard_map/dot_general | solution.py:119
  13.2 2.0 %collective-permute-start.3 = (f32[256,256]{1,0:T(8,128)}, f32[256,256]{1,0:T(8,128)S(1)}, u32[]{:S(2)}, u32[]{:S(2)}) collective-permute-start(f32[256,256]{1,0:T(8,128)} %fusion.20), channel_id=1, source_target_pairs={{0,1},{1,0},{2,3},{3,2},{4,5},{5,4},{6,7},{7,6},{8,10},{9,11},{10,... | collective-permute-start | bytes 786440 | tf_op jit(solution)/shard_map/ppermute | solution.py:112
  15.2 1.6 %collective-permute-start.1 = (f32[128,256]{1,0:T(8,128)S(1)}, f32[128,256]{1,0:T(8,128)S(1)}, u32[]{:S(2)}, u32[]{:S(2)}) collective-permute-start(f32[128,256]{1,0:T(8,128)S(1)} %constant_dynamic-slice_fusion.2), channel_id=1, source_target_pairs={{0,2},{1,3},{2,0},{3,1},{4,6},{5,7},{6,4},{7,5},{8,9},{9,8},{10,11... | collective-permute-start | bytes 393224 | tf_op jit(solution)/shard_map/ppermute | solution.py:112
  16.9 2.6 %fusion.2 = f32[512,256]{1,0:T(8,128)S(1)} fusion(f32[1024,256]{1,0:T(8,128)S(1)} %copy-done, f32[2048,1024]{1,0:T(8,128)} %param.2, s32[]{:T(128)S(6)} %select_n.78), kind=kOutput, calls=%fused_computation.2 | convolution fusion | flops 805306368 | bytes 3670020 | tf_op jit(solution)/shard_map/dot_general | solution.py:119
  19.5 1.3 %collective-permute-done.1 = f32[128,256]{1,0:T(8,128)S(1)} collective-permute-done((f32[128,256]{1,0:T(8,128)S(1)}, f32[128,256]{1,0:T(8,128)S(1)}, u32[]{:S(2)}, u32[]{:S(2)}) %collective-permute-start.1) | collective-permute-done | bytes 131104 | tf_op jit(solution)/shard_map/ppermute | solution.py:112
  20.8 2.7 %collective-permute-start.2 = (f32[128,256]{1,0:T(8,128)S(1)}, f32[128,256]{1,0:T(8,128)}, u32[]{:S(2)}, u32[]{:S(2)}) collective-permute-start(f32[128,256]{1,0:T(8,128)S(1)} %dynamic-slice_add_fusion.2), channel_id=1, source_target_pairs={{0,4},{1,5},{2,6},{3,7},{4,0},{5,1},{6,2},{7,3},{8,12},{9,13},{10,... | collective-permute-start | bytes 393224 | tf_op jit(solution)/shard_map/ppermute | solution.py:112
  24.7 1.8 %fusion.17 = f32[256,256]{1,0:T(8,128)S(1)} fusion(f32[1024,256]{1,0:T(8,128)S(1)} %copy-done, f32[2048,1024]{1,0:T(8,128)} %param.2, s32[]{:T(128)S(6)} %select_n.77), kind=kOutput, calls=%fused_computation.21 | convolution fusion | flops 402653184 | bytes 2359300 | tf_op jit(solution)/shard_map/dot_general | solution.py:119
  27.7 1.5 %collective-permute-done.2 = f32[128,256]{1,0:T(8,128)} collective-permute-done((f32[128,256]{1,0:T(8,128)S(1)}, f32[128,256]{1,0:T(8,128)}, u32[]{:S(2)}, u32[]{:S(2)}) %collective-permute-start.2) | collective-permute-done | bytes 131104 | tf_op jit(solution)/shard_map/ppermute | solution.py:112
  30.2 1.5 %collective-permute-done.7 = f32[256,256]{1,0:T(8,128)S(1)} collective-permute-done((f32[256,256]{1,0:T(8,128)S(1)}, f32[256,256]{1,0:T(8,128)S(1)}, u32[]{:S(2)}, u32[]{:S(2)}) %collective-permute-start.7) | collective-permute-done | bytes 262176 | tf_op jit(solution)/shard_map/ppermute | solution.py:112
  31.7 1.8 %collective-permute-start.8 = (f32[256,256]{1,0:T(8,128)S(1)}, f32[256,256]{1,0:T(8,128)S(1)}, u32[]{:S(2)}, u32[]{:S(2)}) collective-permute-start(f32[256,256]{1,0:T(8,128)S(1)} %dynamic-slice_add_fusion), channel_id=1, source_target_pairs={{0,4},{1,5},{2,6},{3,7},{4,0},{5,1},{6,2},{7,3},{8,12},{9,13},{10,... | collective-permute-start | bytes 786440 | tf_op jit(solution)/shard_map/ppermute | solution.py:112
  36.9 12.4 %collective-permute-done.8 = f32[256,256]{1,0:T(8,128)S(1)} collective-permute-done((f32[256,256]{1,0:T(8,128)S(1)}, f32[256,256]{1,0:T(8,128)S(1)}, u32[]{:S(2)}, u32[]{:S(2)}) %collective-permute-start.8) | collective-permute-done | bytes 262176 | tf_op jit(solution)/shard_map/ppermute | solution.py:112
  49.8 2.0 %fusion.25 = f32[256,1024]{1,0:T(8,128)S(1)} fusion(f32[256,256]{1,0:T(8,128)S(1)} %maximum_select_fusion.1, f32[2048,1024]{1,0:T(8,128)} %param.2, s32[]{:T(128)S(6)} %select_n.71), kind=kOutput, calls=%fused_computation.29 | convolution fusion | flops 402653184 | bytes 2359300 | tf_op jit(solution)/shard_map/dot_general | solution.py:20
  51.8 1.9 %convolution_add_fusion.2 = f32[256,1024]{1,0:T(8,128)S(1)} fusion(f32[256,1024]{1,0:T(8,128)S(1)} %fusion.25, f32[256,256]{1,0:T(8,128)S(1)} %collective-permute-done.9, f32[2048,1024]{1,0:T(8,128)} %param.2, s32[]{:T(128)S(6)} %select_n.73), kind=kOutput, calls=%fused_computation.12 | convolution fusion | flops 402915328 | bytes 3407876 | tf_op jit(solution)/shard_map/dot_general | solution.py:20
  54.1 1.6 %collective-permute-done.10 = f32[256,256]{1,0:T(8,128)S(1)} collective-permute-done((f32[256,256]{1,0:T(8,128)S(1)}, f32[256,256]{1,0:T(8,128)S(1)}, u32[]{:S(2)}, u32[]{:S(2)}) %collective-permute-start.10) | collective-permute-done | bytes 262176 | tf_op jit(solution)/shard_map/ppermute | solution.py:112
  56.5 3.0 %fusion.11 = f32[256,1024]{1,0:T(8,128)S(1)} fusion(f32[256,1024]{1,0:T(8,128)S(1)} %convolution_add_fusion.2, f32[512,256]{1,0:T(8,128)S(1)} %maximum_select_fusion, f32[2048,1024]{1,0:T(8,128)} %param.2, s32[]{:T(128)S(6)} %select_n.78), kind=kOutput, calls=%fused_computation.9 | convolution fusion | flops 805568512 | bytes 4718596 | tf_op jit(solution)/shard_map/dot_general | solution.py:20
  60.1 2.2 %collective-permute-done.13 = f32[128,256]{1,0:T(8,128)S(1)} collective-permute-done((f32[128,256]{1,0:T(8,128)S(1)}, f32[128,256]{1,0:T(8,128)S(1)}, u32[]{:S(2)}, u32[]{:S(2)}) %collective-permute-start.13) | collective-permute-done | bytes 131104 | tf_op jit(solution)/shard_map/ppermute | solution.py:112
  62.6 2.9 %collective-permute-done.12 = f32[512,256]{1,0:T(8,128)S(1)} collective-permute-done((f32[512,256]{1,0:T(8,128)S(1)}, f32[512,256]{1,0:T(8,128)S(1)}, u32[]{:S(2)}, u32[]{:S(2)}) %collective-permute-start.12) | collective-permute-done | bytes 524320 | tf_op jit(solution)/shard_map/ppermute | solution.py:112
  70.0 1.5 %collective-permute-done.15.far_ref = f32[256,256]{1,0:T(8,128)S(1)} collective-permute-done((f32[256,256]{1,0:T(8,128)S(1)}, f32[256,256]{1,0:T(8,128)S(1)}, u32[]{:S(2)}, u32[]{:S(2)}) %collective-permute-start.15) | collective-permute-done | bytes 262176 | tf_op jit(solution)/shard_map/ppermute | solution.py:181
  71.7 24.9 %shard_map.28 = f32[256,256]{1,0:T(8,128)S(1)} custom-call(f32[256,256]{1,0:T(8,128)S(1)} %convolution_add_fusion.3.gram_ref, f32[256,256]{1,0:T(8,128)S(1)} %collective-permute-done.15.far_ref), custom_call_target="tpu_custom_call" | custom-call | flops 1000 | bytes 1000 | tf_op jit(solution)/shard_map/pallas_call | solution.py:80
  96.6 2.5 %fusion.14 = f32[128,1024]{1,0:T(8,128)} fusion(f32[256,1024]{1,0:T(8,128)S(1)} %convolution_add_fusion, f32[256,1024]{1,0:T(8,128)} %collective-permute-done.16, f32[256,256]{1,0:T(8,128)S(1)} %shard_map.28, s32[]{:T(128)S(6)} %select_n.85), kind=kOutput, calls=%fused_computation.18 | convolution fusion | flops 201588736 | bytes 2752516 | tf_op jit(solution)/shard_map/dot_general | solution.py:187
  (52 shorter events, 15.2 us)
Async XLA Ops:
  0.0 1.2 %copy-start = (f32[1024,256]{1,0:T(8,128)S(1)}, f32[1024,256]{1,0:T(8,128)}, u32[]{:S(2)}) copy-start(f32[1024,256]{1,0:T(8,128)} %param.3) | copy-start | bytes 3145732
  3.1 12.1 %collective-permute-start = (f32[256,256]{1,0:T(8,128)S(1)}, f32[256,256]{1,0:T(8,128)S(1)}, u32[]{:S(2)}, u32[]{:S(2)}) collective-permute-start(f32[256,256]{1,0:T(8,128)S(1)} %fusion.23), channel_id=1, source_target_pairs={{0,1},{1,0},{2,3},{3,2},{4,5},{5,4},{6,7},{7,6},{8,10},{9,11},{10,... | collective-permute-start | bytes 786440 | tf_op jit(solution)/shard_map/ppermute | solution.py:112
  8.7 14.8 %collective-permute-start.4 = (f32[512,256]{1,0:T(8,128)S(1)}, f32[512,256]{1,0:T(8,128)S(1)}, u32[]{:S(2)}, u32[]{:S(2)}) collective-permute-start(f32[512,256]{1,0:T(8,128)S(1)} %fusion.6), channel_id=1, source_target_pairs={{0,1},{1,0},{2,3},{3,2},{4,5},{5,4},{6,7},{7,6},{8,10},{9,11},{10,... | collective-permute-start | bytes 1572872 | tf_op jit(solution)/shard_map/ppermute | solution.py:112
  13.2 13.4 %collective-permute-start.3 = (f32[256,256]{1,0:T(8,128)}, f32[256,256]{1,0:T(8,128)S(1)}, u32[]{:S(2)}, u32[]{:S(2)}) collective-permute-start(f32[256,256]{1,0:T(8,128)} %fusion.20), channel_id=1, source_target_pairs={{0,1},{1,0},{2,3},{3,2},{4,5},{5,4},{6,7},{7,6},{8,10},{9,11},{10,... | collective-permute-start | bytes 786440 | tf_op jit(solution)/shard_map/ppermute | solution.py:112
  15.2 5.6 %collective-permute-start.1 = (f32[128,256]{1,0:T(8,128)S(1)}, f32[128,256]{1,0:T(8,128)S(1)}, u32[]{:S(2)}, u32[]{:S(2)}) collective-permute-start(f32[128,256]{1,0:T(8,128)S(1)} %constant_dynamic-slice_fusion.2), channel_id=1, source_target_pairs={{0,2},{1,3},{2,0},{3,1},{4,6},{5,7},{6,4},{7,5},{8,9},{9,8},{10,11... | collective-permute-start | bytes 393224 | tf_op jit(solution)/shard_map/ppermute | solution.py:112
  20.8 8.4 %collective-permute-start.2 = (f32[128,256]{1,0:T(8,128)S(1)}, f32[128,256]{1,0:T(8,128)}, u32[]{:S(2)}, u32[]{:S(2)}) collective-permute-start(f32[128,256]{1,0:T(8,128)S(1)} %dynamic-slice_add_fusion.2), channel_id=1, source_target_pairs={{0,4},{1,5},{2,6},{3,7},{4,0},{5,1},{6,2},{7,3},{8,12},{9,13},{10,... | collective-permute-start | bytes 393224 | tf_op jit(solution)/shard_map/ppermute | solution.py:112
  23.6 8.1 %collective-permute-start.7 = (f32[256,256]{1,0:T(8,128)S(1)}, f32[256,256]{1,0:T(8,128)S(1)}, u32[]{:S(2)}, u32[]{:S(2)}) collective-permute-start(f32[256,256]{1,0:T(8,128)S(1)} %constant_dynamic-slice_fusion.1), channel_id=1, source_target_pairs={{0,2},{1,3},{2,0},{3,1},{4,6},{5,7},{6,4},{7,5},{8,9},{9,8},{10,11... | collective-permute-start | bytes 786440 | tf_op jit(solution)/shard_map/ppermute | solution.py:112
  26.6 6.9 %collective-permute-start.6 = (f32[128,256]{1,0:T(8,128)S(1)}, f32[128,256]{1,0:T(8,128)S(1)}, u32[]{:S(2)}, u32[]{:S(2)}) collective-permute-start(f32[128,256]{1,0:T(8,128)S(1)} %constant_dynamic-slice_fusion), channel_id=1, source_target_pairs={{0,2},{1,3},{2,0},{3,1},{4,6},{5,7},{6,4},{7,5},{8,9},{9,8},{10,11... | collective-permute-start | bytes 393224 | tf_op jit(solution)/shard_map/ppermute | solution.py:112
  30.1 6.0 %collective-permute-start.5 = (f32[128,256]{1,0:T(8,128)S(1)}, f32[128,256]{1,0:T(8,128)S(1)}, u32[]{:S(2)}, u32[]{:S(2)}) collective-permute-start(f32[128,256]{1,0:T(8,128)S(1)} %add.142), channel_id=1, source_target_pairs={{0,2},{1,3},{2,0},{3,1},{4,6},{5,7},{6,4},{7,5},{8,9},{9,8},{10,11... | collective-permute-start | bytes 393224 | tf_op jit(solution)/shard_map/ppermute | solution.py:112
  31.7 17.6 %collective-permute-start.8 = (f32[256,256]{1,0:T(8,128)S(1)}, f32[256,256]{1,0:T(8,128)S(1)}, u32[]{:S(2)}, u32[]{:S(2)}) collective-permute-start(f32[256,256]{1,0:T(8,128)S(1)} %dynamic-slice_add_fusion), channel_id=1, source_target_pairs={{0,4},{1,5},{2,6},{3,7},{4,0},{5,1},{6,2},{7,3},{8,12},{9,13},{10,... | collective-permute-start | bytes 786440 | tf_op jit(solution)/shard_map/ppermute | solution.py:112
  33.5 22.3 %collective-permute-start.11 = (f32[128,256]{1,0:T(8,128)S(1)}, f32[128,256]{1,0:T(8,128)S(1)}, u32[]{:S(2)}, u32[]{:S(2)}) collective-permute-start(f32[128,256]{1,0:T(8,128)S(1)} %dynamic-slice_add_fusion.1), channel_id=1, source_target_pairs={{0,4},{1,5},{2,6},{3,7},{4,0},{5,1},{6,2},{7,3},{8,12},{9,13},{10,... | collective-permute-start | bytes 393224 | tf_op jit(solution)/shard_map/ppermute | solution.py:112
  36.1 15.7 %collective-permute-start.9 = (f32[256,256]{1,0:T(8,128)S(1)}, f32[256,256]{1,0:T(8,128)S(1)}, u32[]{:S(2)}, u32[]{:S(2)}) collective-permute-start(f32[256,256]{1,0:T(8,128)S(1)} %maximum_select_fusion.1), channel_id=1, source_target_pairs={{0,1},{1,0},{2,3},{3,2},{4,5},{5,4},{6,7},{7,6},{8,10},{9,11},{10,... | collective-permute-start | bytes 786440 | tf_op jit(solution)/shard_map/ppermute | solution.py:112
  49.3 6.4 %collective-permute-start.10 = (f32[256,256]{1,0:T(8,128)S(1)}, f32[256,256]{1,0:T(8,128)S(1)}, u32[]{:S(2)}, u32[]{:S(2)}) collective-permute-start(f32[256,256]{1,0:T(8,128)S(1)} %add.146), channel_id=1, source_target_pairs={{0,2},{1,3},{2,0},{3,1},{4,6},{5,7},{6,4},{7,5},{8,9},{9,8},{10,11... | collective-permute-start | bytes 786440 | tf_op jit(solution)/shard_map/ppermute | solution.py:112
  49.8 16.3 %slice-start = ((s8[8388608]{0:T(1024)(128)(4,1)}), s8[4194304]{0:T(1024)(128)(4,1)S(1)}, s32[]{:S(2)}) async-start(s8[8388608]{0:T(1024)(128)(4,1)} %bitcast.24), calls=%async_computation | async-start | bytes 8388608
  55.8 10.3 %slice-start.1 = ((s8[8388608]{0:T(1024)(128)(4,1)}), s8[4194304]{0:T(1024)(128)(4,1)S(1)}, s32[]{:S(2)}) async-start(s8[8388608]{0:T(1024)(128)(4,1)} %bitcast.24), calls=%async_computation.1 | async-start | bytes 8388608
  55.8 6.5 %collective-permute-start.13 = (f32[128,256]{1,0:T(8,128)S(1)}, f32[128,256]{1,0:T(8,128)S(1)}, u32[]{:S(2)}, u32[]{:S(2)}) collective-permute-start(f32[128,256]{1,0:T(8,128)S(1)} %add.149), channel_id=1, source_target_pairs={{0,2},{1,3},{2,0},{3,1},{4,6},{5,7},{6,4},{7,5},{8,9},{9,8},{10,11... | collective-permute-start | bytes 393224 | tf_op jit(solution)/shard_map/ppermute | solution.py:112
  56.3 9.2 %collective-permute-start.12 = (f32[512,256]{1,0:T(8,128)S(1)}, f32[512,256]{1,0:T(8,128)S(1)}, u32[]{:S(2)}, u32[]{:S(2)}) collective-permute-start(f32[512,256]{1,0:T(8,128)S(1)} %maximum_select_fusion), channel_id=1, source_target_pairs={{0,1},{1,0},{2,3},{3,2},{4,5},{5,4},{6,7},{7,6},{8,10},{9,11},{10,... | collective-permute-start | bytes 1572872 | tf_op jit(solution)/shard_map/ppermute | solution.py:112
  62.4 6.4 %collective-permute-start.14 = (f32[256,256]{1,0:T(8,128)S(1)}, f32[256,256]{1,0:T(8,128)S(1)}, u32[]{:S(2)}, u32[]{:S(2)}) collective-permute-start(f32[256,256]{1,0:T(8,128)S(1)} %maximum_select_fusion.2), channel_id=1, source_target_pairs={{0,1},{1,0},{2,3},{3,2},{4,5},{5,4},{6,7},{7,6},{8,10},{9,11},{10,... | collective-permute-start | bytes 786440 | tf_op jit(solution)/shard_map/ppermute | solution.py:112
  69.9 1.6 %collective-permute-start.15 = (f32[256,256]{1,0:T(8,128)S(1)}, f32[256,256]{1,0:T(8,128)S(1)}, u32[]{:S(2)}, u32[]{:S(2)}) collective-permute-start(f32[256,256]{1,0:T(8,128)S(1)} %convolution_add_fusion.3.gram_ref), channel_id=1, source_target_pairs={{0,8},{8,0},{1,9},{9,1},{2,10},{10,2},{3,11},{11,3},{4,12},{12,4},... | collective-permute-start | bytes 786440 | tf_op jit(solution)/shard_map/ppermute | solution.py:181
  71.5 25.0 %collective-permute-start.16 = (f32[256,1024]{1,0:T(8,128)S(1)}, f32[256,1024]{1,0:T(8,128)}, u32[]{:S(2)}, u32[]{:S(2)}) collective-permute-start(f32[256,1024]{1,0:T(8,128)S(1)} %convolution_add_fusion), channel_id=1, source_target_pairs={{0,8},{8,0},{1,9},{9,1},{2,10},{10,2},{3,11},{11,3},{4,12},{12,4},... | collective-permute-start | bytes 3145736 | tf_op jit(solution)/shard_map/ppermute | solution.py:184

commit v6 on v5

--- a/solution.py
+++ b/solution.py
@@ -8,12 +8,65 @@
 from jax.sharding import PartitionSpec as P
 
 HIGH = lax.Precision.HIGH
+STEP = 256
 SIZES = (128, 256, 128)
-MATMULS = [(0, True), (1, True), (0, False), (2, True), (1, False), (2, False)]
-STEPS = [("i", 0), ("l", 0), ("i", 1), ("i", 2), ("b", 0), ("l", 1), ("l", 2), ("o", 0), ("b", 1), ("g", 0), ("f", 0)]
+STEPS = [("m", [(0, True)]), ("m", [(1, True), (0, False)]), ("i", 0), ("m", [(2, True), (1, False), (2, False)])]
+STEPS += [("l", 0), ("i", 1), ("b", 0), ("i", 2), ("l", 1), ("l", 2), ("o", 0), ("g", 0), ("f", 0), ("b", 1)]
 STEPS += [("o", 1), ("b", 2), ("g", 1), ("o", 2), ("f", 1), ("g", 2), ("f", 2)]
 BLOCK = 64
 LIGHT = pl.CostEstimate(flops=1000, bytes_accessed=1000, transcendentals=0)
+
+
+def split(x):
+    high = x.astype(jnp.bfloat16)
+    return high, (x - high.astype(jnp.float32)).astype(jnp.bfloat16)
+
+
+def three_passes(left, right):
+    (left_high, left_low), (right_high, right_low) = left, right
+    dot = lambda x, y: jnp.dot(x, y, preferred_element_type=jnp.float32)
+    return dot(left_high, right_high) + (dot(left_low, right_high) + dot(left_high, right_low))
+
+
+def sketch_kernel(starts_ref, texture_ref, sketch_ref, *rest):
+    outs, (blocks, sketch, sems) = rest[:-3], rest[-3:]
+    count = blocks.shape[0]
+    fetch = [pltpu.make_async_copy(sketch_ref, sketch, sems.at[count])]
+    for k in range(count):
+        start = pl.multiple_of(starts_ref[k], STEP)
+        fetch.append(pltpu.make_async_copy(texture_ref.at[pl.ds(start, STEP), :], blocks.at[k], sems.at[k]))
+    for copy in fetch:
+        copy.start()
+    fetch[0].wait()
+    weights = split(sketch[...])
+    k = 0
+    for out in outs:
+        for row in range(0, out.shape[0], STEP):
+            fetch[k + 1].wait()
+            out[row : row + STEP, :] = three_passes(split(blocks[k]), weights)
+            k += 1
+
+
+def sketched(texture, sketch, parts, earlier):
+    starts = [first + row for first, length in parts for row in range(0, length, STEP)]
+    (starts,) = after([jnp.stack(starts).astype(jnp.int32)], *earlier)
+    count, (scans, rank) = starts.shape[0], sketch.shape
+    there = pl.BlockSpec(memory_space=pl.ANY)
+    return pl.pallas_call(
+        sketch_kernel,
+        out_shape=[jax.ShapeDtypeStruct((length, rank), jnp.float32) for _, length in parts],
+        in_specs=[pl.BlockSpec(memory_space=pltpu.SMEM), there, there],
+        out_specs=[pl.BlockSpec(memory_space=pltpu.VMEM)] * len(parts),
+        scratch_shapes=[
+            pltpu.VMEM((count, STEP, scans), jnp.float32),
+            pltpu.VMEM((scans, rank), jnp.float32),
+            pltpu.SemaphoreType.DMA((count + 1,)),
+        ],
+        compiler_params=pltpu.CompilerParams(vmem_limit_bytes=16 << 20),
+        cost_estimate=pl.CostEstimate(
+            flops=6 * count * STEP * scans * rank, bytes_accessed=4 * scans * (count * STEP + rank), transcendentals=0
+        ),
+    )(starts, texture, sketch)
 
 
 def inner_rows(left, right):
@@ -114,23 +167,26 @@
     def rows_of(k, which):
         return lax.dynamic_slice_in_dim(texture, starts[k] + which * (2 * SIZES[k]), 2 * SIZES[k])
 
-    def sketched(k, which, *earlier):
-        (weights,) = after([sketch], *earlier)
-        return jnp.dot(rows_of(k, which), weights, precision=HIGH, preferred_element_type=jnp.float32)
-
     def part(x, which):
         return lax.dynamic_slice_in_dim(x, which * (x.shape[0] // 2), x.shape[0] // 2)
 
     def joined(own, other):
         return jnp.where(odd == 0, jnp.concatenate([own, other]), jnp.concatenate([other, own]))
 
-    arriving, own, made = {}, {}, ()
-    for k, theirs in MATMULS:
-        made = (sketched(k, 1 - side if theirs else side, *made),)
-        if theirs:
-            arriving[k] = send(made[0], outer)
-        else:
-            own[k] = made[0]
+    arriving, own = {}, {}
+    pinned = [pltpu.with_memory_space_constraint(x, pltpu.HBM) for x in (texture, sketch)]
+
+    def matmuls(group):
+        chosen = [(k, 1 - side if theirs else side) for k, theirs in group]
+        parts = [(starts[k] + which * (2 * SIZES[k]), 2 * SIZES[k]) for k, which in chosen]
+        made = sketched(*pinned, parts, [] if last[0] is None else [last[0]])
+        last[0] = made[0]
+        for (k, theirs), image in zip(group, made):
+            if theirs:
+                arriving[k] = lax.ppermute(image, ("rows", "cols"), outer)
+            else:
+                own[k] = image
+
     kept, half, sums = {}, {}, [()]
 
     def arrived(k):
@@ -164,7 +220,7 @@
     def gather_far(k):
         gather(rows_of(k, 1 - side), arrived(k))
 
-    steps = dict(i=to_inner, l=to_line, b=back_to_inner, o=back_to_outer, g=gather_own, f=gather_far)
+    steps = dict(i=to_inner, l=to_line, b=back_to_inner, o=back_to_outer, g=gather_own, f=gather_far, m=matmuls)
     for name, k in STEPS:
         steps[name](k)
     return sums[0]

time: 99.5 us -> 112 us (1.13)
  starting transfers between devices: 16.7 us -> 30.5 us
  Pallas kernels: 24.9 us -> 37.6 us
  matrix products: 28 us -> 17.1 us
  local copies, waits for them, and re-layouts: 1.3 us -> 0.06 us
    dot_general x6 -> x0, matrix products: 13.2 us -> none  [sketched(): jnp.dot(rows_of(k, which), weights, precision=HIGH, preferred_element_typ...]
    pallas_call x0 -> x3, Pallas kernels: none -> 12.7 us  [sketched(): pl.pallas_call(sketch_kernel, out_shape=[jax.ShapeDtypeStruct((length, ra...]
    ppermute x15 -> x12, starting transfers between devices: 16.5 us -> 25.6 us  [send(): return lax.ppermute(x, ('rows', 'cols'), targets)]
    ppermute x0 -> x3, starting transfers between devices: none -> 4.71 us  [matmuls(): arriving[k] = lax.ppermute(image, ('rows', 'cols'), outer)]
    dot_general x12, matrix products: 12.4 us -> 15.8 us  [inner_rows(): lax.dot_general(left, right, (((0,), (0,)), ((), ())), precision=HIGH, pr...]
    unnamed x6 -> x0, local copies, waits for them, and re-layouts: 1.24 us -> none
    dot_general x1, matrix products: 2.45 us -> 1.23 us  [per_device(): jnp.dot(inverse, product, precision=HIGH, preferred_element_type=jnp.floa...]
    ppermute x15 -> x12, waiting for transfers between devices: 25 us -> 23.9 us  [send(): return lax.ppermute(x, ('rows', 'cols'), targets)]
  transfers between devices with their start and end apart: 17 -> 17, of which waited for: 10 -> 7; matrix products, arithmetic and copies ran while one was open for 24% -> 13% of each run, Pallas kernels for 25% -> 32%
where the time goes in v6:
time: 112 us; the launch traced here: 111 us
  Pallas kernels  37.6 us (34%)
  starting transfers between devices  30.5 us (27%)
  waiting for transfers between devices  25.4 us (23%)
  matrix products  17.1 us (15%)
    ppermute x12, starting transfers between devices, send(): return lax.ppermute(x, ('rows', 'cols'), targets)  25.6 us
    pallas_call x1, Pallas kernels, inverse_cholesky(): pl.pallas_call(factor_kernel, out_shape=jax.ShapeDtypeStruct(gram.shape,...  24.9 us
    ppermute x12, waiting for transfers between devices, send(): return lax.ppermute(x, ('rows', 'cols'), targets)  23.9 us
    dot_general x12, matrix products, inner_rows(): lax.dot_general(left, right, (((0,), (0,)), ((), ())), precision=HIGH, pr...  15.8 us
    pallas_call x3, Pallas kernels, sketched(): pl.pallas_call(sketch_kernel, out_shape=[jax.ShapeDtypeStruct((length, ra...  12.7 us
    ppermute x3, starting transfers between devices, matmuls(): arriving[k] = lax.ppermute(image, ('rows', 'cols'), outer)  4.71 us
  transfers between devices with their start and end apart: 17, of which 7 were waited for; matrix products, arithmetic and copies ran while one was open for 13% of the time, Pallas kernels for 32%

profile of v6, /device:TPU:0, one launch (start us, length us, event | category | flops | bytes accessed | tf_op | source)
XLA Modules:
  0.0 111.4 jit_solution(15663826538402778874)
XLA Ops:
  0.0 2.1 %shard_map.28 = f32[256,256]{1,0:T(8,128)S(1)} custom-call(s32[1]{0:T(128)} %bitcast.3.starts_ref, f32[2048,1024]{1,0:T(8,128)} %texture_ref.5, f32[1024,256]{1,0:T(8,128)} %sketch_ref.5), custom_call_target="tpu_custom_call" | custom-call | flops 402653184 | bytes 2097152 | tf_op jit(solution)/shard_map/pallas_call | solution.py:55
  2.1 3.0 %collective-permute-start = (f32[256,256]{1,0:T(8,128)S(1)}, f32[256,256]{1,0:T(8,128)S(1)}, u32[]{:S(2)}, u32[]{:S(2)}) collective-permute-start(f32[256,256]{1,0:T(8,128)S(1)} %shard_map.28), channel_id=1, source_target_pairs={{0,1},{1,0},{2,3},{3,2},{4,5},{5,4},{6,7},{7,6},{8,10},{9,11},{10,... | collective-permute-start | bytes 786440 | tf_op jit(solution)/shard_map/ppermute | solution.py:186
  5.3 4.6 %shard_map.29 = (f32[512,256]{1,0:T(8,128)S(1)}, f32[256,256]{1,0:T(8,128)S(1)}) custom-call(s32[3]{0:T(128)S(1)} %pad_add_fusion.starts_ref, f32[2048,1024]{1,0:T(8,128)} %texture_ref.5, f32[1024,256]{1,0:T(8,128)} %sketch_ref.5), custom_call_target="tpu_custom_call" | custom-call | flops 1207959552 | bytes 4194304 | tf_op jit(solution)/shard_map/pallas_call | solution.py:55
  10.1 2.1 %collective-permute-start.1 = (f32[128,256]{1,0:T(8,128)S(1)}, f32[128,256]{1,0:T(8,128)S(1)}, u32[]{:S(2)}, u32[]{:S(2)}) collective-permute-start(f32[128,256]{1,0:T(8,128)S(1)} %constant_dynamic-slice_fusion.2), channel_id=1, source_target_pairs={{0,2},{1,3},{2,0},{3,1},{4,6},{5,7},{6,4},{7,5},{8,9},{9,8},{10,11... | collective-permute-start | bytes 393224 | tf_op jit(solution)/shard_map/ppermute | solution.py:165
  12.2 6.0 %shard_map.30 = (f32[256,256]{1,0:T(8,128)S(1)}, f32[512,256]{1,0:T(8,128)S(1)}, f32[256,256]{1,0:T(8,128)S(1)}) custom-call(s32[4]{0:T(128)S(1)} %pad_add_fusion.1.starts_ref, f32[2048,1024]{1,0:T(8,128)} %texture_ref.5, f32[1024,256]{1,0:T(8,128)} %sketch_ref.5), custom_call_target="tpu_custom_call" | custom-call | flops 1610612736 | bytes 5242880 | tf_op jit(solution)/shard_map/pallas_call | solution.py:55
  21.3 2.6 %collective-permute-start.2 = (f32[128,256]{1,0:T(8,128)S(1)}, f32[128,256]{1,0:T(8,128)S(1)}, u32[]{:S(2)}, u32[]{:S(2)}) collective-permute-start(f32[128,256]{1,0:T(8,128)S(1)} %dynamic-slice_add_fusion.2), channel_id=1, source_target_pairs={{0,4},{1,5},{2,6},{3,7},{4,0},{5,1},{6,2},{7,3},{8,12},{9,13},{10,... | collective-permute-start | bytes 393224 | tf_op jit(solution)/shard_map/ppermute | solution.py:165
  23.9 4.6 %collective-permute-done.2 = f32[128,256]{1,0:T(8,128)S(1)} collective-permute-done((f32[128,256]{1,0:T(8,128)S(1)}, f32[128,256]{1,0:T(8,128)S(1)}, u32[]{:S(2)}, u32[]{:S(2)}) %collective-permute-start.2) | collective-permute-done | bytes 131104 | tf_op jit(solution)/shard_map/ppermute | solution.py:165
  28.5 2.5 %collective-permute-start.4 = (f32[128,256]{1,0:T(8,128)S(1)}, f32[128,256]{1,0:T(8,128)S(1)}, u32[]{:S(2)}, u32[]{:S(2)}) collective-permute-start(f32[128,256]{1,0:T(8,128)S(1)} %add.141), channel_id=1, source_target_pairs={{0,2},{1,3},{2,0},{3,1},{4,6},{5,7},{6,4},{7,5},{8,9},{9,8},{10,11... | collective-permute-start | bytes 393224 | tf_op jit(solution)/shard_map/ppermute | solution.py:165
  31.2 4.9 %collective-permute-done.6 = f32[128,256]{1,0:T(8,128)S(1)} collective-permute-done((f32[128,256]{1,0:T(8,128)S(1)}, f32[128,256]{1,0:T(8,128)S(1)}, u32[]{:S(2)}, u32[]{:S(2)}) %collective-permute-start.6) | collective-permute-done | bytes 131104 | tf_op jit(solution)/shard_map/ppermute | solution.py:165
  37.3 4.4 %collective-permute-start.9 = (f32[256,256]{1,0:T(8,128)S(1)}, f32[256,256]{1,0:T(8,128)S(1)}, u32[]{:S(2)}, u32[]{:S(2)}) collective-permute-start(f32[256,256]{1,0:T(8,128)S(1)} %dynamic-slice_add_fusion), channel_id=1, source_target_pairs={{0,4},{1,5},{2,6},{3,7},{4,0},{5,1},{6,2},{7,3},{8,12},{9,13},{10,... | collective-permute-start | bytes 786440 | tf_op jit(solution)/shard_map/ppermute | solution.py:165
  42.1 1.9 %fusion.15 = f32[256,1024]{1,0:T(8,128)S(1)} fusion(f32[256,256]{1,0:T(8,128)S(1)} %maximum_select_fusion.1, f32[2048,1024]{1,0:T(8,128)} %texture_ref.5, s32[]{:T(128)S(6)} %select_n.70), kind=kOutput, calls=%fused_computation.19 | convolution fusion | flops 402653184 | bytes 2359300 | tf_op jit(solution)/shard_map/dot_general | solution.py:73
  44.0 1.9 %convolution_add_fusion.2 = f32[256,1024]{1,0:T(8,128)S(1)} fusion(f32[256,1024]{1,0:T(8,128)S(1)} %fusion.15, f32[256,256]{1,0:T(8,128)S(1)} %collective-permute-done.8, f32[2048,1024]{1,0:T(8,128)} %texture_ref.5, s32[]{:T(128)S(6)} %select_n.71), kind=kOutput, calls=%fused_computation.8 | convolution fusion | flops 402915328 | bytes 3407876 | tf_op jit(solution)/shard_map/dot_general | solution.py:73
  46.2 4.6 %collective-permute-done.9 = f32[256,256]{1,0:T(8,128)S(1)} collective-permute-done((f32[256,256]{1,0:T(8,128)S(1)}, f32[256,256]{1,0:T(8,128)S(1)}, u32[]{:S(2)}, u32[]{:S(2)}) %collective-permute-start.9) | collective-permute-done | bytes 262176 | tf_op jit(solution)/shard_map/ppermute | solution.py:165
  50.9 1.9 %collective-permute-start.10 = (f32[256,256]{1,0:T(8,128)S(1)}, f32[256,256]{1,0:T(8,128)S(1)}, u32[]{:S(2)}, u32[]{:S(2)}) collective-permute-start(f32[256,256]{1,0:T(8,128)S(1)} %add.150), channel_id=1, source_target_pairs={{0,2},{1,3},{2,0},{3,1},{4,6},{5,7},{6,4},{7,5},{8,9},{9,8},{10,11... | collective-permute-start | bytes 786440 | tf_op jit(solution)/shard_map/ppermute | solution.py:165
  52.8 3.4 %collective-permute-start.11 = (f32[128,256]{1,0:T(8,128)S(1)}, f32[128,256]{1,0:T(8,128)S(1)}, u32[]{:S(2)}, u32[]{:S(2)}) collective-permute-start(f32[128,256]{1,0:T(8,128)S(1)} %dynamic-slice_add_fusion.1), channel_id=1, source_target_pairs={{0,4},{1,5},{2,6},{3,7},{4,0},{5,1},{6,2},{7,3},{8,12},{9,13},{10,... | collective-permute-start | bytes 393224 | tf_op jit(solution)/shard_map/ppermute | solution.py:165
  56.2 4.6 %collective-permute-done.10 = f32[256,256]{1,0:T(8,128)S(1)} collective-permute-done((f32[256,256]{1,0:T(8,128)S(1)}, f32[256,256]{1,0:T(8,128)S(1)}, u32[]{:S(2)}, u32[]{:S(2)}) %collective-permute-start.10) | collective-permute-done | bytes 262176 | tf_op jit(solution)/shard_map/ppermute | solution.py:165
  62.3 4.0 %collective-permute-start.13 = (f32[128,256]{1,0:T(8,128)S(1)}, f32[128,256]{1,0:T(8,128)S(1)}, u32[]{:S(2)}, u32[]{:S(2)}) collective-permute-start(f32[128,256]{1,0:T(8,128)S(1)} %add.151), channel_id=1, source_target_pairs={{0,2},{1,3},{2,0},{3,1},{4,6},{5,7},{6,4},{7,5},{8,9},{9,8},{10,11... | collective-permute-start | bytes 393224 | tf_op jit(solution)/shard_map/ppermute | solution.py:165
  66.3 2.7 %fusion.4 = f32[256,1024]{1,0:T(8,128)S(1)} fusion(f32[256,1024]{1,0:T(8,128)S(1)} %convolution_add_fusion.2, f32[512,256]{1,0:T(8,128)S(1)} %maximum_select_fusion, f32[2048,1024]{1,0:T(8,128)} %texture_ref.5, s32[]{:T(128)S(6)} %select_n.74), kind=kOutput, calls=%fused_computation.4 | convolution fusion | flops 805568512 | bytes 4718596 | tf_op jit(solution)/shard_map/dot_general | solution.py:73
  69.6 2.1 %collective-permute-start.14 = (f32[256,256]{1,0:T(8,128)S(1)}, f32[256,256]{1,0:T(8,128)S(1)}, u32[]{:S(2)}, u32[]{:S(2)}) collective-permute-start(f32[256,256]{1,0:T(8,128)S(1)} %maximum_select_fusion.2), channel_id=1, source_target_pairs={{0,1},{1,0},{2,3},{3,2},{4,5},{5,4},{6,7},{7,6},{8,10},{9,11},{10,... | collective-permute-start | bytes 786440 | tf_op jit(solution)/shard_map/ppermute | solution.py:165
  71.7 3.7 %collective-permute-done.12 = f32[512,256]{1,0:T(8,128)S(1)} collective-permute-done((f32[512,256]{1,0:T(8,128)S(1)}, f32[512,256]{1,0:T(8,128)S(1)}, u32[]{:S(2)}, u32[]{:S(2)}) %collective-permute-start.12) | collective-permute-done | bytes 524320 | tf_op jit(solution)/shard_map/ppermute | solution.py:165
  76.0 2.9 %fusion.7 = f32[256,1024]{1,0:T(8,128)S(1)} fusion(f32[256,1024]{1,0:T(8,128)S(1)} %fusion.4, f32[512,256]{1,0:T(8,128)S(1)} %collective-permute-done.12, f32[2048,1024]{1,0:T(8,128)} %texture_ref.5, s32[]{:T(128)S(6)} %select_n.76), kind=kOutput, calls=%fused_computation.5 | convolution fusion | flops 805568512 | bytes 4718596 | tf_op jit(solution)/shard_map/dot_general | solution.py:73
  78.9 1.9 %convolution_add_fusion.1 = f32[256,1024]{1,0:T(8,128)S(1)} fusion(f32[256,1024]{1,0:T(8,128)S(1)} %fusion.7, f32[256,256]{1,0:T(8,128)S(1)} %maximum_select_fusion.2, f32[2048,1024]{1,0:T(8,128)} %texture_ref.5, s32[]{:T(128)S(6)} %select_n.77), kind=kOutput, calls=%fused_computation.7 | convolution fusion | flops 402915328 | bytes 3407876 | tf_op jit(solution)/shard_map/dot_general | solution.py:73
  81.7 1.9 %convolution_add_fusion = f32[256,1024]{1,0:T(8,128)S(1)} fusion(f32[256,1024]{1,0:T(8,128)S(1)} %convolution_add_fusion.1, f32[256,256]{1,0:T(8,128)S(1)} %collective-permute-done.14, f32[2048,1024]{1,0:T(8,128)} %texture_ref.5, s32[]{:T(128)S(6)} %select_n.78), kind=kOutput, calls=%fused_computation.6 | convolution fusion | flops 402915328 | bytes 3407876 | tf_op jit(solution)/shard_map/dot_general | solution.py:73
  85.3 24.9 %shard_map.31 = f32[256,256]{1,0:T(8,128)S(1)} custom-call(f32[256,256]{1,0:T(8,128)S(1)} %convolution_add_fusion.3.gram_ref, f32[256,256]{1,0:T(8,128)S(1)} %collective-permute-done.15.far_ref), custom_call_target="tpu_custom_call" | custom-call | flops 1000 | bytes 1000 | tf_op jit(solution)/shard_map/pallas_call | solution.py:133
  (44 shorter events, 12.1 us)
Async XLA Ops:
  2.1 7.9 %collective-permute-start = (f32[256,256]{1,0:T(8,128)S(1)}, f32[256,256]{1,0:T(8,128)S(1)}, u32[]{:S(2)}, u32[]{:S(2)}) collective-permute-start(f32[256,256]{1,0:T(8,128)S(1)} %shard_map.28), channel_id=1, source_target_pairs={{0,1},{1,0},{2,3},{3,2},{4,5},{5,4},{6,7},{7,6},{8,10},{9,11},{10,... | collective-permute-start | bytes 786440 | tf_op jit(solution)/shard_map/ppermute | solution.py:186
  9.9 9.9 %collective-permute-start.3 = (f32[512,256]{1,0:T(8,128)S(1)}, f32[512,256]{1,0:T(8,128)S(1)}, u32[]{:S(2)}, u32[]{:S(2)}) collective-permute-start(f32[512,256]{1,0:T(8,128)S(1)} %get-tuple-element.45), channel_id=1, source_target_pairs={{0,1},{1,0},{2,3},{3,2},{4,5},{5,4},{6,7},{7,6},{8,10},{9,11},{10,... | collective-permute-start | bytes 1572872 | tf_op jit(solution)/shard_map/ppermute | solution.py:186
  10.1 9.7 %collective-permute-start.1 = (f32[128,256]{1,0:T(8,128)S(1)}, f32[128,256]{1,0:T(8,128)S(1)}, u32[]{:S(2)}, u32[]{:S(2)}) collective-permute-start(f32[128,256]{1,0:T(8,128)S(1)} %constant_dynamic-slice_fusion.2), channel_id=1, source_target_pairs={{0,2},{1,3},{2,0},{3,1},{4,6},{5,7},{6,4},{7,5},{8,9},{9,8},{10,11... | collective-permute-start | bytes 393224 | tf_op jit(solution)/shard_map/ppermute | solution.py:165
  18.2 12.8 %collective-permute-start.5 = (f32[256,256]{1,0:T(8,128)S(1)}, f32[256,256]{1,0:T(8,128)S(1)}, u32[]{:S(2)}, u32[]{:S(2)}) collective-permute-start(f32[256,256]{1,0:T(8,128)S(1)} %get-tuple-element.48), channel_id=1, source_target_pairs={{0,1},{1,0},{2,3},{3,2},{4,5},{5,4},{6,7},{7,6},{8,10},{9,11},{10,... | collective-permute-start | bytes 786440 | tf_op jit(solution)/shard_map/ppermute | solution.py:186
  19.9 11.2 %collective-permute-start.7 = (f32[256,256]{1,0:T(8,128)S(1)}, f32[256,256]{1,0:T(8,128)S(1)}, u32[]{:S(2)}, u32[]{:S(2)}) collective-permute-start(f32[256,256]{1,0:T(8,128)S(1)} %constant_dynamic-slice_fusion.1), channel_id=1, source_target_pairs={{0,2},{1,3},{2,0},{3,1},{4,6},{5,7},{6,4},{7,5},{8,9},{9,8},{10,11... | collective-permute-start | bytes 786440 | tf_op jit(solution)/shard_map/ppermute | solution.py:165
  21.3 7.2 %collective-permute-start.2 = (f32[128,256]{1,0:T(8,128)S(1)}, f32[128,256]{1,0:T(8,128)S(1)}, u32[]{:S(2)}, u32[]{:S(2)}) collective-permute-start(f32[128,256]{1,0:T(8,128)S(1)} %dynamic-slice_add_fusion.2), channel_id=1, source_target_pairs={{0,4},{1,5},{2,6},{3,7},{4,0},{5,1},{6,2},{7,3},{8,12},{9,13},{10,... | collective-permute-start | bytes 393224 | tf_op jit(solution)/shard_map/ppermute | solution.py:165
  28.5 7.6 %collective-permute-start.4 = (f32[128,256]{1,0:T(8,128)S(1)}, f32[128,256]{1,0:T(8,128)S(1)}, u32[]{:S(2)}, u32[]{:S(2)}) collective-permute-start(f32[128,256]{1,0:T(8,128)S(1)} %add.141), channel_id=1, source_target_pairs={{0,2},{1,3},{2,0},{3,1},{4,6},{5,7},{6,4},{7,5},{8,9},{9,8},{10,11... | collective-permute-start | bytes 393224 | tf_op jit(solution)/shard_map/ppermute | solution.py:165
  31.0 5.0 %collective-permute-start.6 = (f32[128,256]{1,0:T(8,128)S(1)}, f32[128,256]{1,0:T(8,128)S(1)}, u32[]{:S(2)}, u32[]{:S(2)}) collective-permute-start(f32[128,256]{1,0:T(8,128)S(1)} %constant_dynamic-slice_fusion), channel_id=1, source_target_pairs={{0,2},{1,3},{2,0},{3,1},{4,6},{5,7},{6,4},{7,5},{8,9},{9,8},{10,11... | collective-permute-start | bytes 393224 | tf_op jit(solution)/shard_map/ppermute | solution.py:165
  36.1 7.8 %collective-permute-start.8 = (f32[256,256]{1,0:T(8,128)S(1)}, f32[256,256]{1,0:T(8,128)S(1)}, u32[]{:S(2)}, u32[]{:S(2)}) collective-permute-start(f32[256,256]{1,0:T(8,128)S(1)} %maximum_select_fusion.1), channel_id=1, source_target_pairs={{0,1},{1,0},{2,3},{3,2},{4,5},{5,4},{6,7},{7,6},{8,10},{9,11},{10,... | collective-permute-start | bytes 786440 | tf_op jit(solution)/shard_map/ppermute | solution.py:165
  37.3 13.5 %collective-permute-start.9 = (f32[256,256]{1,0:T(8,128)S(1)}, f32[256,256]{1,0:T(8,128)S(1)}, u32[]{:S(2)}, u32[]{:S(2)}) collective-permute-start(f32[256,256]{1,0:T(8,128)S(1)} %dynamic-slice_add_fusion), channel_id=1, source_target_pairs={{0,4},{1,5},{2,6},{3,7},{4,0},{5,1},{6,2},{7,3},{8,12},{9,13},{10,... | collective-permute-start | bytes 786440 | tf_op jit(solution)/shard_map/ppermute | solution.py:165
  50.9 9.9 %collective-permute-start.10 = (f32[256,256]{1,0:T(8,128)S(1)}, f32[256,256]{1,0:T(8,128)S(1)}, u32[]{:S(2)}, u32[]{:S(2)}) collective-permute-start(f32[256,256]{1,0:T(8,128)S(1)} %add.150), channel_id=1, source_target_pairs={{0,2},{1,3},{2,0},{3,1},{4,6},{5,7},{6,4},{7,5},{8,9},{9,8},{10,11... | collective-permute-start | bytes 786440 | tf_op jit(solution)/shard_map/ppermute | solution.py:165
  52.8 9.5 %collective-permute-start.11 = (f32[128,256]{1,0:T(8,128)S(1)}, f32[128,256]{1,0:T(8,128)S(1)}, u32[]{:S(2)}, u32[]{:S(2)}) collective-permute-start(f32[128,256]{1,0:T(8,128)S(1)} %dynamic-slice_add_fusion.1), channel_id=1, source_target_pairs={{0,4},{1,5},{2,6},{3,7},{4,0},{5,1},{6,2},{7,3},{8,12},{9,13},{10,... | collective-permute-start | bytes 393224 | tf_op jit(solution)/shard_map/ppermute | solution.py:165
  62.3 7.3 %collective-permute-start.13 = (f32[128,256]{1,0:T(8,128)S(1)}, f32[128,256]{1,0:T(8,128)S(1)}, u32[]{:S(2)}, u32[]{:S(2)}) collective-permute-start(f32[128,256]{1,0:T(8,128)S(1)} %add.151), channel_id=1, source_target_pairs={{0,2},{1,3},{2,0},{3,1},{4,6},{5,7},{6,4},{7,5},{8,9},{9,8},{10,11... | collective-permute-start | bytes 393224 | tf_op jit(solution)/shard_map/ppermute | solution.py:165
  66.3 9.2 %collective-permute-start.12 = (f32[512,256]{1,0:T(8,128)S(1)}, f32[512,256]{1,0:T(8,128)S(1)}, u32[]{:S(2)}, u32[]{:S(2)}) collective-permute-start(f32[512,256]{1,0:T(8,128)S(1)} %maximum_select_fusion), channel_id=1, source_target_pairs={{0,1},{1,0},{2,3},{3,2},{4,5},{5,4},{6,7},{7,6},{8,10},{9,11},{10,... | collective-permute-start | bytes 1572872 | tf_op jit(solution)/shard_map/ppermute | solution.py:165
  69.6 11.6 %collective-permute-start.14 = (f32[256,256]{1,0:T(8,128)S(1)}, f32[256,256]{1,0:T(8,128)S(1)}, u32[]{:S(2)}, u32[]{:S(2)}) collective-permute-start(f32[256,256]{1,0:T(8,128)S(1)} %maximum_select_fusion.2), channel_id=1, source_target_pairs={{0,1},{1,0},{2,3},{3,2},{4,5},{5,4},{6,7},{7,6},{8,10},{9,11},{10,... | collective-permute-start | bytes 786440 | tf_op jit(solution)/shard_map/ppermute | solution.py:165
  83.5 1.6 %collective-permute-start.15 = (f32[256,256]{1,0:T(8,128)S(1)}, f32[256,256]{1,0:T(8,128)S(1)}, u32[]{:S(2)}, u32[]{:S(2)}) collective-permute-start(f32[256,256]{1,0:T(8,128)S(1)} %convolution_add_fusion.3.gram_ref), channel_id=1, source_target_pairs={{0,8},{8,0},{1,9},{9,1},{2,10},{10,2},{3,11},{11,3},{4,12},{12,4},... | collective-permute-start | bytes 786440 | tf_op jit(solution)/shard_map/ppermute | solution.py:237
  85.1 25.0 %collective-permute-start.16 = (f32[256,1024]{1,0:T(8,128)S(1)}, f32[256,1024]{1,0:T(8,128)S(1)}, u32[]{:S(2)}, u32[]{:S(2)}) collective-permute-start(f32[256,1024]{1,0:T(8,128)S(1)} %convolution_add_fusion), channel_id=1, source_target_pairs={{0,8},{8,0},{1,9},{9,1},{2,10},{10,2},{3,11},{11,3},{4,12},{12,4},... | collective-permute-start | bytes 3145736 | tf_op jit(solution)/shard_map/ppermute | solution.py:240

commit v7 on v6

--- a/solution.py
+++ b/solution.py
@@ -10,9 +10,9 @@
 HIGH = lax.Precision.HIGH
 STEP = 256
 SIZES = (128, 256, 128)
-STEPS = [("m", [(0, True)]), ("m", [(1, True), (0, False)]), ("i", 0), ("m", [(2, True), (1, False), (2, False)])]
-STEPS += [("l", 0), ("i", 1), ("b", 0), ("i", 2), ("l", 1), ("l", 2), ("o", 0), ("g", 0), ("f", 0), ("b", 1)]
-STEPS += [("o", 1), ("b", 2), ("g", 1), ("o", 2), ("f", 1), ("g", 2), ("f", 2)]
+STEPS = [("s", 0, True), ("m", 1, True), ("m", 0, False), ("i", 0), ("m", 2, True), ("l", 0), ("m", 1, False), ("i", 1)]
+STEPS += [("m", 2, False), ("i", 2), ("b", 0), ("l", 1), ("l", 2), ("o", 0), ("b", 1), ("w", 0), ("g", 0), ("o", 1), ("b", 2), ("f", 0), ("o", 2)]
+STEPS += [("g", 1), ("f", 1), ("g", 2), ("f", 2)]
 BLOCK = 64
 LIGHT = pl.CostEstimate(flops=1000, bytes_accessed=1000, transcendentals=0)
 
@@ -174,18 +174,24 @@
         return jnp.where(odd == 0, jnp.concatenate([own, other]), jnp.concatenate([other, own]))
 
     arriving, own = {}, {}
-    pinned = [pltpu.with_memory_space_constraint(x, pltpu.HBM) for x in (texture, sketch)]
-
-    def matmuls(group):
-        chosen = [(k, 1 - side if theirs else side) for k, theirs in group]
-        parts = [(starts[k] + which * (2 * SIZES[k]), 2 * SIZES[k]) for k, which in chosen]
-        made = sketched(*pinned, parts, [] if last[0] is None else [last[0]])
-        last[0] = made[0]
-        for (k, theirs), image in zip(group, made):
-            if theirs:
-                arriving[k] = lax.ppermute(image, ("rows", "cols"), outer)
-            else:
-                own[k] = image
+
+    def placed(k, theirs, image):
+        last[0] = image
+        if theirs:
+            arriving[k] = lax.ppermute(image, ("rows", "cols"), outer)
+        else:
+            own[k] = image
+
+    def first_matmul(k, theirs):
+        pinned = [pltpu.with_memory_space_constraint(x, pltpu.HBM) for x in (texture, sketch)]
+        which = 1 - side if theirs else side
+        parts = [(starts[k] + which * (2 * SIZES[k]), 2 * SIZES[k])]
+        placed(k, theirs, sketched(*pinned, parts, [])[0])
+
+    def matmul(k, theirs):
+        (weights,) = after([sketch], last[0])
+        rows = rows_of(k, 1 - side if theirs else side)
+        placed(k, theirs, jnp.dot(rows, weights, precision=HIGH, preferred_element_type=jnp.float32))
 
     kept, half, sums = {}, {}, [()]
 
@@ -217,12 +223,15 @@
     def gather_own(k):
         gather(rows_of(k, side), *after([half[k]], last[0]))
 
+    def wait_far(k):
+        arriving[k] = last[0] = arrived(k)
+
     def gather_far(k):
         gather(rows_of(k, 1 - side), arrived(k))
 
-    steps = dict(i=to_inner, l=to_line, b=back_to_inner, o=back_to_outer, g=gather_own, f=gather_far, m=matmuls)
-    for name, k in STEPS:
-        steps[name](k)
+    steps = dict(i=to_inner, l=to_line, b=back_to_inner, o=back_to_outer, g=gather_own, f=gather_far, w=wait_far, s=first_matmul, m=matmul)
+    for name, *chunk in STEPS:
+        steps[name](*chunk)
     return sums[0]
 
 

time: 112 us -> 96.2 us (0.86)
  starting transfers between devices: 30.5 us -> 19 us
  Pallas kernels: 37.6 us -> 27.1 us
  matrix products: 17.1 us -> 23.8 us
    ppermute x12, starting transfers between devices: 25.6 us -> 14.1 us  [send(): return lax.ppermute(x, ('rows', 'cols'), targets)]
    dot_general x0 -> x5, matrix products: none -> 10.7 us  [matmul(): jnp.dot(rows, weights, precision=HIGH, preferred_element_type=jnp.float32)]
    pallas_call x3 -> x1, Pallas kernels: 12.7 us -> 2.22 us  [sketched(): pl.pallas_call(sketch_kernel, out_shape=[jax.ShapeDtypeStruct((length, ra...]
    dot_general x12, matrix products: 15.8 us -> 11.9 us  [inner_rows(): lax.dot_general(left, right, (((0,), (0,)), ((), ())), precision=HIGH, pr...]
  transfers between devices with their start and end apart: 17 -> 17, of which waited for: 7 -> 9; matrix products, arithmetic and copies ran while one was open for 13% -> 23% of each run, Pallas kernels for 32% -> 26%
where the time goes in v7:
time: 96.2 us; the launch traced here: 95.8 us
  Pallas kernels  27.1 us (28%)
  waiting for transfers between devices  25.1 us (26%)
  matrix products  23.8 us (25%)
  starting transfers between devices  19 us (20%)
    pallas_call x1, Pallas kernels, inverse_cholesky(): pl.pallas_call(factor_kernel, out_shape=jax.ShapeDtypeStruct(gram.shape,...  24.9 us
    ppermute x12, waiting for transfers between devices, send(): return lax.ppermute(x, ('rows', 'cols'), targets)  23.6 us
    ppermute x12, starting transfers between devices, send(): return lax.ppermute(x, ('rows', 'cols'), targets)  14.1 us
    dot_general x12, matrix products, inner_rows(): lax.dot_general(left, right, (((0,), (0,)), ((), ())), precision=HIGH, pr...  11.9 us
    dot_general x5, matrix products, matmul(): jnp.dot(rows, weights, precision=HIGH, preferred_element_type=jnp.float32)  10.7 us
    ppermute x3, starting transfers between devices, placed(): arriving[k] = lax.ppermute(image, ('rows', 'cols'), outer)  4.71 us
    pallas_call x1, Pallas kernels, sketched(): pl.pallas_call(sketch_kernel, out_shape=[jax.ShapeDtypeStruct((length, ra...  2.22 us
  transfers between devices with their start and end apart: 17, of which 9 were waited for; matrix products, arithmetic and copies ran while one was open for 23% of the time, Pallas kernels for 26%

profile of v7, /device:TPU:0, one launch (start us, length us, event | category | flops | bytes accessed | tf_op | source)
XLA Modules:
  0.0 95.8 jit_solution(16146815934930550349)
XLA Ops:
  0.0 2.2 %shard_map.28 = f32[256,256]{1,0:T(8,128)S(1)} custom-call(s32[1]{0:T(128)} %bitcast.starts_ref, f32[2048,1024]{1,0:T(8,128)} %texture_ref.1, f32[1024,256]{1,0:T(8,128)} %sketch_ref.1), custom_call_target="tpu_custom_call" | custom-call | flops 402653184 | bytes 2097152 | tf_op jit(solution)/shard_map/pallas_call | solution.py:55
  2.2 3.0 %collective-permute-start = (f32[256,256]{1,0:T(8,128)S(1)}, f32[256,256]{1,0:T(8,128)S(1)}, u32[]{:S(2)}, u32[]{:S(2)}) collective-permute-start(f32[256,256]{1,0:T(8,128)S(1)} %shard_map.28), channel_id=1, source_target_pairs={{0,1},{1,0},{2,3},{3,2},{4,5},{5,4},{6,7},{7,6},{8,10},{9,11},{10,... | collective-permute-start | bytes 786440 | tf_op jit(solution)/shard_map/ppermute | solution.py:181
  5.3 2.6 %fusion.6 = f32[512,256]{1,0:T(8,128)S(1)} fusion(f32[1024,256]{1,0:T(8,128)S(1)} %copy-done, f32[2048,1024]{1,0:T(8,128)} %texture_ref.1, s32[]{:T(128)S(6)} %select_n.71), kind=kOutput, calls=%fused_computation.6 | convolution fusion | flops 805306368 | bytes 3670020 | tf_op jit(solution)/shard_map/dot_general | solution.py:194
  8.0 1.8 %fusion.25 = f32[256,256]{1,0:T(8,128)S(1)} fusion(f32[1024,256]{1,0:T(8,128)S(1)} %copy-done, f32[2048,1024]{1,0:T(8,128)} %texture_ref.1, s32[]{:T(128)S(6)} %select_n.70), kind=kOutput, calls=%fused_computation.29 | convolution fusion | flops 402653184 | bytes 2359300 | tf_op jit(solution)/shard_map/dot_general | solution.py:194
  9.9 2.1 %collective-permute-start.1 = (f32[128,256]{1,0:T(8,128)S(1)}, f32[128,256]{1,0:T(8,128)S(1)}, u32[]{:S(2)}, u32[]{:S(2)}) collective-permute-start(f32[128,256]{1,0:T(8,128)S(1)} %constant_dynamic-slice_fusion.2), channel_id=1, source_target_pairs={{0,2},{1,3},{2,0},{3,1},{4,6},{5,7},{6,4},{7,5},{8,9},{9,8},{10,11... | collective-permute-start | bytes 393224 | tf_op jit(solution)/shard_map/ppermute | solution.py:165
  12.0 1.8 %fusion.21 = f32[256,256]{1,0:T(8,128)S(1)} fusion(f32[1024,256]{1,0:T(8,128)S(1)} %copy-done, f32[2048,1024]{1,0:T(8,128)} %texture_ref.1, s32[]{:T(128)S(6)} %select_n.74), kind=kOutput, calls=%fused_computation.25 | convolution fusion | flops 402653184 | bytes 2359300 | tf_op jit(solution)/shard_map/dot_general | solution.py:194
  13.8 1.6 %collective-permute-start.4 = (f32[256,256]{1,0:T(8,128)S(1)}, f32[256,256]{1,0:T(8,128)S(1)}, u32[]{:S(2)}, u32[]{:S(2)}) collective-permute-start(f32[256,256]{1,0:T(8,128)S(1)} %fusion.21), channel_id=1, source_target_pairs={{0,1},{1,0},{2,3},{3,2},{4,5},{5,4},{6,7},{7,6},{8,10},{9,11},{10,... | collective-permute-start | bytes 786440 | tf_op jit(solution)/shard_map/ppermute | solution.py:181
  16.4 3.1 %collective-permute-start.2 = (f32[128,256]{1,0:T(8,128)S(1)}, f32[128,256]{1,0:T(8,128)S(1)}, u32[]{:S(2)}, u32[]{:S(2)}) collective-permute-start(f32[128,256]{1,0:T(8,128)S(1)} %dynamic-slice_add_fusion.2), channel_id=1, source_target_pairs={{0,4},{1,5},{2,6},{3,7},{4,0},{5,1},{6,2},{7,3},{8,12},{9,13},{10,... | collective-permute-start | bytes 393224 | tf_op jit(solution)/shard_map/ppermute | solution.py:165
  19.5 2.6 %fusion.2 = f32[512,256]{1,0:T(8,128)S(1)} fusion(f32[1024,256]{1,0:T(8,128)S(1)} %copy-done, f32[2048,1024]{1,0:T(8,128)} %texture_ref.1, s32[]{:T(128)S(6)} %select_n.76), kind=kOutput, calls=%fused_computation.2 | convolution fusion | flops 805306368 | bytes 3670020 | tf_op jit(solution)/shard_map/dot_general | solution.py:194
  22.2 1.4 %collective-permute-start.7 = (f32[256,256]{1,0:T(8,128)S(1)}, f32[256,256]{1,0:T(8,128)S(1)}, u32[]{:S(2)}, u32[]{:S(2)}) collective-permute-start(f32[256,256]{1,0:T(8,128)S(1)} %constant_dynamic-slice_fusion.1), channel_id=1, source_target_pairs={{0,2},{1,3},{2,0},{3,1},{4,6},{5,7},{6,4},{7,5},{8,9},{9,8},{10,11... | collective-permute-start | bytes 786440 | tf_op jit(solution)/shard_map/ppermute | solution.py:165
  23.6 1.8 %fusion.18 = f32[256,256]{1,0:T(8,128)S(1)} fusion(f32[1024,256]{1,0:T(8,128)S(1)} %copy-done, f32[2048,1024]{1,0:T(8,128)} %texture_ref.1, s32[]{:T(128)S(6)} %select_n.75), kind=kOutput, calls=%fused_computation.22 | convolution fusion | flops 402653184 | bytes 2359300 | tf_op jit(solution)/shard_map/dot_general | solution.py:194
  26.3 1.4 %collective-permute-start.5 = (f32[128,256]{1,0:T(8,128)S(1)}, f32[128,256]{1,0:T(8,128)S(1)}, u32[]{:S(2)}, u32[]{:S(2)}) collective-permute-start(f32[128,256]{1,0:T(8,128)S(1)} %add.140), channel_id=1, source_target_pairs={{0,2},{1,3},{2,0},{3,1},{4,6},{5,7},{6,4},{7,5},{8,9},{9,8},{10,11... | collective-permute-start | bytes 393224 | tf_op jit(solution)/shard_map/ppermute | solution.py:165
  28.9 5.0 %collective-permute-done.6 = f32[128,256]{1,0:T(8,128)S(1)} collective-permute-done((f32[128,256]{1,0:T(8,128)S(1)}, f32[128,256]{1,0:T(8,128)S(1)}, u32[]{:S(2)}, u32[]{:S(2)}) %collective-permute-start.6) | collective-permute-done | bytes 131104 | tf_op jit(solution)/shard_map/ppermute | solution.py:165
  33.9 4.7 %collective-permute-done.5 = f32[128,256]{1,0:T(8,128)S(1)} collective-permute-done((f32[128,256]{1,0:T(8,128)S(1)}, f32[128,256]{1,0:T(8,128)S(1)}, u32[]{:S(2)}, u32[]{:S(2)}) %collective-permute-start.5) | collective-permute-done | bytes 131104 | tf_op jit(solution)/shard_map/ppermute | solution.py:165
  38.6 2.9 %collective-permute-start.8 = (f32[256,256]{1,0:T(8,128)S(1)}, f32[256,256]{1,0:T(8,128)S(1)}, u32[]{:S(2)}, u32[]{:S(2)}) collective-permute-start(f32[256,256]{1,0:T(8,128)S(1)} %maximum_select_fusion.1), channel_id=1, source_target_pairs={{0,1},{1,0},{2,3},{3,2},{4,5},{5,4},{6,7},{7,6},{8,10},{9,11},{10,... | collective-permute-start | bytes 786440 | tf_op jit(solution)/shard_map/ppermute | solution.py:165
  41.4 1.8 %collective-permute-done.9 = f32[256,256]{1,0:T(8,128)S(1)} collective-permute-done((f32[256,256]{1,0:T(8,128)S(1)}, f32[256,256]{1,0:T(8,128)S(1)}, u32[]{:S(2)}, u32[]{:S(2)}) %collective-permute-start.9) | collective-permute-done | bytes 262176 | tf_op jit(solution)/shard_map/ppermute | solution.py:165
  44.0 2.2 %collective-permute-done.8 = f32[256,256]{1,0:T(8,128)S(1)} collective-permute-done((f32[256,256]{1,0:T(8,128)S(1)}, f32[256,256]{1,0:T(8,128)S(1)}, u32[]{:S(2)}, u32[]{:S(2)}) %collective-permute-start.8) | collective-permute-done | bytes 262176 | tf_op jit(solution)/shard_map/ppermute | solution.py:165
  46.1 1.9 %fusion.23 = f32[256,1024]{1,0:T(8,128)S(1)} fusion(f32[256,256]{1,0:T(8,128)S(1)} %maximum_select_fusion.1, f32[2048,1024]{1,0:T(8,128)} %texture_ref.1, s32[]{:T(128)S(6)} %select_n.70), kind=kOutput, calls=%fused_computation.27 | convolution fusion | flops 402653184 | bytes 2359300 | tf_op jit(solution)/shard_map/dot_general | solution.py:73
  48.4 4.8 %collective-permute-done.11 = f32[256,256]{1,0:T(8,128)S(1)} collective-permute-done((f32[256,256]{1,0:T(8,128)S(1)}, f32[256,256]{1,0:T(8,128)S(1)}, u32[]{:S(2)}, u32[]{:S(2)}) %collective-permute-start.11) | collective-permute-done | bytes 262176 | tf_op jit(solution)/shard_map/ppermute | solution.py:165
  54.5 1.9 %convolution_add_fusion.2 = f32[256,1024]{1,0:T(8,128)S(1)} fusion(f32[256,1024]{1,0:T(8,128)S(1)} %fusion.23, f32[256,256]{1,0:T(8,128)S(1)} %collective-permute-done.8, f32[2048,1024]{1,0:T(8,128)} %texture_ref.1, s32[]{:T(128)S(6)} %select_n.82), kind=kOutput, calls=%fused_computation.12 | convolution fusion | flops 402915328 | bytes 3407876 | tf_op jit(solution)/shard_map/dot_general | solution.py:73
  56.7 3.1 %collective-permute-done.12 = f32[128,256]{1,0:T(8,128)S(1)} collective-permute-done((f32[128,256]{1,0:T(8,128)S(1)}, f32[128,256]{1,0:T(8,128)S(1)}, u32[]{:S(2)}, u32[]{:S(2)}) %collective-permute-start.12) | collective-permute-done | bytes 131104 | tf_op jit(solution)/shard_map/ppermute | solution.py:165
  61.0 2.7 %fusion.11 = f32[256,1024]{1,0:T(8,128)S(1)} fusion(f32[256,1024]{1,0:T(8,128)S(1)} %convolution_add_fusion.2, f32[512,256]{1,0:T(8,128)S(1)} %maximum_select_fusion, f32[2048,1024]{1,0:T(8,128)} %texture_ref.1, s32[]{:T(128)S(6)} %select_n.76), kind=kOutput, calls=%fused_computation.9 | convolution fusion | flops 805568512 | bytes 4718596 | tf_op jit(solution)/shard_map/dot_general | solution.py:73
  68.0 1.5 %collective-permute-done.15.far_ref = f32[256,256]{1,0:T(8,128)S(1)} collective-permute-done((f32[256,256]{1,0:T(8,128)S(1)}, f32[256,256]{1,0:T(8,128)S(1)}, u32[]{:S(2)}, u32[]{:S(2)}) %collective-permute-start.15) | collective-permute-done | bytes 262176 | tf_op jit(solution)/shard_map/ppermute | solution.py:246
  69.7 24.9 %shard_map.29 = f32[256,256]{1,0:T(8,128)S(1)} custom-call(f32[256,256]{1,0:T(8,128)S(1)} %convolution_add_fusion.3.gram_ref, f32[256,256]{1,0:T(8,128)S(1)} %collective-permute-done.15.far_ref), custom_call_target="tpu_custom_call" | custom-call | flops 1000 | bytes 1000 | tf_op jit(solution)/shard_map/pallas_call | solution.py:133
  (52 shorter events, 12.7 us)
Async XLA Ops:
  0.0 5.3 %copy-start = (f32[1024,256]{1,0:T(8,128)S(1)}, f32[1024,256]{1,0:T(8,128)}, u32[]{:S(2)}) copy-start(f32[1024,256]{1,0:T(8,128)} %sketch_ref.1) | copy-start | bytes 3145732
  2.2 7.6 %collective-permute-start = (f32[256,256]{1,0:T(8,128)S(1)}, f32[256,256]{1,0:T(8,128)S(1)}, u32[]{:S(2)}, u32[]{:S(2)}) collective-permute-start(f32[256,256]{1,0:T(8,128)S(1)} %shard_map.28), channel_id=1, source_target_pairs={{0,1},{1,0},{2,3},{3,2},{4,5},{5,4},{6,7},{7,6},{8,10},{9,11},{10,... | collective-permute-start | bytes 786440 | tf_op jit(solution)/shard_map/ppermute | solution.py:181
  7.9 14.3 %collective-permute-start.3 = (f32[512,256]{1,0:T(8,128)S(1)}, f32[512,256]{1,0:T(8,128)S(1)}, u32[]{:S(2)}, u32[]{:S(2)}) collective-permute-start(f32[512,256]{1,0:T(8,128)S(1)} %fusion.6), channel_id=1, source_target_pairs={{0,1},{1,0},{2,3},{3,2},{4,5},{5,4},{6,7},{7,6},{8,10},{9,11},{10,... | collective-permute-start | bytes 1572872 | tf_op jit(solution)/shard_map/ppermute | solution.py:181
  9.9 6.5 %collective-permute-start.1 = (f32[128,256]{1,0:T(8,128)S(1)}, f32[128,256]{1,0:T(8,128)S(1)}, u32[]{:S(2)}, u32[]{:S(2)}) collective-permute-start(f32[128,256]{1,0:T(8,128)S(1)} %constant_dynamic-slice_fusion.2), channel_id=1, source_target_pairs={{0,2},{1,3},{2,0},{3,1},{4,6},{5,7},{6,4},{7,5},{8,9},{9,8},{10,11... | collective-permute-start | bytes 393224 | tf_op jit(solution)/shard_map/ppermute | solution.py:165
  13.8 11.6 %collective-permute-start.4 = (f32[256,256]{1,0:T(8,128)S(1)}, f32[256,256]{1,0:T(8,128)S(1)}, u32[]{:S(2)}, u32[]{:S(2)}) collective-permute-start(f32[256,256]{1,0:T(8,128)S(1)} %fusion.21), channel_id=1, source_target_pairs={{0,1},{1,0},{2,3},{3,2},{4,5},{5,4},{6,7},{7,6},{8,10},{9,11},{10,... | collective-permute-start | bytes 786440 | tf_op jit(solution)/shard_map/ppermute | solution.py:181
  16.4 9.9 %collective-permute-start.2 = (f32[128,256]{1,0:T(8,128)S(1)}, f32[128,256]{1,0:T(8,128)S(1)}, u32[]{:S(2)}, u32[]{:S(2)}) collective-permute-start(f32[128,256]{1,0:T(8,128)S(1)} %dynamic-slice_add_fusion.2), channel_id=1, source_target_pairs={{0,4},{1,5},{2,6},{3,7},{4,0},{5,1},{6,2},{7,3},{8,12},{9,13},{10,... | collective-permute-start | bytes 393224 | tf_op jit(solution)/shard_map/ppermute | solution.py:165
  22.2 6.4 %collective-permute-start.7 = (f32[256,256]{1,0:T(8,128)S(1)}, f32[256,256]{1,0:T(8,128)S(1)}, u32[]{:S(2)}, u32[]{:S(2)}) collective-permute-start(f32[256,256]{1,0:T(8,128)S(1)} %constant_dynamic-slice_fusion.1), channel_id=1, source_target_pairs={{0,2},{1,3},{2,0},{3,1},{4,6},{5,7},{6,4},{7,5},{8,9},{9,8},{10,11... | collective-permute-start | bytes 786440 | tf_op jit(solution)/shard_map/ppermute | solution.py:165
  25.5 8.3 %collective-permute-start.6 = (f32[128,256]{1,0:T(8,128)S(1)}, f32[128,256]{1,0:T(8,128)S(1)}, u32[]{:S(2)}, u32[]{:S(2)}) collective-permute-start(f32[128,256]{1,0:T(8,128)S(1)} %constant_dynamic-slice_fusion), channel_id=1, source_target_pairs={{0,2},{1,3},{2,0},{3,1},{4,6},{5,7},{6,4},{7,5},{8,9},{9,8},{10,11... | collective-permute-start | bytes 393224 | tf_op jit(solution)/shard_map/ppermute | solution.py:165
  26.3 12.2 %collective-permute-start.5 = (f32[128,256]{1,0:T(8,128)S(1)}, f32[128,256]{1,0:T(8,128)S(1)}, u32[]{:S(2)}, u32[]{:S(2)}) collective-permute-start(f32[128,256]{1,0:T(8,128)S(1)} %add.140), channel_id=1, source_target_pairs={{0,2},{1,3},{2,0},{3,1},{4,6},{5,7},{6,4},{7,5},{8,9},{9,8},{10,11... | collective-permute-start | bytes 393224 | tf_op jit(solution)/shard_map/ppermute | solution.py:165
  28.7 14.5 %collective-permute-start.9 = (f32[256,256]{1,0:T(8,128)S(1)}, f32[256,256]{1,0:T(8,128)S(1)}, u32[]{:S(2)}, u32[]{:S(2)}) collective-permute-start(f32[256,256]{1,0:T(8,128)S(1)} %dynamic-slice_add_fusion), channel_id=1, source_target_pairs={{0,4},{1,5},{2,6},{3,7},{4,0},{5,1},{6,2},{7,3},{8,12},{9,13},{10,... | collective-permute-start | bytes 786440 | tf_op jit(solution)/shard_map/ppermute | solution.py:165
  38.6 7.6 %collective-permute-start.8 = (f32[256,256]{1,0:T(8,128)S(1)}, f32[256,256]{1,0:T(8,128)S(1)}, u32[]{:S(2)}, u32[]{:S(2)}) collective-permute-start(f32[256,256]{1,0:T(8,128)S(1)} %maximum_select_fusion.1), channel_id=1, source_target_pairs={{0,1},{1,0},{2,3},{3,2},{4,5},{5,4},{6,7},{7,6},{8,10},{9,11},{10,... | collective-permute-start | bytes 786440 | tf_op jit(solution)/shard_map/ppermute | solution.py:165
  41.4 11.8 %collective-permute-start.10 = (f32[128,256]{1,0:T(8,128)S(1)}, f32[128,256]{1,0:T(8,128)S(1)}, u32[]{:S(2)}, u32[]{:S(2)}) collective-permute-start(f32[128,256]{1,0:T(8,128)S(1)} %dynamic-slice_add_fusion.1), channel_id=1, source_target_pairs={{0,4},{1,5},{2,6},{3,7},{4,0},{5,1},{6,2},{7,3},{8,12},{9,13},{10,... | collective-permute-start | bytes 393224 | tf_op jit(solution)/shard_map/ppermute | solution.py:165
  43.3 21.1 %slice-start = ((s8[8388608]{0:T(1024)(128)(4,1)}), s8[4194304]{0:T(1024)(128)(4,1)S(1)}, s32[]{:S(2)}) async-start(s8[8388608]{0:T(1024)(128)(4,1)} %bitcast.24), calls=%async_computation | async-start | bytes 8388608
  43.3 9.9 %collective-permute-start.11 = (f32[256,256]{1,0:T(8,128)S(1)}, f32[256,256]{1,0:T(8,128)S(1)}, u32[]{:S(2)}, u32[]{:S(2)}) collective-permute-start(f32[256,256]{1,0:T(8,128)S(1)} %add.144), channel_id=1, source_target_pairs={{0,2},{1,3},{2,0},{3,1},{4,6},{5,7},{6,4},{7,5},{8,9},{9,8},{10,11... | collective-permute-start | bytes 786440 | tf_op jit(solution)/shard_map/ppermute | solution.py:165
  53.3 6.5 %collective-permute-start.12 = (f32[128,256]{1,0:T(8,128)S(1)}, f32[128,256]{1,0:T(8,128)S(1)}, u32[]{:S(2)}, u32[]{:S(2)}) collective-permute-start(f32[128,256]{1,0:T(8,128)S(1)} %add.145), channel_id=1, source_target_pairs={{0,2},{1,3},{2,0},{3,1},{4,6},{5,7},{6,4},{7,5},{8,9},{9,8},{10,11... | collective-permute-start | bytes 393224 | tf_op jit(solution)/shard_map/ppermute | solution.py:165
  53.4 10.3 %collective-permute-start.13 = (f32[512,256]{1,0:T(8,128)S(1)}, f32[512,256]{1,0:T(8,128)S(1)}, u32[]{:S(2)}, u32[]{:S(2)}) collective-permute-start(f32[512,256]{1,0:T(8,128)S(1)} %maximum_select_fusion), channel_id=1, source_target_pairs={{0,1},{1,0},{2,3},{3,2},{4,5},{5,4},{6,7},{7,6},{8,10},{9,11},{10,... | collective-permute-start | bytes 1572872 | tf_op jit(solution)/shard_map/ppermute | solution.py:165
  56.3 8.0 %slice-start.1 = ((s8[8388608]{0:T(1024)(128)(4,1)}), s8[4194304]{0:T(1024)(128)(4,1)S(1)}, s32[]{:S(2)}) async-start(s8[8388608]{0:T(1024)(128)(4,1)} %bitcast.24), calls=%async_computation.1 | async-start | bytes 8388608
  59.8 7.0 %collective-permute-start.14 = (f32[256,256]{1,0:T(8,128)S(1)}, f32[256,256]{1,0:T(8,128)S(1)}, u32[]{:S(2)}, u32[]{:S(2)}) collective-permute-start(f32[256,256]{1,0:T(8,128)S(1)} %maximum_select_fusion.2), channel_id=1, source_target_pairs={{0,1},{1,0},{2,3},{3,2},{4,5},{5,4},{6,7},{7,6},{8,10},{9,11},{10,... | collective-permute-start | bytes 786440 | tf_op jit(solution)/shard_map/ppermute | solution.py:165
  67.9 1.6 %collective-permute-start.15 = (f32[256,256]{1,0:T(8,128)S(1)}, f32[256,256]{1,0:T(8,128)S(1)}, u32[]{:S(2)}, u32[]{:S(2)}) collective-permute-start(f32[256,256]{1,0:T(8,128)S(1)} %convolution_add_fusion.3.gram_ref), channel_id=1, source_target_pairs={{0,8},{8,0},{1,9},{9,1},{2,10},{10,2},{3,11},{11,3},{4,12},{12,4},... | collective-permute-start | bytes 786440 | tf_op jit(solution)/shard_map/ppermute | solution.py:246
  69.5 25.0 %collective-permute-start.16 = (f32[256,1024]{1,0:T(8,128)S(1)}, f32[256,1024]{1,0:T(8,128)S(1)}, u32[]{:S(2)}, u32[]{:S(2)}) collective-permute-start(f32[256,1024]{1,0:T(8,128)S(1)} %convolution_add_fusion), channel_id=1, source_target_pairs={{0,8},{8,0},{1,9},{9,1},{2,10},{10,2},{3,11},{11,3},{4,12},{12,4},... | collective-permute-start | bytes 3145736 | tf_op jit(solution)/shard_map/ppermute | solution.py:249

commit v8 on v7

--- a/solution.py
+++ b/solution.py
@@ -14,6 +14,7 @@
 STEPS += [("m", 2, False), ("i", 2), ("b", 0), ("l", 1), ("l", 2), ("o", 0), ("b", 1), ("w", 0), ("g", 0), ("o", 1), ("b", 2), ("f", 0), ("o", 2)]
 STEPS += [("g", 1), ("f", 1), ("g", 2), ("f", 2)]
 BLOCK = 64
+TILE = 8
 LIGHT = pl.CostEstimate(flops=1000, bytes_accessed=1000, transcendentals=0)
 
 
@@ -91,18 +92,38 @@
 
 def inverse_factor(block):
     size = block.shape[0]
-    row = lax.broadcasted_iota(jnp.int32, block.shape, 0)
-    col = lax.broadcasted_iota(jnp.int32, block.shape, 1)
-    rows = lax.broadcasted_iota(jnp.int32, (size, 1), 0)
-    pivots = jnp.ones((size, 1), jnp.float32)
-    for j in range(size):
-        pivot = block[j : j + 1, j : j + 1]
-        factor = jnp.where(rows > j, block[:, j : j + 1] * (1.0 / pivot), 0.0)
-        pivots = jnp.where(rows == j, pivot, pivots)
-        line = jnp.where(col[0:1] == j, 1.0, block[j : j + 1, :])
-        block = jnp.where((col == j) & (row != j), 0.0, block) - factor * line
-    unit = jnp.where(col == row, 1.0, jnp.where(col < row, block, 0.0))
-    return unit * lax.rsqrt(pivots)
+    sub = lax.broadcasted_iota(jnp.int32, (TILE, size), 0)
+    lane = lax.broadcasted_iota(jnp.int32, (TILE, size), 1)
+    along = lambda x, l: jnp.broadcast_to(x[:, l : l + 1], (TILE, size))
+    down = lambda x, j: jnp.broadcast_to(x[j : j + 1, :], (TILE, size))
+    tiles = [block[row : row + TILE, :] for row in range(0, size, TILE)]
+    outs = []
+    for s, lines in enumerate(tiles):
+        low = s * TILE
+        inside = (lane >= low) & (lane < low + TILE)
+        corner = [along(lines, low + c) for c in range(TILE)]
+        lines = jnp.where(inside, jnp.where(lane - low == sub, 1.0, 0.0), lines)
+        out = jnp.zeros((TILE, size), jnp.float32)
+        scale = jnp.ones((TILE, size), jnp.float32)
+        for j in range(TILE):
+            pivot = down(corner[j], j)
+            inverse = 1.0 / pivot
+            factor = jnp.where(sub == j, 0.0, corner[j] * inverse)
+            scale = jnp.where(sub == j, inverse, scale)
+            line = down(lines, j)
+            out = jnp.where(sub == j, line * lax.rsqrt(pivot), out)
+            for c in range(j + 1, TILE):
+                corner[c] = corner[c] - factor * down(corner[c], j)
+            lines = lines - factor * line
+        outs.append(jnp.where(lane < low + TILE, out, 0.0))
+        lines = lines * scale
+        rows = [down(lines, c) for c in range(TILE)]
+        for t in range(s + 1, len(tiles)):
+            term = along(tiles[t], low) * rows[0]
+            for c in range(1, TILE):
+                term = term + along(tiles[t], low + c) * rows[c]
+            tiles[t] = jnp.where(inside, 0.0, tiles[t]) - term
+    return jnp.concatenate(outs, axis=0)
 
 
 def factor_kernel(gram_ref, far_ref, out_ref, work):

time: 96.2 us -> 81.2 us (0.84)
  Pallas kernels: 27.1 us -> 12.1 us
    pallas_call x1, Pallas kernels: 24.9 us -> 9.91 us  [inverse_cholesky(): pl.pallas_call(factor_kernel, out_shape=jax.ShapeDtypeStruct(gram.shape,...]
  transfers between devices with their start and end apart: 17 -> 17, of which waited for: 9 -> 9; matrix products, arithmetic and copies ran while one was open for 23% -> 27% of each run, Pallas kernels for 26% -> 12%
where the time goes in v8:
time: 81.2 us; the launch traced here: 80.8 us
  waiting for transfers between devices  25.1 us (31%)
  matrix products  23.8 us (29%)
  starting transfers between devices  19 us (23%)
  Pallas kernels  12.1 us (15%)
    ppermute x12, waiting for transfers between devices, send(): return lax.ppermute(x, ('rows', 'cols'), targets)  23.6 us
    ppermute x12, starting transfers between devices, send(): return lax.ppermute(x, ('rows', 'cols'), targets)  14.1 us
    dot_general x12, matrix products, inner_rows(): lax.dot_general(left, right, (((0,), (0,)), ((), ())), precision=HIGH, pr...  11.9 us
    dot_general x5, matrix products, matmul(): jnp.dot(rows, weights, precision=HIGH, preferred_element_type=jnp.float32)  10.7 us
    pallas_call x1, Pallas kernels, inverse_cholesky(): pl.pallas_call(factor_kernel, out_shape=jax.ShapeDtypeStruct(gram.shape,...  9.91 us
    ppermute x3, starting transfers between devices, placed(): arriving[k] = lax.ppermute(image, ('rows', 'cols'), outer)  4.71 us
    pallas_call x1, Pallas kernels, sketched(): pl.pallas_call(sketch_kernel, out_shape=[jax.ShapeDtypeStruct((length, ra...  2.22 us
  transfers between devices with their start and end apart: 17, of which 9 were waited for; matrix products, arithmetic and copies ran while one was open for 27% of the time, Pallas kernels for 12%

profile of v8, /device:TPU:0, one launch (start us, length us, event | category | flops | bytes accessed | tf_op | source)
XLA Modules:
  0.0 80.8 jit_solution(4863059420855266750)
XLA Ops:
  0.0 2.2 %shard_map.28 = f32[256,256]{1,0:T(8,128)S(1)} custom-call(s32[1]{0:T(128)} %bitcast.starts_ref, f32[2048,1024]{1,0:T(8,128)} %texture_ref.1, f32[1024,256]{1,0:T(8,128)} %sketch_ref.1), custom_call_target="tpu_custom_call" | custom-call | flops 402653184 | bytes 2097152 | tf_op jit(solution)/shard_map/pallas_call | solution.py:56
  2.2 3.0 %collective-permute-start = (f32[256,256]{1,0:T(8,128)S(1)}, f32[256,256]{1,0:T(8,128)S(1)}, u32[]{:S(2)}, u32[]{:S(2)}) collective-permute-start(f32[256,256]{1,0:T(8,128)S(1)} %shard_map.28), channel_id=1, source_target_pairs={{0,1},{1,0},{2,3},{3,2},{4,5},{5,4},{6,7},{7,6},{8,10},{9,11},{10,... | collective-permute-start | bytes 786440 | tf_op jit(solution)/shard_map/ppermute | solution.py:202
  5.3 2.6 %fusion.6 = f32[512,256]{1,0:T(8,128)S(1)} fusion(f32[1024,256]{1,0:T(8,128)S(1)} %copy-done, f32[2048,1024]{1,0:T(8,128)} %texture_ref.1, s32[]{:T(128)S(6)} %select_n.71), kind=kOutput, calls=%fused_computation.6 | convolution fusion | flops 805306368 | bytes 3670020 | tf_op jit(solution)/shard_map/dot_general | solution.py:215
  8.0 1.8 %fusion.25 = f32[256,256]{1,0:T(8,128)S(1)} fusion(f32[1024,256]{1,0:T(8,128)S(1)} %copy-done, f32[2048,1024]{1,0:T(8,128)} %texture_ref.1, s32[]{:T(128)S(6)} %select_n.70), kind=kOutput, calls=%fused_computation.29 | convolution fusion | flops 402653184 | bytes 2359300 | tf_op jit(solution)/shard_map/dot_general | solution.py:215
  9.9 2.1 %collective-permute-start.1 = (f32[128,256]{1,0:T(8,128)S(1)}, f32[128,256]{1,0:T(8,128)S(1)}, u32[]{:S(2)}, u32[]{:S(2)}) collective-permute-start(f32[128,256]{1,0:T(8,128)S(1)} %constant_dynamic-slice_fusion.2), channel_id=1, source_target_pairs={{0,2},{1,3},{2,0},{3,1},{4,6},{5,7},{6,4},{7,5},{8,9},{9,8},{10,11... | collective-permute-start | bytes 393224 | tf_op jit(solution)/shard_map/ppermute | solution.py:186
  12.0 1.8 %fusion.21 = f32[256,256]{1,0:T(8,128)S(1)} fusion(f32[1024,256]{1,0:T(8,128)S(1)} %copy-done, f32[2048,1024]{1,0:T(8,128)} %texture_ref.1, s32[]{:T(128)S(6)} %select_n.74), kind=kOutput, calls=%fused_computation.25 | convolution fusion | flops 402653184 | bytes 2359300 | tf_op jit(solution)/shard_map/dot_general | solution.py:215
  13.8 1.6 %collective-permute-start.4 = (f32[256,256]{1,0:T(8,128)S(1)}, f32[256,256]{1,0:T(8,128)S(1)}, u32[]{:S(2)}, u32[]{:S(2)}) collective-permute-start(f32[256,256]{1,0:T(8,128)S(1)} %fusion.21), channel_id=1, source_target_pairs={{0,1},{1,0},{2,3},{3,2},{4,5},{5,4},{6,7},{7,6},{8,10},{9,11},{10,... | collective-permute-start | bytes 786440 | tf_op jit(solution)/shard_map/ppermute | solution.py:202
  16.4 3.1 %collective-permute-start.2 = (f32[128,256]{1,0:T(8,128)S(1)}, f32[128,256]{1,0:T(8,128)S(1)}, u32[]{:S(2)}, u32[]{:S(2)}) collective-permute-start(f32[128,256]{1,0:T(8,128)S(1)} %dynamic-slice_add_fusion.2), channel_id=1, source_target_pairs={{0,4},{1,5},{2,6},{3,7},{4,0},{5,1},{6,2},{7,3},{8,12},{9,13},{10,... | collective-permute-start | bytes 393224 | tf_op jit(solution)/shard_map/ppermute | solution.py:186
  19.5 2.6 %fusion.2 = f32[512,256]{1,0:T(8,128)S(1)} fusion(f32[1024,256]{1,0:T(8,128)S(1)} %copy-done, f32[2048,1024]{1,0:T(8,128)} %texture_ref.1, s32[]{:T(128)S(6)} %select_n.76), kind=kOutput, calls=%fused_computation.2 | convolution fusion | flops 805306368 | bytes 3670020 | tf_op jit(solution)/shard_map/dot_general | solution.py:215
  22.2 1.4 %collective-permute-start.7 = (f32[256,256]{1,0:T(8,128)S(1)}, f32[256,256]{1,0:T(8,128)S(1)}, u32[]{:S(2)}, u32[]{:S(2)}) collective-permute-start(f32[256,256]{1,0:T(8,128)S(1)} %constant_dynamic-slice_fusion.1), channel_id=1, source_target_pairs={{0,2},{1,3},{2,0},{3,1},{4,6},{5,7},{6,4},{7,5},{8,9},{9,8},{10,11... | collective-permute-start | bytes 786440 | tf_op jit(solution)/shard_map/ppermute | solution.py:186
  23.6 1.8 %fusion.18 = f32[256,256]{1,0:T(8,128)S(1)} fusion(f32[1024,256]{1,0:T(8,128)S(1)} %copy-done, f32[2048,1024]{1,0:T(8,128)} %texture_ref.1, s32[]{:T(128)S(6)} %select_n.75), kind=kOutput, calls=%fused_computation.22 | convolution fusion | flops 402653184 | bytes 2359300 | tf_op jit(solution)/shard_map/dot_general | solution.py:215
  26.3 1.4 %collective-permute-start.5 = (f32[128,256]{1,0:T(8,128)S(1)}, f32[128,256]{1,0:T(8,128)S(1)}, u32[]{:S(2)}, u32[]{:S(2)}) collective-permute-start(f32[128,256]{1,0:T(8,128)S(1)} %add.140), channel_id=1, source_target_pairs={{0,2},{1,3},{2,0},{3,1},{4,6},{5,7},{6,4},{7,5},{8,9},{9,8},{10,11... | collective-permute-start | bytes 393224 | tf_op jit(solution)/shard_map/ppermute | solution.py:186
  28.9 5.0 %collective-permute-done.6 = f32[128,256]{1,0:T(8,128)S(1)} collective-permute-done((f32[128,256]{1,0:T(8,128)S(1)}, f32[128,256]{1,0:T(8,128)S(1)}, u32[]{:S(2)}, u32[]{:S(2)}) %collective-permute-start.6) | collective-permute-done | bytes 131104 | tf_op jit(solution)/shard_map/ppermute | solution.py:186
  33.9 4.7 %collective-permute-done.5 = f32[128,256]{1,0:T(8,128)S(1)} collective-permute-done((f32[128,256]{1,0:T(8,128)S(1)}, f32[128,256]{1,0:T(8,128)S(1)}, u32[]{:S(2)}, u32[]{:S(2)}) %collective-permute-start.5) | collective-permute-done | bytes 131104 | tf_op jit(solution)/shard_map/ppermute | solution.py:186
  38.6 2.9 %collective-permute-start.8 = (f32[256,256]{1,0:T(8,128)S(1)}, f32[256,256]{1,0:T(8,128)S(1)}, u32[]{:S(2)}, u32[]{:S(2)}) collective-permute-start(f32[256,256]{1,0:T(8,128)S(1)} %maximum_select_fusion.1), channel_id=1, source_target_pairs={{0,1},{1,0},{2,3},{3,2},{4,5},{5,4},{6,7},{7,6},{8,10},{9,11},{10,... | collective-permute-start | bytes 786440 | tf_op jit(solution)/shard_map/ppermute | solution.py:186
  41.4 1.8 %collective-permute-done.9 = f32[256,256]{1,0:T(8,128)S(1)} collective-permute-done((f32[256,256]{1,0:T(8,128)S(1)}, f32[256,256]{1,0:T(8,128)S(1)}, u32[]{:S(2)}, u32[]{:S(2)}) %collective-permute-start.9) | collective-permute-done | bytes 262176 | tf_op jit(solution)/shard_map/ppermute | solution.py:186
  44.0 2.2 %collective-permute-done.8 = f32[256,256]{1,0:T(8,128)S(1)} collective-permute-done((f32[256,256]{1,0:T(8,128)S(1)}, f32[256,256]{1,0:T(8,128)S(1)}, u32[]{:S(2)}, u32[]{:S(2)}) %collective-permute-start.8) | collective-permute-done | bytes 262176 | tf_op jit(solution)/shard_map/ppermute | solution.py:186
  46.1 1.9 %fusion.23 = f32[256,1024]{1,0:T(8,128)S(1)} fusion(f32[256,256]{1,0:T(8,128)S(1)} %maximum_select_fusion.1, f32[2048,1024]{1,0:T(8,128)} %texture_ref.1, s32[]{:T(128)S(6)} %select_n.70), kind=kOutput, calls=%fused_computation.27 | convolution fusion | flops 402653184 | bytes 2359300 | tf_op jit(solution)/shard_map/dot_general | solution.py:74
  48.4 4.8 %collective-permute-done.11 = f32[256,256]{1,0:T(8,128)S(1)} collective-permute-done((f32[256,256]{1,0:T(8,128)S(1)}, f32[256,256]{1,0:T(8,128)S(1)}, u32[]{:S(2)}, u32[]{:S(2)}) %collective-permute-start.11) | collective-permute-done | bytes 262176 | tf_op jit(solution)/shard_map/ppermute | solution.py:186
  54.5 1.9 %convolution_add_fusion.2 = f32[256,1024]{1,0:T(8,128)S(1)} fusion(f32[256,1024]{1,0:T(8,128)S(1)} %fusion.23, f32[256,256]{1,0:T(8,128)S(1)} %collective-permute-done.8, f32[2048,1024]{1,0:T(8,128)} %texture_ref.1, s32[]{:T(128)S(6)} %select_n.82), kind=kOutput, calls=%fused_computation.12 | convolution fusion | flops 402915328 | bytes 3407876 | tf_op jit(solution)/shard_map/dot_general | solution.py:74
  56.7 3.1 %collective-permute-done.12 = f32[128,256]{1,0:T(8,128)S(1)} collective-permute-done((f32[128,256]{1,0:T(8,128)S(1)}, f32[128,256]{1,0:T(8,128)S(1)}, u32[]{:S(2)}, u32[]{:S(2)}) %collective-permute-start.12) | collective-permute-done | bytes 131104 | tf_op jit(solution)/shard_map/ppermute | solution.py:186
  61.0 2.7 %fusion.11 = f32[256,1024]{1,0:T(8,128)S(1)} fusion(f32[256,1024]{1,0:T(8,128)S(1)} %convolution_add_fusion.2, f32[512,256]{1,0:T(8,128)S(1)} %maximum_select_fusion, f32[2048,1024]{1,0:T(8,128)} %texture_ref.1, s32[]{:T(128)S(6)} %select_n.76), kind=kOutput, calls=%fused_computation.9 | convolution fusion | flops 805568512 | bytes 4718596 | tf_op jit(solution)/shard_map/dot_general | solution.py:74
  68.0 1.5 %collective-permute-done.15.far_ref = f32[256,256]{1,0:T(8,128)S(1)} collective-permute-done((f32[256,256]{1,0:T(8,128)S(1)}, f32[256,256]{1,0:T(8,128)S(1)}, u32[]{:S(2)}, u32[]{:S(2)}) %collective-permute-start.15) | collective-permute-done | bytes 262176 | tf_op jit(solution)/shard_map/ppermute | solution.py:267
  69.7 9.9 %shard_map.29 = f32[256,256]{1,0:T(8,128)S(1)} custom-call(f32[256,256]{1,0:T(8,128)S(1)} %convolution_add_fusion.3.gram_ref, f32[256,256]{1,0:T(8,128)S(1)} %collective-permute-done.15.far_ref), custom_call_target="tpu_custom_call" | custom-call | flops 1000 | bytes 1000 | tf_op jit(solution)/shard_map/pallas_call | solution.py:154
  (52 shorter events, 12.7 us)
Async XLA Ops:
  0.0 5.3 %copy-start = (f32[1024,256]{1,0:T(8,128)S(1)}, f32[1024,256]{1,0:T(8,128)}, u32[]{:S(2)}) copy-start(f32[1024,256]{1,0:T(8,128)} %sketch_ref.1) | copy-start | bytes 3145732
  2.2 7.6 %collective-permute-start = (f32[256,256]{1,0:T(8,128)S(1)}, f32[256,256]{1,0:T(8,128)S(1)}, u32[]{:S(2)}, u32[]{:S(2)}) collective-permute-start(f32[256,256]{1,0:T(8,128)S(1)} %shard_map.28), channel_id=1, source_target_pairs={{0,1},{1,0},{2,3},{3,2},{4,5},{5,4},{6,7},{7,6},{8,10},{9,11},{10,... | collective-permute-start | bytes 786440 | tf_op jit(solution)/shard_map/ppermute | solution.py:202
  7.9 14.3 %collective-permute-start.3 = (f32[512,256]{1,0:T(8,128)S(1)}, f32[512,256]{1,0:T(8,128)S(1)}, u32[]{:S(2)}, u32[]{:S(2)}) collective-permute-start(f32[512,256]{1,0:T(8,128)S(1)} %fusion.6), channel_id=1, source_target_pairs={{0,1},{1,0},{2,3},{3,2},{4,5},{5,4},{6,7},{7,6},{8,10},{9,11},{10,... | collective-permute-start | bytes 1572872 | tf_op jit(solution)/shard_map/ppermute | solution.py:202
  9.9 6.5 %collective-permute-start.1 = (f32[128,256]{1,0:T(8,128)S(1)}, f32[128,256]{1,0:T(8,128)S(1)}, u32[]{:S(2)}, u32[]{:S(2)}) collective-permute-start(f32[128,256]{1,0:T(8,128)S(1)} %constant_dynamic-slice_fusion.2), channel_id=1, source_target_pairs={{0,2},{1,3},{2,0},{3,1},{4,6},{5,7},{6,4},{7,5},{8,9},{9,8},{10,11... | collective-permute-start | bytes 393224 | tf_op jit(solution)/shard_map/ppermute | solution.py:186
  13.8 11.6 %collective-permute-start.4 = (f32[256,256]{1,0:T(8,128)S(1)}, f32[256,256]{1,0:T(8,128)S(1)}, u32[]{:S(2)}, u32[]{:S(2)}) collective-permute-start(f32[256,256]{1,0:T(8,128)S(1)} %fusion.21), channel_id=1, source_target_pairs={{0,1},{1,0},{2,3},{3,2},{4,5},{5,4},{6,7},{7,6},{8,10},{9,11},{10,... | collective-permute-start | bytes 786440 | tf_op jit(solution)/shard_map/ppermute | solution.py:202
  16.4 9.9 %collective-permute-start.2 = (f32[128,256]{1,0:T(8,128)S(1)}, f32[128,256]{1,0:T(8,128)S(1)}, u32[]{:S(2)}, u32[]{:S(2)}) collective-permute-start(f32[128,256]{1,0:T(8,128)S(1)} %dynamic-slice_add_fusion.2), channel_id=1, source_target_pairs={{0,4},{1,5},{2,6},{3,7},{4,0},{5,1},{6,2},{7,3},{8,12},{9,13},{10,... | collective-permute-start | bytes 393224 | tf_op jit(solution)/shard_map/ppermute | solution.py:186
  22.2 6.4 %collective-permute-start.7 = (f32[256,256]{1,0:T(8,128)S(1)}, f32[256,256]{1,0:T(8,128)S(1)}, u32[]{:S(2)}, u32[]{:S(2)}) collective-permute-start(f32[256,256]{1,0:T(8,128)S(1)} %constant_dynamic-slice_fusion.1), channel_id=1, source_target_pairs={{0,2},{1,3},{2,0},{3,1},{4,6},{5,7},{6,4},{7,5},{8,9},{9,8},{10,11... | collective-permute-start | bytes 786440 | tf_op jit(solution)/shard_map/ppermute | solution.py:186
  25.5 8.3 %collective-permute-start.6 = (f32[128,256]{1,0:T(8,128)S(1)}, f32[128,256]{1,0:T(8,128)S(1)}, u32[]{:S(2)}, u32[]{:S(2)}) collective-permute-start(f32[128,256]{1,0:T(8,128)S(1)} %constant_dynamic-slice_fusion), channel_id=1, source_target_pairs={{0,2},{1,3},{2,0},{3,1},{4,6},{5,7},{6,4},{7,5},{8,9},{9,8},{10,11... | collective-permute-start | bytes 393224 | tf_op jit(solution)/shard_map/ppermute | solution.py:186
  26.3 12.2 %collective-permute-start.5 = (f32[128,256]{1,0:T(8,128)S(1)}, f32[128,256]{1,0:T(8,128)S(1)}, u32[]{:S(2)}, u32[]{:S(2)}) collective-permute-start(f32[128,256]{1,0:T(8,128)S(1)} %add.140), channel_id=1, source_target_pairs={{0,2},{1,3},{2,0},{3,1},{4,6},{5,7},{6,4},{7,5},{8,9},{9,8},{10,11... | collective-permute-start | bytes 393224 | tf_op jit(solution)/shard_map/ppermute | solution.py:186
  28.7 14.5 %collective-permute-start.9 = (f32[256,256]{1,0:T(8,128)S(1)}, f32[256,256]{1,0:T(8,128)S(1)}, u32[]{:S(2)}, u32[]{:S(2)}) collective-permute-start(f32[256,256]{1,0:T(8,128)S(1)} %dynamic-slice_add_fusion), channel_id=1, source_target_pairs={{0,4},{1,5},{2,6},{3,7},{4,0},{5,1},{6,2},{7,3},{8,12},{9,13},{10,... | collective-permute-start | bytes 786440 | tf_op jit(solution)/shard_map/ppermute | solution.py:186
  38.6 7.6 %collective-permute-start.8 = (f32[256,256]{1,0:T(8,128)S(1)}, f32[256,256]{1,0:T(8,128)S(1)}, u32[]{:S(2)}, u32[]{:S(2)}) collective-permute-start(f32[256,256]{1,0:T(8,128)S(1)} %maximum_select_fusion.1), channel_id=1, source_target_pairs={{0,1},{1,0},{2,3},{3,2},{4,5},{5,4},{6,7},{7,6},{8,10},{9,11},{10,... | collective-permute-start | bytes 786440 | tf_op jit(solution)/shard_map/ppermute | solution.py:186
  41.4 11.8 %collective-permute-start.10 = (f32[128,256]{1,0:T(8,128)S(1)}, f32[128,256]{1,0:T(8,128)S(1)}, u32[]{:S(2)}, u32[]{:S(2)}) collective-permute-start(f32[128,256]{1,0:T(8,128)S(1)} %dynamic-slice_add_fusion.1), channel_id=1, source_target_pairs={{0,4},{1,5},{2,6},{3,7},{4,0},{5,1},{6,2},{7,3},{8,12},{9,13},{10,... | collective-permute-start | bytes 393224 | tf_op jit(solution)/shard_map/ppermute | solution.py:186
  43.3 21.1 %slice-start = ((s8[8388608]{0:T(1024)(128)(4,1)}), s8[4194304]{0:T(1024)(128)(4,1)S(1)}, s32[]{:S(2)}) async-start(s8[8388608]{0:T(1024)(128)(4,1)} %bitcast.24), calls=%async_computation | async-start | bytes 8388608
  43.3 9.9 %collective-permute-start.11 = (f32[256,256]{1,0:T(8,128)S(1)}, f32[256,256]{1,0:T(8,128)S(1)}, u32[]{:S(2)}, u32[]{:S(2)}) collective-permute-start(f32[256,256]{1,0:T(8,128)S(1)} %add.144), channel_id=1, source_target_pairs={{0,2},{1,3},{2,0},{3,1},{4,6},{5,7},{6,4},{7,5},{8,9},{9,8},{10,11... | collective-permute-start | bytes 786440 | tf_op jit(solution)/shard_map/ppermute | solution.py:186
  53.3 6.5 %collective-permute-start.12 = (f32[128,256]{1,0:T(8,128)S(1)}, f32[128,256]{1,0:T(8,128)S(1)}, u32[]{:S(2)}, u32[]{:S(2)}) collective-permute-start(f32[128,256]{1,0:T(8,128)S(1)} %add.145), channel_id=1, source_target_pairs={{0,2},{1,3},{2,0},{3,1},{4,6},{5,7},{6,4},{7,5},{8,9},{9,8},{10,11... | collective-permute-start | bytes 393224 | tf_op jit(solution)/shard_map/ppermute | solution.py:186
  53.4 10.3 %collective-permute-start.13 = (f32[512,256]{1,0:T(8,128)S(1)}, f32[512,256]{1,0:T(8,128)S(1)}, u32[]{:S(2)}, u32[]{:S(2)}) collective-permute-start(f32[512,256]{1,0:T(8,128)S(1)} %maximum_select_fusion), channel_id=1, source_target_pairs={{0,1},{1,0},{2,3},{3,2},{4,5},{5,4},{6,7},{7,6},{8,10},{9,11},{10,... | collective-permute-start | bytes 1572872 | tf_op jit(solution)/shard_map/ppermute | solution.py:186
  56.3 8.0 %slice-start.1 = ((s8[8388608]{0:T(1024)(128)(4,1)}), s8[4194304]{0:T(1024)(128)(4,1)S(1)}, s32[]{:S(2)}) async-start(s8[8388608]{0:T(1024)(128)(4,1)} %bitcast.24), calls=%async_computation.1 | async-start | bytes 8388608
  59.8 7.0 %collective-permute-start.14 = (f32[256,256]{1,0:T(8,128)S(1)}, f32[256,256]{1,0:T(8,128)S(1)}, u32[]{:S(2)}, u32[]{:S(2)}) collective-permute-start(f32[256,256]{1,0:T(8,128)S(1)} %maximum_select_fusion.2), channel_id=1, source_target_pairs={{0,1},{1,0},{2,3},{3,2},{4,5},{5,4},{6,7},{7,6},{8,10},{9,11},{10,... | collective-permute-start | bytes 786440 | tf_op jit(solution)/shard_map/ppermute | solution.py:186
  67.9 1.6 %collective-permute-start.15 = (f32[256,256]{1,0:T(8,128)S(1)}, f32[256,256]{1,0:T(8,128)S(1)}, u32[]{:S(2)}, u32[]{:S(2)}) collective-permute-start(f32[256,256]{1,0:T(8,128)S(1)} %convolution_add_fusion.3.gram_ref), channel_id=1, source_target_pairs={{0,8},{8,0},{1,9},{9,1},{2,10},{10,2},{3,11},{11,3},{4,12},{12,4},... | collective-permute-start | bytes 786440 | tf_op jit(solution)/shard_map/ppermute | solution.py:267
  69.5 10.1 %collective-permute-start.16 = (f32[256,1024]{1,0:T(8,128)S(1)}, f32[256,1024]{1,0:T(8,128)S(1)}, u32[]{:S(2)}, u32[]{:S(2)}) collective-permute-start(f32[256,1024]{1,0:T(8,128)S(1)} %convolution_add_fusion), channel_id=1, source_target_pairs={{0,8},{8,0},{1,9},{9,1},{2,10},{10,2},{3,11},{11,3},{4,12},{12,4},... | collective-permute-start | bytes 3145736 | tf_op jit(solution)/shard_map/ppermute | solution.py:270

commit v9 on v8

--- a/solution.py
+++ b/solution.py
@@ -10,10 +10,11 @@
 HIGH = lax.Precision.HIGH
 STEP = 256
 SIZES = (128, 256, 128)
+CROSSED = (True, True, True)
 STEPS = [("s", 0, True), ("m", 1, True), ("m", 0, False), ("i", 0), ("m", 2, True), ("l", 0), ("m", 1, False), ("i", 1)]
 STEPS += [("m", 2, False), ("i", 2), ("b", 0), ("l", 1), ("l", 2), ("o", 0), ("b", 1), ("w", 0), ("g", 0), ("o", 1), ("b", 2), ("f", 0), ("o", 2)]
 STEPS += [("g", 1), ("f", 1), ("g", 2), ("f", 2)]
-BLOCK = 64
+BLOCK = 128
 TILE = 8
 LIGHT = pl.CostEstimate(flops=1000, bytes_accessed=1000, transcendentals=0)
 
@@ -101,28 +102,38 @@
     for s, lines in enumerate(tiles):
         low = s * TILE
         inside = (lane >= low) & (lane < low + TILE)
-        corner = [along(lines, low + c) for c in range(TILE)]
+        corner = [jnp.where(sub < TILE, along(lines, low + c), 0.0) for c in range(TILE)]
         lines = jnp.where(inside, jnp.where(lane - low == sub, 1.0, 0.0), lines)
         out = jnp.zeros((TILE, size), jnp.float32)
-        scale = jnp.ones((TILE, size), jnp.float32)
-        for j in range(TILE):
-            pivot = down(corner[j], j)
-            inverse = 1.0 / pivot
-            factor = jnp.where(sub == j, 0.0, corner[j] * inverse)
-            scale = jnp.where(sub == j, inverse, scale)
-            line = down(lines, j)
-            out = jnp.where(sub == j, line * lax.rsqrt(pivot), out)
-            for c in range(j + 1, TILE):
-                corner[c] = corner[c] - factor * down(corner[c], j)
-            lines = lines - factor * line
+        same = jnp.ones((TILE, size), jnp.float32)
+        cross = jnp.zeros((TILE, size), jnp.float32)
+        for j in range(0, TILE, 2):
+            both = (sub == j) | (sub == j + 1)
+            left, right = corner[j], corner[j + 1]
+            a, b, c = down(left, j), down(right, j), down(right, j + 1)
+            inverse = 1.0 / (a * c - b * b)
+            a_over, b_over, c_over = a * inverse, b * inverse, c * inverse
+            first = jnp.where(both, 0.0, left * c_over - right * b_over)
+            second = jnp.where(both, 0.0, right * a_over - left * b_over)
+            upper, lower = down(lines, j), down(lines, j + 1)
+            root = lax.rsqrt(a)
+            ratio = b * (root * root)
+            lower_out = (lower - ratio * upper) * lax.rsqrt(c - b * ratio)
+            out = jnp.where(sub == j, upper * root, jnp.where(sub == j + 1, lower_out, out))
+            same = jnp.where(sub == j, c_over, jnp.where(sub == j + 1, a_over, same))
+            cross = jnp.where(both, b_over, cross)
+            for k in range(j + 2, TILE):
+                corner[k] = corner[k] - (first * down(corner[k], j) + second * down(corner[k], j + 1))
+            lines = lines - (first * upper + second * lower)
         outs.append(jnp.where(lane < low + TILE, out, 0.0))
-        lines = lines * scale
+        partner = jnp.where(sub % 2 == 0, pltpu.roll(lines, TILE - 1, 0), pltpu.roll(lines, 1, 0))
+        lines = lines * same - cross * partner
         rows = [down(lines, c) for c in range(TILE)]
         for t in range(s + 1, len(tiles)):
-            term = along(tiles[t], low) * rows[0]
-            for c in range(1, TILE):
-                term = term + along(tiles[t], low + c) * rows[c]
-            tiles[t] = jnp.where(inside, 0.0, tiles[t]) - term
+            terms = [along(tiles[t], low + c) * rows[c] for c in range(TILE)]
+            while len(terms) > 1:
+                terms = [x + y for x, y in zip(terms[::2], terms[1::2])]
+            tiles[t] = jnp.where(inside, 0.0, tiles[t]) - terms[0]
     return jnp.concatenate(outs, axis=0)
 
 
@@ -170,13 +181,15 @@
 def exchanged(texture, sketch):
     col, row = lax.axis_index("cols"), lax.axis_index("rows")
     bits = lax.rem(col, 2), lax.rem(lax.div(col, 2), 2)
-    side = jnp.where(row == 0, bits[0], bits[1])
-    odd = jnp.where(row == 0, bits[1], bits[0])
 
     def pairs(first_core, second_core):
         return [(8 * r + c, 8 * r + (c ^ step)) for r, step in ((0, first_core), (1, second_core)) for c in range(8)]
 
-    outer, inner, line = pairs(1, 2), pairs(2, 1), pairs(4, 4)
+    line = pairs(4, 4)
+    outer = [pairs(1, 2 if crossed else 1) for crossed in CROSSED]
+    inner = [pairs(2, 1 if crossed else 2) for crossed in CROSSED]
+    side = [jnp.where(row == 0, bits[0], bits[1]) if crossed else bits[0] for crossed in CROSSED]
+    odd = [jnp.where(row == 0, bits[1], bits[0]) if crossed else bits[1] for crossed in CROSSED]
     chunks = range(len(SIZES))
     starts = [4 * sum(SIZES[:k]) for k in chunks]
     last = [None]
@@ -191,27 +204,27 @@
     def part(x, which):
         return lax.dynamic_slice_in_dim(x, which * (x.shape[0] // 2), x.shape[0] // 2)
 
-    def joined(own, other):
-        return jnp.where(odd == 0, jnp.concatenate([own, other]), jnp.concatenate([other, own]))
+    def joined(k, own, other):
+        return jnp.where(odd[k] == 0, jnp.concatenate([own, other]), jnp.concatenate([other, own]))
 
     arriving, own = {}, {}
 
     def placed(k, theirs, image):
         last[0] = image
         if theirs:
-            arriving[k] = lax.ppermute(image, ("rows", "cols"), outer)
+            arriving[k] = lax.ppermute(image, ("rows", "cols"), outer[k])
         else:
             own[k] = image
 
     def first_matmul(k, theirs):
         pinned = [pltpu.with_memory_space_constraint(x, pltpu.HBM) for x in (texture, sketch)]
-        which = 1 - side if theirs else side
+        which = 1 - side[k] if theirs else side[k]
         parts = [(starts[k] + which * (2 * SIZES[k]), 2 * SIZES[k])]
         placed(k, theirs, sketched(*pinned, parts, [])[0])
 
     def matmul(k, theirs):
         (weights,) = after([sketch], last[0])
-        rows = rows_of(k, 1 - side if theirs else side)
+        rows = rows_of(k, 1 - side[k] if theirs else side[k])
         placed(k, theirs, jnp.dot(rows, weights, precision=HIGH, preferred_element_type=jnp.float32))
 
     kept, half, sums = {}, {}, [()]
@@ -221,8 +234,8 @@
 
     def to_inner(k):
         total = own[k] + arrived(k)
-        kept[k] = part(total, odd)
-        arriving[k] = send(part(total, 1 - odd), inner)
+        kept[k] = part(total, odd[k])
+        arriving[k] = send(part(total, 1 - odd[k]), inner[k])
 
     def to_line(k):
         kept[k] = kept[k] + arrived(k)
@@ -230,11 +243,11 @@
 
     def back_to_inner(k):
         kept[k] = kept[k] + arrived(k)
-        arriving[k] = send(kept[k], inner)
+        arriving[k] = send(kept[k], inner[k])
 
     def back_to_outer(k):
-        half[k] = joined(kept[k], arrived(k))
-        arriving[k] = send(half[k], outer)
+        half[k] = joined(k, kept[k], arrived(k))
+        arriving[k] = send(half[k], outer[k])
 
     def gather(rows, image):
         terms = inner_rows(image, image), inner_rows(image, rows)
@@ -242,13 +255,13 @@
         last[0] = sums[0][0]
 
     def gather_own(k):
-        gather(rows_of(k, side), *after([half[k]], last[0]))
+        gather(rows_of(k, side[k]), *after([half[k]], last[0]))
 
     def wait_far(k):
         arriving[k] = last[0] = arrived(k)
 
     def gather_far(k):
-        gather(rows_of(k, 1 - side), arrived(k))
+        gather(rows_of(k, 1 - side[k]), arrived(k))
 
     steps = dict(i=to_inner, l=to_line, b=back_to_inner, o=back_to_outer, g=gather_own, f=gather_far, w=wait_far, s=first_matmul, m=matmul)
     for name, *chunk in STEPS:

time: 81.2 us -> 78.8 us (0.970)
  Pallas kernels: 12.1 us -> 9.71 us
    pallas_call x1, Pallas kernels: 9.91 us -> 7.49 us  [inverse_cholesky(): pl.pallas_call(factor_kernel, out_shape=jax.ShapeDtypeStruct(gram.shape,...]
  transfers between devices with their start and end apart: 17 -> 17, of which waited for: 9 -> 9; matrix products, arithmetic and copies ran while one was open for 27% -> 28% of each run, Pallas kernels for 12% -> 10%
where the time goes in v9:
time: 78.8 us; the launch traced here: 78.4 us
  waiting for transfers between devices  25.1 us (32%)
  matrix products  23.8 us (30%)
  starting transfers between devices  19 us (24%)
  Pallas kernels  9.71 us (12%)
    ppermute x12, waiting for transfers between devices, send(): return lax.ppermute(x, ('rows', 'cols'), targets)  23.6 us
    ppermute x12, starting transfers between devices, send(): return lax.ppermute(x, ('rows', 'cols'), targets)  14.1 us
    dot_general x12, matrix products, inner_rows(): lax.dot_general(left, right, (((0,), (0,)), ((), ())), precision=HIGH, pr...  11.9 us
    dot_general x5, matrix products, matmul(): jnp.dot(rows, weights, precision=HIGH, preferred_element_type=jnp.float32)  10.7 us
    pallas_call x1, Pallas kernels, inverse_cholesky(): pl.pallas_call(factor_kernel, out_shape=jax.ShapeDtypeStruct(gram.shape,...  7.49 us
    ppermute x3, starting transfers between devices, placed(): arriving[k] = lax.ppermute(image, ('rows', 'cols'), outer[k])  4.71 us
    pallas_call x1, Pallas kernels, sketched(): pl.pallas_call(sketch_kernel, out_shape=[jax.ShapeDtypeStruct((length, ra...  2.22 us
  transfers between devices with their start and end apart: 17, of which 9 were waited for; matrix products, arithmetic and copies ran while one was open for 28% of the time, Pallas kernels for 10%

profile of v9, /device:TPU:0, one launch (start us, length us, event | category | flops | bytes accessed | tf_op | source)
XLA Modules:
  0.0 78.4 jit_solution(3566512408407620573)
XLA Ops:
  0.0 2.2 %shard_map.28 = f32[256,256]{1,0:T(8,128)S(1)} custom-call(s32[1]{0:T(128)} %bitcast.starts_ref, f32[2048,1024]{1,0:T(8,128)} %texture_ref.1, f32[1024,256]{1,0:T(8,128)} %sketch_ref.1), custom_call_target="tpu_custom_call" | custom-call | flops 402653184 | bytes 2097152 | tf_op jit(solution)/shard_map/pallas_call | solution.py:57
  2.2 3.0 %collective-permute-start = (f32[256,256]{1,0:T(8,128)S(1)}, f32[256,256]{1,0:T(8,128)S(1)}, u32[]{:S(2)}, u32[]{:S(2)}) collective-permute-start(f32[256,256]{1,0:T(8,128)S(1)} %shard_map.28), channel_id=1, source_target_pairs={{0,1},{1,0},{2,3},{3,2},{4,5},{5,4},{6,7},{7,6},{8,10},{9,11},{10,... | collective-permute-start | bytes 786440 | tf_op jit(solution)/shard_map/ppermute | solution.py:215
  5.3 2.6 %fusion.6 = f32[512,256]{1,0:T(8,128)S(1)} fusion(f32[1024,256]{1,0:T(8,128)S(1)} %copy-done, f32[2048,1024]{1,0:T(8,128)} %texture_ref.1, s32[]{:T(128)S(6)} %select_n.75), kind=kOutput, calls=%fused_computation.6 | convolution fusion | flops 805306368 | bytes 3670020 | tf_op jit(solution)/shard_map/dot_general | solution.py:228
  8.0 1.8 %fusion.25 = f32[256,256]{1,0:T(8,128)S(1)} fusion(f32[1024,256]{1,0:T(8,128)S(1)} %copy-done, f32[2048,1024]{1,0:T(8,128)} %texture_ref.1, s32[]{:T(128)S(6)} %select_n.74), kind=kOutput, calls=%fused_computation.29 | convolution fusion | flops 402653184 | bytes 2359300 | tf_op jit(solution)/shard_map/dot_general | solution.py:228
  9.9 2.1 %collective-permute-start.1 = (f32[128,256]{1,0:T(8,128)S(1)}, f32[128,256]{1,0:T(8,128)S(1)}, u32[]{:S(2)}, u32[]{:S(2)}) collective-permute-start(f32[128,256]{1,0:T(8,128)S(1)} %constant_dynamic-slice_fusion.2), channel_id=1, source_target_pairs={{0,2},{1,3},{2,0},{3,1},{4,6},{5,7},{6,4},{7,5},{8,9},{9,8},{10,11... | collective-permute-start | bytes 393224 | tf_op jit(solution)/shard_map/ppermute | solution.py:199
  12.0 1.8 %fusion.21 = f32[256,256]{1,0:T(8,128)S(1)} fusion(f32[1024,256]{1,0:T(8,128)S(1)} %copy-done, f32[2048,1024]{1,0:T(8,128)} %texture_ref.1, s32[]{:T(128)S(6)} %select_n.78), kind=kOutput, calls=%fused_computation.25 | convolution fusion | flops 402653184 | bytes 2359300 | tf_op jit(solution)/shard_map/dot_general | solution.py:228
  13.8 1.6 %collective-permute-start.4 = (f32[256,256]{1,0:T(8,128)S(1)}, f32[256,256]{1,0:T(8,128)S(1)}, u32[]{:S(2)}, u32[]{:S(2)}) collective-permute-start(f32[256,256]{1,0:T(8,128)S(1)} %fusion.21), channel_id=1, source_target_pairs={{0,1},{1,0},{2,3},{3,2},{4,5},{5,4},{6,7},{7,6},{8,10},{9,11},{10,... | collective-permute-start | bytes 786440 | tf_op jit(solution)/shard_map/ppermute | solution.py:215
  16.4 3.1 %collective-permute-start.2 = (f32[128,256]{1,0:T(8,128)S(1)}, f32[128,256]{1,0:T(8,128)S(1)}, u32[]{:S(2)}, u32[]{:S(2)}) collective-permute-start(f32[128,256]{1,0:T(8,128)S(1)} %dynamic-slice_add_fusion.2), channel_id=1, source_target_pairs={{0,4},{1,5},{2,6},{3,7},{4,0},{5,1},{6,2},{7,3},{8,12},{9,13},{10,... | collective-permute-start | bytes 393224 | tf_op jit(solution)/shard_map/ppermute | solution.py:199
  19.5 2.6 %fusion.2 = f32[512,256]{1,0:T(8,128)S(1)} fusion(f32[1024,256]{1,0:T(8,128)S(1)} %copy-done, f32[2048,1024]{1,0:T(8,128)} %texture_ref.1, s32[]{:T(128)S(6)} %select_n.80), kind=kOutput, calls=%fused_computation.2 | convolution fusion | flops 805306368 | bytes 3670020 | tf_op jit(solution)/shard_map/dot_general | solution.py:228
  22.2 1.4 %collective-permute-start.7 = (f32[256,256]{1,0:T(8,128)S(1)}, f32[256,256]{1,0:T(8,128)S(1)}, u32[]{:S(2)}, u32[]{:S(2)}) collective-permute-start(f32[256,256]{1,0:T(8,128)S(1)} %constant_dynamic-slice_fusion.1), channel_id=1, source_target_pairs={{0,2},{1,3},{2,0},{3,1},{4,6},{5,7},{6,4},{7,5},{8,9},{9,8},{10,11... | collective-permute-start | bytes 786440 | tf_op jit(solution)/shard_map/ppermute | solution.py:199
  23.6 1.8 %fusion.18 = f32[256,256]{1,0:T(8,128)S(1)} fusion(f32[1024,256]{1,0:T(8,128)S(1)} %copy-done, f32[2048,1024]{1,0:T(8,128)} %texture_ref.1, s32[]{:T(128)S(6)} %select_n.79), kind=kOutput, calls=%fused_computation.22 | convolution fusion | flops 402653184 | bytes 2359300 | tf_op jit(solution)/shard_map/dot_general | solution.py:228
  26.3 1.4 %collective-permute-start.5 = (f32[128,256]{1,0:T(8,128)S(1)}, f32[128,256]{1,0:T(8,128)S(1)}, u32[]{:S(2)}, u32[]{:S(2)}) collective-permute-start(f32[128,256]{1,0:T(8,128)S(1)} %add.140), channel_id=1, source_target_pairs={{0,2},{1,3},{2,0},{3,1},{4,6},{5,7},{6,4},{7,5},{8,9},{9,8},{10,11... | collective-permute-start | bytes 393224 | tf_op jit(solution)/shard_map/ppermute | solution.py:199
  28.9 5.0 %collective-permute-done.6 = f32[128,256]{1,0:T(8,128)S(1)} collective-permute-done((f32[128,256]{1,0:T(8,128)S(1)}, f32[128,256]{1,0:T(8,128)S(1)}, u32[]{:S(2)}, u32[]{:S(2)}) %collective-permute-start.6) | collective-permute-done | bytes 131104 | tf_op jit(solution)/shard_map/ppermute | solution.py:199
  33.9 4.7 %collective-permute-done.5 = f32[128,256]{1,0:T(8,128)S(1)} collective-permute-done((f32[128,256]{1,0:T(8,128)S(1)}, f32[128,256]{1,0:T(8,128)S(1)}, u32[]{:S(2)}, u32[]{:S(2)}) %collective-permute-start.5) | collective-permute-done | bytes 131104 | tf_op jit(solution)/shard_map/ppermute | solution.py:199
  38.6 2.9 %collective-permute-start.8 = (f32[256,256]{1,0:T(8,128)S(1)}, f32[256,256]{1,0:T(8,128)S(1)}, u32[]{:S(2)}, u32[]{:S(2)}) collective-permute-start(f32[256,256]{1,0:T(8,128)S(1)} %maximum_select_fusion.1), channel_id=1, source_target_pairs={{0,1},{1,0},{2,3},{3,2},{4,5},{5,4},{6,7},{7,6},{8,10},{9,11},{10,... | collective-permute-start | bytes 786440 | tf_op jit(solution)/shard_map/ppermute | solution.py:199
  41.4 1.8 %collective-permute-done.9 = f32[256,256]{1,0:T(8,128)S(1)} collective-permute-done((f32[256,256]{1,0:T(8,128)S(1)}, f32[256,256]{1,0:T(8,128)S(1)}, u32[]{:S(2)}, u32[]{:S(2)}) %collective-permute-start.9) | collective-permute-done | bytes 262176 | tf_op jit(solution)/shard_map/ppermute | solution.py:199
  44.0 2.2 %collective-permute-done.8 = f32[256,256]{1,0:T(8,128)S(1)} collective-permute-done((f32[256,256]{1,0:T(8,128)S(1)}, f32[256,256]{1,0:T(8,128)S(1)}, u32[]{:S(2)}, u32[]{:S(2)}) %collective-permute-start.8) | collective-permute-done | bytes 262176 | tf_op jit(solution)/shard_map/ppermute | solution.py:199
  46.1 1.9 %fusion.23 = f32[256,1024]{1,0:T(8,128)S(1)} fusion(f32[256,256]{1,0:T(8,128)S(1)} %maximum_select_fusion.1, f32[2048,1024]{1,0:T(8,128)} %texture_ref.1, s32[]{:T(128)S(6)} %select_n.74), kind=kOutput, calls=%fused_computation.27 | convolution fusion | flops 402653184 | bytes 2359300 | tf_op jit(solution)/shard_map/dot_general | solution.py:75
  48.4 4.8 %collective-permute-done.11 = f32[256,256]{1,0:T(8,128)S(1)} collective-permute-done((f32[256,256]{1,0:T(8,128)S(1)}, f32[256,256]{1,0:T(8,128)S(1)}, u32[]{:S(2)}, u32[]{:S(2)}) %collective-permute-start.11) | collective-permute-done | bytes 262176 | tf_op jit(solution)/shard_map/ppermute | solution.py:199
  54.5 1.9 %convolution_add_fusion.2 = f32[256,1024]{1,0:T(8,128)S(1)} fusion(f32[256,1024]{1,0:T(8,128)S(1)} %fusion.23, f32[256,256]{1,0:T(8,128)S(1)} %collective-permute-done.8, f32[2048,1024]{1,0:T(8,128)} %texture_ref.1, s32[]{:T(128)S(6)} %select_n.86), kind=kOutput, calls=%fused_computation.12 | convolution fusion | flops 402915328 | bytes 3407876 | tf_op jit(solution)/shard_map/dot_general | solution.py:75
  56.7 3.1 %collective-permute-done.12 = f32[128,256]{1,0:T(8,128)S(1)} collective-permute-done((f32[128,256]{1,0:T(8,128)S(1)}, f32[128,256]{1,0:T(8,128)S(1)}, u32[]{:S(2)}, u32[]{:S(2)}) %collective-permute-start.12) | collective-permute-done | bytes 131104 | tf_op jit(solution)/shard_map/ppermute | solution.py:199
  61.0 2.7 %fusion.11 = f32[256,1024]{1,0:T(8,128)S(1)} fusion(f32[256,1024]{1,0:T(8,128)S(1)} %convolution_add_fusion.2, f32[512,256]{1,0:T(8,128)S(1)} %maximum_select_fusion, f32[2048,1024]{1,0:T(8,128)} %texture_ref.1, s32[]{:T(128)S(6)} %select_n.80), kind=kOutput, calls=%fused_computation.9 | convolution fusion | flops 805568512 | bytes 4718596 | tf_op jit(solution)/shard_map/dot_general | solution.py:75
  68.0 1.5 %collective-permute-done.15.far_ref = f32[256,256]{1,0:T(8,128)S(1)} collective-permute-done((f32[256,256]{1,0:T(8,128)S(1)}, f32[256,256]{1,0:T(8,128)S(1)}, u32[]{:S(2)}, u32[]{:S(2)}) %collective-permute-start.15) | collective-permute-done | bytes 262176 | tf_op jit(solution)/shard_map/ppermute | solution.py:280
  69.7 7.5 %shard_map.29 = f32[256,256]{1,0:T(8,128)S(1)} custom-call(f32[256,256]{1,0:T(8,128)S(1)} %convolution_add_fusion.3.gram_ref, f32[256,256]{1,0:T(8,128)S(1)} %collective-permute-done.15.far_ref), custom_call_target="tpu_custom_call" | custom-call | flops 1000 | bytes 1000 | tf_op jit(solution)/shard_map/pallas_call | solution.py:165
  (52 shorter events, 12.7 us)
Async XLA Ops:
  0.0 5.3 %copy-start = (f32[1024,256]{1,0:T(8,128)S(1)}, f32[1024,256]{1,0:T(8,128)}, u32[]{:S(2)}) copy-start(f32[1024,256]{1,0:T(8,128)} %sketch_ref.1) | copy-start | bytes 3145732
  2.2 7.6 %collective-permute-start = (f32[256,256]{1,0:T(8,128)S(1)}, f32[256,256]{1,0:T(8,128)S(1)}, u32[]{:S(2)}, u32[]{:S(2)}) collective-permute-start(f32[256,256]{1,0:T(8,128)S(1)} %shard_map.28), channel_id=1, source_target_pairs={{0,1},{1,0},{2,3},{3,2},{4,5},{5,4},{6,7},{7,6},{8,10},{9,11},{10,... | collective-permute-start | bytes 786440 | tf_op jit(solution)/shard_map/ppermute | solution.py:215
  7.9 14.3 %collective-permute-start.3 = (f32[512,256]{1,0:T(8,128)S(1)}, f32[512,256]{1,0:T(8,128)S(1)}, u32[]{:S(2)}, u32[]{:S(2)}) collective-permute-start(f32[512,256]{1,0:T(8,128)S(1)} %fusion.6), channel_id=1, source_target_pairs={{0,1},{1,0},{2,3},{3,2},{4,5},{5,4},{6,7},{7,6},{8,10},{9,11},{10,... | collective-permute-start | bytes 1572872 | tf_op jit(solution)/shard_map/ppermute | solution.py:215
  9.9 6.5 %collective-permute-start.1 = (f32[128,256]{1,0:T(8,128)S(1)}, f32[128,256]{1,0:T(8,128)S(1)}, u32[]{:S(2)}, u32[]{:S(2)}) collective-permute-start(f32[128,256]{1,0:T(8,128)S(1)} %constant_dynamic-slice_fusion.2), channel_id=1, source_target_pairs={{0,2},{1,3},{2,0},{3,1},{4,6},{5,7},{6,4},{7,5},{8,9},{9,8},{10,11... | collective-permute-start | bytes 393224 | tf_op jit(solution)/shard_map/ppermute | solution.py:199
  13.8 11.6 %collective-permute-start.4 = (f32[256,256]{1,0:T(8,128)S(1)}, f32[256,256]{1,0:T(8,128)S(1)}, u32[]{:S(2)}, u32[]{:S(2)}) collective-permute-start(f32[256,256]{1,0:T(8,128)S(1)} %fusion.21), channel_id=1, source_target_pairs={{0,1},{1,0},{2,3},{3,2},{4,5},{5,4},{6,7},{7,6},{8,10},{9,11},{10,... | collective-permute-start | bytes 786440 | tf_op jit(solution)/shard_map/ppermute | solution.py:215
  16.4 9.9 %collective-permute-start.2 = (f32[128,256]{1,0:T(8,128)S(1)}, f32[128,256]{1,0:T(8,128)S(1)}, u32[]{:S(2)}, u32[]{:S(2)}) collective-permute-start(f32[128,256]{1,0:T(8,128)S(1)} %dynamic-slice_add_fusion.2), channel_id=1, source_target_pairs={{0,4},{1,5},{2,6},{3,7},{4,0},{5,1},{6,2},{7,3},{8,12},{9,13},{10,... | collective-permute-start | bytes 393224 | tf_op jit(solution)/shard_map/ppermute | solution.py:199
  22.2 6.4 %collective-permute-start.7 = (f32[256,256]{1,0:T(8,128)S(1)}, f32[256,256]{1,0:T(8,128)S(1)}, u32[]{:S(2)}, u32[]{:S(2)}) collective-permute-start(f32[256,256]{1,0:T(8,128)S(1)} %constant_dynamic-slice_fusion.1), channel_id=1, source_target_pairs={{0,2},{1,3},{2,0},{3,1},{4,6},{5,7},{6,4},{7,5},{8,9},{9,8},{10,11... | collective-permute-start | bytes 786440 | tf_op jit(solution)/shard_map/ppermute | solution.py:199
  25.5 8.3 %collective-permute-start.6 = (f32[128,256]{1,0:T(8,128)S(1)}, f32[128,256]{1,0:T(8,128)S(1)}, u32[]{:S(2)}, u32[]{:S(2)}) collective-permute-start(f32[128,256]{1,0:T(8,128)S(1)} %constant_dynamic-slice_fusion), channel_id=1, source_target_pairs={{0,2},{1,3},{2,0},{3,1},{4,6},{5,7},{6,4},{7,5},{8,9},{9,8},{10,11... | collective-permute-start | bytes 393224 | tf_op jit(solution)/shard_map/ppermute | solution.py:199
  26.3 12.2 %collective-permute-start.5 = (f32[128,256]{1,0:T(8,128)S(1)}, f32[128,256]{1,0:T(8,128)S(1)}, u32[]{:S(2)}, u32[]{:S(2)}) collective-permute-start(f32[128,256]{1,0:T(8,128)S(1)} %add.140), channel_id=1, source_target_pairs={{0,2},{1,3},{2,0},{3,1},{4,6},{5,7},{6,4},{7,5},{8,9},{9,8},{10,11... | collective-permute-start | bytes 393224 | tf_op jit(solution)/shard_map/ppermute | solution.py:199
  28.7 14.5 %collective-permute-start.9 = (f32[256,256]{1,0:T(8,128)S(1)}, f32[256,256]{1,0:T(8,128)S(1)}, u32[]{:S(2)}, u32[]{:S(2)}) collective-permute-start(f32[256,256]{1,0:T(8,128)S(1)} %dynamic-slice_add_fusion), channel_id=1, source_target_pairs={{0,4},{1,5},{2,6},{3,7},{4,0},{5,1},{6,2},{7,3},{8,12},{9,13},{10,... | collective-permute-start | bytes 786440 | tf_op jit(solution)/shard_map/ppermute | solution.py:199
  38.6 7.6 %collective-permute-start.8 = (f32[256,256]{1,0:T(8,128)S(1)}, f32[256,256]{1,0:T(8,128)S(1)}, u32[]{:S(2)}, u32[]{:S(2)}) collective-permute-start(f32[256,256]{1,0:T(8,128)S(1)} %maximum_select_fusion.1), channel_id=1, source_target_pairs={{0,1},{1,0},{2,3},{3,2},{4,5},{5,4},{6,7},{7,6},{8,10},{9,11},{10,... | collective-permute-start | bytes 786440 | tf_op jit(solution)/shard_map/ppermute | solution.py:199
  41.4 11.8 %collective-permute-start.10 = (f32[128,256]{1,0:T(8,128)S(1)}, f32[128,256]{1,0:T(8,128)S(1)}, u32[]{:S(2)}, u32[]{:S(2)}) collective-permute-start(f32[128,256]{1,0:T(8,128)S(1)} %dynamic-slice_add_fusion.1), channel_id=1, source_target_pairs={{0,4},{1,5},{2,6},{3,7},{4,0},{5,1},{6,2},{7,3},{8,12},{9,13},{10,... | collective-permute-start | bytes 393224 | tf_op jit(solution)/shard_map/ppermute | solution.py:199
  43.3 21.1 %slice-start = ((s8[8388608]{0:T(1024)(128)(4,1)}), s8[4194304]{0:T(1024)(128)(4,1)S(1)}, s32[]{:S(2)}) async-start(s8[8388608]{0:T(1024)(128)(4,1)} %bitcast.24), calls=%async_computation | async-start | bytes 8388608
  43.3 9.9 %collective-permute-start.11 = (f32[256,256]{1,0:T(8,128)S(1)}, f32[256,256]{1,0:T(8,128)S(1)}, u32[]{:S(2)}, u32[]{:S(2)}) collective-permute-start(f32[256,256]{1,0:T(8,128)S(1)} %add.144), channel_id=1, source_target_pairs={{0,2},{1,3},{2,0},{3,1},{4,6},{5,7},{6,4},{7,5},{8,9},{9,8},{10,11... | collective-permute-start | bytes 786440 | tf_op jit(solution)/shard_map/ppermute | solution.py:199
  53.3 6.5 %collective-permute-start.12 = (f32[128,256]{1,0:T(8,128)S(1)}, f32[128,256]{1,0:T(8,128)S(1)}, u32[]{:S(2)}, u32[]{:S(2)}) collective-permute-start(f32[128,256]{1,0:T(8,128)S(1)} %add.145), channel_id=1, source_target_pairs={{0,2},{1,3},{2,0},{3,1},{4,6},{5,7},{6,4},{7,5},{8,9},{9,8},{10,11... | collective-permute-start | bytes 393224 | tf_op jit(solution)/shard_map/ppermute | solution.py:199
  53.4 10.3 %collective-permute-start.13 = (f32[512,256]{1,0:T(8,128)S(1)}, f32[512,256]{1,0:T(8,128)S(1)}, u32[]{:S(2)}, u32[]{:S(2)}) collective-permute-start(f32[512,256]{1,0:T(8,128)S(1)} %maximum_select_fusion), channel_id=1, source_target_pairs={{0,1},{1,0},{2,3},{3,2},{4,5},{5,4},{6,7},{7,6},{8,10},{9,11},{10,... | collective-permute-start | bytes 1572872 | tf_op jit(solution)/shard_map/ppermute | solution.py:199
  56.3 8.0 %slice-start.1 = ((s8[8388608]{0:T(1024)(128)(4,1)}), s8[4194304]{0:T(1024)(128)(4,1)S(1)}, s32[]{:S(2)}) async-start(s8[8388608]{0:T(1024)(128)(4,1)} %bitcast.24), calls=%async_computation.1 | async-start | bytes 8388608
  59.8 7.0 %collective-permute-start.14 = (f32[256,256]{1,0:T(8,128)S(1)}, f32[256,256]{1,0:T(8,128)S(1)}, u32[]{:S(2)}, u32[]{:S(2)}) collective-permute-start(f32[256,256]{1,0:T(8,128)S(1)} %maximum_select_fusion.2), channel_id=1, source_target_pairs={{0,1},{1,0},{2,3},{3,2},{4,5},{5,4},{6,7},{7,6},{8,10},{9,11},{10,... | collective-permute-start | bytes 786440 | tf_op jit(solution)/shard_map/ppermute | solution.py:199
  67.9 1.6 %collective-permute-start.15 = (f32[256,256]{1,0:T(8,128)S(1)}, f32[256,256]{1,0:T(8,128)S(1)}, u32[]{:S(2)}, u32[]{:S(2)}) collective-permute-start(f32[256,256]{1,0:T(8,128)S(1)} %convolution_add_fusion.3.gram_ref), channel_id=1, source_target_pairs={{0,8},{8,0},{1,9},{9,1},{2,10},{10,2},{3,11},{11,3},{4,12},{12,4},... | collective-permute-start | bytes 786440 | tf_op jit(solution)/shard_map/ppermute | solution.py:280
  69.5 7.6 %collective-permute-start.16 = (f32[256,1024]{1,0:T(8,128)S(1)}, f32[256,1024]{1,0:T(8,128)S(1)}, u32[]{:S(2)}, u32[]{:S(2)}) collective-permute-start(f32[256,1024]{1,0:T(8,128)S(1)} %convolution_add_fusion), channel_id=1, source_target_pairs={{0,8},{8,0},{1,9},{9,1},{2,10},{10,2},{3,11},{11,3},{4,12},{12,4},... | collective-permute-start | bytes 3145736 | tf_op jit(solution)/shard_map/ppermute | solution.py:283

commit v10 on v9

--- a/solution.py
+++ b/solution.py
@@ -11,8 +11,8 @@
 STEP = 256
 SIZES = (128, 256, 128)
 CROSSED = (True, True, True)
-STEPS = [("s", 0, True), ("m", 1, True), ("m", 0, False), ("i", 0), ("m", 2, True), ("l", 0), ("m", 1, False), ("i", 1)]
-STEPS += [("m", 2, False), ("i", 2), ("b", 0), ("l", 1), ("l", 2), ("o", 0), ("b", 1), ("w", 0), ("g", 0), ("o", 1), ("b", 2), ("f", 0), ("o", 2)]
+STEPS = [("s", 0, True), ("m", 1, True), ("m", 0, False), ("i", 0), ("m", 2, True), ("m", 1, False), ("l", 0), ("i", 1)]
+STEPS += [("m", 2, False), ("i", 2), ("b", 0), ("l", 1), ("l", 2), ("b", 1), ("o", 0), ("w", 0), ("g", 0), ("o", 1), ("b", 2), ("f", 0), ("o", 2)]
 STEPS += [("g", 1), ("f", 1), ("g", 2), ("f", 2)]
 BLOCK = 128
 TILE = 8
@@ -228,6 +228,7 @@
         placed(k, theirs, jnp.dot(rows, weights, precision=HIGH, preferred_element_type=jnp.float32))
 
     kept, half, sums = {}, {}, [()]
+    left = [name for name, *_ in STEPS if name in ("g", "f")]
 
     def arrived(k):
         return after([arriving[k]], last[0])[0]
@@ -251,7 +252,9 @@
 
     def gather(rows, image):
         terms = inner_rows(image, image), inner_rows(image, rows)
-        sums[0] = lax.optimization_barrier(tuple(map(jnp.add, sums[0], terms)) if sums[0] else terms)
+        terms = tuple(map(jnp.add, sums[0], terms)) if sums[0] else terms
+        left.pop()
+        sums[0] = lax.optimization_barrier(terms) if left else terms
         last[0] = sums[0][0]
 
     def gather_own(k):

time: 78.8 us -> 75 us (0.952)
  waiting for transfers between devices: 25.1 us -> 19.3 us
  starting transfers between devices: 19 us -> 21 us
    ppermute x12, waiting for transfers between devices: 23.6 us -> 18.5 us  [send(): return lax.ppermute(x, ('rows', 'cols'), targets)]
    ppermute x12, starting transfers between devices: 14.1 us -> 16.1 us  [send(): return lax.ppermute(x, ('rows', 'cols'), targets)]
  transfers between devices with their start and end apart: 17 -> 17, of which waited for: 9 -> 7; matrix products, arithmetic and copies ran while one was open for 28% -> 30% of each run, Pallas kernels for 10% -> 10%
where the time goes in v10:
time: 75 us; the launch traced here: 74.6 us
  matrix products  23.8 us (32%)
  starting transfers between devices  21 us (28%)
  waiting for transfers between devices  19.3 us (26%)
  Pallas kernels  9.71 us (13%)
    ppermute x12, waiting for transfers between devices, send(): return lax.ppermute(x, ('rows', 'cols'), targets)  18.5 us
    ppermute x12, starting transfers between devices, send(): return lax.ppermute(x, ('rows', 'cols'), targets)  16.1 us
    dot_general x12, matrix products, inner_rows(): lax.dot_general(left, right, (((0,), (0,)), ((), ())), precision=HIGH, pr...  11.9 us
    dot_general x5, matrix products, matmul(): jnp.dot(rows, weights, precision=HIGH, preferred_element_type=jnp.float32)  10.7 us
    pallas_call x1, Pallas kernels, inverse_cholesky(): pl.pallas_call(factor_kernel, out_shape=jax.ShapeDtypeStruct(gram.shape,...  7.49 us
    ppermute x3, starting transfers between devices, placed(): arriving[k] = lax.ppermute(image, ('rows', 'cols'), outer[k])  4.71 us
    pallas_call x1, Pallas kernels, sketched(): pl.pallas_call(sketch_kernel, out_shape=[jax.ShapeDtypeStruct((length, ra...  2.22 us
  transfers between devices with their start and end apart: 17, of which 7 were waited for; matrix products, arithmetic and copies ran while one was open for 30% of the time, Pallas kernels for 10%

profile of v10, /device:TPU:0, one launch (start us, length us, event | category | flops | bytes accessed | tf_op | source)
XLA Modules:
  0.0 74.6 jit_solution(11944847072979097858)
XLA Ops:
  0.0 2.2 %shard_map.28 = f32[256,256]{1,0:T(8,128)S(1)} custom-call(s32[1]{0:T(128)} %bitcast.starts_ref, f32[2048,1024]{1,0:T(8,128)} %texture_ref.1, f32[1024,256]{1,0:T(8,128)} %sketch_ref.1), custom_call_target="tpu_custom_call" | custom-call | flops 402653184 | bytes 2097152 | tf_op jit(solution)/shard_map/pallas_call | solution.py:57
  2.2 3.0 %collective-permute-start = (f32[256,256]{1,0:T(8,128)S(1)}, f32[256,256]{1,0:T(8,128)S(1)}, u32[]{:S(2)}, u32[]{:S(2)}) collective-permute-start(f32[256,256]{1,0:T(8,128)S(1)} %shard_map.28), channel_id=1, source_target_pairs={{0,1},{1,0},{2,3},{3,2},{4,5},{5,4},{6,7},{7,6},{8,10},{9,11},{10,... | collective-permute-start | bytes 786440 | tf_op jit(solution)/shard_map/ppermute | solution.py:215
  5.3 2.6 %fusion.6 = f32[512,256]{1,0:T(8,128)S(1)} fusion(f32[1024,256]{1,0:T(8,128)S(1)} %copy-done, f32[2048,1024]{1,0:T(8,128)} %texture_ref.1, s32[]{:T(128)S(6)} %select_n.75), kind=kOutput, calls=%fused_computation.6 | convolution fusion | flops 805306368 | bytes 3670020 | tf_op jit(solution)/shard_map/dot_general | solution.py:228
  8.0 1.8 %fusion.25 = f32[256,256]{1,0:T(8,128)S(1)} fusion(f32[1024,256]{1,0:T(8,128)S(1)} %copy-done, f32[2048,1024]{1,0:T(8,128)} %texture_ref.1, s32[]{:T(128)S(6)} %select_n.74), kind=kOutput, calls=%fused_computation.29 | convolution fusion | flops 402653184 | bytes 2359300 | tf_op jit(solution)/shard_map/dot_general | solution.py:228
  9.9 2.1 %collective-permute-start.1 = (f32[128,256]{1,0:T(8,128)S(1)}, f32[128,256]{1,0:T(8,128)S(1)}, u32[]{:S(2)}, u32[]{:S(2)}) collective-permute-start(f32[128,256]{1,0:T(8,128)S(1)} %constant_dynamic-slice_fusion.2), channel_id=1, source_target_pairs={{0,2},{1,3},{2,0},{3,1},{4,6},{5,7},{6,4},{7,5},{8,9},{9,8},{10,11... | collective-permute-start | bytes 393224 | tf_op jit(solution)/shard_map/ppermute | solution.py:199
  12.0 1.8 %fusion.21 = f32[256,256]{1,0:T(8,128)S(1)} fusion(f32[1024,256]{1,0:T(8,128)S(1)} %copy-done, f32[2048,1024]{1,0:T(8,128)} %texture_ref.1, s32[]{:T(128)S(6)} %select_n.79), kind=kOutput, calls=%fused_computation.25 | convolution fusion | flops 402653184 | bytes 2359300 | tf_op jit(solution)/shard_map/dot_general | solution.py:228
  13.8 1.6 %collective-permute-start.4 = (f32[256,256]{1,0:T(8,128)S(1)}, f32[256,256]{1,0:T(8,128)S(1)}, u32[]{:S(2)}, u32[]{:S(2)}) collective-permute-start(f32[256,256]{1,0:T(8,128)S(1)} %fusion.21), channel_id=1, source_target_pairs={{0,1},{1,0},{2,3},{3,2},{4,5},{5,4},{6,7},{7,6},{8,10},{9,11},{10,... | collective-permute-start | bytes 786440 | tf_op jit(solution)/shard_map/ppermute | solution.py:215
  15.4 2.6 %fusion.2 = f32[512,256]{1,0:T(8,128)S(1)} fusion(f32[1024,256]{1,0:T(8,128)S(1)} %copy-done, f32[2048,1024]{1,0:T(8,128)} %texture_ref.1, s32[]{:T(128)S(6)} %select_n.78), kind=kOutput, calls=%fused_computation.2 | convolution fusion | flops 805306368 | bytes 3670020 | tf_op jit(solution)/shard_map/dot_general | solution.py:228
  18.1 2.7 %collective-permute-start.2 = (f32[128,256]{1,0:T(8,128)S(1)}, f32[128,256]{1,0:T(8,128)S(1)}, u32[]{:S(2)}, u32[]{:S(2)}) collective-permute-start(f32[128,256]{1,0:T(8,128)S(1)} %dynamic-slice_add_fusion.2), channel_id=1, source_target_pairs={{0,4},{1,5},{2,6},{3,7},{4,0},{5,1},{6,2},{7,3},{8,12},{9,13},{10,... | collective-permute-start | bytes 393224 | tf_op jit(solution)/shard_map/ppermute | solution.py:199
  21.3 1.8 %fusion.18 = f32[256,256]{1,0:T(8,128)S(1)} fusion(f32[1024,256]{1,0:T(8,128)S(1)} %copy-done, f32[2048,1024]{1,0:T(8,128)} %texture_ref.1, s32[]{:T(128)S(6)} %select_n.80), kind=kOutput, calls=%fused_computation.22 | convolution fusion | flops 402653184 | bytes 2359300 | tf_op jit(solution)/shard_map/dot_general | solution.py:228
  23.2 1.6 %collective-permute-start.8 = (f32[128,256]{1,0:T(8,128)S(1)}, f32[128,256]{1,0:T(8,128)S(1)}, u32[]{:S(2)}, u32[]{:S(2)}) collective-permute-start(f32[128,256]{1,0:T(8,128)S(1)} %constant_dynamic-slice_fusion), channel_id=1, source_target_pairs={{0,2},{1,3},{2,0},{3,1},{4,6},{5,7},{6,4},{7,5},{8,9},{9,8},{10,11... | collective-permute-start | bytes 393224 | tf_op jit(solution)/shard_map/ppermute | solution.py:199
  24.9 1.4 %collective-permute-done.2 = f32[128,256]{1,0:T(8,128)S(1)} collective-permute-done((f32[128,256]{1,0:T(8,128)S(1)}, f32[128,256]{1,0:T(8,128)S(1)}, u32[]{:S(2)}, u32[]{:S(2)}) %collective-permute-start.2) | collective-permute-done | bytes 131104 | tf_op jit(solution)/shard_map/ppermute | solution.py:199
  26.3 2.7 %collective-permute-done.6 = f32[256,256]{1,0:T(8,128)S(1)} collective-permute-done((f32[256,256]{1,0:T(8,128)S(1)}, f32[256,256]{1,0:T(8,128)S(1)}, u32[]{:S(2)}, u32[]{:S(2)}) %collective-permute-start.6) | collective-permute-done | bytes 262176 | tf_op jit(solution)/shard_map/ppermute | solution.py:199
  29.2 1.3 %collective-permute-start.5 = (f32[128,256]{1,0:T(8,128)S(1)}, f32[128,256]{1,0:T(8,128)S(1)}, u32[]{:S(2)}, u32[]{:S(2)}) collective-permute-start(f32[128,256]{1,0:T(8,128)S(1)} %add.140), channel_id=1, source_target_pairs={{0,2},{1,3},{2,0},{3,1},{4,6},{5,7},{6,4},{7,5},{8,9},{9,8},{10,11... | collective-permute-start | bytes 393224 | tf_op jit(solution)/shard_map/ppermute | solution.py:199
  31.4 8.2 %collective-permute-done.7 = f32[256,256]{1,0:T(8,128)S(1)} collective-permute-done((f32[256,256]{1,0:T(8,128)S(1)}, f32[256,256]{1,0:T(8,128)S(1)}, u32[]{:S(2)}, u32[]{:S(2)}) %collective-permute-start.7) | collective-permute-done | bytes 262176 | tf_op jit(solution)/shard_map/ppermute | solution.py:199
  40.3 3.7 %collective-permute-start.11 = (f32[256,256]{1,0:T(8,128)S(1)}, f32[256,256]{1,0:T(8,128)S(1)}, u32[]{:S(2)}, u32[]{:S(2)}) collective-permute-start(f32[256,256]{1,0:T(8,128)S(1)} %add.144), channel_id=1, source_target_pairs={{0,2},{1,3},{2,0},{3,1},{4,6},{5,7},{6,4},{7,5},{8,9},{9,8},{10,11... | collective-permute-start | bytes 786440 | tf_op jit(solution)/shard_map/ppermute | solution.py:199
  44.0 3.3 %collective-permute-done.9 = f32[256,256]{1,0:T(8,128)S(1)} collective-permute-done((f32[256,256]{1,0:T(8,128)S(1)}, f32[256,256]{1,0:T(8,128)S(1)}, u32[]{:S(2)}, u32[]{:S(2)}) %collective-permute-start.9) | collective-permute-done | bytes 262176 | tf_op jit(solution)/shard_map/ppermute | solution.py:199
  47.3 1.9 %fusion.23 = f32[256,1024]{1,0:T(8,128)S(1)} fusion(f32[256,256]{1,0:T(8,128)S(1)} %maximum_select_fusion.1, f32[2048,1024]{1,0:T(8,128)} %texture_ref.1, s32[]{:T(128)S(6)} %select_n.74), kind=kOutput, calls=%fused_computation.27 | convolution fusion | flops 402653184 | bytes 2359300 | tf_op jit(solution)/shard_map/dot_general | solution.py:75
  49.6 1.2 %collective-permute-start.12 = (f32[128,256]{1,0:T(8,128)S(1)}, f32[128,256]{1,0:T(8,128)S(1)}, u32[]{:S(2)}, u32[]{:S(2)}) collective-permute-start(f32[128,256]{1,0:T(8,128)S(1)} %add.145), channel_id=1, source_target_pairs={{0,2},{1,3},{2,0},{3,1},{4,6},{5,7},{6,4},{7,5},{8,9},{9,8},{10,11... | collective-permute-start | bytes 393224 | tf_op jit(solution)/shard_map/ppermute | solution.py:199
  51.9 1.9 %convolution_add_fusion.2 = f32[256,1024]{1,0:T(8,128)S(1)} fusion(f32[256,1024]{1,0:T(8,128)S(1)} %fusion.23, f32[256,256]{1,0:T(8,128)S(1)} %collective-permute-done.9, f32[2048,1024]{1,0:T(8,128)} %texture_ref.1, s32[]{:T(128)S(6)} %select_n.86), kind=kOutput, calls=%fused_computation.12 | convolution fusion | flops 402915328 | bytes 3407876 | tf_op jit(solution)/shard_map/dot_general | solution.py:75
  54.2 1.9 %collective-permute-done.12 = f32[128,256]{1,0:T(8,128)S(1)} collective-permute-done((f32[128,256]{1,0:T(8,128)S(1)}, f32[128,256]{1,0:T(8,128)S(1)}, u32[]{:S(2)}, u32[]{:S(2)}) %collective-permute-start.12) | collective-permute-done | bytes 131104 | tf_op jit(solution)/shard_map/ppermute | solution.py:199
  56.1 1.2 %collective-permute-start.14 = (f32[256,256]{1,0:T(8,128)S(1)}, f32[256,256]{1,0:T(8,128)S(1)}, u32[]{:S(2)}, u32[]{:S(2)}) collective-permute-start(f32[256,256]{1,0:T(8,128)S(1)} %maximum_select_fusion.2), channel_id=1, source_target_pairs={{0,1},{1,0},{2,3},{3,2},{4,5},{5,4},{6,7},{7,6},{8,10},{9,11},{10,... | collective-permute-start | bytes 786440 | tf_op jit(solution)/shard_map/ppermute | solution.py:199
  57.9 2.7 %fusion.11 = f32[256,1024]{1,0:T(8,128)S(1)} fusion(f32[256,1024]{1,0:T(8,128)S(1)} %convolution_add_fusion.2, f32[512,256]{1,0:T(8,128)S(1)} %maximum_select_fusion, f32[2048,1024]{1,0:T(8,128)} %texture_ref.1, s32[]{:T(128)S(6)} %select_n.78), kind=kOutput, calls=%fused_computation.9 | convolution fusion | flops 805568512 | bytes 4718596 | tf_op jit(solution)/shard_map/dot_general | solution.py:75
  65.9 7.5 %shard_map.29 = f32[256,256]{1,0:T(8,128)S(1)} custom-call(f32[256,256]{1,0:T(8,128)S(1)} %convolution_add_fusion.3.gram_ref, f32[256,256]{1,0:T(8,128)S(1)} %collective-permute-done.15.far_ref), custom_call_target="tpu_custom_call" | custom-call | flops 1000 | bytes 1000 | tf_op jit(solution)/shard_map/pallas_call | solution.py:165
  (52 shorter events, 11.4 us)
Async XLA Ops:
  0.0 5.3 %copy-start = (f32[1024,256]{1,0:T(8,128)S(1)}, f32[1024,256]{1,0:T(8,128)}, u32[]{:S(2)}) copy-start(f32[1024,256]{1,0:T(8,128)} %sketch_ref.1) | copy-start | bytes 3145732
  2.2 7.6 %collective-permute-start = (f32[256,256]{1,0:T(8,128)S(1)}, f32[256,256]{1,0:T(8,128)S(1)}, u32[]{:S(2)}, u32[]{:S(2)}) collective-permute-start(f32[256,256]{1,0:T(8,128)S(1)} %shard_map.28), channel_id=1, source_target_pairs={{0,1},{1,0},{2,3},{3,2},{4,5},{5,4},{6,7},{7,6},{8,10},{9,11},{10,... | collective-permute-start | bytes 786440 | tf_op jit(solution)/shard_map/ppermute | solution.py:215
  7.9 12.8 %collective-permute-start.3 = (f32[512,256]{1,0:T(8,128)S(1)}, f32[512,256]{1,0:T(8,128)S(1)}, u32[]{:S(2)}, u32[]{:S(2)}) collective-permute-start(f32[512,256]{1,0:T(8,128)S(1)} %fusion.6), channel_id=1, source_target_pairs={{0,1},{1,0},{2,3},{3,2},{4,5},{5,4},{6,7},{7,6},{8,10},{9,11},{10,... | collective-permute-start | bytes 1572872 | tf_op jit(solution)/shard_map/ppermute | solution.py:215
  9.9 8.1 %collective-permute-start.1 = (f32[128,256]{1,0:T(8,128)S(1)}, f32[128,256]{1,0:T(8,128)S(1)}, u32[]{:S(2)}, u32[]{:S(2)}) collective-permute-start(f32[128,256]{1,0:T(8,128)S(1)} %constant_dynamic-slice_fusion.2), channel_id=1, source_target_pairs={{0,2},{1,3},{2,0},{3,1},{4,6},{5,7},{6,4},{7,5},{8,9},{9,8},{10,11... | collective-permute-start | bytes 393224 | tf_op jit(solution)/shard_map/ppermute | solution.py:199
  13.8 9.3 %collective-permute-start.4 = (f32[256,256]{1,0:T(8,128)S(1)}, f32[256,256]{1,0:T(8,128)S(1)}, u32[]{:S(2)}, u32[]{:S(2)}) collective-permute-start(f32[256,256]{1,0:T(8,128)S(1)} %fusion.21), channel_id=1, source_target_pairs={{0,1},{1,0},{2,3},{3,2},{4,5},{5,4},{6,7},{7,6},{8,10},{9,11},{10,... | collective-permute-start | bytes 786440 | tf_op jit(solution)/shard_map/ppermute | solution.py:215
  18.1 8.3 %collective-permute-start.2 = (f32[128,256]{1,0:T(8,128)S(1)}, f32[128,256]{1,0:T(8,128)S(1)}, u32[]{:S(2)}, u32[]{:S(2)}) collective-permute-start(f32[128,256]{1,0:T(8,128)S(1)} %dynamic-slice_add_fusion.2), channel_id=1, source_target_pairs={{0,4},{1,5},{2,6},{3,7},{4,0},{5,1},{6,2},{7,3},{8,12},{9,13},{10,... | collective-permute-start | bytes 393224 | tf_op jit(solution)/shard_map/ppermute | solution.py:199
  20.8 8.2 %collective-permute-start.6 = (f32[256,256]{1,0:T(8,128)S(1)}, f32[256,256]{1,0:T(8,128)S(1)}, u32[]{:S(2)}, u32[]{:S(2)}) collective-permute-start(f32[256,256]{1,0:T(8,128)S(1)} %constant_dynamic-slice_fusion.1), channel_id=1, source_target_pairs={{0,2},{1,3},{2,0},{3,1},{4,6},{5,7},{6,4},{7,5},{8,9},{9,8},{10,11... | collective-permute-start | bytes 786440 | tf_op jit(solution)/shard_map/ppermute | solution.py:199
  23.2 8.2 %collective-permute-start.8 = (f32[128,256]{1,0:T(8,128)S(1)}, f32[128,256]{1,0:T(8,128)S(1)}, u32[]{:S(2)}, u32[]{:S(2)}) collective-permute-start(f32[128,256]{1,0:T(8,128)S(1)} %constant_dynamic-slice_fusion), channel_id=1, source_target_pairs={{0,2},{1,3},{2,0},{3,1},{4,6},{5,7},{6,4},{7,5},{8,9},{9,8},{10,11... | collective-permute-start | bytes 393224 | tf_op jit(solution)/shard_map/ppermute | solution.py:199
  29.1 10.6 %collective-permute-start.7 = (f32[256,256]{1,0:T(8,128)S(1)}, f32[256,256]{1,0:T(8,128)S(1)}, u32[]{:S(2)}, u32[]{:S(2)}) collective-permute-start(f32[256,256]{1,0:T(8,128)S(1)} %dynamic-slice_add_fusion), channel_id=1, source_target_pairs={{0,4},{1,5},{2,6},{3,7},{4,0},{5,1},{6,2},{7,3},{8,12},{9,13},{10,... | collective-permute-start | bytes 786440 | tf_op jit(solution)/shard_map/ppermute | solution.py:199
  29.2 10.5 %collective-permute-start.5 = (f32[128,256]{1,0:T(8,128)S(1)}, f32[128,256]{1,0:T(8,128)S(1)}, u32[]{:S(2)}, u32[]{:S(2)}) collective-permute-start(f32[128,256]{1,0:T(8,128)S(1)} %add.140), channel_id=1, source_target_pairs={{0,2},{1,3},{2,0},{3,1},{4,6},{5,7},{6,4},{7,5},{8,9},{9,8},{10,11... | collective-permute-start | bytes 393224 | tf_op jit(solution)/shard_map/ppermute | solution.py:199
  39.8 7.5 %collective-permute-start.9 = (f32[256,256]{1,0:T(8,128)S(1)}, f32[256,256]{1,0:T(8,128)S(1)}, u32[]{:S(2)}, u32[]{:S(2)}) collective-permute-start(f32[256,256]{1,0:T(8,128)S(1)} %maximum_select_fusion.1), channel_id=1, source_target_pairs={{0,1},{1,0},{2,3},{3,2},{4,5},{5,4},{6,7},{7,6},{8,10},{9,11},{10,... | collective-permute-start | bytes 786440 | tf_op jit(solution)/shard_map/ppermute | solution.py:199
  40.3 20.9 %slice-start = ((s8[8388608]{0:T(1024)(128)(4,1)}), s8[4194304]{0:T(1024)(128)(4,1)S(1)}, s32[]{:S(2)}) async-start(s8[8388608]{0:T(1024)(128)(4,1)} %bitcast.24), calls=%async_computation | async-start | bytes 8388608
  40.3 9.3 %collective-permute-start.10 = (f32[128,256]{1,0:T(8,128)S(1)}, f32[128,256]{1,0:T(8,128)S(1)}, u32[]{:S(2)}, u32[]{:S(2)}) collective-permute-start(f32[128,256]{1,0:T(8,128)S(1)} %dynamic-slice_add_fusion.1), channel_id=1, source_target_pairs={{0,4},{1,5},{2,6},{3,7},{4,0},{5,1},{6,2},{7,3},{8,12},{9,13},{10,... | collective-permute-start | bytes 393224 | tf_op jit(solution)/shard_map/ppermute | solution.py:199
  40.3 9.2 %collective-permute-start.11 = (f32[256,256]{1,0:T(8,128)S(1)}, f32[256,256]{1,0:T(8,128)S(1)}, u32[]{:S(2)}, u32[]{:S(2)}) collective-permute-start(f32[256,256]{1,0:T(8,128)S(1)} %add.144), channel_id=1, source_target_pairs={{0,2},{1,3},{2,0},{3,1},{4,6},{5,7},{6,4},{7,5},{8,9},{9,8},{10,11... | collective-permute-start | bytes 786440 | tf_op jit(solution)/shard_map/ppermute | solution.py:199
  49.6 6.5 %collective-permute-start.12 = (f32[128,256]{1,0:T(8,128)S(1)}, f32[128,256]{1,0:T(8,128)S(1)}, u32[]{:S(2)}, u32[]{:S(2)}) collective-permute-start(f32[128,256]{1,0:T(8,128)S(1)} %add.145), channel_id=1, source_target_pairs={{0,2},{1,3},{2,0},{3,1},{4,6},{5,7},{6,4},{7,5},{8,9},{9,8},{10,11... | collective-permute-start | bytes 393224 | tf_op jit(solution)/shard_map/ppermute | solution.py:199
  50.8 9.8 %collective-permute-start.13 = (f32[512,256]{1,0:T(8,128)S(1)}, f32[512,256]{1,0:T(8,128)S(1)}, u32[]{:S(2)}, u32[]{:S(2)}) collective-permute-start(f32[512,256]{1,0:T(8,128)S(1)} %maximum_select_fusion), channel_id=1, source_target_pairs={{0,1},{1,0},{2,3},{3,2},{4,5},{5,4},{6,7},{7,6},{8,10},{9,11},{10,... | collective-permute-start | bytes 1572872 | tf_op jit(solution)/shard_map/ppermute | solution.py:199
  53.8 7.5 %slice-start.1 = ((s8[8388608]{0:T(1024)(128)(4,1)}), s8[4194304]{0:T(1024)(128)(4,1)S(1)}, s32[]{:S(2)}) async-start(s8[8388608]{0:T(1024)(128)(4,1)} %bitcast.24), calls=%async_computation.1 | async-start | bytes 8388608
  56.1 7.6 %collective-permute-start.14 = (f32[256,256]{1,0:T(8,128)S(1)}, f32[256,256]{1,0:T(8,128)S(1)}, u32[]{:S(2)}, u32[]{:S(2)}) collective-permute-start(f32[256,256]{1,0:T(8,128)S(1)} %maximum_select_fusion.2), channel_id=1, source_target_pairs={{0,1},{1,0},{2,3},{3,2},{4,5},{5,4},{6,7},{7,6},{8,10},{9,11},{10,... | collective-permute-start | bytes 786440 | tf_op jit(solution)/shard_map/ppermute | solution.py:199
  64.1 1.6 %collective-permute-start.15 = (f32[256,256]{1,0:T(8,128)S(1)}, f32[256,256]{1,0:T(8,128)S(1)}, u32[]{:S(2)}, u32[]{:S(2)}) collective-permute-start(f32[256,256]{1,0:T(8,128)S(1)} %convolution_add_fusion.3.gram_ref), channel_id=1, source_target_pairs={{0,8},{8,0},{1,9},{9,1},{2,10},{10,2},{3,11},{11,3},{4,12},{12,4},... | collective-permute-start | bytes 786440 | tf_op jit(solution)/shard_map/ppermute | solution.py:283
  65.7 7.6 %collective-permute-start.16 = (f32[256,1024]{1,0:T(8,128)S(1)}, f32[256,1024]{1,0:T(8,128)S(1)}, u32[]{:S(2)}, u32[]{:S(2)}) collective-permute-start(f32[256,1024]{1,0:T(8,128)S(1)} %convolution_add_fusion), channel_id=1, source_target_pairs={{0,8},{8,0},{1,9},{9,1},{2,10},{10,2},{3,11},{11,3},{4,12},{12,4},... | collective-permute-start | bytes 3145736 | tf_op jit(solution)/shard_map/ppermute | solution.py:286

commit v11 on v10

--- a/solution.py
+++ b/solution.py
@@ -139,7 +139,8 @@
 
 def factor_kernel(gram_ref, far_ref, out_ref, work):
     size = gram_ref.shape[0]
-    work[...] = gram_ref[...] + far_ref[...]
+    root = lax.rsqrt(gram_ref[0:1, 0:1] + far_ref[0:1, 0:1])
+    work[...] = (gram_ref[...] + far_ref[...]) * root * root
     for start in range(0, size, BLOCK):
         stop = start + BLOCK
         corner = inverse_factor(work[start:stop, start:stop])
@@ -152,7 +153,7 @@
         )
         lines = small_dot(corner, work[start:stop, :], ((1,), (0,)))
         lines = jnp.where((lane >= start) & (lane < stop), wide, lines)
-        out_ref[start:stop, :] = jnp.where(lane < stop, lines, 0.0)
+        out_ref[start:stop, :] = jnp.where(lane < stop, lines, 0.0) * root
         if stop < size:
             factor = small_dot(work[stop:, start:stop], corner, ((1,), (1,)))
             lane = lax.broadcasted_iota(jnp.int32, (size - stop, size), 1)

time: 75 us -> 75.1 us (level)
  no operation moved by 1% of the time
where the time goes in v11:
time: 75.1 us; the launch traced here: 74.7 us
  matrix products  23.8 us (32%)
  starting transfers between devices  21 us (28%)
  waiting for transfers between devices  19.3 us (26%)
  Pallas kernels  9.81 us (13%)
    ppermute x12, waiting for transfers between devices, send(): return lax.ppermute(x, ('rows', 'cols'), targets)  18.5 us
    ppermute x12, starting transfers between devices, send(): return lax.ppermute(x, ('rows', 'cols'), targets)  16.1 us
    dot_general x12, matrix products, inner_rows(): lax.dot_general(left, right, (((0,), (0,)), ((), ())), precision=HIGH, pr...  11.9 us
    dot_general x5, matrix products, matmul(): jnp.dot(rows, weights, precision=HIGH, preferred_element_type=jnp.float32)  10.7 us
    pallas_call x1, Pallas kernels, inverse_cholesky(): pl.pallas_call(factor_kernel, out_shape=jax.ShapeDtypeStruct(gram.shape,...  7.58 us
    ppermute x3, starting transfers between devices, placed(): arriving[k] = lax.ppermute(image, ('rows', 'cols'), outer[k])  4.71 us
    pallas_call x1, Pallas kernels, sketched(): pl.pallas_call(sketch_kernel, out_shape=[jax.ShapeDtypeStruct((length, ra...  2.22 us
  transfers between devices with their start and end apart: 17, of which 7 were waited for; matrix products, arithmetic and copies ran while one was open for 30% of the time, Pallas kernels for 10%

profile of v11, /device:TPU:0, one launch (start us, length us, event | category | flops | bytes accessed | tf_op | source)
XLA Modules:
  0.0 74.7 jit_solution(13957391503148120191)
XLA Ops:
  0.0 2.2 %shard_map.28 = f32[256,256]{1,0:T(8,128)S(1)} custom-call(s32[1]{0:T(128)} %bitcast.starts_ref, f32[2048,1024]{1,0:T(8,128)} %texture_ref.1, f32[1024,256]{1,0:T(8,128)} %sketch_ref.1), custom_call_target="tpu_custom_call" | custom-call | flops 402653184 | bytes 2097152 | tf_op jit(solution)/shard_map/pallas_call | solution.py:57
  2.2 3.0 %collective-permute-start = (f32[256,256]{1,0:T(8,128)S(1)}, f32[256,256]{1,0:T(8,128)S(1)}, u32[]{:S(2)}, u32[]{:S(2)}) collective-permute-start(f32[256,256]{1,0:T(8,128)S(1)} %shard_map.28), channel_id=1, source_target_pairs={{0,1},{1,0},{2,3},{3,2},{4,5},{5,4},{6,7},{7,6},{8,10},{9,11},{10,... | collective-permute-start | bytes 786440 | tf_op jit(solution)/shard_map/ppermute | solution.py:216
  5.3 2.6 %fusion.6 = f32[512,256]{1,0:T(8,128)S(1)} fusion(f32[1024,256]{1,0:T(8,128)S(1)} %copy-done, f32[2048,1024]{1,0:T(8,128)} %texture_ref.1, s32[]{:T(128)S(6)} %select_n.75), kind=kOutput, calls=%fused_computation.6 | convolution fusion | flops 805306368 | bytes 3670020 | tf_op jit(solution)/shard_map/dot_general | solution.py:229
  8.0 1.8 %fusion.25 = f32[256,256]{1,0:T(8,128)S(1)} fusion(f32[1024,256]{1,0:T(8,128)S(1)} %copy-done, f32[2048,1024]{1,0:T(8,128)} %texture_ref.1, s32[]{:T(128)S(6)} %select_n.74), kind=kOutput, calls=%fused_computation.29 | convolution fusion | flops 402653184 | bytes 2359300 | tf_op jit(solution)/shard_map/dot_general | solution.py:229
  9.9 2.1 %collective-permute-start.1 = (f32[128,256]{1,0:T(8,128)S(1)}, f32[128,256]{1,0:T(8,128)S(1)}, u32[]{:S(2)}, u32[]{:S(2)}) collective-permute-start(f32[128,256]{1,0:T(8,128)S(1)} %constant_dynamic-slice_fusion.2), channel_id=1, source_target_pairs={{0,2},{1,3},{2,0},{3,1},{4,6},{5,7},{6,4},{7,5},{8,9},{9,8},{10,11... | collective-permute-start | bytes 393224 | tf_op jit(solution)/shard_map/ppermute | solution.py:200
  12.0 1.8 %fusion.21 = f32[256,256]{1,0:T(8,128)S(1)} fusion(f32[1024,256]{1,0:T(8,128)S(1)} %copy-done, f32[2048,1024]{1,0:T(8,128)} %texture_ref.1, s32[]{:T(128)S(6)} %select_n.79), kind=kOutput, calls=%fused_computation.25 | convolution fusion | flops 402653184 | bytes 2359300 | tf_op jit(solution)/shard_map/dot_general | solution.py:229
  13.8 1.6 %collective-permute-start.4 = (f32[256,256]{1,0:T(8,128)S(1)}, f32[256,256]{1,0:T(8,128)S(1)}, u32[]{:S(2)}, u32[]{:S(2)}) collective-permute-start(f32[256,256]{1,0:T(8,128)S(1)} %fusion.21), channel_id=1, source_target_pairs={{0,1},{1,0},{2,3},{3,2},{4,5},{5,4},{6,7},{7,6},{8,10},{9,11},{10,... | collective-permute-start | bytes 786440 | tf_op jit(solution)/shard_map/ppermute | solution.py:216
  15.4 2.6 %fusion.2 = f32[512,256]{1,0:T(8,128)S(1)} fusion(f32[1024,256]{1,0:T(8,128)S(1)} %copy-done, f32[2048,1024]{1,0:T(8,128)} %texture_ref.1, s32[]{:T(128)S(6)} %select_n.78), kind=kOutput, calls=%fused_computation.2 | convolution fusion | flops 805306368 | bytes 3670020 | tf_op jit(solution)/shard_map/dot_general | solution.py:229
  18.1 2.7 %collective-permute-start.2 = (f32[128,256]{1,0:T(8,128)S(1)}, f32[128,256]{1,0:T(8,128)S(1)}, u32[]{:S(2)}, u32[]{:S(2)}) collective-permute-start(f32[128,256]{1,0:T(8,128)S(1)} %dynamic-slice_add_fusion.2), channel_id=1, source_target_pairs={{0,4},{1,5},{2,6},{3,7},{4,0},{5,1},{6,2},{7,3},{8,12},{9,13},{10,... | collective-permute-start | bytes 393224 | tf_op jit(solution)/shard_map/ppermute | solution.py:200
  21.3 1.8 %fusion.18 = f32[256,256]{1,0:T(8,128)S(1)} fusion(f32[1024,256]{1,0:T(8,128)S(1)} %copy-done, f32[2048,1024]{1,0:T(8,128)} %texture_ref.1, s32[]{:T(128)S(6)} %select_n.80), kind=kOutput, calls=%fused_computation.22 | convolution fusion | flops 402653184 | bytes 2359300 | tf_op jit(solution)/shard_map/dot_general | solution.py:229
  23.2 1.6 %collective-permute-start.8 = (f32[128,256]{1,0:T(8,128)S(1)}, f32[128,256]{1,0:T(8,128)S(1)}, u32[]{:S(2)}, u32[]{:S(2)}) collective-permute-start(f32[128,256]{1,0:T(8,128)S(1)} %constant_dynamic-slice_fusion), channel_id=1, source_target_pairs={{0,2},{1,3},{2,0},{3,1},{4,6},{5,7},{6,4},{7,5},{8,9},{9,8},{10,11... | collective-permute-start | bytes 393224 | tf_op jit(solution)/shard_map/ppermute | solution.py:200
  24.9 1.4 %collective-permute-done.2 = f32[128,256]{1,0:T(8,128)S(1)} collective-permute-done((f32[128,256]{1,0:T(8,128)S(1)}, f32[128,256]{1,0:T(8,128)S(1)}, u32[]{:S(2)}, u32[]{:S(2)}) %collective-permute-start.2) | collective-permute-done | bytes 131104 | tf_op jit(solution)/shard_map/ppermute | solution.py:200
  26.3 2.7 %collective-permute-done.6 = f32[256,256]{1,0:T(8,128)S(1)} collective-permute-done((f32[256,256]{1,0:T(8,128)S(1)}, f32[256,256]{1,0:T(8,128)S(1)}, u32[]{:S(2)}, u32[]{:S(2)}) %collective-permute-start.6) | collective-permute-done | bytes 262176 | tf_op jit(solution)/shard_map/ppermute | solution.py:200
  29.2 1.3 %collective-permute-start.5 = (f32[128,256]{1,0:T(8,128)S(1)}, f32[128,256]{1,0:T(8,128)S(1)}, u32[]{:S(2)}, u32[]{:S(2)}) collective-permute-start(f32[128,256]{1,0:T(8,128)S(1)} %add.140), channel_id=1, source_target_pairs={{0,2},{1,3},{2,0},{3,1},{4,6},{5,7},{6,4},{7,5},{8,9},{9,8},{10,11... | collective-permute-start | bytes 393224 | tf_op jit(solution)/shard_map/ppermute | solution.py:200
  31.4 8.2 %collective-permute-done.7 = f32[256,256]{1,0:T(8,128)S(1)} collective-permute-done((f32[256,256]{1,0:T(8,128)S(1)}, f32[256,256]{1,0:T(8,128)S(1)}, u32[]{:S(2)}, u32[]{:S(2)}) %collective-permute-start.7) | collective-permute-done | bytes 262176 | tf_op jit(solution)/shard_map/ppermute | solution.py:200
  40.3 3.7 %collective-permute-start.11 = (f32[256,256]{1,0:T(8,128)S(1)}, f32[256,256]{1,0:T(8,128)S(1)}, u32[]{:S(2)}, u32[]{:S(2)}) collective-permute-start(f32[256,256]{1,0:T(8,128)S(1)} %add.144), channel_id=1, source_target_pairs={{0,2},{1,3},{2,0},{3,1},{4,6},{5,7},{6,4},{7,5},{8,9},{9,8},{10,11... | collective-permute-start | bytes 786440 | tf_op jit(solution)/shard_map/ppermute | solution.py:200
  44.0 3.3 %collective-permute-done.9 = f32[256,256]{1,0:T(8,128)S(1)} collective-permute-done((f32[256,256]{1,0:T(8,128)S(1)}, f32[256,256]{1,0:T(8,128)S(1)}, u32[]{:S(2)}, u32[]{:S(2)}) %collective-permute-start.9) | collective-permute-done | bytes 262176 | tf_op jit(solution)/shard_map/ppermute | solution.py:200
  47.3 1.9 %fusion.23 = f32[256,1024]{1,0:T(8,128)S(1)} fusion(f32[256,256]{1,0:T(8,128)S(1)} %maximum_select_fusion.1, f32[2048,1024]{1,0:T(8,128)} %texture_ref.1, s32[]{:T(128)S(6)} %select_n.74), kind=kOutput, calls=%fused_computation.27 | convolution fusion | flops 402653184 | bytes 2359300 | tf_op jit(solution)/shard_map/dot_general | solution.py:75
  49.6 1.2 %collective-permute-start.12 = (f32[128,256]{1,0:T(8,128)S(1)}, f32[128,256]{1,0:T(8,128)S(1)}, u32[]{:S(2)}, u32[]{:S(2)}) collective-permute-start(f32[128,256]{1,0:T(8,128)S(1)} %add.145), channel_id=1, source_target_pairs={{0,2},{1,3},{2,0},{3,1},{4,6},{5,7},{6,4},{7,5},{8,9},{9,8},{10,11... | collective-permute-start | bytes 393224 | tf_op jit(solution)/shard_map/ppermute | solution.py:200
  51.9 1.9 %convolution_add_fusion.2 = f32[256,1024]{1,0:T(8,128)S(1)} fusion(f32[256,1024]{1,0:T(8,128)S(1)} %fusion.23, f32[256,256]{1,0:T(8,128)S(1)} %collective-permute-done.9, f32[2048,1024]{1,0:T(8,128)} %texture_ref.1, s32[]{:T(128)S(6)} %select_n.86), kind=kOutput, calls=%fused_computation.12 | convolution fusion | flops 402915328 | bytes 3407876 | tf_op jit(solution)/shard_map/dot_general | solution.py:75
  54.2 1.9 %collective-permute-done.12 = f32[128,256]{1,0:T(8,128)S(1)} collective-permute-done((f32[128,256]{1,0:T(8,128)S(1)}, f32[128,256]{1,0:T(8,128)S(1)}, u32[]{:S(2)}, u32[]{:S(2)}) %collective-permute-start.12) | collective-permute-done | bytes 131104 | tf_op jit(solution)/shard_map/ppermute | solution.py:200
  57.9 2.7 %fusion.11 = f32[256,1024]{1,0:T(8,128)S(1)} fusion(f32[256,1024]{1,0:T(8,128)S(1)} %convolution_add_fusion.2, f32[512,256]{1,0:T(8,128)S(1)} %maximum_select_fusion, f32[2048,1024]{1,0:T(8,128)} %texture_ref.1, s32[]{:T(128)S(6)} %select_n.78), kind=kOutput, calls=%fused_computation.9 | convolution fusion | flops 805568512 | bytes 4718596 | tf_op jit(solution)/shard_map/dot_general | solution.py:75
  65.9 7.6 %shard_map.29 = f32[256,256]{1,0:T(8,128)S(1)} custom-call(f32[256,256]{1,0:T(8,128)S(1)} %convolution_add_fusion.3.gram_ref, f32[256,256]{1,0:T(8,128)S(1)} %collective-permute-done.15.far_ref), custom_call_target="tpu_custom_call" | custom-call | flops 1000 | bytes 1000 | tf_op jit(solution)/shard_map/pallas_call | solution.py:166
  73.5 1.2 %fusion.14 = f32[128,1024]{1,0:T(8,128)} fusion(f32[256,1024]{1,0:T(8,128)S(1)} %convolution_add_fusion, f32[256,1024]{1,0:T(8,128)S(1)} %collective-permute-done.16, f32[256,256]{1,0:T(8,128)S(1)} %shard_map.29, s32[]{:T(128)S(6)} %select_n.88), kind=kOutput, calls=%fused_computation.18 | convolution fusion | flops 201588736 | bytes 2752516 | tf_op jit(solution)/shard_map/dot_general | solution.py:290
  (52 shorter events, 11.4 us)
Async XLA Ops:
  0.0 5.3 %copy-start = (f32[1024,256]{1,0:T(8,128)S(1)}, f32[1024,256]{1,0:T(8,128)}, u32[]{:S(2)}) copy-start(f32[1024,256]{1,0:T(8,128)} %sketch_ref.1) | copy-start | bytes 3145732
  2.2 7.6 %collective-permute-start = (f32[256,256]{1,0:T(8,128)S(1)}, f32[256,256]{1,0:T(8,128)S(1)}, u32[]{:S(2)}, u32[]{:S(2)}) collective-permute-start(f32[256,256]{1,0:T(8,128)S(1)} %shard_map.28), channel_id=1, source_target_pairs={{0,1},{1,0},{2,3},{3,2},{4,5},{5,4},{6,7},{7,6},{8,10},{9,11},{10,... | collective-permute-start | bytes 786440 | tf_op jit(solution)/shard_map/ppermute | solution.py:216
  7.9 12.8 %collective-permute-start.3 = (f32[512,256]{1,0:T(8,128)S(1)}, f32[512,256]{1,0:T(8,128)S(1)}, u32[]{:S(2)}, u32[]{:S(2)}) collective-permute-start(f32[512,256]{1,0:T(8,128)S(1)} %fusion.6), channel_id=1, source_target_pairs={{0,1},{1,0},{2,3},{3,2},{4,5},{5,4},{6,7},{7,6},{8,10},{9,11},{10,... | collective-permute-start | bytes 1572872 | tf_op jit(solution)/shard_map/ppermute | solution.py:216
  9.9 8.1 %collective-permute-start.1 = (f32[128,256]{1,0:T(8,128)S(1)}, f32[128,256]{1,0:T(8,128)S(1)}, u32[]{:S(2)}, u32[]{:S(2)}) collective-permute-start(f32[128,256]{1,0:T(8,128)S(1)} %constant_dynamic-slice_fusion.2), channel_id=1, source_target_pairs={{0,2},{1,3},{2,0},{3,1},{4,6},{5,7},{6,4},{7,5},{8,9},{9,8},{10,11... | collective-permute-start | bytes 393224 | tf_op jit(solution)/shard_map/ppermute | solution.py:200
  13.8 9.3 %collective-permute-start.4 = (f32[256,256]{1,0:T(8,128)S(1)}, f32[256,256]{1,0:T(8,128)S(1)}, u32[]{:S(2)}, u32[]{:S(2)}) collective-permute-start(f32[256,256]{1,0:T(8,128)S(1)} %fusion.21), channel_id=1, source_target_pairs={{0,1},{1,0},{2,3},{3,2},{4,5},{5,4},{6,7},{7,6},{8,10},{9,11},{10,... | collective-permute-start | bytes 786440 | tf_op jit(solution)/shard_map/ppermute | solution.py:216
  18.1 8.3 %collective-permute-start.2 = (f32[128,256]{1,0:T(8,128)S(1)}, f32[128,256]{1,0:T(8,128)S(1)}, u32[]{:S(2)}, u32[]{:S(2)}) collective-permute-start(f32[128,256]{1,0:T(8,128)S(1)} %dynamic-slice_add_fusion.2), channel_id=1, source_target_pairs={{0,4},{1,5},{2,6},{3,7},{4,0},{5,1},{6,2},{7,3},{8,12},{9,13},{10,... | collective-permute-start | bytes 393224 | tf_op jit(solution)/shard_map/ppermute | solution.py:200
  20.8 8.2 %collective-permute-start.6 = (f32[256,256]{1,0:T(8,128)S(1)}, f32[256,256]{1,0:T(8,128)S(1)}, u32[]{:S(2)}, u32[]{:S(2)}) collective-permute-start(f32[256,256]{1,0:T(8,128)S(1)} %constant_dynamic-slice_fusion.1), channel_id=1, source_target_pairs={{0,2},{1,3},{2,0},{3,1},{4,6},{5,7},{6,4},{7,5},{8,9},{9,8},{10,11... | collective-permute-start | bytes 786440 | tf_op jit(solution)/shard_map/ppermute | solution.py:200
  23.2 8.2 %collective-permute-start.8 = (f32[128,256]{1,0:T(8,128)S(1)}, f32[128,256]{1,0:T(8,128)S(1)}, u32[]{:S(2)}, u32[]{:S(2)}) collective-permute-start(f32[128,256]{1,0:T(8,128)S(1)} %constant_dynamic-slice_fusion), channel_id=1, source_target_pairs={{0,2},{1,3},{2,0},{3,1},{4,6},{5,7},{6,4},{7,5},{8,9},{9,8},{10,11... | collective-permute-start | bytes 393224 | tf_op jit(solution)/shard_map/ppermute | solution.py:200
  29.1 10.6 %collective-permute-start.7 = (f32[256,256]{1,0:T(8,128)S(1)}, f32[256,256]{1,0:T(8,128)S(1)}, u32[]{:S(2)}, u32[]{:S(2)}) collective-permute-start(f32[256,256]{1,0:T(8,128)S(1)} %dynamic-slice_add_fusion), channel_id=1, source_target_pairs={{0,4},{1,5},{2,6},{3,7},{4,0},{5,1},{6,2},{7,3},{8,12},{9,13},{10,... | collective-permute-start | bytes 786440 | tf_op jit(solution)/shard_map/ppermute | solution.py:200
  29.2 10.5 %collective-permute-start.5 = (f32[128,256]{1,0:T(8,128)S(1)}, f32[128,256]{1,0:T(8,128)S(1)}, u32[]{:S(2)}, u32[]{:S(2)}) collective-permute-start(f32[128,256]{1,0:T(8,128)S(1)} %add.140), channel_id=1, source_target_pairs={{0,2},{1,3},{2,0},{3,1},{4,6},{5,7},{6,4},{7,5},{8,9},{9,8},{10,11... | collective-permute-start | bytes 393224 | tf_op jit(solution)/shard_map/ppermute | solution.py:200
  39.8 7.5 %collective-permute-start.9 = (f32[256,256]{1,0:T(8,128)S(1)}, f32[256,256]{1,0:T(8,128)S(1)}, u32[]{:S(2)}, u32[]{:S(2)}) collective-permute-start(f32[256,256]{1,0:T(8,128)S(1)} %maximum_select_fusion.1), channel_id=1, source_target_pairs={{0,1},{1,0},{2,3},{3,2},{4,5},{5,4},{6,7},{7,6},{8,10},{9,11},{10,... | collective-permute-start | bytes 786440 | tf_op jit(solution)/shard_map/ppermute | solution.py:200
  40.3 20.9 %slice-start = ((s8[8388608]{0:T(1024)(128)(4,1)}), s8[4194304]{0:T(1024)(128)(4,1)S(1)}, s32[]{:S(2)}) async-start(s8[8388608]{0:T(1024)(128)(4,1)} %bitcast.24), calls=%async_computation | async-start | bytes 8388608
  40.3 9.3 %collective-permute-start.10 = (f32[128,256]{1,0:T(8,128)S(1)}, f32[128,256]{1,0:T(8,128)S(1)}, u32[]{:S(2)}, u32[]{:S(2)}) collective-permute-start(f32[128,256]{1,0:T(8,128)S(1)} %dynamic-slice_add_fusion.1), channel_id=1, source_target_pairs={{0,4},{1,5},{2,6},{3,7},{4,0},{5,1},{6,2},{7,3},{8,12},{9,13},{10,... | collective-permute-start | bytes 393224 | tf_op jit(solution)/shard_map/ppermute | solution.py:200
  40.3 9.2 %collective-permute-start.11 = (f32[256,256]{1,0:T(8,128)S(1)}, f32[256,256]{1,0:T(8,128)S(1)}, u32[]{:S(2)}, u32[]{:S(2)}) collective-permute-start(f32[256,256]{1,0:T(8,128)S(1)} %add.144), channel_id=1, source_target_pairs={{0,2},{1,3},{2,0},{3,1},{4,6},{5,7},{6,4},{7,5},{8,9},{9,8},{10,11... | collective-permute-start | bytes 786440 | tf_op jit(solution)/shard_map/ppermute | solution.py:200
  49.6 6.5 %collective-permute-start.12 = (f32[128,256]{1,0:T(8,128)S(1)}, f32[128,256]{1,0:T(8,128)S(1)}, u32[]{:S(2)}, u32[]{:S(2)}) collective-permute-start(f32[128,256]{1,0:T(8,128)S(1)} %add.145), channel_id=1, source_target_pairs={{0,2},{1,3},{2,0},{3,1},{4,6},{5,7},{6,4},{7,5},{8,9},{9,8},{10,11... | collective-permute-start | bytes 393224 | tf_op jit(solution)/shard_map/ppermute | solution.py:200
  50.8 9.8 %collective-permute-start.13 = (f32[512,256]{1,0:T(8,128)S(1)}, f32[512,256]{1,0:T(8,128)S(1)}, u32[]{:S(2)}, u32[]{:S(2)}) collective-permute-start(f32[512,256]{1,0:T(8,128)S(1)} %maximum_select_fusion), channel_id=1, source_target_pairs={{0,1},{1,0},{2,3},{3,2},{4,5},{5,4},{6,7},{7,6},{8,10},{9,11},{10,... | collective-permute-start | bytes 1572872 | tf_op jit(solution)/shard_map/ppermute | solution.py:200
  53.8 7.5 %slice-start.1 = ((s8[8388608]{0:T(1024)(128)(4,1)}), s8[4194304]{0:T(1024)(128)(4,1)S(1)}, s32[]{:S(2)}) async-start(s8[8388608]{0:T(1024)(128)(4,1)} %bitcast.24), calls=%async_computation.1 | async-start | bytes 8388608
  56.1 7.6 %collective-permute-start.14 = (f32[256,256]{1,0:T(8,128)S(1)}, f32[256,256]{1,0:T(8,128)S(1)}, u32[]{:S(2)}, u32[]{:S(2)}) collective-permute-start(f32[256,256]{1,0:T(8,128)S(1)} %maximum_select_fusion.2), channel_id=1, source_target_pairs={{0,1},{1,0},{2,3},{3,2},{4,5},{5,4},{6,7},{7,6},{8,10},{9,11},{10,... | collective-permute-start | bytes 786440 | tf_op jit(solution)/shard_map/ppermute | solution.py:200
  64.1 1.6 %collective-permute-start.15 = (f32[256,256]{1,0:T(8,128)S(1)}, f32[256,256]{1,0:T(8,128)S(1)}, u32[]{:S(2)}, u32[]{:S(2)}) collective-permute-start(f32[256,256]{1,0:T(8,128)S(1)} %convolution_add_fusion.3.gram_ref), channel_id=1, source_target_pairs={{0,8},{8,0},{1,9},{9,1},{2,10},{10,2},{3,11},{11,3},{4,12},{12,4},... | collective-permute-start | bytes 786440 | tf_op jit(solution)/shard_map/ppermute | solution.py:284
  65.7 7.7 %collective-permute-start.16 = (f32[256,1024]{1,0:T(8,128)S(1)}, f32[256,1024]{1,0:T(8,128)S(1)}, u32[]{:S(2)}, u32[]{:S(2)}) collective-permute-start(f32[256,1024]{1,0:T(8,128)S(1)} %convolution_add_fusion), channel_id=1, source_target_pairs={{0,8},{8,0},{1,9},{9,1},{2,10},{10,2},{3,11},{11,3},{4,12},{12,4},... | collective-permute-start | bytes 3145736 | tf_op jit(solution)/shard_map/ppermute | solution.py:287

commit v12 on v11

--- a/solution.py
+++ b/solution.py
@@ -144,21 +144,19 @@
     for start in range(0, size, BLOCK):
         stop = start + BLOCK
         corner = inverse_factor(work[start:stop, start:stop])
-        lane = lax.broadcasted_iota(jnp.int32, (BLOCK, size), 1)
-        wide = jnp.concatenate(
-            [jnp.zeros((BLOCK, start), jnp.float32)] * (start > 0)
-            + [corner]
-            + [jnp.zeros((BLOCK, size - stop), jnp.float32)] * (stop < size),
-            axis=1,
-        )
-        lines = small_dot(corner, work[start:stop, :], ((1,), (0,)))
-        lines = jnp.where((lane >= start) & (lane < stop), wide, lines)
-        out_ref[start:stop, :] = jnp.where(lane < stop, lines, 0.0) * root
-        if stop < size:
+        rest = stop < size
+        if rest:
+            right = small_dot(corner, work[start:stop, stop:], ((1,), (0,)))
             factor = small_dot(work[stop:, start:stop], corner, ((1,), (1,)))
-            lane = lax.broadcasted_iota(jnp.int32, (size - stop, size), 1)
-            old = jnp.where((lane >= start) & (lane < stop), 0.0, work[stop:, :])
-            work[stop:, :] = old - small_dot(factor, lines, ((1,), (0,)))
+            work[stop:, stop:] = work[stop:, stop:] - small_dot(factor, right, ((1,), (0,)))
+            work[stop:, start:stop] = -small_dot(factor, corner, ((1,), (0,)))
+            out_ref[start:stop, stop:] = jnp.zeros((BLOCK, size - stop), jnp.float32)
+        out_ref[start:stop, start:stop] = corner * root
+        if start > 0:
+            left = small_dot(corner, work[start:stop, :start], ((1,), (0,)))
+            out_ref[start:stop, :start] = left * root
+            if rest:
+                work[stop:, :start] = work[stop:, :start] - small_dot(factor, left, ((1,), (0,)))
 
 
 def inverse_cholesky(gram, far):

time: 75.1 us -> 74.8 us (level)
  no operation moved by 1% of the time
where the time goes in v12:
time: 74.8 us; the launch traced here: 74.4 us
  matrix products  23.8 us (32%)
  starting transfers between devices  21 us (28%)
  waiting for transfers between devices  19.3 us (26%)
  Pallas kernels  9.52 us (13%)
    ppermute x12, waiting for transfers between devices, send(): return lax.ppermute(x, ('rows', 'cols'), targets)  18.5 us
    ppermute x12, starting transfers between devices, send(): return lax.ppermute(x, ('rows', 'cols'), targets)  16.1 us
    dot_general x12, matrix products, inner_rows(): lax.dot_general(left, right, (((0,), (0,)), ((), ())), precision=HIGH, pr...  11.9 us
    dot_general x5, matrix products, matmul(): jnp.dot(rows, weights, precision=HIGH, preferred_element_type=jnp.float32)  10.7 us
    pallas_call x1, Pallas kernels, inverse_cholesky(): pl.pallas_call(factor_kernel, out_shape=jax.ShapeDtypeStruct(gram.shape,...  7.29 us
    ppermute x3, starting transfers between devices, placed(): arriving[k] = lax.ppermute(image, ('rows', 'cols'), outer[k])  4.71 us
    pallas_call x1, Pallas kernels, sketched(): pl.pallas_call(sketch_kernel, out_shape=[jax.ShapeDtypeStruct((length, ra...  2.22 us
  transfers between devices with their start and end apart: 17, of which 7 were waited for; matrix products, arithmetic and copies ran while one was open for 30% of the time, Pallas kernels for 10%

profile of v12, /device:TPU:0, one launch (start us, length us, event | category | flops | bytes accessed | tf_op | source)
XLA Modules:
  0.0 74.4 jit_solution(9314781110081496604)
XLA Ops:
  0.0 2.2 %shard_map.28 = f32[256,256]{1,0:T(8,128)S(1)} custom-call(s32[1]{0:T(128)} %bitcast.starts_ref, f32[2048,1024]{1,0:T(8,128)} %texture_ref.1, f32[1024,256]{1,0:T(8,128)} %sketch_ref.1), custom_call_target="tpu_custom_call" | custom-call | flops 402653184 | bytes 2097152 | tf_op jit(solution)/shard_map/pallas_call | solution.py:57
  2.2 3.0 %collective-permute-start = (f32[256,256]{1,0:T(8,128)S(1)}, f32[256,256]{1,0:T(8,128)S(1)}, u32[]{:S(2)}, u32[]{:S(2)}) collective-permute-start(f32[256,256]{1,0:T(8,128)S(1)} %shard_map.28), channel_id=1, source_target_pairs={{0,1},{1,0},{2,3},{3,2},{4,5},{5,4},{6,7},{7,6},{8,10},{9,11},{10,... | collective-permute-start | bytes 786440 | tf_op jit(solution)/shard_map/ppermute | solution.py:214
  5.3 2.6 %fusion.6 = f32[512,256]{1,0:T(8,128)S(1)} fusion(f32[1024,256]{1,0:T(8,128)S(1)} %copy-done, f32[2048,1024]{1,0:T(8,128)} %texture_ref.1, s32[]{:T(128)S(6)} %select_n.75), kind=kOutput, calls=%fused_computation.6 | convolution fusion | flops 805306368 | bytes 3670020 | tf_op jit(solution)/shard_map/dot_general | solution.py:227
  8.0 1.8 %fusion.25 = f32[256,256]{1,0:T(8,128)S(1)} fusion(f32[1024,256]{1,0:T(8,128)S(1)} %copy-done, f32[2048,1024]{1,0:T(8,128)} %texture_ref.1, s32[]{:T(128)S(6)} %select_n.74), kind=kOutput, calls=%fused_computation.29 | convolution fusion | flops 402653184 | bytes 2359300 | tf_op jit(solution)/shard_map/dot_general | solution.py:227
  9.9 2.1 %collective-permute-start.1 = (f32[128,256]{1,0:T(8,128)S(1)}, f32[128,256]{1,0:T(8,128)S(1)}, u32[]{:S(2)}, u32[]{:S(2)}) collective-permute-start(f32[128,256]{1,0:T(8,128)S(1)} %constant_dynamic-slice_fusion.2), channel_id=1, source_target_pairs={{0,2},{1,3},{2,0},{3,1},{4,6},{5,7},{6,4},{7,5},{8,9},{9,8},{10,11... | collective-permute-start | bytes 393224 | tf_op jit(solution)/shard_map/ppermute | solution.py:198
  12.0 1.8 %fusion.21 = f32[256,256]{1,0:T(8,128)S(1)} fusion(f32[1024,256]{1,0:T(8,128)S(1)} %copy-done, f32[2048,1024]{1,0:T(8,128)} %texture_ref.1, s32[]{:T(128)S(6)} %select_n.79), kind=kOutput, calls=%fused_computation.25 | convolution fusion | flops 402653184 | bytes 2359300 | tf_op jit(solution)/shard_map/dot_general | solution.py:227
  13.8 1.6 %collective-permute-start.4 = (f32[256,256]{1,0:T(8,128)S(1)}, f32[256,256]{1,0:T(8,128)S(1)}, u32[]{:S(2)}, u32[]{:S(2)}) collective-permute-start(f32[256,256]{1,0:T(8,128)S(1)} %fusion.21), channel_id=1, source_target_pairs={{0,1},{1,0},{2,3},{3,2},{4,5},{5,4},{6,7},{7,6},{8,10},{9,11},{10,... | collective-permute-start | bytes 786440 | tf_op jit(solution)/shard_map/ppermute | solution.py:214
  15.4 2.6 %fusion.2 = f32[512,256]{1,0:T(8,128)S(1)} fusion(f32[1024,256]{1,0:T(8,128)S(1)} %copy-done, f32[2048,1024]{1,0:T(8,128)} %texture_ref.1, s32[]{:T(128)S(6)} %select_n.78), kind=kOutput, calls=%fused_computation.2 | convolution fusion | flops 805306368 | bytes 3670020 | tf_op jit(solution)/shard_map/dot_general | solution.py:227
  18.1 2.7 %collective-permute-start.2 = (f32[128,256]{1,0:T(8,128)S(1)}, f32[128,256]{1,0:T(8,128)S(1)}, u32[]{:S(2)}, u32[]{:S(2)}) collective-permute-start(f32[128,256]{1,0:T(8,128)S(1)} %dynamic-slice_add_fusion.2), channel_id=1, source_target_pairs={{0,4},{1,5},{2,6},{3,7},{4,0},{5,1},{6,2},{7,3},{8,12},{9,13},{10,... | collective-permute-start | bytes 393224 | tf_op jit(solution)/shard_map/ppermute | solution.py:198
  21.3 1.8 %fusion.18 = f32[256,256]{1,0:T(8,128)S(1)} fusion(f32[1024,256]{1,0:T(8,128)S(1)} %copy-done, f32[2048,1024]{1,0:T(8,128)} %texture_ref.1, s32[]{:T(128)S(6)} %select_n.80), kind=kOutput, calls=%fused_computation.22 | convolution fusion | flops 402653184 | bytes 2359300 | tf_op jit(solution)/shard_map/dot_general | solution.py:227
  23.2 1.6 %collective-permute-start.8 = (f32[128,256]{1,0:T(8,128)S(1)}, f32[128,256]{1,0:T(8,128)S(1)}, u32[]{:S(2)}, u32[]{:S(2)}) collective-permute-start(f32[128,256]{1,0:T(8,128)S(1)} %constant_dynamic-slice_fusion), channel_id=1, source_target_pairs={{0,2},{1,3},{2,0},{3,1},{4,6},{5,7},{6,4},{7,5},{8,9},{9,8},{10,11... | collective-permute-start | bytes 393224 | tf_op jit(solution)/shard_map/ppermute | solution.py:198
  24.9 1.4 %collective-permute-done.2 = f32[128,256]{1,0:T(8,128)S(1)} collective-permute-done((f32[128,256]{1,0:T(8,128)S(1)}, f32[128,256]{1,0:T(8,128)S(1)}, u32[]{:S(2)}, u32[]{:S(2)}) %collective-permute-start.2) | collective-permute-done | bytes 131104 | tf_op jit(solution)/shard_map/ppermute | solution.py:198
  26.3 2.7 %collective-permute-done.6 = f32[256,256]{1,0:T(8,128)S(1)} collective-permute-done((f32[256,256]{1,0:T(8,128)S(1)}, f32[256,256]{1,0:T(8,128)S(1)}, u32[]{:S(2)}, u32[]{:S(2)}) %collective-permute-start.6) | collective-permute-done | bytes 262176 | tf_op jit(solution)/shard_map/ppermute | solution.py:198
  29.2 1.3 %collective-permute-start.5 = (f32[128,256]{1,0:T(8,128)S(1)}, f32[128,256]{1,0:T(8,128)S(1)}, u32[]{:S(2)}, u32[]{:S(2)}) collective-permute-start(f32[128,256]{1,0:T(8,128)S(1)} %add.140), channel_id=1, source_target_pairs={{0,2},{1,3},{2,0},{3,1},{4,6},{5,7},{6,4},{7,5},{8,9},{9,8},{10,11... | collective-permute-start | bytes 393224 | tf_op jit(solution)/shard_map/ppermute | solution.py:198
  31.4 8.2 %collective-permute-done.7 = f32[256,256]{1,0:T(8,128)S(1)} collective-permute-done((f32[256,256]{1,0:T(8,128)S(1)}, f32[256,256]{1,0:T(8,128)S(1)}, u32[]{:S(2)}, u32[]{:S(2)}) %collective-permute-start.7) | collective-permute-done | bytes 262176 | tf_op jit(solution)/shard_map/ppermute | solution.py:198
  40.3 3.7 %collective-permute-start.11 = (f32[256,256]{1,0:T(8,128)S(1)}, f32[256,256]{1,0:T(8,128)S(1)}, u32[]{:S(2)}, u32[]{:S(2)}) collective-permute-start(f32[256,256]{1,0:T(8,128)S(1)} %add.144), channel_id=1, source_target_pairs={{0,2},{1,3},{2,0},{3,1},{4,6},{5,7},{6,4},{7,5},{8,9},{9,8},{10,11... | collective-permute-start | bytes 786440 | tf_op jit(solution)/shard_map/ppermute | solution.py:198
  44.0 3.3 %collective-permute-done.9 = f32[256,256]{1,0:T(8,128)S(1)} collective-permute-done((f32[256,256]{1,0:T(8,128)S(1)}, f32[256,256]{1,0:T(8,128)S(1)}, u32[]{:S(2)}, u32[]{:S(2)}) %collective-permute-start.9) | collective-permute-done | bytes 262176 | tf_op jit(solution)/shard_map/ppermute | solution.py:198
  47.3 1.9 %fusion.23 = f32[256,1024]{1,0:T(8,128)S(1)} fusion(f32[256,256]{1,0:T(8,128)S(1)} %maximum_select_fusion.1, f32[2048,1024]{1,0:T(8,128)} %texture_ref.1, s32[]{:T(128)S(6)} %select_n.74), kind=kOutput, calls=%fused_computation.27 | convolution fusion | flops 402653184 | bytes 2359300 | tf_op jit(solution)/shard_map/dot_general | solution.py:75
  49.6 1.2 %collective-permute-start.12 = (f32[128,256]{1,0:T(8,128)S(1)}, f32[128,256]{1,0:T(8,128)S(1)}, u32[]{:S(2)}, u32[]{:S(2)}) collective-permute-start(f32[128,256]{1,0:T(8,128)S(1)} %add.145), channel_id=1, source_target_pairs={{0,2},{1,3},{2,0},{3,1},{4,6},{5,7},{6,4},{7,5},{8,9},{9,8},{10,11... | collective-permute-start | bytes 393224 | tf_op jit(solution)/shard_map/ppermute | solution.py:198
  51.9 1.9 %convolution_add_fusion.2 = f32[256,1024]{1,0:T(8,128)S(1)} fusion(f32[256,1024]{1,0:T(8,128)S(1)} %fusion.23, f32[256,256]{1,0:T(8,128)S(1)} %collective-permute-done.9, f32[2048,1024]{1,0:T(8,128)} %texture_ref.1, s32[]{:T(128)S(6)} %select_n.86), kind=kOutput, calls=%fused_computation.12 | convolution fusion | flops 402915328 | bytes 3407876 | tf_op jit(solution)/shard_map/dot_general | solution.py:75
  54.2 1.9 %collective-permute-done.12 = f32[128,256]{1,0:T(8,128)S(1)} collective-permute-done((f32[128,256]{1,0:T(8,128)S(1)}, f32[128,256]{1,0:T(8,128)S(1)}, u32[]{:S(2)}, u32[]{:S(2)}) %collective-permute-start.12) | collective-permute-done | bytes 131104 | tf_op jit(solution)/shard_map/ppermute | solution.py:198
  56.1 1.2 %collective-permute-start.14 = (f32[256,256]{1,0:T(8,128)S(1)}, f32[256,256]{1,0:T(8,128)S(1)}, u32[]{:S(2)}, u32[]{:S(2)}) collective-permute-start(f32[256,256]{1,0:T(8,128)S(1)} %maximum_select_fusion.2), channel_id=1, source_target_pairs={{0,1},{1,0},{2,3},{3,2},{4,5},{5,4},{6,7},{7,6},{8,10},{9,11},{10,... | collective-permute-start | bytes 786440 | tf_op jit(solution)/shard_map/ppermute | solution.py:198
  57.9 2.7 %fusion.11 = f32[256,1024]{1,0:T(8,128)S(1)} fusion(f32[256,1024]{1,0:T(8,128)S(1)} %convolution_add_fusion.2, f32[512,256]{1,0:T(8,128)S(1)} %maximum_select_fusion, f32[2048,1024]{1,0:T(8,128)} %texture_ref.1, s32[]{:T(128)S(6)} %select_n.78), kind=kOutput, calls=%fused_computation.9 | convolution fusion | flops 805568512 | bytes 4718596 | tf_op jit(solution)/shard_map/dot_general | solution.py:75
  65.9 7.3 %shard_map.29 = f32[256,256]{1,0:T(8,128)S(1)} custom-call(f32[256,256]{1,0:T(8,128)S(1)} %convolution_add_fusion.3.gram_ref, f32[256,256]{1,0:T(8,128)S(1)} %collective-permute-done.15.far_ref), custom_call_target="tpu_custom_call" | custom-call | flops 1000 | bytes 1000 | tf_op jit(solution)/shard_map/pallas_call | solution.py:164
  (52 shorter events, 11.4 us)
Async XLA Ops:
  0.0 5.3 %copy-start = (f32[1024,256]{1,0:T(8,128)S(1)}, f32[1024,256]{1,0:T(8,128)}, u32[]{:S(2)}) copy-start(f32[1024,256]{1,0:T(8,128)} %sketch_ref.1) | copy-start | bytes 3145732
  2.2 7.6 %collective-permute-start = (f32[256,256]{1,0:T(8,128)S(1)}, f32[256,256]{1,0:T(8,128)S(1)}, u32[]{:S(2)}, u32[]{:S(2)}) collective-permute-start(f32[256,256]{1,0:T(8,128)S(1)} %shard_map.28), channel_id=1, source_target_pairs={{0,1},{1,0},{2,3},{3,2},{4,5},{5,4},{6,7},{7,6},{8,10},{9,11},{10,... | collective-permute-start | bytes 786440 | tf_op jit(solution)/shard_map/ppermute | solution.py:214
  7.9 12.8 %collective-permute-start.3 = (f32[512,256]{1,0:T(8,128)S(1)}, f32[512,256]{1,0:T(8,128)S(1)}, u32[]{:S(2)}, u32[]{:S(2)}) collective-permute-start(f32[512,256]{1,0:T(8,128)S(1)} %fusion.6), channel_id=1, source_target_pairs={{0,1},{1,0},{2,3},{3,2},{4,5},{5,4},{6,7},{7,6},{8,10},{9,11},{10,... | collective-permute-start | bytes 1572872 | tf_op jit(solution)/shard_map/ppermute | solution.py:214
  9.9 8.1 %collective-permute-start.1 = (f32[128,256]{1,0:T(8,128)S(1)}, f32[128,256]{1,0:T(8,128)S(1)}, u32[]{:S(2)}, u32[]{:S(2)}) collective-permute-start(f32[128,256]{1,0:T(8,128)S(1)} %constant_dynamic-slice_fusion.2), channel_id=1, source_target_pairs={{0,2},{1,3},{2,0},{3,1},{4,6},{5,7},{6,4},{7,5},{8,9},{9,8},{10,11... | collective-permute-start | bytes 393224 | tf_op jit(solution)/shard_map/ppermute | solution.py:198
  13.8 9.3 %collective-permute-start.4 = (f32[256,256]{1,0:T(8,128)S(1)}, f32[256,256]{1,0:T(8,128)S(1)}, u32[]{:S(2)}, u32[]{:S(2)}) collective-permute-start(f32[256,256]{1,0:T(8,128)S(1)} %fusion.21), channel_id=1, source_target_pairs={{0,1},{1,0},{2,3},{3,2},{4,5},{5,4},{6,7},{7,6},{8,10},{9,11},{10,... | collective-permute-start | bytes 786440 | tf_op jit(solution)/shard_map/ppermute | solution.py:214
  18.1 8.3 %collective-permute-start.2 = (f32[128,256]{1,0:T(8,128)S(1)}, f32[128,256]{1,0:T(8,128)S(1)}, u32[]{:S(2)}, u32[]{:S(2)}) collective-permute-start(f32[128,256]{1,0:T(8,128)S(1)} %dynamic-slice_add_fusion.2), channel_id=1, source_target_pairs={{0,4},{1,5},{2,6},{3,7},{4,0},{5,1},{6,2},{7,3},{8,12},{9,13},{10,... | collective-permute-start | bytes 393224 | tf_op jit(solution)/shard_map/ppermute | solution.py:198
  20.8 8.2 %collective-permute-start.6 = (f32[256,256]{1,0:T(8,128)S(1)}, f32[256,256]{1,0:T(8,128)S(1)}, u32[]{:S(2)}, u32[]{:S(2)}) collective-permute-start(f32[256,256]{1,0:T(8,128)S(1)} %constant_dynamic-slice_fusion.1), channel_id=1, source_target_pairs={{0,2},{1,3},{2,0},{3,1},{4,6},{5,7},{6,4},{7,5},{8,9},{9,8},{10,11... | collective-permute-start | bytes 786440 | tf_op jit(solution)/shard_map/ppermute | solution.py:198
  23.2 8.2 %collective-permute-start.8 = (f32[128,256]{1,0:T(8,128)S(1)}, f32[128,256]{1,0:T(8,128)S(1)}, u32[]{:S(2)}, u32[]{:S(2)}) collective-permute-start(f32[128,256]{1,0:T(8,128)S(1)} %constant_dynamic-slice_fusion), channel_id=1, source_target_pairs={{0,2},{1,3},{2,0},{3,1},{4,6},{5,7},{6,4},{7,5},{8,9},{9,8},{10,11... | collective-permute-start | bytes 393224 | tf_op jit(solution)/shard_map/ppermute | solution.py:198
  29.1 10.6 %collective-permute-start.7 = (f32[256,256]{1,0:T(8,128)S(1)}, f32[256,256]{1,0:T(8,128)S(1)}, u32[]{:S(2)}, u32[]{:S(2)}) collective-permute-start(f32[256,256]{1,0:T(8,128)S(1)} %dynamic-slice_add_fusion), channel_id=1, source_target_pairs={{0,4},{1,5},{2,6},{3,7},{4,0},{5,1},{6,2},{7,3},{8,12},{9,13},{10,... | collective-permute-start | bytes 786440 | tf_op jit(solution)/shard_map/ppermute | solution.py:198
  29.2 10.5 %collective-permute-start.5 = (f32[128,256]{1,0:T(8,128)S(1)}, f32[128,256]{1,0:T(8,128)S(1)}, u32[]{:S(2)}, u32[]{:S(2)}) collective-permute-start(f32[128,256]{1,0:T(8,128)S(1)} %add.140), channel_id=1, source_target_pairs={{0,2},{1,3},{2,0},{3,1},{4,6},{5,7},{6,4},{7,5},{8,9},{9,8},{10,11... | collective-permute-start | bytes 393224 | tf_op jit(solution)/shard_map/ppermute | solution.py:198
  39.8 7.5 %collective-permute-start.9 = (f32[256,256]{1,0:T(8,128)S(1)}, f32[256,256]{1,0:T(8,128)S(1)}, u32[]{:S(2)}, u32[]{:S(2)}) collective-permute-start(f32[256,256]{1,0:T(8,128)S(1)} %maximum_select_fusion.1), channel_id=1, source_target_pairs={{0,1},{1,0},{2,3},{3,2},{4,5},{5,4},{6,7},{7,6},{8,10},{9,11},{10,... | collective-permute-start | bytes 786440 | tf_op jit(solution)/shard_map/ppermute | solution.py:198
  40.3 20.9 %slice-start = ((s8[8388608]{0:T(1024)(128)(4,1)}), s8[4194304]{0:T(1024)(128)(4,1)S(1)}, s32[]{:S(2)}) async-start(s8[8388608]{0:T(1024)(128)(4,1)} %bitcast.24), calls=%async_computation | async-start | bytes 8388608
  40.3 9.3 %collective-permute-start.10 = (f32[128,256]{1,0:T(8,128)S(1)}, f32[128,256]{1,0:T(8,128)S(1)}, u32[]{:S(2)}, u32[]{:S(2)}) collective-permute-start(f32[128,256]{1,0:T(8,128)S(1)} %dynamic-slice_add_fusion.1), channel_id=1, source_target_pairs={{0,4},{1,5},{2,6},{3,7},{4,0},{5,1},{6,2},{7,3},{8,12},{9,13},{10,... | collective-permute-start | bytes 393224 | tf_op jit(solution)/shard_map/ppermute | solution.py:198
  40.3 9.2 %collective-permute-start.11 = (f32[256,256]{1,0:T(8,128)S(1)}, f32[256,256]{1,0:T(8,128)S(1)}, u32[]{:S(2)}, u32[]{:S(2)}) collective-permute-start(f32[256,256]{1,0:T(8,128)S(1)} %add.144), channel_id=1, source_target_pairs={{0,2},{1,3},{2,0},{3,1},{4,6},{5,7},{6,4},{7,5},{8,9},{9,8},{10,11... | collective-permute-start | bytes 786440 | tf_op jit(solution)/shard_map/ppermute | solution.py:198
  49.6 6.5 %collective-permute-start.12 = (f32[128,256]{1,0:T(8,128)S(1)}, f32[128,256]{1,0:T(8,128)S(1)}, u32[]{:S(2)}, u32[]{:S(2)}) collective-permute-start(f32[128,256]{1,0:T(8,128)S(1)} %add.145), channel_id=1, source_target_pairs={{0,2},{1,3},{2,0},{3,1},{4,6},{5,7},{6,4},{7,5},{8,9},{9,8},{10,11... | collective-permute-start | bytes 393224 | tf_op jit(solution)/shard_map/ppermute | solution.py:198
  50.8 9.8 %collective-permute-start.13 = (f32[512,256]{1,0:T(8,128)S(1)}, f32[512,256]{1,0:T(8,128)S(1)}, u32[]{:S(2)}, u32[]{:S(2)}) collective-permute-start(f32[512,256]{1,0:T(8,128)S(1)} %maximum_select_fusion), channel_id=1, source_target_pairs={{0,1},{1,0},{2,3},{3,2},{4,5},{5,4},{6,7},{7,6},{8,10},{9,11},{10,... | collective-permute-start | bytes 1572872 | tf_op jit(solution)/shard_map/ppermute | solution.py:198
  53.8 7.5 %slice-start.1 = ((s8[8388608]{0:T(1024)(128)(4,1)}), s8[4194304]{0:T(1024)(128)(4,1)S(1)}, s32[]{:S(2)}) async-start(s8[8388608]{0:T(1024)(128)(4,1)} %bitcast.24), calls=%async_computation.1 | async-start | bytes 8388608
  56.1 7.6 %collective-permute-start.14 = (f32[256,256]{1,0:T(8,128)S(1)}, f32[256,256]{1,0:T(8,128)S(1)}, u32[]{:S(2)}, u32[]{:S(2)}) collective-permute-start(f32[256,256]{1,0:T(8,128)S(1)} %maximum_select_fusion.2), channel_id=1, source_target_pairs={{0,1},{1,0},{2,3},{3,2},{4,5},{5,4},{6,7},{7,6},{8,10},{9,11},{10,... | collective-permute-start | bytes 786440 | tf_op jit(solution)/shard_map/ppermute | solution.py:198
  64.1 1.6 %collective-permute-start.15 = (f32[256,256]{1,0:T(8,128)S(1)}, f32[256,256]{1,0:T(8,128)S(1)}, u32[]{:S(2)}, u32[]{:S(2)}) collective-permute-start(f32[256,256]{1,0:T(8,128)S(1)} %convolution_add_fusion.3.gram_ref), channel_id=1, source_target_pairs={{0,8},{8,0},{1,9},{9,1},{2,10},{10,2},{3,11},{11,3},{4,12},{12,4},... | collective-permute-start | bytes 786440 | tf_op jit(solution)/shard_map/ppermute | solution.py:282
  65.7 7.4 %collective-permute-start.16 = (f32[256,1024]{1,0:T(8,128)S(1)}, f32[256,1024]{1,0:T(8,128)S(1)}, u32[]{:S(2)}, u32[]{:S(2)}) collective-permute-start(f32[256,1024]{1,0:T(8,128)S(1)} %convolution_add_fusion), channel_id=1, source_target_pairs={{0,8},{8,0},{1,9},{9,1},{2,10},{10,2},{3,11},{11,3},{4,12},{12,4},... | collective-permute-start | bytes 3145736 | tf_op jit(solution)/shard_map/ppermute | solution.py:285

commit v13 on v12

--- a/solution.py
+++ b/solution.py
@@ -13,7 +13,7 @@
 CROSSED = (True, True, True)
 STEPS = [("s", 0, True), ("m", 1, True), ("m", 0, False), ("i", 0), ("m", 2, True), ("m", 1, False), ("l", 0), ("i", 1)]
 STEPS += [("m", 2, False), ("i", 2), ("b", 0), ("l", 1), ("l", 2), ("b", 1), ("o", 0), ("w", 0), ("g", 0), ("o", 1), ("b", 2), ("f", 0), ("o", 2)]
-STEPS += [("g", 1), ("f", 1), ("g", 2), ("f", 2)]
+STEPS += [("g", 1), ("g", 2), ("f", 1), ("f", 2)]
 BLOCK = 128
 TILE = 8
 LIGHT = pl.CostEstimate(flops=1000, bytes_accessed=1000, transcendentals=0)

time: 74.8 us -> 74.8 us (level)
  no operation moved by 1% of the time
where the time goes in v13:
time: 74.8 us; the launch traced here: 74.4 us
  matrix products  23.8 us (32%)
  starting transfers between devices  21 us (28%)
  waiting for transfers between devices  19.3 us (26%)
  Pallas kernels  9.52 us (13%)
    ppermute x12, waiting for transfers between devices, send(): return lax.ppermute(x, ('rows', 'cols'), targets)  18.4 us
    ppermute x12, starting transfers between devices, send(): return lax.ppermute(x, ('rows', 'cols'), targets)  16.1 us
    dot_general x12, matrix products, inner_rows(): lax.dot_general(left, right, (((0,), (0,)), ((), ())), precision=HIGH, pr...  11.9 us
    dot_general x5, matrix products, matmul(): jnp.dot(rows, weights, precision=HIGH, preferred_element_type=jnp.float32)  10.7 us
    pallas_call x1, Pallas kernels, inverse_cholesky(): pl.pallas_call(factor_kernel, out_shape=jax.ShapeDtypeStruct(gram.shape,...  7.29 us
    ppermute x3, starting transfers between devices, placed(): arriving[k] = lax.ppermute(image, ('rows', 'cols'), outer[k])  4.71 us
    pallas_call x1, Pallas kernels, sketched(): pl.pallas_call(sketch_kernel, out_shape=[jax.ShapeDtypeStruct((length, ra...  2.22 us
  transfers between devices with their start and end apart: 17, of which 7 were waited for; matrix products, arithmetic and copies ran while one was open for 30% of the time, Pallas kernels for 10%

profile of v13, /device:TPU:0, one launch (start us, length us, event | category | flops | bytes accessed | tf_op | source)
XLA Modules:
  0.0 74.4 jit_solution(2344345954284338930)
XLA Ops:
  0.0 2.2 %shard_map.28 = f32[256,256]{1,0:T(8,128)S(1)} custom-call(s32[1]{0:T(128)} %bitcast.starts_ref, f32[2048,1024]{1,0:T(8,128)} %texture_ref.1, f32[1024,256]{1,0:T(8,128)} %sketch_ref.1), custom_call_target="tpu_custom_call" | custom-call | flops 402653184 | bytes 2097152 | tf_op jit(solution)/shard_map/pallas_call | solution.py:57
  2.2 3.0 %collective-permute-start = (f32[256,256]{1,0:T(8,128)S(1)}, f32[256,256]{1,0:T(8,128)S(1)}, u32[]{:S(2)}, u32[]{:S(2)}) collective-permute-start(f32[256,256]{1,0:T(8,128)S(1)} %shard_map.28), channel_id=1, source_target_pairs={{0,1},{1,0},{2,3},{3,2},{4,5},{5,4},{6,7},{7,6},{8,10},{9,11},{10,... | collective-permute-start | bytes 786440 | tf_op jit(solution)/shard_map/ppermute | solution.py:214
  5.3 2.6 %fusion.6 = f32[512,256]{1,0:T(8,128)S(1)} fusion(f32[1024,256]{1,0:T(8,128)S(1)} %copy-done, f32[2048,1024]{1,0:T(8,128)} %texture_ref.1, s32[]{:T(128)S(6)} %select_n.75), kind=kOutput, calls=%fused_computation.6 | convolution fusion | flops 805306368 | bytes 3670020 | tf_op jit(solution)/shard_map/dot_general | solution.py:227
  8.0 1.8 %fusion.25 = f32[256,256]{1,0:T(8,128)S(1)} fusion(f32[1024,256]{1,0:T(8,128)S(1)} %copy-done, f32[2048,1024]{1,0:T(8,128)} %texture_ref.1, s32[]{:T(128)S(6)} %select_n.74), kind=kOutput, calls=%fused_computation.29 | convolution fusion | flops 402653184 | bytes 2359300 | tf_op jit(solution)/shard_map/dot_general | solution.py:227
  9.9 2.1 %collective-permute-start.1 = (f32[128,256]{1,0:T(8,128)S(1)}, f32[128,256]{1,0:T(8,128)S(1)}, u32[]{:S(2)}, u32[]{:S(2)}) collective-permute-start(f32[128,256]{1,0:T(8,128)S(1)} %constant_dynamic-slice_fusion.2), channel_id=1, source_target_pairs={{0,2},{1,3},{2,0},{3,1},{4,6},{5,7},{6,4},{7,5},{8,9},{9,8},{10,11... | collective-permute-start | bytes 393224 | tf_op jit(solution)/shard_map/ppermute | solution.py:198
  12.0 1.8 %fusion.21 = f32[256,256]{1,0:T(8,128)S(1)} fusion(f32[1024,256]{1,0:T(8,128)S(1)} %copy-done, f32[2048,1024]{1,0:T(8,128)} %texture_ref.1, s32[]{:T(128)S(6)} %select_n.79), kind=kOutput, calls=%fused_computation.25 | convolution fusion | flops 402653184 | bytes 2359300 | tf_op jit(solution)/shard_map/dot_general | solution.py:227
  13.8 1.6 %collective-permute-start.4 = (f32[256,256]{1,0:T(8,128)S(1)}, f32[256,256]{1,0:T(8,128)S(1)}, u32[]{:S(2)}, u32[]{:S(2)}) collective-permute-start(f32[256,256]{1,0:T(8,128)S(1)} %fusion.21), channel_id=1, source_target_pairs={{0,1},{1,0},{2,3},{3,2},{4,5},{5,4},{6,7},{7,6},{8,10},{9,11},{10,... | collective-permute-start | bytes 786440 | tf_op jit(solution)/shard_map/ppermute | solution.py:214
  15.4 2.6 %fusion.2 = f32[512,256]{1,0:T(8,128)S(1)} fusion(f32[1024,256]{1,0:T(8,128)S(1)} %copy-done, f32[2048,1024]{1,0:T(8,128)} %texture_ref.1, s32[]{:T(128)S(6)} %select_n.78), kind=kOutput, calls=%fused_computation.2 | convolution fusion | flops 805306368 | bytes 3670020 | tf_op jit(solution)/shard_map/dot_general | solution.py:227
  18.1 2.7 %collective-permute-start.2 = (f32[128,256]{1,0:T(8,128)S(1)}, f32[128,256]{1,0:T(8,128)S(1)}, u32[]{:S(2)}, u32[]{:S(2)}) collective-permute-start(f32[128,256]{1,0:T(8,128)S(1)} %dynamic-slice_add_fusion.2), channel_id=1, source_target_pairs={{0,4},{1,5},{2,6},{3,7},{4,0},{5,1},{6,2},{7,3},{8,12},{9,13},{10,... | collective-permute-start | bytes 393224 | tf_op jit(solution)/shard_map/ppermute | solution.py:198
  21.3 1.8 %fusion.18 = f32[256,256]{1,0:T(8,128)S(1)} fusion(f32[1024,256]{1,0:T(8,128)S(1)} %copy-done, f32[2048,1024]{1,0:T(8,128)} %texture_ref.1, s32[]{:T(128)S(6)} %select_n.80), kind=kOutput, calls=%fused_computation.22 | convolution fusion | flops 402653184 | bytes 2359300 | tf_op jit(solution)/shard_map/dot_general | solution.py:227
  23.2 1.6 %collective-permute-start.8 = (f32[128,256]{1,0:T(8,128)S(1)}, f32[128,256]{1,0:T(8,128)S(1)}, u32[]{:S(2)}, u32[]{:S(2)}) collective-permute-start(f32[128,256]{1,0:T(8,128)S(1)} %constant_dynamic-slice_fusion), channel_id=1, source_target_pairs={{0,2},{1,3},{2,0},{3,1},{4,6},{5,7},{6,4},{7,5},{8,9},{9,8},{10,11... | collective-permute-start | bytes 393224 | tf_op jit(solution)/shard_map/ppermute | solution.py:198
  24.9 1.4 %collective-permute-done.2 = f32[128,256]{1,0:T(8,128)S(1)} collective-permute-done((f32[128,256]{1,0:T(8,128)S(1)}, f32[128,256]{1,0:T(8,128)S(1)}, u32[]{:S(2)}, u32[]{:S(2)}) %collective-permute-start.2) | collective-permute-done | bytes 131104 | tf_op jit(solution)/shard_map/ppermute | solution.py:198
  26.3 2.7 %collective-permute-done.6 = f32[256,256]{1,0:T(8,128)S(1)} collective-permute-done((f32[256,256]{1,0:T(8,128)S(1)}, f32[256,256]{1,0:T(8,128)S(1)}, u32[]{:S(2)}, u32[]{:S(2)}) %collective-permute-start.6) | collective-permute-done | bytes 262176 | tf_op jit(solution)/shard_map/ppermute | solution.py:198
  29.2 1.3 %collective-permute-start.5 = (f32[128,256]{1,0:T(8,128)S(1)}, f32[128,256]{1,0:T(8,128)S(1)}, u32[]{:S(2)}, u32[]{:S(2)}) collective-permute-start(f32[128,256]{1,0:T(8,128)S(1)} %add.140), channel_id=1, source_target_pairs={{0,2},{1,3},{2,0},{3,1},{4,6},{5,7},{6,4},{7,5},{8,9},{9,8},{10,11... | collective-permute-start | bytes 393224 | tf_op jit(solution)/shard_map/ppermute | solution.py:198
  31.4 8.2 %collective-permute-done.7 = f32[256,256]{1,0:T(8,128)S(1)} collective-permute-done((f32[256,256]{1,0:T(8,128)S(1)}, f32[256,256]{1,0:T(8,128)S(1)}, u32[]{:S(2)}, u32[]{:S(2)}) %collective-permute-start.7) | collective-permute-done | bytes 262176 | tf_op jit(solution)/shard_map/ppermute | solution.py:198
  40.3 3.7 %collective-permute-start.11 = (f32[256,256]{1,0:T(8,128)S(1)}, f32[256,256]{1,0:T(8,128)S(1)}, u32[]{:S(2)}, u32[]{:S(2)}) collective-permute-start(f32[256,256]{1,0:T(8,128)S(1)} %add.144), channel_id=1, source_target_pairs={{0,2},{1,3},{2,0},{3,1},{4,6},{5,7},{6,4},{7,5},{8,9},{9,8},{10,11... | collective-permute-start | bytes 786440 | tf_op jit(solution)/shard_map/ppermute | solution.py:198
  44.0 3.3 %collective-permute-done.9 = f32[256,256]{1,0:T(8,128)S(1)} collective-permute-done((f32[256,256]{1,0:T(8,128)S(1)}, f32[256,256]{1,0:T(8,128)S(1)}, u32[]{:S(2)}, u32[]{:S(2)}) %collective-permute-start.9) | collective-permute-done | bytes 262176 | tf_op jit(solution)/shard_map/ppermute | solution.py:198
  47.3 1.9 %fusion.23 = f32[256,1024]{1,0:T(8,128)S(1)} fusion(f32[256,256]{1,0:T(8,128)S(1)} %maximum_select_fusion.1, f32[2048,1024]{1,0:T(8,128)} %texture_ref.1, s32[]{:T(128)S(6)} %select_n.74), kind=kOutput, calls=%fused_computation.27 | convolution fusion | flops 402653184 | bytes 2359300 | tf_op jit(solution)/shard_map/dot_general | solution.py:75
  49.6 1.2 %collective-permute-start.12 = (f32[128,256]{1,0:T(8,128)S(1)}, f32[128,256]{1,0:T(8,128)S(1)}, u32[]{:S(2)}, u32[]{:S(2)}) collective-permute-start(f32[128,256]{1,0:T(8,128)S(1)} %add.145), channel_id=1, source_target_pairs={{0,2},{1,3},{2,0},{3,1},{4,6},{5,7},{6,4},{7,5},{8,9},{9,8},{10,11... | collective-permute-start | bytes 393224 | tf_op jit(solution)/shard_map/ppermute | solution.py:198
  51.9 1.9 %convolution_add_fusion.2 = f32[256,1024]{1,0:T(8,128)S(1)} fusion(f32[256,1024]{1,0:T(8,128)S(1)} %fusion.23, f32[256,256]{1,0:T(8,128)S(1)} %collective-permute-done.9, f32[2048,1024]{1,0:T(8,128)} %texture_ref.1, s32[]{:T(128)S(6)} %select_n.86), kind=kOutput, calls=%fused_computation.12 | convolution fusion | flops 402915328 | bytes 3407876 | tf_op jit(solution)/shard_map/dot_general | solution.py:75
  54.2 1.8 %collective-permute-done.12 = f32[128,256]{1,0:T(8,128)S(1)} collective-permute-done((f32[128,256]{1,0:T(8,128)S(1)}, f32[128,256]{1,0:T(8,128)S(1)}, u32[]{:S(2)}, u32[]{:S(2)}) %collective-permute-start.12) | collective-permute-done | bytes 131104 | tf_op jit(solution)/shard_map/ppermute | solution.py:198
  56.1 1.2 %collective-permute-start.14 = (f32[256,256]{1,0:T(8,128)S(1)}, f32[256,256]{1,0:T(8,128)S(1)}, u32[]{:S(2)}, u32[]{:S(2)}) collective-permute-start(f32[256,256]{1,0:T(8,128)S(1)} %maximum_select_fusion.2), channel_id=1, source_target_pairs={{0,1},{1,0},{2,3},{3,2},{4,5},{5,4},{6,7},{7,6},{8,10},{9,11},{10,... | collective-permute-start | bytes 786440 | tf_op jit(solution)/shard_map/ppermute | solution.py:198
  57.9 2.7 %fusion.11 = f32[256,1024]{1,0:T(8,128)S(1)} fusion(f32[256,1024]{1,0:T(8,128)S(1)} %convolution_add_fusion.2, f32[512,256]{1,0:T(8,128)S(1)} %maximum_select_fusion, f32[2048,1024]{1,0:T(8,128)} %texture_ref.1, s32[]{:T(128)S(6)} %select_n.78), kind=kOutput, calls=%fused_computation.9 | convolution fusion | flops 805568512 | bytes 4718596 | tf_op jit(solution)/shard_map/dot_general | solution.py:75
  65.9 7.3 %shard_map.29 = f32[256,256]{1,0:T(8,128)S(1)} custom-call(f32[256,256]{1,0:T(8,128)S(1)} %convolution_add_fusion.3.gram_ref, f32[256,256]{1,0:T(8,128)S(1)} %collective-permute-done.15.far_ref), custom_call_target="tpu_custom_call" | custom-call | flops 1000 | bytes 1000 | tf_op jit(solution)/shard_map/pallas_call | solution.py:164
  (52 shorter events, 11.4 us)
Async XLA Ops:
  0.0 5.3 %copy-start = (f32[1024,256]{1,0:T(8,128)S(1)}, f32[1024,256]{1,0:T(8,128)}, u32[]{:S(2)}) copy-start(f32[1024,256]{1,0:T(8,128)} %sketch_ref.1) | copy-start | bytes 3145732
  2.2 7.6 %collective-permute-start = (f32[256,256]{1,0:T(8,128)S(1)}, f32[256,256]{1,0:T(8,128)S(1)}, u32[]{:S(2)}, u32[]{:S(2)}) collective-permute-start(f32[256,256]{1,0:T(8,128)S(1)} %shard_map.28), channel_id=1, source_target_pairs={{0,1},{1,0},{2,3},{3,2},{4,5},{5,4},{6,7},{7,6},{8,10},{9,11},{10,... | collective-permute-start | bytes 786440 | tf_op jit(solution)/shard_map/ppermute | solution.py:214
  7.9 12.8 %collective-permute-start.3 = (f32[512,256]{1,0:T(8,128)S(1)}, f32[512,256]{1,0:T(8,128)S(1)}, u32[]{:S(2)}, u32[]{:S(2)}) collective-permute-start(f32[512,256]{1,0:T(8,128)S(1)} %fusion.6), channel_id=1, source_target_pairs={{0,1},{1,0},{2,3},{3,2},{4,5},{5,4},{6,7},{7,6},{8,10},{9,11},{10,... | collective-permute-start | bytes 1572872 | tf_op jit(solution)/shard_map/ppermute | solution.py:214
  9.9 8.1 %collective-permute-start.1 = (f32[128,256]{1,0:T(8,128)S(1)}, f32[128,256]{1,0:T(8,128)S(1)}, u32[]{:S(2)}, u32[]{:S(2)}) collective-permute-start(f32[128,256]{1,0:T(8,128)S(1)} %constant_dynamic-slice_fusion.2), channel_id=1, source_target_pairs={{0,2},{1,3},{2,0},{3,1},{4,6},{5,7},{6,4},{7,5},{8,9},{9,8},{10,11... | collective-permute-start | bytes 393224 | tf_op jit(solution)/shard_map/ppermute | solution.py:198
  13.8 9.3 %collective-permute-start.4 = (f32[256,256]{1,0:T(8,128)S(1)}, f32[256,256]{1,0:T(8,128)S(1)}, u32[]{:S(2)}, u32[]{:S(2)}) collective-permute-start(f32[256,256]{1,0:T(8,128)S(1)} %fusion.21), channel_id=1, source_target_pairs={{0,1},{1,0},{2,3},{3,2},{4,5},{5,4},{6,7},{7,6},{8,10},{9,11},{10,... | collective-permute-start | bytes 786440 | tf_op jit(solution)/shard_map/ppermute | solution.py:214
  18.1 8.3 %collective-permute-start.2 = (f32[128,256]{1,0:T(8,128)S(1)}, f32[128,256]{1,0:T(8,128)S(1)}, u32[]{:S(2)}, u32[]{:S(2)}) collective-permute-start(f32[128,256]{1,0:T(8,128)S(1)} %dynamic-slice_add_fusion.2), channel_id=1, source_target_pairs={{0,4},{1,5},{2,6},{3,7},{4,0},{5,1},{6,2},{7,3},{8,12},{9,13},{10,... | collective-permute-start | bytes 393224 | tf_op jit(solution)/shard_map/ppermute | solution.py:198
  20.8 8.2 %collective-permute-start.6 = (f32[256,256]{1,0:T(8,128)S(1)}, f32[256,256]{1,0:T(8,128)S(1)}, u32[]{:S(2)}, u32[]{:S(2)}) collective-permute-start(f32[256,256]{1,0:T(8,128)S(1)} %constant_dynamic-slice_fusion.1), channel_id=1, source_target_pairs={{0,2},{1,3},{2,0},{3,1},{4,6},{5,7},{6,4},{7,5},{8,9},{9,8},{10,11... | collective-permute-start | bytes 786440 | tf_op jit(solution)/shard_map/ppermute | solution.py:198
  23.2 8.2 %collective-permute-start.8 = (f32[128,256]{1,0:T(8,128)S(1)}, f32[128,256]{1,0:T(8,128)S(1)}, u32[]{:S(2)}, u32[]{:S(2)}) collective-permute-start(f32[128,256]{1,0:T(8,128)S(1)} %constant_dynamic-slice_fusion), channel_id=1, source_target_pairs={{0,2},{1,3},{2,0},{3,1},{4,6},{5,7},{6,4},{7,5},{8,9},{9,8},{10,11... | collective-permute-start | bytes 393224 | tf_op jit(solution)/shard_map/ppermute | solution.py:198
  29.1 10.6 %collective-permute-start.7 = (f32[256,256]{1,0:T(8,128)S(1)}, f32[256,256]{1,0:T(8,128)S(1)}, u32[]{:S(2)}, u32[]{:S(2)}) collective-permute-start(f32[256,256]{1,0:T(8,128)S(1)} %dynamic-slice_add_fusion), channel_id=1, source_target_pairs={{0,4},{1,5},{2,6},{3,7},{4,0},{5,1},{6,2},{7,3},{8,12},{9,13},{10,... | collective-permute-start | bytes 786440 | tf_op jit(solution)/shard_map/ppermute | solution.py:198
  29.2 10.5 %collective-permute-start.5 = (f32[128,256]{1,0:T(8,128)S(1)}, f32[128,256]{1,0:T(8,128)S(1)}, u32[]{:S(2)}, u32[]{:S(2)}) collective-permute-start(f32[128,256]{1,0:T(8,128)S(1)} %add.140), channel_id=1, source_target_pairs={{0,2},{1,3},{2,0},{3,1},{4,6},{5,7},{6,4},{7,5},{8,9},{9,8},{10,11... | collective-permute-start | bytes 393224 | tf_op jit(solution)/shard_map/ppermute | solution.py:198
  39.8 7.5 %collective-permute-start.9 = (f32[256,256]{1,0:T(8,128)S(1)}, f32[256,256]{1,0:T(8,128)S(1)}, u32[]{:S(2)}, u32[]{:S(2)}) collective-permute-start(f32[256,256]{1,0:T(8,128)S(1)} %maximum_select_fusion.1), channel_id=1, source_target_pairs={{0,1},{1,0},{2,3},{3,2},{4,5},{5,4},{6,7},{7,6},{8,10},{9,11},{10,... | collective-permute-start | bytes 786440 | tf_op jit(solution)/shard_map/ppermute | solution.py:198
  40.3 20.7 %slice-start = ((s8[8388608]{0:T(1024)(128)(4,1)}), s8[4194304]{0:T(1024)(128)(4,1)S(1)}, s32[]{:S(2)}) async-start(s8[8388608]{0:T(1024)(128)(4,1)} %bitcast.24), calls=%async_computation | async-start | bytes 8388608
  40.3 9.3 %collective-permute-start.10 = (f32[128,256]{1,0:T(8,128)S(1)}, f32[128,256]{1,0:T(8,128)S(1)}, u32[]{:S(2)}, u32[]{:S(2)}) collective-permute-start(f32[128,256]{1,0:T(8,128)S(1)} %dynamic-slice_add_fusion.1), channel_id=1, source_target_pairs={{0,4},{1,5},{2,6},{3,7},{4,0},{5,1},{6,2},{7,3},{8,12},{9,13},{10,... | collective-permute-start | bytes 393224 | tf_op jit(solution)/shard_map/ppermute | solution.py:198
  40.3 9.2 %collective-permute-start.11 = (f32[256,256]{1,0:T(8,128)S(1)}, f32[256,256]{1,0:T(8,128)S(1)}, u32[]{:S(2)}, u32[]{:S(2)}) collective-permute-start(f32[256,256]{1,0:T(8,128)S(1)} %add.144), channel_id=1, source_target_pairs={{0,2},{1,3},{2,0},{3,1},{4,6},{5,7},{6,4},{7,5},{8,9},{9,8},{10,11... | collective-permute-start | bytes 786440 | tf_op jit(solution)/shard_map/ppermute | solution.py:198
  49.6 6.5 %collective-permute-start.12 = (f32[128,256]{1,0:T(8,128)S(1)}, f32[128,256]{1,0:T(8,128)S(1)}, u32[]{:S(2)}, u32[]{:S(2)}) collective-permute-start(f32[128,256]{1,0:T(8,128)S(1)} %add.145), channel_id=1, source_target_pairs={{0,2},{1,3},{2,0},{3,1},{4,6},{5,7},{6,4},{7,5},{8,9},{9,8},{10,11... | collective-permute-start | bytes 393224 | tf_op jit(solution)/shard_map/ppermute | solution.py:198
  50.8 10.9 %collective-permute-start.13 = (f32[512,256]{1,0:T(8,128)S(1)}, f32[512,256]{1,0:T(8,128)S(1)}, u32[]{:S(2)}, u32[]{:S(2)}) collective-permute-start(f32[512,256]{1,0:T(8,128)S(1)} %maximum_select_fusion), channel_id=1, source_target_pairs={{0,1},{1,0},{2,3},{3,2},{4,5},{5,4},{6,7},{7,6},{8,10},{9,11},{10,... | collective-permute-start | bytes 1572872 | tf_op jit(solution)/shard_map/ppermute | solution.py:198
  53.8 7.2 %slice-start.1 = ((s8[8388608]{0:T(1024)(128)(4,1)}), s8[4194304]{0:T(1024)(128)(4,1)S(1)}, s32[]{:S(2)}) async-start(s8[8388608]{0:T(1024)(128)(4,1)} %bitcast.24), calls=%async_computation.1 | async-start | bytes 8388608
  56.1 7.6 %collective-permute-start.14 = (f32[256,256]{1,0:T(8,128)S(1)}, f32[256,256]{1,0:T(8,128)S(1)}, u32[]{:S(2)}, u32[]{:S(2)}) collective-permute-start(f32[256,256]{1,0:T(8,128)S(1)} %maximum_select_fusion.2), channel_id=1, source_target_pairs={{0,1},{1,0},{2,3},{3,2},{4,5},{5,4},{6,7},{7,6},{8,10},{9,11},{10,... | collective-permute-start | bytes 786440 | tf_op jit(solution)/shard_map/ppermute | solution.py:198
  64.1 1.6 %collective-permute-start.15 = (f32[256,256]{1,0:T(8,128)S(1)}, f32[256,256]{1,0:T(8,128)S(1)}, u32[]{:S(2)}, u32[]{:S(2)}) collective-permute-start(f32[256,256]{1,0:T(8,128)S(1)} %convolution_add_fusion.3.gram_ref), channel_id=1, source_target_pairs={{0,8},{8,0},{1,9},{9,1},{2,10},{10,2},{3,11},{11,3},{4,12},{12,4},... | collective-permute-start | bytes 786440 | tf_op jit(solution)/shard_map/ppermute | solution.py:282
  65.7 7.4 %collective-permute-start.16 = (f32[256,1024]{1,0:T(8,128)S(1)}, f32[256,1024]{1,0:T(8,128)S(1)}, u32[]{:S(2)}, u32[]{:S(2)}) collective-permute-start(f32[256,1024]{1,0:T(8,128)S(1)} %convolution_add_fusion), channel_id=1, source_target_pairs={{0,8},{8,0},{1,9},{9,1},{2,10},{10,2},{3,11},{11,3},{4,12},{12,4},... | collective-permute-start | bytes 3145736 | tf_op jit(solution)/shard_map/ppermute | solution.py:285
